TPU v7x, 256 devices: a whole 4x4x8 slice. The times are simulated.
256 devices in a mesh: elem: 64 (over y, z, core), dir: 4 (over x).
Axes of the slice: x: 4, y: 4, z: 8, core: 2. Of those that a mesh axis runs over, the one named last changes fastest.
Arguments:
- history: bfloat16 [8, 32, 24576], P(None, 'dir', 'elem'), may hold values from -6 to 6
- incident: bfloat16 [2, 32, 24576], P(None, 'dir', 'elem'), may hold values from -6 to 6
- ztiles: bfloat16 [192, 32, 128, 128], P('elem'), may hold values from -0.09375 to 0.09375
- zinv: bfloat16 [192, 128, 128], P('elem'), may hold values from -0.5 to 0.5
- columns: int32 [192, 32], P('elem'), may hold values from 0 to 191, as said below
- lags: int32 [192, 32], P('elem'), may hold values from 1 to 8
- counts: int32 [192], P('elem'), may hold values from 8 to 32
- basis: bfloat16 [24576, 256], P('elem'), may hold values from -0.109375 to 0.109375
Outputs:
- densities: bfloat16 [2, 32, 24576], P(None, 'dir', 'elem')
- far_field: float32 [2, 32, 256], P(None, 'dir', 'elem')
Inputs may be any that keep to these rules, and one draw needn't show every extreme that they name: A block row's slots at or beyond counts are unused; a source block may repeat within a row. `columns`: all slots, used or not, of the block rows of one index of elem name blocks whose panels lie on any one index of elem at most 4 times, and exactly 4 times for some index.
All inputs are finite; a program needn't handle non-finite values.
Results may differ from a plain program's by a relative error of at most 0.005.
Values may be sent and summed in bfloat16 or wider, within the bound.
No kernel may reach another device: no remote copies, remote signals or barrier semaphores. Data moves between devices by JAX's collectives and lax.ppermute only.
A program may use at most 64 MiB of HBM per device.

v0:
```python
import jax
import jax.numpy as jnp
from jax import lax
from jax.sharding import PartitionSpec as P

STEPS = 2


def side_by_side(arrays, axis, split_dim, concat_dim, along):
    widths = [a.shape[along] for a in arrays]
    both = jnp.concatenate(arrays, axis=along)
    whole = lax.all_to_all(both, axis, split_axis=split_dim, concat_axis=concat_dim, tiled=True)
    return tuple(jnp.split(whole, [sum(widths[:k]) for k in range(1, len(widths))], axis=along))


def split_up(value, dim, length):
    shape = value.shape
    pieces = value.reshape(*shape[:dim], length, shape[dim] // length, *shape[dim + 1 :])
    return jnp.moveaxis(pieces, dim, 0)


def summed_on_arrival(value, axis, dim):
    length = lax.axis_size(axis)
    pieces = lax.all_to_all(split_up(value, dim, length), axis, 0, 0, tiled=True)
    return jnp.sum(pieces, axis=0)


def tile_product(picked, ztiles, counts):
    slot_index = jnp.arange(ztiles.shape[1], dtype=jnp.int32)
    active = slot_index[None, :] < counts[:, None]
    picked = jnp.where(active[:, :, None, None], picked, jnp.zeros((), picked.dtype))
    return jnp.einsum("rkdj,rkji->dri", picked, ztiles, preferred_element_type=jnp.float32)


def finish_step(history_sum, own_field, zinv):
    dir_count, rows_block, tile_size = history_sum.shape
    own = own_field.astype(jnp.float32).reshape(dir_count, rows_block, tile_size)
    source = (own - history_sum).astype(jnp.bfloat16)
    density = jnp.einsum("drj,rji->dri", source, zinv, preferred_element_type=jnp.float32)
    return density.reshape(dir_count, rows_block * tile_size).astype(jnp.bfloat16)


def on_device(history, incident, ztiles, zinv, columns, lags, counts, basis):
    dens_list = []
    far_list = []
    owners_count = lax.axis_size("elem")
    rows_dev, slot_count, tile_size = (ztiles.shape[0], ztiles.shape[1], ztiles.shape[2])
    slots_dev = rows_dev * slot_count
    capacity = max(4, (slots_dev + owners_count - 1) // owners_count)
    flat_cols = columns.reshape(slots_dev)
    flat_lags = lags.reshape(slots_dev) - 1
    owner_of = flat_cols // rows_dev
    local_block = flat_cols - owner_of * rows_dev
    slot_ids = jnp.arange(slots_dev, dtype=jnp.int32)
    same_owner = (owner_of[:, None] == owner_of[None, :]) & (slot_ids[None, :] < slot_ids[:, None])
    position = jnp.sum(same_owner.astype(jnp.int32), axis=1)
    owner_ids = jnp.arange(owners_count, dtype=jnp.int32)
    place_ids = jnp.arange(capacity, dtype=jnp.int32)
    placed = (
        (owner_of[None, None, :] == owner_ids[:, None, None])
        & (position[None, None, :] == place_ids[None, :, None])
    ).astype(jnp.int32)
    want_block = jnp.sum(placed * local_block[None, None, :], axis=2)
    want_lag = jnp.sum(placed * flat_lags[None, None, :], axis=2)
    asked_block, asked_lag = side_by_side((want_block, want_lag), "elem", 0, 0, 1)
    window = history
    for step_index in range(STEPS):
        levels, dir_count, panels = window.shape
        grid = window.reshape(levels, dir_count, panels // tile_size, tile_size)
        reply = grid[asked_lag, :, asked_block, :]
        received = lax.all_to_all(reply, "elem", split_axis=0, concat_axis=0, tiled=True)
        picked = received[owner_of, position].reshape(rows_dev, slot_count, dir_count, tile_size)
        history_sum = tile_product(picked, ztiles, counts)
        density = finish_step(history_sum, incident[step_index], zinv)
        dens_list.append(density)
        far_list.append(jnp.dot(density, basis, preferred_element_type=jnp.float32))
        window = jnp.concatenate([density[None], window[:-1]], axis=0)
    far_field = summed_on_arrival(jnp.stack(far_list), "elem", 2)
    return (jnp.stack(dens_list), far_field)


def solution(mesh):
    in_specs = (
        P(None, "dir", "elem"),
        P(None, "dir", "elem"),
        P("elem", None, None, None),
        P("elem", None, None),
        P("elem", None),
        P("elem", None),
        P("elem"),
        P("elem", None),
    )
    out_specs = (P(None, "dir", "elem"), P(None, "dir", "elem"))
    return jax.shard_map(
        on_device, mesh=mesh, in_specs=in_specs, out_specs=out_specs, check_vma=False
    )
```

profile of v0, /device:TPU:1, one launch (start us, length us, event | category | flops | bytes accessed | tf_op | source)
XLA Modules:
  0.0 105.4 jit_solution(11189065958002321009)
XLA Ops:
  0.6 0.9 reshape.285
  1.6 0.2 convert_reduce_fusion
  1.8 0.7 broadcast_add_fusion
  2.6 0.2 fusion.14
  2.8 0.1 copy.20
  2.9 22.2 %all_to_all.27 = s32[64,1,8]{2,1,0:T(1,128)S(1)} all-to-all(s32[64,1,8]{2,1,0:T(1,128)S(1)} %bitcast.87), channel_id=1, replica_groups=mesh['elem'=64,'dir'=4] {'elem'}, dimensions={0} | all-to-all | bytes 4096 | tf_op jit(solution)/shard_map/all_to_all | solution.py:12
  25.2 0.1 reshape.292
  25.3 2.7 %gather_fusion = bf16[256,8,128]{2,1,0:T(8,128)(2,1)} fusion(bf16[8,8,3,128]{3,1,2,0:T(8,128)(2,1)} %bitcast.80, s32[256]{0:T(256)S(1)} %reshape.292), kind=kCustom, calls=%fused_computation | custom fusion | bytes 1050624 | tf_op jit(solution)/shard_map/gather | solution.py:70
  28.0 5.5 %all-to-all-start.1 = ((bf16[64,4,8,128]{3,2,1,0:T(8,128)(2,1)}), bf16[64,4,8,128]{3,2,1,0:T(8,128)(2,1)}, u32[]{:S(2)}, u32[]{:S(2)}) async-start(bf16[64,4,8,128]{3,2,1,0:T(8,128)(2,1)} %bitcast.81), calls=%async_computation.1 | async-start | bytes 1048576 | tf_op jit(solution)/shard_map/all_to_all | solution.py:71
  33.6 0.7 broadcast_divide_fusion
  34.3 0.7 fusion.34
  35.0 0.1 and.52
  35.1 0.7 iota_compare_fusion.3
  35.9 0.8 slice_bitcast_fusion
  36.7 14.1 %all-to-all-done.1 = bf16[64,4,8,128]{3,2,1,0:T(8,128)(2,1)} async-done(((bf16[64,4,8,128]{3,2,1,0:T(8,128)(2,1)}), bf16[64,4,8,128]{3,2,1,0:T(8,128)(2,1)}, u32[]{:S(2)}, u32[]{:S(2)}) %all-to-all-start.1) | async-done | bytes 524320 | tf_op jit(solution)/shard_map/all_to_all | solution.py:71
  50.8 2.2 %gather_fusion.1 = bf16[96,8,128]{2,1,0:T(8,128)(2,1)S(1)} fusion(bf16[64,4,8,128]{3,2,1,0:T(8,128)(2,1)} %all-to-all-done.1, s32[96]{0:T(128)S(1)} %fusion.38), kind=kCustom, calls=%fused_computation.1 | custom fusion | bytes 393984 | tf_op jit(solution)/shard_map/gather | solution.py:72
  53.0 1.6 %convolution_convert_fusion.1 = bf16[3,8,128]{2,1,0:T(8,128)(2,1)S(1)} fusion(bf16[3,128,128]{2,1,0:T(8,128)(2,1)} %param.11, bf16[3,32,128,128]{3,2,1,0:T(8,128)(2,1)S(1)} %copy-done, bf16[3,32,8,128]{3,2,1,0:T(8,128)(2,1)S(1)} %bitcast.84, pred[3,32]{1,0:T(4,128)(4,1)S(1)} %iota_compare_fusion.3, bf16[2,8,384]{2,1,0:T(8,128)(2,1)} %param.9), kind=kOutput, calls=%fused_computation.11 | convolution fusion | flops 26062848 | bytes 3453024 | tf_op jit(solution)/shard_map/drj,rji->dri/dot_general | solution.py:39
  54.6 1.9 %gather_fusion.2 = bf16[256,8,128]{2,1,0:T(8,128)(2,1)} fusion(bf16[8,8,3,128]{3,1,2,0:T(8,128)(2,1)S(1)} %pad_maximum_fusion, s32[256]{0:T(256)S(1)} %reshape.292), kind=kCustom, calls=%fused_computation.2 | custom fusion | bytes 1050624 | tf_op jit(solution)/shard_map/gather | solution.py:70
  56.5 6.6 %all-to-all-start.2 = ((bf16[64,4,8,128]{3,2,1,0:T(8,128)(2,1)}), bf16[64,4,8,128]{3,2,1,0:T(8,128)(2,1)}, u32[]{:S(2)}, u32[]{:S(2)}) async-start(bf16[64,4,8,128]{3,2,1,0:T(8,128)(2,1)} %bitcast.82), calls=%async_computation.2 | async-start | bytes 1048576 | tf_op jit(solution)/shard_map/all_to_all | solution.py:71
  63.1 1.1 %copy.21 = bf16[256,384]{1,0:T(8,128)(2,1)S(1)} copy(bf16[256,384]{0,1:T(8,128)(2,1)} %bitcast.86) | data formatting | bytes 393216 | tf_op jit(solution)/shard_map/dot_general | solution.py:76
  64.2 0.8 convolution_bitcast_fusion.1
  65.1 15.2 %all-to-all-done.2 = bf16[64,4,8,128]{3,2,1,0:T(8,128)(2,1)} async-done(((bf16[64,4,8,128]{3,2,1,0:T(8,128)(2,1)}), bf16[64,4,8,128]{3,2,1,0:T(8,128)(2,1)}, u32[]{:S(2)}, u32[]{:S(2)}) %all-to-all-start.2) | async-done | bytes 524320 | tf_op jit(solution)/shard_map/all_to_all | solution.py:71
  80.3 2.2 %gather_fusion.3 = bf16[96,8,128]{2,1,0:T(8,128)(2,1)S(1)} fusion(bf16[64,4,8,128]{3,2,1,0:T(8,128)(2,1)} %all-to-all-done.2, s32[96]{0:T(128)S(1)} %fusion.38), kind=kCustom, calls=%fused_computation.3 | custom fusion | bytes 393984 | tf_op jit(solution)/shard_map/gather | solution.py:72
  82.4 1.6 %convolution_convert_fusion = bf16[3,8,128]{2,1,0:T(8,128)(2,1)S(1)} fusion(bf16[3,128,128]{2,1,0:T(8,128)(2,1)} %param.11, bf16[3,32,128,128]{3,2,1,0:T(8,128)(2,1)S(1)} %copy-done, bf16[3,32,8,128]{3,2,1,0:T(8,128)(2,1)S(1)} %bitcast.83, pred[3,32]{1,0:T(4,128)(4,1)} %copy-done.2, bf16[2,8,384]{2,1,0:T(8,128)(2,1)} %param.9), kind=kOutput, calls=%fused_computation.10 | convolution fusion | flops 26062848 | bytes 3453440 | tf_op jit(solution)/shard_map/drj,rji->dri/dot_general | solution.py:39
  84.1 0.6 copy-done.1
  84.7 0.2 convolution_bitcast_fusion
  84.9 0.7 maximum_bitcast_fusion
  85.6 0.8 copy.24
  86.4 6.3 %all-to-all-start.3 = ((f32[64,2,8,4]{2,3,1,0:T(4,128)}), f32[64,2,8,4]{2,3,1,0:T(4,128)S(1)}, u32[]{:S(2)}, u32[]{:S(2)}) async-start(f32[64,2,8,4]{2,3,1,0:T(4,128)} %copy.24), calls=%async_computation.3 | async-start | bytes 524288 | tf_op jit(solution)/shard_map/all_to_all | solution.py:24
  92.7 1.3 %pad_maximum_fusion.1 = bf16[2,8,384]{2,1,0:T(8,128)(2,1)} fusion(bf16[1,8,384]{2,1,0:T(8,128)(2,1)} %bitcast.90, bf16[1,8,384]{2,1,0:T(8,128)(2,1)S(1)} %bitcast.89), kind=kLoop, calls=%fused_computation.40 | loop fusion | flops 6144 | bytes 24576 | tf_op jit(solution)/shard_map/stack | solution.py:79
  94.0 10.7 %all-to-all-done.3 = f32[64,2,8,4]{2,3,1,0:T(4,128)S(1)} async-done(((f32[64,2,8,4]{2,3,1,0:T(4,128)}), f32[64,2,8,4]{2,3,1,0:T(4,128)S(1)}, u32[]{:S(2)}, u32[]{:S(2)}) %all-to-all-start.3) | async-done | bytes 16416 | tf_op jit(solution)/shard_map/all_to_all | solution.py:24
  104.7 0.7 reduce_sum.42
  (15 shorter events, 0.4 us)
Async XLA Ops:
  0.6 52.3 %copy-start = (bf16[3,32,128,128]{3,2,1,0:T(8,128)(2,1)S(1)}, bf16[3,32,128,128]{3,2,1,0:T(8,128)(2,1)}, u32[]{:S(2)}) copy-start(bf16[3,32,128,128]{3,2,1,0:T(8,128)(2,1)} %param.10) | copy-start | bytes 9437188
  28.0 22.8 %all-to-all-start.1 = ((bf16[64,4,8,128]{3,2,1,0:T(8,128)(2,1)}), bf16[64,4,8,128]{3,2,1,0:T(8,128)(2,1)}, u32[]{:S(2)}, u32[]{:S(2)}) async-start(bf16[64,4,8,128]{3,2,1,0:T(8,128)(2,1)} %bitcast.81), calls=%async_computation.1 | async-start | bytes 1048576 | tf_op jit(solution)/shard_map/all_to_all | solution.py:71
  35.9 20.7 %copy-start.2 = (pred[3,32]{1,0:T(4,128)(4,1)}, pred[3,32]{1,0:T(4,128)(4,1)S(1)}, u32[]{:S(2)}) copy-start(pred[3,32]{1,0:T(4,128)(4,1)S(1)} %iota_compare_fusion.3) | copy-start | bytes 292
  56.5 23.8 %all-to-all-start.2 = ((bf16[64,4,8,128]{3,2,1,0:T(8,128)(2,1)}), bf16[64,4,8,128]{3,2,1,0:T(8,128)(2,1)}, u32[]{:S(2)}, u32[]{:S(2)}) async-start(bf16[64,4,8,128]{3,2,1,0:T(8,128)(2,1)} %bitcast.82), calls=%async_computation.2 | async-start | bytes 1048576 | tf_op jit(solution)/shard_map/all_to_all | solution.py:71
  84.1 0.6 copy-start.1
  86.4 18.3 %all-to-all-start.3 = ((f32[64,2,8,4]{2,3,1,0:T(4,128)}), f32[64,2,8,4]{2,3,1,0:T(4,128)S(1)}, u32[]{:S(2)}, u32[]{:S(2)}) async-start(f32[64,2,8,4]{2,3,1,0:T(4,128)} %copy.24), calls=%async_computation.3 | async-start | bytes 524288 | tf_op jit(solution)/shard_map/all_to_all | solution.py:24
where the time goes:
time: 106 us; the launch traced here: 105 us
  waiting for transfers between devices  40 us (38%)
  blocking collectives  22.2 us (21%)
  starting transfers between devices  18.4 us (17%)
  local copies, waits for them, and re-layouts  13.7 us (13%)
  other arithmetic  6.08 us (6%)
  matrix products  4.22 us (4%)
    all_to_all x2, waiting for transfers between devices, on_device(): lax.all_to_all(reply, 'elem', split_axis=0, concat_axis=0, tiled=True)  29.4 us
    all_to_all x1, blocking collectives, side_by_side(): lax.all_to_all(both, axis, split_axis=split_dim, concat_axis=concat_dim,...  22.2 us
    all_to_all x2, starting transfers between devices, on_device(): lax.all_to_all(reply, 'elem', split_axis=0, concat_axis=0, tiled=True)  12.1 us
    all_to_all x1, waiting for transfers between devices, summed_on_arrival(): lax.all_to_all(split_up(value, dim, length), axis, 0, 0, tiled=True)  10.7 us
    all_to_all x1, starting transfers between devices, summed_on_arrival(): lax.all_to_all(split_up(value, dim, length), axis, 0, 0, tiled=True)  6.29 us
    gather x2, local copies, waits for them, and re-layouts, on_device(): reply = grid[asked_lag, :, asked_block, :]  4.62 us
    gather x2, local copies, waits for them, and re-layouts, on_device(): received[owner_of, position]  4.31 us
    dot_general x2, matrix products, finish_step(): jnp.einsum('drj,rji->dri', source, zinv, preferred_element_type=jnp.float32)  3.21 us
  transfers between devices with their start and end apart: 3, of which 3 were waited for; matrix products, arithmetic and copies ran while one was open for 6% of the time, Pallas kernels for 0%

commit v1 on v0

v1 whole, which is shorter than its diff:
```python
import jax
import jax.numpy as jnp
from jax import lax
from jax.experimental import pallas as pl
from jax.experimental.pallas import tpu as pltpu
from jax.sharding import Mesh, PartitionSpec as P

STEPS = 2
Y, Z, C = 4, 8, 2
GROUPS = Y * C
E = ("y", "z", "c")
BLOCK_CAP = 4


def vmem():
    return pl.BlockSpec(memory_space=pltpu.VMEM)


def smem():
    return pl.BlockSpec(memory_space=pltpu.SMEM)


def spread(value, axis, length):
    whole = jnp.broadcast_to(value[None], (length, *value.shape))
    return lax.all_to_all(whole, axis, 0, 0, tiled=True)


def pick_kernel(asked, held, first, second):
    back = held.shape[0] // (Z * 8)

    @pl.loop(0, first.shape[0], step=16)
    def _(base):
        for k in range(16):
            spot = asked[base + k]
            first[base + k] = held[spot]
            second[base + k] = held[jnp.maximum(spot - back, 0)]


def pick(asked, held):
    out = jax.ShapeDtypeStruct((asked.shape[0], *held.shape[1:]), held.dtype)
    return pl.pallas_call(
        pick_kernel,
        out_shape=(out, out),
        in_specs=[smem(), vmem()],
        out_specs=(vmem(), vmem()),
        name="pick",
    )(asked, held)


def row_density(load, counts, ztiles, zinv, own, row):
    slots, tile = ztiles.shape[1], ztiles.shape[2]
    live = counts[row]
    parts = []
    for k in range(slots):
        tile_k = load(row * slots + k)
        parts.append(jnp.where(k < live, tile_k, jnp.zeros_like(tile_k)))
    picked = jnp.concatenate(parts, axis=1)
    flat = ztiles[row].reshape(slots * tile, tile)
    total = jnp.dot(picked, flat, preferred_element_type=jnp.float32)
    source = (own.astype(jnp.float32) - total).astype(jnp.bfloat16)
    density = jnp.dot(source, zinv[row], preferred_element_type=jnp.float32)
    return density.astype(jnp.bfloat16)


def first_kernel(spots, counts, held, ztiles, zinv, incident, out):
    tile = ztiles.shape[2]
    for row in range(ztiles.shape[0]):
        own = incident[0, :, row * tile : (row + 1) * tile]
        out[row] = row_density(lambda s: held[spots[s]], counts, ztiles, zinv, own, row)


def first_step(spots, counts, held, ztiles, zinv, incident):
    rows, tile, dirs = ztiles.shape[0], ztiles.shape[2], held.shape[1]
    return pl.pallas_call(
        first_kernel,
        out_shape=jax.ShapeDtypeStruct((rows, dirs, tile), jnp.bfloat16),
        in_specs=[smem(), smem(), vmem(), vmem(), vmem(), vmem()],
        out_specs=vmem(),
        name="first_step",
    )(spots, counts, held, ztiles, zinv, incident)


def second_kernel(spots, counts, before, old, here, there, ztiles, zinv, incident, basis, dens, far, pool, flipped, sems):
    rows, tile = ztiles.shape[0], ztiles.shape[2]
    near = here.shape[0]
    copies = [
        pltpu.make_async_copy(old, pool.at[pl.ds(0, old.shape[0])], sems.at[0]),
        pltpu.make_async_copy(here, pool.at[pl.ds(old.shape[0], near)], sems.at[1]),
        pltpu.make_async_copy(there, pool.at[pl.ds(old.shape[0] + near, near)], sems.at[2]),
    ]
    for copy in copies:
        copy.start()
    for copy in copies:
        copy.wait()
    earlier, later = [], []
    for row in range(rows):
        own = incident[1, :, row * tile : (row + 1) * tile]
        later.append(row_density(lambda s: pool[spots[s]], counts, ztiles, zinv, own, row))
        earlier.append(before[row])
    steps = [jnp.concatenate(earlier, axis=1), jnp.concatenate(later, axis=1)]
    sums = []
    for step, value in enumerate(steps):
        dens[step] = value
        sums.append(jnp.dot(value, basis[...], preferred_element_type=jnp.float32))
    total = jnp.concatenate(sums, axis=0)
    lanes = total.shape[0]
    flipped[:, :lanes] = total.T
    each = basis.shape[1] // far.shape[0]
    cols = [flipped[pl.ds(c, far.shape[0], stride=each), :] for c in range(each)]
    far[...] = jnp.concatenate(
        [c[:, :lanes] for c in cols] + [jnp.zeros((far.shape[0], 128 - each * lanes), jnp.float32)], axis=1
    )


def second_step(spots, counts, before, old, here, there, ztiles, zinv, incident, basis, owners):
    dirs = before.shape[1]
    panels, harmonics = basis.shape
    anywhere = pl.BlockSpec(memory_space=pl.ANY)
    return pl.pallas_call(
        second_kernel,
        out_shape=(
            jax.ShapeDtypeStruct((STEPS, dirs, panels), jnp.bfloat16),
            jax.ShapeDtypeStruct((owners, 128), jnp.float32),
        ),
        in_specs=[smem(), smem(), vmem(), anywhere, anywhere, anywhere, vmem(), vmem(), vmem(), vmem()],
        out_specs=(vmem(), vmem()),
        scratch_shapes=[
            pltpu.VMEM((old.shape[0] + 2 * here.shape[0], *old.shape[1:]), jnp.bfloat16),
            pltpu.VMEM((harmonics, 128), jnp.float32),
            pltpu.SemaphoreType.DMA((3,)),
        ],
        name="second_step",
    )(spots, counts, before, old, here, there, ztiles, zinv, incident, basis)


def sum_kernel(parts, out):
    total = jnp.sum(parts[...], axis=0, keepdims=True)
    steps, each, dirs = out.shape
    for step in range(steps):
        for c in range(each):
            at = (c * steps + step) * dirs
            out[step, c : c + 1, :] = total[:, at : at + dirs]


def sum_parts(parts, steps, each, dirs):
    return pl.pallas_call(
        sum_kernel,
        out_shape=jax.ShapeDtypeStruct((steps, each, dirs), jnp.float32),
        in_specs=[vmem()],
        out_specs=vmem(),
        name="sum_parts",
    )(parts)


def on_device(history, incident, ztiles, zinv, columns, lags, counts, basis):
    rows, slots, tile = ztiles.shape[0], ztiles.shape[1], ztiles.shape[2]
    levels, dirs, panels = history.shape
    slots_dev = rows * slots
    owners = Y * Z * C
    cap = BLOCK_CAP * Z
    mine = history.reshape(levels, dirs, rows, tile).transpose(0, 2, 1, 3)
    held = spread(mine.reshape(levels * rows, dirs, tile), "z", Z)
    held = held.reshape(Z * levels * rows, dirs, tile)
    flat_cols = columns.reshape(slots_dev)
    flat_lags = lags.reshape(slots_dev) - 1
    owner = flat_cols // rows
    local = flat_cols - owner * rows
    own_c = owner % C
    own_z = (owner // C) % Z
    own_y = owner // (C * Z)
    group = own_y * C + own_c
    spot = (own_z * levels + flat_lags) * rows + local
    ids = jnp.arange(slots_dev, dtype=jnp.int32)
    earlier = (group[:, None] == group[None, :]) & (ids[None, :] < ids[:, None])
    position = jnp.sum(earlier.astype(jnp.int32), axis=1)
    at = group * cap + position
    asks = jnp.arange(GROUPS * cap, dtype=jnp.int32)
    wanted = jnp.sum(jnp.where(at[None, :] == asks[:, None], spot[None, :], 0), axis=1)
    asked = lax.all_to_all(wanted.reshape(GROUPS, cap), ("y", "c"), 0, 0, tiled=True)
    first, second = pick(asked.reshape(GROUPS * cap), held)
    shape = (GROUPS, cap, dirs, tile)
    got = lax.all_to_all(first.reshape(shape), ("y", "c"), 0, 0, tiled=True)
    density = first_step(at, counts, got.reshape(GROUPS * cap, dirs, tile), ztiles, zinv, incident)
    old = lax.all_to_all(second.reshape(shape), ("y", "c"), 0, 0, tiled=True)
    here = spread(density, ("y", "z"), Y * Z).reshape(Y * Z * rows, dirs, tile)
    there = lax.ppermute(here, "c", [(0, 1), (1, 0)])
    far_side = (own_c != lax.axis_index("c")).astype(jnp.int32)
    fresh = GROUPS * cap + (far_side * (Y * Z) + own_y * Z + own_z) * rows + local
    spots = jnp.where(flat_lags == 0, fresh, at)
    dens, far = second_step(
        spots, counts, density, old.reshape(GROUPS * cap, dirs, tile), here, there, ztiles, zinv, incident, basis, owners
    )
    each = basis.shape[1] // owners
    parts = lax.all_to_all(far.reshape(owners, 1, 128), E, 0, 0, tiled=True).reshape(owners, 128)
    total = sum_parts(parts, STEPS, each, dirs)
    return dens, total.transpose(0, 2, 1)


def solution(mesh):
    fine = Mesh(mesh.devices.reshape(Y, Z, C, mesh.shape["dir"]), ("y", "z", "c", "dir"))
    in_specs = (
        P(None, "dir", E),
        P(None, "dir", E),
        P(E, None, None, None),
        P(E, None, None),
        P(E, None),
        P(E, None),
        P(E),
        P(E, None),
    )
    out_specs = (P(None, "dir", E), P(None, "dir", E))
    return jax.shard_map(on_device, mesh=fine, in_specs=in_specs, out_specs=out_specs, check_vma=False)
```

time: 106 us -> 111 us (1.047)
  blocking collectives: 22.2 us -> 42.4 us
  waiting for transfers between devices: 40 us -> 25.4 us
  Pallas kernels: 0 us -> 12.5 us
  local copies, waits for them, and re-layouts: 13.7 us -> 6.56 us
  matrix products: 4.22 us -> 0 us
  other arithmetic: 6.08 us -> 2.27 us
  starting transfers between devices: 18.4 us -> 20.5 us
    all_to_all x1 -> x3, blocking collectives: 22.2 us -> 42.4 us  [the longest x1 15.1 us: on_device(): lax.all_to_all(far.reshape(owners, 1, 128), E, 0, 0, tiled=True)]
    all_to_all x3, waiting for transfers between devices: 40 us -> 25.4 us  [the longest x1 12.4 us: spread(): return lax.all_to_all(whole, axis, 0, 0, tiled=True)]
    pallas_call x0 -> x4, Pallas kernels: none -> 12.5 us  [the longest x1 4.9 us: second_step(): pl.pallas_call(second_kernel, out_shape=(jax.ShapeDtypeStruct((STEPS, dir...]
    gather x4 -> x0, local copies, waits for them, and re-layouts: 8.94 us -> none  [the longest x2 4.62 us: on_device(): reply = grid[asked_lag, :, asked_block, :]]
    dot_general x4 -> x0, matrix products: 4.22 us -> none  [the longest x2 3.21 us: finish_step(): jnp.einsum('drj,rji->dri', source, zinv, preferred_element_type=jnp.float32)]
    all_to_all x3, starting transfers between devices: 18.4 us -> 20.3 us  [the longest x1 7.71 us: spread(): return lax.all_to_all(whole, axis, 0, 0, tiled=True)]
    broadcast_in_dim x0 -> x2, local copies, waits for them, and re-layouts: none -> 1.5 us  [spread(): whole = jnp.broadcast_to(value[None], (length, *value.shape))]
    another operation x1 -> x0, other arithmetic: 1.3 us -> none  [on_device(): return (jnp.stack(dens_list), far_field)]
  transfers between devices with their start and end apart: 3 -> 4, of which waited for: 3 -> 3; matrix products, arithmetic and copies ran while one was open for 6% -> 2% of each run, Pallas kernels for 0% -> 0%
where the time goes in v1:
time: 111 us; the launch traced here: 110 us
  blocking collectives  42.4 us (38%)
  waiting for transfers between devices  25.4 us (23%)
  starting transfers between devices  20.5 us (18%)
  Pallas kernels  12.5 us (11%)
  local copies, waits for them, and re-layouts  6.56 us (6%)
  other arithmetic  2.27 us (2%)
    all_to_all x1, blocking collectives, on_device(): lax.all_to_all(far.reshape(owners, 1, 128), E, 0, 0, tiled=True)  15.1 us
    all_to_all x1, blocking collectives, on_device(): got = lax.all_to_all(first.reshape(shape), ('y', 'c'), 0, 0, tiled=True)  14.8 us
    all_to_all x1, blocking collectives, spread(): return lax.all_to_all(whole, axis, 0, 0, tiled=True)  12.5 us
    all_to_all x1, waiting for transfers between devices, spread(): return lax.all_to_all(whole, axis, 0, 0, tiled=True)  12.4 us
    all_to_all x1, waiting for transfers between devices, on_device(): old = lax.all_to_all(second.reshape(shape), ('y', 'c'), 0, 0, tiled=True)  9.19 us
    all_to_all x1, starting transfers between devices, spread(): return lax.all_to_all(whole, axis, 0, 0, tiled=True)  7.71 us
    all_to_all x1, starting transfers between devices, on_device(): lax.all_to_all(wanted.reshape(GROUPS, cap), ('y', 'c'), 0, 0, tiled=True)  6.41 us
    all_to_all x1, starting transfers between devices, on_device(): old = lax.all_to_all(second.reshape(shape), ('y', 'c'), 0, 0, tiled=True)  6.21 us
  transfers between devices with their start and end apart: 4, of which 3 were waited for; matrix products, arithmetic and copies ran while one was open for 2% of the time, Pallas kernels for 0%

profile of v1, /device:TPU:1, one launch (start us, length us, event | category | flops | bytes accessed | tf_op | source)
XLA Modules:
  0.0 110.4 jit_solution(3518712144177907296)
XLA Ops:
  0.6 0.8 reshape.190
  1.4 0.7 broadcast_add_fusion
  2.1 0.1 sub.28
  2.2 0.2 convert_reduce_fusion
  2.4 0.6 compare_select_fusion.3
  3.0 0.1 select_reduce_fusion
  3.1 0.7 all_to_all.21
  3.8 6.4 %all-to-all-start = ((s32[8,1,32]{2,1,0:T(1,128)}), s32[8,1,32]{2,1,0:T(1,128)S(1)}, u32[]{:S(2)}, u32[]{:S(2)}) async-start(s32[8,1,32]{2,1,0:T(1,128)} %all_to_all.21), calls=%async_computation | async-start | bytes 8192 | tf_op jit(solution)/shard_map/all_to_all | solution.py:179
  10.2 0.8 fusion.4
  11.0 3.8 %all-to-all-done = s32[8,1,32]{2,1,0:T(1,128)S(1)} async-done(((s32[8,1,32]{2,1,0:T(1,128)}), s32[8,1,32]{2,1,0:T(1,128)S(1)}, u32[]{:S(2)}, u32[]{:S(2)}) %all-to-all-start) | async-done | bytes 1056 | tf_op jit(solution)/shard_map/all_to_all | solution.py:179
  14.7 0.8 broadcast_in_dim.21
  15.5 7.7 %all-to-all-start.1 = ((bf16[8,24,8,128]{3,2,1,0:T(8,128)(2,1)}), bf16[8,24,8,128]{3,2,1,0:T(8,128)(2,1)S(1)}, u32[]{:S(2)}, u32[]{:S(2)}) async-start(bf16[8,24,8,128]{3,2,1,0:T(8,128)(2,1)} %broadcast_in_dim.21), calls=%async_computation.1 | async-start | bytes 786432 | tf_op jit(solution)/shard_map/all_to_all | solution.py:25
  23.2 0.5 broadcast.320
  23.8 0.7 reduce.3
  24.4 0.6 reshape.191.asked
  25.1 12.4 %all-to-all-done.1 = bf16[8,24,8,128]{3,2,1,0:T(8,128)(2,1)S(1)} async-done(((bf16[8,24,8,128]{3,2,1,0:T(8,128)(2,1)}), bf16[8,24,8,128]{3,2,1,0:T(8,128)(2,1)S(1)}, u32[]{:S(2)}, u32[]{:S(2)}) %all-to-all-start.1) | async-done | bytes 393248 | tf_op jit(solution)/shard_map/all_to_all | solution.py:25
  37.5 0.8 copy-done.1
  38.2 2.7 %pick.1 = (bf16[256,8,128]{2,1,0:T(8,128)(2,1)}, bf16[256,8,128]{2,1,0:T(8,128)(2,1)}) custom-call(s32[256]{0:T(256)} %reshape.191.asked, bf16[192,8,128]{2,1,0:T(8,128)(2,1)} %bitcast.14), custom_call_target="tpu_custom_call" | custom-call | tf_op jit(solution)/shard_map/pick/pallas_call | solution.py:41
  40.9 14.8 %all_to_all.34 = bf16[8,32,8,128]{3,2,1,0:T(8,128)(2,1)} all-to-all(bf16[8,32,8,128]{3,2,1,0:T(8,128)(2,1)} %bitcast.17), channel_id=1, replica_groups=mesh['y'=4,'z'=8,'c'=2,'dir'=4] {'y','c'}, dimensions={0} | all-to-all | bytes 1048576 | tf_op jit(solution)/shard_map/all_to_all | solution.py:182
  55.8 3.5 %first_step.1.before = bf16[3,8,128]{2,1,0:T(8,128)(2,1)} custom-call(s32[96]{0:T(128)} %copy-done.4, s32[3]{0:T(128)} %counts.3, bf16[256,8,128]{2,1,0:T(8,128)(2,1)} %bitcast.13, bf16[3,32,128,128]{3,2,1,0:T(8,128)(2,1)} %ztiles.3, bf16[3,128,128]{2,1,0:T(8,128)(2,1)} %zinv.3, bf16[2,8,384]{2,1,0:T(8,128)(2,1)} %incident.3), custom_call_target="tpu_custom_call" | custom-call | tf_op jit(solution)/shard_map/first_step/pallas_call | solution.py:74
  59.2 0.7 broadcast_in_dim.36
  60.0 12.5 %all_to_all.35 = bf16[32,3,8,128]{3,2,1,0:T(8,128)(2,1)S(1)} all-to-all(bf16[32,3,8,128]{3,2,1,0:T(8,128)(2,1)S(1)} %broadcast_in_dim.36), channel_id=1, replica_groups=mesh['y'=4,'z'=8,'c'=2,'dir'=4] {'y','z'}, dimensions={0} | all-to-all | bytes 393216 | tf_op jit(solution)/shard_map/all_to_all | solution.py:25
  72.4 6.2 %all-to-all-start.3 = ((bf16[8,32,8,128]{3,2,1,0:T(8,128)(2,1)}), bf16[8,32,8,128]{3,2,1,0:T(8,128)(2,1)S(1)}, u32[]{:S(2)}, u32[]{:S(2)}) async-start(bf16[8,32,8,128]{3,2,1,0:T(8,128)(2,1)} %bitcast.4), calls=%async_computation.3 | async-start | bytes 1048576 | tf_op jit(solution)/shard_map/all_to_all | solution.py:184
  78.6 0.2 collective-permute-start
  78.8 9.2 %all-to-all-done.3 = bf16[8,32,8,128]{3,2,1,0:T(8,128)(2,1)S(1)} async-done(((bf16[8,32,8,128]{3,2,1,0:T(8,128)(2,1)}), bf16[8,32,8,128]{3,2,1,0:T(8,128)(2,1)S(1)}, u32[]{:S(2)}, u32[]{:S(2)}) %all-to-all-start.3) | async-done | bytes 524320 | tf_op jit(solution)/shard_map/all_to_all | solution.py:184
  88.0 0.0 collective-permute-done.there
  88.0 0.0 copy-done.2
  88.0 0.8 copy-done
  88.8 0.1 copy-done.3
  88.9 4.9 %second_step.1 = (bf16[2,8,384]{2,1,0:T(8,128)(2,1)}, f32[64,128]{1,0:T(8,128)}) custom-call(s32[96]{0:T(128)} %get-tuple-element.13.spots, s32[3]{0:T(128)} %counts.3, bf16[3,8,128]{2,1,0:T(8,128)(2,1)} %first_step.1.before, bf16[256,8,128]{2,1,0:T(8,128)(2,1)} %bitcast.12, bf16[96,8,128]{2,1,0:T(8,128)(2,1)} %bitcast.16, bf16[96,8,128]{2,1,0:T(8,128)(2,1)} %copy-done.3, ...), custom_call_target="tpu_custom_call" | custom-call | tf_op jit(solution)/shard_map/second_step/pallas_call | solution.py:119
  93.8 15.1 %all_to_all.36 = f32[64,1,128]{2,1,0:T(1,128)} all-to-all(f32[64,1,128]{2,1,0:T(1,128)} %bitcast.20), channel_id=1, replica_groups=mesh['y'=4,'z'=8,'c'=2,'dir'=4] {'y','z','c'}, dimensions={0} | all-to-all | bytes 65536 | tf_op jit(solution)/shard_map/all_to_all | solution.py:194
  108.9 1.4 %sum_parts.1 = f32[2,4,8]{2,1,0:T(4,128)} custom-call(f32[64,128]{1,0:T(8,128)} %bitcast.19), custom_call_target="tpu_custom_call" | custom-call | tf_op jit(solution)/shard_map/sum_parts/pallas_call | solution.py:146
  (9 shorter events, 0.1 us)
Async XLA Ops:
  3.0 52.8 %copy-start.4 = (s32[96]{0:T(128)}, s32[96]{0:T(128)S(1)}, u32[]{:S(2)}) copy-start(s32[96]{0:T(128)S(1)} %get-tuple-element.14.spots) | copy-start | bytes 1156
  3.8 11.0 %all-to-all-start = ((s32[8,1,32]{2,1,0:T(1,128)}), s32[8,1,32]{2,1,0:T(1,128)S(1)}, u32[]{:S(2)}, u32[]{:S(2)}) async-start(s32[8,1,32]{2,1,0:T(1,128)} %all_to_all.21), calls=%async_computation | async-start | bytes 8192 | tf_op jit(solution)/shard_map/all_to_all | solution.py:179
  15.5 21.9 %all-to-all-start.1 = ((bf16[8,24,8,128]{3,2,1,0:T(8,128)(2,1)}), bf16[8,24,8,128]{3,2,1,0:T(8,128)(2,1)S(1)}, u32[]{:S(2)}, u32[]{:S(2)}) async-start(bf16[8,24,8,128]{3,2,1,0:T(8,128)(2,1)} %broadcast_in_dim.21), calls=%async_computation.1 | async-start | bytes 786432 | tf_op jit(solution)/shard_map/all_to_all | solution.py:25
  37.5 0.8 copy-start.1
  72.4 15.6 %copy-start.2 = (bf16[32,3,8,128]{3,2,1,0:T(8,128)(2,1)}, bf16[32,3,8,128]{3,2,1,0:T(8,128)(2,1)S(1)}, u32[]{:S(2)}) copy-start(bf16[32,3,8,128]{3,2,1,0:T(8,128)(2,1)S(1)} %all_to_all.35) | copy-start | bytes 589828
  72.4 15.6 %all-to-all-start.3 = ((bf16[8,32,8,128]{3,2,1,0:T(8,128)(2,1)}), bf16[8,32,8,128]{3,2,1,0:T(8,128)(2,1)S(1)}, u32[]{:S(2)}, u32[]{:S(2)}) async-start(bf16[8,32,8,128]{3,2,1,0:T(8,128)(2,1)} %bitcast.4), calls=%async_computation.3 | async-start | bytes 1048576 | tf_op jit(solution)/shard_map/all_to_all | solution.py:184
  78.6 9.4 %collective-permute-start = (bf16[96,8,128]{2,1,0:T(8,128)(2,1)S(1)}, bf16[96,8,128]{2,1,0:T(8,128)(2,1)S(1)}, u32[]{:S(2)}, u32[]{:S(2)}) collective-permute-start(bf16[96,8,128]{2,1,0:T(8,128)(2,1)S(1)} %bitcast.15), channel_id=1, source_target_pairs={{0,4},{4,0},{1,5},{5,1},{2,6},{6,2},{3,7},{7,3},{8,12},{12,8},{9,1... | collective-permute-start | bytes 589832 | tf_op jit(solution)/shard_map/ppermute | solution.py:186
  88.0 0.8 copy-start
  88.0 0.9 copy-start.3

commit v2 on v1

--- a/solution.py
+++ b/solution.py
@@ -5,11 +5,17 @@
 from jax.experimental.pallas import tpu as pltpu
 from jax.sharding import Mesh, PartitionSpec as P
 
+
 STEPS = 2
 Y, Z, C = 4, 8, 2
 GROUPS = Y * C
 E = ("y", "z", "c")
 BLOCK_CAP = 4
+LEVELS = 8
+
+
+def grant(mib):
+    return pltpu.CompilerParams(vmem_limit_bytes=mib << 20)
 
 
 def vmem():
@@ -25,26 +31,36 @@
     return lax.all_to_all(whole, axis, 0, 0, tiled=True)
 
 
-def pick_kernel(asked, held, first, second):
-    back = held.shape[0] // (Z * 8)
-
-    @pl.loop(0, first.shape[0], step=16)
-    def _(base):
-        for k in range(16):
-            spot = asked[base + k]
-            first[base + k] = held[spot]
-            second[base + k] = held[jnp.maximum(spot - back, 0)]
-
-
-def pick(asked, held):
-    out = jax.ShapeDtypeStruct((asked.shape[0], *held.shape[1:]), held.dtype)
+def pick_kernel(place, *refs):
+    lists, held, first, later = refs[:Y], refs[Y], refs[Y + 1], refs[Y + 2 :]
+    y, c = place[0], place[1]
+    cap = first.shape[0] // GROUPS
+    back = held.shape[0] // (Z * LEVELS)
+    mine = (y * C + c) * cap
+    for shift in range(Y):
+        for other in range(C):
+            whose = (lax.rem(y - shift + Y, Y) * C + (c if other == 0 else 1 - c)) * cap
+
+            @pl.loop(0, cap, step=16)
+            def _(base):
+                for k in range(16):
+                    spot = lists[shift][other * GROUPS * cap + mine + base + k]
+                    first[whose + base + k] = held[spot]
+                    later[shift][other * cap + base + k] = held[jnp.maximum(spot - back, 0)]
+
+
+def pick(place, lists, held, cap):
+    def out(entries):
+        return jax.ShapeDtypeStruct((entries, *held.shape[1:]), held.dtype)
+
     return pl.pallas_call(
         pick_kernel,
-        out_shape=(out, out),
-        in_specs=[smem(), vmem()],
-        out_specs=(vmem(), vmem()),
+        out_shape=(out(GROUPS * cap), *[out(C * cap)] * Y),
+        in_specs=[smem()] * (1 + Y) + [vmem()],
+        out_specs=[vmem()] * (1 + Y),
+        compiler_params=grant(8),
         name="pick",
-    )(asked, held)
+    )(place, *lists, held)
 
 
 def row_density(load, counts, ztiles, zinv, own, row):
@@ -76,18 +92,24 @@
         out_shape=jax.ShapeDtypeStruct((rows, dirs, tile), jnp.bfloat16),
         in_specs=[smem(), smem(), vmem(), vmem(), vmem(), vmem()],
         out_specs=vmem(),
+        compiler_params=grant(16),
         name="first_step",
     )(spots, counts, held, ztiles, zinv, incident)
 
 
-def second_kernel(spots, counts, before, old, here, there, ztiles, zinv, incident, basis, dens, far, pool, flipped, sems):
+def second_kernel(spots, counts, before, *refs):
+    near, cross = refs[:Y], refs[Y : 2 * Y]
+    here, there, ztiles, zinv, incident, basis, dens, far, pool, flipped, sems = refs[2 * Y :]
     rows, tile = ztiles.shape[0], ztiles.shape[2]
-    near = here.shape[0]
-    copies = [
-        pltpu.make_async_copy(old, pool.at[pl.ds(0, old.shape[0])], sems.at[0]),
-        pltpu.make_async_copy(here, pool.at[pl.ds(old.shape[0], near)], sems.at[1]),
-        pltpu.make_async_copy(there, pool.at[pl.ds(old.shape[0] + near, near)], sems.at[2]),
-    ]
+    cap = near[0].shape[0] // C
+    pieces = []
+    for shift in range(Y):
+        pieces += [near[shift].at[pl.ds(0, cap)], cross[shift].at[pl.ds(cap, cap)]]
+    copies, start = [], 0
+    for piece in (*pieces, here, there):
+        length = piece.shape[0]
+        copies.append(pltpu.make_async_copy(piece, pool.at[pl.ds(start, length)], sems.at[len(copies)]))
+        start += length
     for copy in copies:
         copy.start()
     for copy in copies:
@@ -112,7 +134,7 @@
     )
 
 
-def second_step(spots, counts, before, old, here, there, ztiles, zinv, incident, basis, owners):
+def second_step(spots, counts, before, near, cross, here, there, ztiles, zinv, incident, basis, owners):
     dirs = before.shape[1]
     panels, harmonics = basis.shape
     anywhere = pl.BlockSpec(memory_space=pl.ANY)
@@ -122,15 +144,16 @@
             jax.ShapeDtypeStruct((STEPS, dirs, panels), jnp.bfloat16),
             jax.ShapeDtypeStruct((owners, 128), jnp.float32),
         ),
-        in_specs=[smem(), smem(), vmem(), anywhere, anywhere, anywhere, vmem(), vmem(), vmem(), vmem()],
+        in_specs=[smem(), smem(), vmem()] + [anywhere] * (2 * Y + 2) + [vmem()] * 4,
         out_specs=(vmem(), vmem()),
         scratch_shapes=[
-            pltpu.VMEM((old.shape[0] + 2 * here.shape[0], *old.shape[1:]), jnp.bfloat16),
+            pltpu.VMEM((Y * near[0].shape[0] + 2 * here.shape[0], *here.shape[1:]), jnp.bfloat16),
             pltpu.VMEM((harmonics, 128), jnp.float32),
-            pltpu.SemaphoreType.DMA((3,)),
+            pltpu.SemaphoreType.DMA((2 * Y + 2,)),
         ],
+        compiler_params=grant(16),
         name="second_step",
-    )(spots, counts, before, old, here, there, ztiles, zinv, incident, basis)
+    )(spots, counts, before, *near, *cross, here, there, ztiles, zinv, incident, basis)
 
 
 def sum_kernel(parts, out):
@@ -148,13 +171,14 @@
         out_shape=jax.ShapeDtypeStruct((steps, each, dirs), jnp.float32),
         in_specs=[vmem()],
         out_specs=vmem(),
+        compiler_params=grant(4),
         name="sum_parts",
     )(parts)
 
 
-def on_device(history, incident, ztiles, zinv, columns, lags, counts, basis):
+def march(history, incident, ztiles, zinv, columns, lags, counts, basis):
     rows, slots, tile = ztiles.shape[0], ztiles.shape[1], ztiles.shape[2]
-    levels, dirs, panels = history.shape
+    levels, dirs, _ = history.shape
     slots_dev = rows * slots
     owners = Y * Z * C
     cap = BLOCK_CAP * Z
@@ -176,19 +200,25 @@
     at = group * cap + position
     asks = jnp.arange(GROUPS * cap, dtype=jnp.int32)
     wanted = jnp.sum(jnp.where(at[None, :] == asks[:, None], spot[None, :], 0), axis=1)
-    asked = lax.all_to_all(wanted.reshape(GROUPS, cap), ("y", "c"), 0, 0, tiled=True)
-    first, second = pick(asked.reshape(GROUPS * cap), held)
-    shape = (GROUPS, cap, dirs, tile)
-    got = lax.all_to_all(first.reshape(shape), ("y", "c"), 0, 0, tiled=True)
+    swap = [(0, 1), (1, 0)]
+    both = jnp.concatenate([wanted, lax.ppermute(wanted, "c", swap)])
+    lists = [both] + [lax.ppermute(both, "y", [(i, (i + s) % Y) for i in range(Y)]) for s in range(1, Y)]
+    y, c = lax.axis_index("y"), lax.axis_index("c")
+    first, *later = pick(jnp.stack([y, c]), lists, held, cap)
+    got = lax.all_to_all(first.reshape(GROUPS, cap, dirs, tile), ("y", "c"), 0, 0, tiled=True)
     density = first_step(at, counts, got.reshape(GROUPS * cap, dirs, tile), ztiles, zinv, incident)
-    old = lax.all_to_all(second.reshape(shape), ("y", "c"), 0, 0, tiled=True)
     here = spread(density, ("y", "z"), Y * Z).reshape(Y * Z * rows, dirs, tile)
-    there = lax.ppermute(here, "c", [(0, 1), (1, 0)])
-    far_side = (own_c != lax.axis_index("c")).astype(jnp.int32)
-    fresh = GROUPS * cap + (far_side * (Y * Z) + own_y * Z + own_z) * rows + local
-    spots = jnp.where(flat_lags == 0, fresh, at)
+    near = later[:1] + [
+        lax.ppermute(later[s], "y", [(i, (i - s) % Y) for i in range(Y)]) for s in range(1, Y)
+    ]
+    cross = [lax.ppermute(piece, "c", swap) for piece in near]
+    there = lax.ppermute(here, "c", swap)
+    other = (own_c != c).astype(jnp.int32)
+    aged = (((own_y - y) % Y) * C + other) * cap + position
+    fresh = GROUPS * cap + (other * (Y * Z) + own_y * Z + own_z) * rows + local
+    spots = jnp.where(flat_lags == 0, fresh, aged)
     dens, far = second_step(
-        spots, counts, density, old.reshape(GROUPS * cap, dirs, tile), here, there, ztiles, zinv, incident, basis, owners
+        spots, counts, density, near, cross, here, there, ztiles, zinv, incident, basis, owners
     )
     each = basis.shape[1] // owners
     parts = lax.all_to_all(far.reshape(owners, 1, 128), E, 0, 0, tiled=True).reshape(owners, 128)
@@ -209,4 +239,4 @@
         P(E, None),
     )
     out_specs = (P(None, "dir", E), P(None, "dir", E))
-    return jax.shard_map(on_device, mesh=fine, in_specs=in_specs, out_specs=out_specs, check_vma=False)
+    return jax.shard_map(march, mesh=fine, in_specs=in_specs, out_specs=out_specs, check_vma=False)

time: 111 us -> 90.5 us (0.82)
  blocking collectives: 42.4 us -> 31.2 us
  waiting for transfers between devices: 25.4 us -> 15.5 us
  Pallas kernels: 12.5 us -> 6.79 us
  starting transfers between devices: 20.5 us -> 25.3 us
  local copies, waits for them, and re-layouts: 6.56 us -> 9.2 us
  other arithmetic: 2.27 us -> 1.12 us
    all_to_all x2 -> x0, waiting for transfers between devices: 13 us -> none  [the longest x1 9.19 us: on_device(): old = lax.all_to_all(second.reshape(shape), ('y', 'c'), 0, 0, tiled=True)]
    all_to_all x2 -> x0, starting transfers between devices: 12.6 us -> none  [the longest x1 6.41 us: on_device(): lax.all_to_all(wanted.reshape(GROUPS, cap), ('y', 'c'), 0, 0, tiled=True)]
    ppermute x1 -> x12, starting transfers between devices: 0.19 us -> 12.4 us  [the longest x3 3.77 us: march(): lax.ppermute(both, 'y', [(i, (i + s) % Y) for i in range(Y)])]
    all_to_all x3 -> x2, blocking collectives: 42.4 us -> 31.2 us  [the longest x1 16.2 us: march(): lax.all_to_all(far.reshape(owners, 1, 128), E, 0, 0, tiled=True)]
    ppermute x1 -> x12, waiting for transfers between devices: 0.01 us -> 6.24 us  [the longest x3 3.17 us: march(): lax.ppermute(both, 'y', [(i, (i + s) % Y) for i in range(Y)])]
    all_to_all x1 -> x2, starting transfers between devices: 7.71 us -> 12.9 us  [spread(): return lax.all_to_all(whole, axis, 0, 0, tiled=True)]
    unnamed x10 -> x28, local copies, waits for them, and re-layouts: 1.62 us -> 6 us
    all_to_all x1 -> x2, waiting for transfers between devices: 12.4 us -> 9.28 us  [spread(): return lax.all_to_all(whole, axis, 0, 0, tiled=True)]
  transfers between devices with their start and end apart: 4 -> 14, of which waited for: 3 -> 7; matrix products, arithmetic and copies ran while one was open for 2% -> 2% of each run, Pallas kernels for 0% -> 0%
where the time goes in v2:
time: 90.5 us; the launch traced here: 89.9 us
  blocking collectives  31.2 us (34%)
  starting transfers between devices  25.3 us (28%)
  waiting for transfers between devices  15.5 us (17%)
  local copies, waits for them, and re-layouts  9.2 us (10%)
  Pallas kernels  6.79 us (8%)
  other arithmetic  1.12 us (1%)
    all_to_all x1, blocking collectives, march(): lax.all_to_all(far.reshape(owners, 1, 128), E, 0, 0, tiled=True)  16.2 us
    all_to_all x1, blocking collectives, march(): lax.all_to_all(first.reshape(GROUPS, cap, dirs, tile), ('y', 'c'), 0, 0,...  15 us
    all_to_all x2, starting transfers between devices, spread(): return lax.all_to_all(whole, axis, 0, 0, tiled=True)  12.9 us
    all_to_all x2, waiting for transfers between devices, spread(): return lax.all_to_all(whole, axis, 0, 0, tiled=True)  9.28 us
    unnamed x28, local copies, waits for them, and re-layouts  6 us
    ppermute x3, starting transfers between devices, march(): lax.ppermute(both, 'y', [(i, (i + s) % Y) for i in range(Y)])  3.77 us
    ppermute x3, starting transfers between devices, march(): lax.ppermute(later[s], 'y', [(i, (i - s) % Y) for i in range(Y)])  3.66 us
    pallas_call x1, Pallas kernels, second_step(): pl.pallas_call(second_kernel, out_shape=(jax.ShapeDtypeStruct((STEPS, dir...  3.31 us
  transfers between devices with their start and end apart: 14, of which 7 were waited for; matrix products, arithmetic and copies ran while one was open for 2% of the time, Pallas kernels for 0%

profile of v2, /device:TPU:1, one launch (start us, length us, event | category | flops | bytes accessed | tf_op | source)
XLA Modules:
  0.0 89.9 jit_solution(1194816534275688866)
XLA Ops:
  0.6 0.8 fusion.9
  1.4 0.8 broadcast_in_dim.21
  2.2 9.0 %all-to-all-start = ((bf16[8,24,8,128]{3,2,1,0:T(8,128)(2,1)}), bf16[8,24,8,128]{3,2,1,0:T(8,128)(2,1)S(1)}, u32[]{:S(2)}, u32[]{:S(2)}) async-start(bf16[8,24,8,128]{3,2,1,0:T(8,128)(2,1)} %broadcast_in_dim.21), calls=%async_computation | async-start | bytes 786432 | tf_op jit(solution)/shard_map/all_to_all | solution.py:31
  11.2 0.8 reshape.176
  12.1 0.7 broadcast_add_fusion
  13.2 1.0 %collective-permute-start = (s32[256]{0:T(256)S(1)}, s32[256]{0:T(256)S(1)}, u32[]{:S(2)}, u32[]{:S(2)}) collective-permute-start(s32[256]{0:T(256)S(1)} %select_reduce_fusion), channel_id=1, source_target_pairs={{0,4},{4,0},{1,5},{5,1},{2,6},{6,2},{3,7},{7,3},{8,12},{12,8},{9,1... | collective-permute-start | bytes 3080 | tf_op jit(solution)/shard_map/ppermute | solution.py:204
  14.2 0.8 collective-permute-done
  15.1 2.7 %collective-permute-start.3 = (s32[512]{0:T(512)S(1)}, s32[512]{0:T(512)S(1)}, u32[]{:S(2)}, u32[]{:S(2)}) collective-permute-start(s32[512]{0:T(512)S(1)} %pad_add_fusion.refs_0_), channel_id=1, source_target_pairs={{0,192},{64,0},{128,64},{192,128},{1,193},{65,1},{129,65},{193,129... | collective-permute-start | bytes 6152 | tf_op jit(solution)/shard_map/ppermute | solution.py:205
  18.1 0.7 collective-permute-start.1
  18.9 3.1 %collective-permute-done.2.refs_2_ = s32[512]{0:T(512)S(1)} collective-permute-done((s32[512]{0:T(512)S(1)}, s32[512]{0:T(512)S(1)}, u32[]{:S(2)}, u32[]{:S(2)}) %collective-permute-start.2) | collective-permute-done | bytes 2080 | tf_op jit(solution)/shard_map/ppermute | solution.py:205
  22.1 3.4 %all-to-all-done = bf16[8,24,8,128]{3,2,1,0:T(8,128)(2,1)S(1)} async-done(((bf16[8,24,8,128]{3,2,1,0:T(8,128)(2,1)}), bf16[8,24,8,128]{3,2,1,0:T(8,128)(2,1)S(1)}, u32[]{:S(2)}, u32[]{:S(2)}) %all-to-all-start) | async-done | bytes 393248 | tf_op jit(solution)/shard_map/all_to_all | solution.py:31
  25.5 1.4 %pick.1 = (bf16[256,8,128]{2,1,0:T(8,128)(2,1)S(1)}, bf16[64,8,128]{2,1,0:T(8,128)(2,1)S(1)}, bf16[64,8,128]{2,1,0:T(8,128)(2,1)S(1)}, bf16[64,8,128]{2,1,0:T(8,128)(2,1)S(1)}, bf16[64,8,128]{2,1,0:T(8,128)(2,1)S(1)}) custom-call(s32[2]{0:T(128)S(1)} %pad_add_fusion.1.place, s32[512]{0:T(512)S(1)} %pad_add_fusion.refs_0_, ...), custom_call_target="tpu_custom_call" | custom-call | tf_op jit(solution)/shard_map/pick/pallas_call | solution.py:56
  26.9 15.0 %all_to_all.20 = bf16[8,32,8,128]{3,2,1,0:T(8,128)(2,1)S(1)} all-to-all(bf16[8,32,8,128]{3,2,1,0:T(8,128)(2,1)S(1)} %bitcast.16), channel_id=1, replica_groups=mesh['y'=4,'z'=8,'c'=2,'dir'=4] {'y','c'}, dimensions={0} | all-to-all | bytes 1048576 | tf_op jit(solution)/shard_map/all_to_all | solution.py:208
  41.9 1.9 %copy-done = bf16[3,32,128,128]{3,2,1,0:T(8,128)(2,1)S(1)} copy-done((bf16[3,32,128,128]{3,2,1,0:T(8,128)(2,1)S(1)}, bf16[3,32,128,128]{3,2,1,0:T(8,128)(2,1)}, u32[]{:S(2)}) %copy-start) | copy-done | bytes 3145752
  43.8 0.9 copy-done.2
  44.7 0.7 copy-done.7
  45.4 0.7 copy-done.9
  46.1 1.4 %first_step.1.before = bf16[3,8,128]{2,1,0:T(8,128)(2,1)S(1)} custom-call(s32[96]{0:T(128)S(1)} %get-tuple-element.24.spots, s32[3]{0:T(128)S(1)} %copy-done.9, bf16[256,8,128]{2,1,0:T(8,128)(2,1)S(1)} %bitcast.12, bf16[3,32,128,128]{3,2,1,0:T(8,128)(2,1)S(1)} %copy-done, bf16[3,128,128]{2,1,0:T(8,128)(2,1)S(1)} %copy-done.2, bf16[2,8,384]{2,1,0:T(8,128)(2,1)S(1)} %copy-done.7), custom_call_target="tpu_custom_call" | custom-call | tf_op jit(solution)/shard_map/first_step/pallas_call | solution.py:90
  47.5 0.7 broadcast_in_dim.36
  48.2 3.9 %all-to-all-start.2 = ((bf16[32,3,8,128]{3,2,1,0:T(8,128)(2,1)}), bf16[32,3,8,128]{3,2,1,0:T(8,128)(2,1)S(1)}, u32[]{:S(2)}, u32[]{:S(2)}) async-start(bf16[32,3,8,128]{3,2,1,0:T(8,128)(2,1)} %broadcast_in_dim.36), calls=%async_computation.2 | async-start | bytes 393216 | tf_op jit(solution)/shard_map/all_to_all | solution.py:31
  52.1 2.6 %collective-permute-start.4 = (bf16[64,8,128]{2,1,0:T(8,128)(2,1)}, bf16[64,8,128]{2,1,0:T(8,128)(2,1)}, u32[]{:S(2)}, u32[]{:S(2)}) collective-permute-start(bf16[64,8,128]{2,1,0:T(8,128)(2,1)} %copy-done.13), channel_id=1, source_target_pairs={{0,192},{64,0},{128,64},{192,128},{1,193},{65,1},{129,65},{193,129... | collective-permute-start | bytes 393224 | tf_op jit(solution)/shard_map/ppermute | solution.py:212
  55.1 0.6 collective-permute-start.6
  55.7 5.9 %all-to-all-done.2 = bf16[32,3,8,128]{3,2,1,0:T(8,128)(2,1)S(1)} async-done(((bf16[32,3,8,128]{3,2,1,0:T(8,128)(2,1)}), bf16[32,3,8,128]{3,2,1,0:T(8,128)(2,1)S(1)}, u32[]{:S(2)}, u32[]{:S(2)}) %all-to-all-start.2) | async-done | bytes 196640 | tf_op jit(solution)/shard_map/all_to_all | solution.py:31
  61.6 2.8 %collective-permute-start.11 = (bf16[96,8,128]{2,1,0:T(8,128)(2,1)S(1)}, bf16[96,8,128]{2,1,0:T(8,128)(2,1)S(1)}, u32[]{:S(2)}, u32[]{:S(2)}) collective-permute-start(bf16[96,8,128]{2,1,0:T(8,128)(2,1)S(1)} %bitcast.14), channel_id=1, source_target_pairs={{0,4},{4,0},{1,5},{5,1},{2,6},{6,2},{3,7},{7,3},{8,12},{12,8},{9,1... | collective-permute-start | bytes 589832 | tf_op jit(solution)/shard_map/ppermute | solution.py:215
  64.4 0.5 collective-permute-start.8
  65.1 1.0 %collective-permute-done.6.refs_3_ = bf16[64,8,128]{2,1,0:T(8,128)(2,1)} collective-permute-done((bf16[64,8,128]{2,1,0:T(8,128)(2,1)}, bf16[64,8,128]{2,1,0:T(8,128)(2,1)}, u32[]{:S(2)}, u32[]{:S(2)}) %collective-permute-start.6) | collective-permute-done | bytes 131104 | tf_op jit(solution)/shard_map/ppermute | solution.py:212
  66.6 1.2 %collective-permute-done.10.refs_7_ = bf16[64,8,128]{2,1,0:T(8,128)(2,1)S(1)} collective-permute-done((bf16[64,8,128]{2,1,0:T(8,128)(2,1)}, bf16[64,8,128]{2,1,0:T(8,128)(2,1)S(1)}, u32[]{:S(2)}, u32[]{:S(2)}) %collective-permute-start.10) | collective-permute-done | bytes 131104 | tf_op jit(solution)/shard_map/ppermute | solution.py:214
  67.9 0.9 %copy-done.4 = bf16[384,256]{1,0:T(8,128)(2,1)S(1)} copy-done((bf16[384,256]{1,0:T(8,128)(2,1)S(1)}, bf16[384,256]{1,0:T(8,128)(2,1)}, u32[]{:S(2)}) %copy-start.4) | copy-done | bytes 196632
  68.8 0.9 %copy-done.6 = bf16[64,8,128]{2,1,0:T(8,128)(2,1)S(1)} copy-done((bf16[64,8,128]{2,1,0:T(8,128)(2,1)S(1)}, bf16[64,8,128]{2,1,0:T(8,128)(2,1)}, u32[]{:S(2)}) %copy-start.6) | copy-done | bytes 131096
  69.7 3.3 %second_step.1 = (bf16[2,8,384]{2,1,0:T(8,128)(2,1)}, f32[64,128]{1,0:T(8,128)S(1)}) custom-call(s32[96]{0:T(128)S(1)} %get-tuple-element.25.spots, s32[3]{0:T(128)S(1)} %copy-done.10, bf16[3,8,128]{2,1,0:T(8,128)(2,1)S(1)} %first_step.1.before, bf16[64,8,128]{2,1,0:T(8,128)(2,1)S(1)} %copy-done.6, bf16[64,8,128]{2,1,0:T(8,128)(2,1)} %collective-permute-done.4.refs_1_, ...), custom_call_target="tpu_custom_call" | custom-call | tf_op jit(solution)/shard_map/second_step/pallas_call | solution.py:141
  73.0 16.2 %all_to_all.21 = f32[64,1,128]{2,1,0:T(1,128)S(1)} all-to-all(f32[64,1,128]{2,1,0:T(1,128)S(1)} %bitcast.18), channel_id=1, replica_groups=mesh['y'=4,'z'=8,'c'=2,'dir'=4] {'y','z','c'}, dimensions={0} | all-to-all | bytes 65536 | tf_op jit(solution)/shard_map/all_to_all | solution.py:224
  89.2 0.7 sum_parts.1
  (44 shorter events, 2.1 us)
Async XLA Ops:
  2.2 23.3 %all-to-all-start = ((bf16[8,24,8,128]{3,2,1,0:T(8,128)(2,1)}), bf16[8,24,8,128]{3,2,1,0:T(8,128)(2,1)S(1)}, u32[]{:S(2)}, u32[]{:S(2)}) async-start(bf16[8,24,8,128]{3,2,1,0:T(8,128)(2,1)} %broadcast_in_dim.21), calls=%async_computation | async-start | bytes 786432 | tf_op jit(solution)/shard_map/all_to_all | solution.py:31
  11.2 56.6 %copy-start.3 = (bf16[3,128,128]{2,1,0:T(8,128)(2,1)S(1)}, bf16[3,128,128]{2,1,0:T(8,128)(2,1)}, u32[]{:S(2)}) copy-start(bf16[3,128,128]{2,1,0:T(8,128)(2,1)} %refs_11_.1) | copy-start | bytes 294916
  11.2 56.6 %copy-start.8 = (bf16[2,8,384]{2,1,0:T(8,128)(2,1)S(1)}, bf16[2,8,384]{2,1,0:T(8,128)(2,1)}, u32[]{:S(2)}) copy-start(bf16[2,8,384]{2,1,0:T(8,128)(2,1)} %refs_12_.1) | copy-start | bytes 36868
  11.2 56.6 %copy-start.10 = (s32[3]{0:T(128)S(1)}, s32[3]{0:T(128)}, u32[]{:S(2)}) copy-start(s32[3]{0:T(128)} %counts.3) | copy-start | bytes 40
  13.2 1.9 %collective-permute-start = (s32[256]{0:T(256)S(1)}, s32[256]{0:T(256)S(1)}, u32[]{:S(2)}, u32[]{:S(2)}) collective-permute-start(s32[256]{0:T(256)S(1)} %select_reduce_fusion), channel_id=1, source_target_pairs={{0,4},{4,0},{1,5},{5,1},{2,6},{6,2},{3,7},{7,3},{8,12},{12,8},{9,1... | collective-permute-start | bytes 3080 | tf_op jit(solution)/shard_map/ppermute | solution.py:204
  15.1 3.9 %collective-permute-start.3 = (s32[512]{0:T(512)S(1)}, s32[512]{0:T(512)S(1)}, u32[]{:S(2)}, u32[]{:S(2)}) collective-permute-start(s32[512]{0:T(512)S(1)} %pad_add_fusion.refs_0_), channel_id=1, source_target_pairs={{0,192},{64,0},{128,64},{192,128},{1,193},{65,1},{129,65},{193,129... | collective-permute-start | bytes 6152 | tf_op jit(solution)/shard_map/ppermute | solution.py:205
  17.8 4.2 %collective-permute-start.2 = (s32[512]{0:T(512)S(1)}, s32[512]{0:T(512)S(1)}, u32[]{:S(2)}, u32[]{:S(2)}) collective-permute-start(s32[512]{0:T(512)S(1)} %pad_add_fusion.refs_0_), channel_id=1, source_target_pairs={{0,128},{64,192},{128,0},{192,64},{1,129},{65,193},{129,1},{193,65... | collective-permute-start | bytes 6152 | tf_op jit(solution)/shard_map/ppermute | solution.py:205
  18.1 3.9 %collective-permute-start.1 = (s32[512]{0:T(512)S(1)}, s32[512]{0:T(512)S(1)}, u32[]{:S(2)}, u32[]{:S(2)}) collective-permute-start(s32[512]{0:T(512)S(1)} %pad_add_fusion.refs_0_), channel_id=1, source_target_pairs={{0,64},{64,128},{128,192},{192,0},{1,65},{65,129},{129,193},{193,1... | collective-permute-start | bytes 6152 | tf_op jit(solution)/shard_map/ppermute | solution.py:205
  26.9 15.0 %copy-start.5 = (bf16[64,8,128]{2,1,0:T(8,128)(2,1)}, bf16[64,8,128]{2,1,0:T(8,128)(2,1)S(1)}, u32[]{:S(2)}) copy-start(bf16[64,8,128]{2,1,0:T(8,128)(2,1)S(1)} %get-tuple-element.10.refs_0_) | copy-start | bytes 393220
  26.9 15.0 %copy-start.11 = (bf16[64,8,128]{2,1,0:T(8,128)(2,1)}, bf16[64,8,128]{2,1,0:T(8,128)(2,1)S(1)}, u32[]{:S(2)}) copy-start(bf16[64,8,128]{2,1,0:T(8,128)(2,1)S(1)} %get-tuple-element.13) | copy-start | bytes 393220
  26.9 15.0 %copy-start.12 = (bf16[64,8,128]{2,1,0:T(8,128)(2,1)}, bf16[64,8,128]{2,1,0:T(8,128)(2,1)S(1)}, u32[]{:S(2)}) copy-start(bf16[64,8,128]{2,1,0:T(8,128)(2,1)S(1)} %get-tuple-element.12) | copy-start | bytes 393220
  26.9 15.0 %copy-start.13 = (bf16[64,8,128]{2,1,0:T(8,128)(2,1)}, bf16[64,8,128]{2,1,0:T(8,128)(2,1)S(1)}, u32[]{:S(2)}) copy-start(bf16[64,8,128]{2,1,0:T(8,128)(2,1)S(1)} %get-tuple-element.11) | copy-start | bytes 393220
  41.9 1.9 %copy-start = (bf16[3,32,128,128]{3,2,1,0:T(8,128)(2,1)S(1)}, bf16[3,32,128,128]{3,2,1,0:T(8,128)(2,1)}, u32[]{:S(2)}) copy-start(bf16[3,32,128,128]{3,2,1,0:T(8,128)(2,1)} %refs_10_.1) | copy-start | bytes 9437188
  43.8 0.9 copy-start.2
  44.7 0.7 copy-start.7
  45.4 0.7 copy-start.9
  46.1 21.8 %copy-start.1 = (bf16[3,32,128,128]{3,2,1,0:T(8,128)(2,1)S(1)}, bf16[3,32,128,128]{3,2,1,0:T(8,128)(2,1)}, u32[]{:S(2)}) copy-start(bf16[3,32,128,128]{3,2,1,0:T(8,128)(2,1)} %refs_10_.1) | copy-start | bytes 9437188
  48.2 13.4 %all-to-all-start.2 = ((bf16[32,3,8,128]{3,2,1,0:T(8,128)(2,1)}), bf16[32,3,8,128]{3,2,1,0:T(8,128)(2,1)S(1)}, u32[]{:S(2)}, u32[]{:S(2)}) async-start(bf16[32,3,8,128]{3,2,1,0:T(8,128)(2,1)} %broadcast_in_dim.36), calls=%async_computation.2 | async-start | bytes 393216 | tf_op jit(solution)/shard_map/all_to_all | solution.py:31
  52.1 12.3 %collective-permute-start.4 = (bf16[64,8,128]{2,1,0:T(8,128)(2,1)}, bf16[64,8,128]{2,1,0:T(8,128)(2,1)}, u32[]{:S(2)}, u32[]{:S(2)}) collective-permute-start(bf16[64,8,128]{2,1,0:T(8,128)(2,1)} %copy-done.13), channel_id=1, source_target_pairs={{0,192},{64,0},{128,64},{192,128},{1,193},{65,1},{129,65},{193,129... | collective-permute-start | bytes 393224 | tf_op jit(solution)/shard_map/ppermute | solution.py:212
  54.6 10.3 %collective-permute-start.5 = (bf16[64,8,128]{2,1,0:T(8,128)(2,1)}, bf16[64,8,128]{2,1,0:T(8,128)(2,1)}, u32[]{:S(2)}, u32[]{:S(2)}) collective-permute-start(bf16[64,8,128]{2,1,0:T(8,128)(2,1)} %copy-done.12), channel_id=1, source_target_pairs={{0,128},{64,192},{128,0},{192,64},{1,129},{65,193},{129,1},{193,65... | collective-permute-start | bytes 393224 | tf_op jit(solution)/shard_map/ppermute | solution.py:212
  55.1 11.0 %collective-permute-start.6 = (bf16[64,8,128]{2,1,0:T(8,128)(2,1)}, bf16[64,8,128]{2,1,0:T(8,128)(2,1)}, u32[]{:S(2)}, u32[]{:S(2)}) collective-permute-start(bf16[64,8,128]{2,1,0:T(8,128)(2,1)} %copy-done.11), channel_id=1, source_target_pairs={{0,64},{64,128},{128,192},{192,0},{1,65},{65,129},{129,193},{193,1... | collective-permute-start | bytes 393224 | tf_op jit(solution)/shard_map/ppermute | solution.py:212
  61.6 6.2 %collective-permute-start.11 = (bf16[96,8,128]{2,1,0:T(8,128)(2,1)S(1)}, bf16[96,8,128]{2,1,0:T(8,128)(2,1)S(1)}, u32[]{:S(2)}, u32[]{:S(2)}) collective-permute-start(bf16[96,8,128]{2,1,0:T(8,128)(2,1)S(1)} %bitcast.14), channel_id=1, source_target_pairs={{0,4},{4,0},{1,5},{5,1},{2,6},{6,2},{3,7},{7,3},{8,12},{12,8},{9,1... | collective-permute-start | bytes 589832 | tf_op jit(solution)/shard_map/ppermute | solution.py:215
  64.4 2.2 %collective-permute-start.7 = (bf16[64,8,128]{2,1,0:T(8,128)(2,1)}, bf16[64,8,128]{2,1,0:T(8,128)(2,1)S(1)}, u32[]{:S(2)}, u32[]{:S(2)}) collective-permute-start(bf16[64,8,128]{2,1,0:T(8,128)(2,1)} %copy-done.5), channel_id=1, source_target_pairs={{0,4},{4,0},{1,5},{5,1},{2,6},{6,2},{3,7},{7,3},{8,12},{12,8},{9,1... | collective-permute-start | bytes 393224 | tf_op jit(solution)/shard_map/ppermute | solution.py:214
  64.4 2.2 %collective-permute-start.8 = (bf16[64,8,128]{2,1,0:T(8,128)(2,1)}, bf16[64,8,128]{2,1,0:T(8,128)(2,1)S(1)}, u32[]{:S(2)}, u32[]{:S(2)}) collective-permute-start(bf16[64,8,128]{2,1,0:T(8,128)(2,1)} %collective-permute-done.4.refs_1_), channel_id=1, source_target_pairs={{0,4},{4,0},{1,5},{5,1},{2,6},{6,2},{3,7},{7,3},{8,12},{12,8},{9,1... | collective-permute-start | bytes 393224 | tf_op jit(solution)/shard_map/ppermute | solution.py:214
  64.9 1.7 %collective-permute-start.9 = (bf16[64,8,128]{2,1,0:T(8,128)(2,1)}, bf16[64,8,128]{2,1,0:T(8,128)(2,1)S(1)}, u32[]{:S(2)}, u32[]{:S(2)}) collective-permute-start(bf16[64,8,128]{2,1,0:T(8,128)(2,1)} %collective-permute-done.5.refs_2_), channel_id=1, source_target_pairs={{0,4},{4,0},{1,5},{5,1},{2,6},{6,2},{3,7},{7,3},{8,12},{12,8},{9,1... | collective-permute-start | bytes 393224 | tf_op jit(solution)/shard_map/ppermute | solution.py:214
  66.1 1.7 %collective-permute-start.10 = (bf16[64,8,128]{2,1,0:T(8,128)(2,1)}, bf16[64,8,128]{2,1,0:T(8,128)(2,1)S(1)}, u32[]{:S(2)}, u32[]{:S(2)}) collective-permute-start(bf16[64,8,128]{2,1,0:T(8,128)(2,1)} %collective-permute-done.6.refs_3_), channel_id=1, source_target_pairs={{0,4},{4,0},{1,5},{5,1},{2,6},{6,2},{3,7},{7,3},{8,12},{12,8},{9,1... | collective-permute-start | bytes 393224 | tf_op jit(solution)/shard_map/ppermute | solution.py:214
  67.8 0.9 %copy-start.4 = (bf16[384,256]{1,0:T(8,128)(2,1)S(1)}, bf16[384,256]{1,0:T(8,128)(2,1)}, u32[]{:S(2)}) copy-start(bf16[384,256]{1,0:T(8,128)(2,1)} %refs_13_.1) | copy-start | bytes 589828
  68.8 0.9 %copy-start.6 = (bf16[64,8,128]{2,1,0:T(8,128)(2,1)S(1)}, bf16[64,8,128]{2,1,0:T(8,128)(2,1)}, u32[]{:S(2)}) copy-start(bf16[64,8,128]{2,1,0:T(8,128)(2,1)} %copy-done.5) | copy-start | bytes 393220

commit v3 on v2

v3 whole, which is shorter than its diff:
```python
import jax
import jax.numpy as jnp
from jax import lax
from jax.experimental import pallas as pl
from jax.experimental.pallas import tpu as pltpu
from jax.sharding import Mesh, PartitionSpec as P


STEPS = 2
LEVELS = 8
Y, Z, C = 4, 8, 2
GROUPS = Y * C
E = ("y", "z", "c")
BLOCK_CAP = 4
CHUNK = 8
WHOLE = 65_000_000
SMALL = 8 << 20
SWAP = [(0, 1), (1, 0)]


def vmem():
    return pl.BlockSpec(memory_space=pltpu.VMEM)


def smem():
    return pl.BlockSpec(memory_space=pltpu.SMEM)


def hbm():
    return pl.BlockSpec(memory_space=pltpu.HBM)


def anywhere():
    return pl.BlockSpec(memory_space=pl.ANY)


def kernel_call(body, grant, **options):
    return pl.pallas_call(body, compiler_params=pltpu.CompilerParams(vmem_limit_bytes=grant), **options)


def fan_kernel(history, out):
    levels, _, panels = history.shape
    tile = out.shape[3]
    rows = panels // tile
    for level in range(levels):
        for row in range(rows):
            value = history[level, :, row * tile : (row + 1) * tile]
            for z in range(Z):
                out[z, level * rows + row] = value


def fan(history, tile):
    levels, dirs, panels = history.shape
    return kernel_call(
        fan_kernel,
        SMALL,
        out_shape=jax.ShapeDtypeStruct((Z, levels * panels // tile, dirs, tile), history.dtype),
        in_specs=[vmem()],
        out_specs=vmem(),
    )(history)


def whose(place, shift, other):
    y, c = place[0], place[1]
    return lax.rem(y - shift + Y, Y) * C + (c if other == 0 else 1 - c)


def pick_kernel(place, *refs):
    lists, held, first = refs[:Y], refs[Y], refs[Y + 1]
    cap = first.shape[0] // GROUPS
    mine = (place[0] * C + place[1]) * cap
    for shift in range(Y):
        for other in range(C):
            to = whose(place, shift, other) * cap

            @pl.loop(0, cap, step=16)
            def _(base):
                for k in range(16):
                    first[to + base + k] = held[lists[shift][other * GROUPS * cap + mine + base + k]]


def pick_later_kernel(place, *refs):
    lists, held, later = refs[:Y], refs[Y], refs[Y + 1 :]
    cap = later[0].shape[0] // C
    back = held.shape[0] // (Z * LEVELS)
    mine = (place[0] * C + place[1]) * cap
    for shift in range(Y):
        for other in range(C):

            @pl.loop(0, cap, step=16)
            def _(base):
                for k in range(16):
                    spot = lists[shift][other * GROUPS * cap + mine + base + k]
                    later[shift][other * cap + base + k] = held[jnp.maximum(spot - back, 0)]


def picks(place, lists, held, cap):
    def out(entries):
        return jax.ShapeDtypeStruct((entries, *held.shape[1:]), held.dtype)

    specs = [smem()] * (1 + Y) + [vmem()]
    first = kernel_call(
        pick_kernel, SMALL, out_shape=out(GROUPS * cap), in_specs=specs, out_specs=vmem()
    )(place, *lists, held)
    later = kernel_call(
        pick_later_kernel, SMALL, out_shape=[out(C * cap)] * Y, in_specs=specs, out_specs=[vmem()] * Y
    )(place, *lists, held)
    return first, later


def row_sum(spots, pool, ztiles, row):
    slots, tile = ztiles.shape[1], ztiles.shape[2]
    parts = []
    for k in range(slots):
        spot = spots[row * slots + k]
        value = pool[jnp.maximum(spot, 0)]
        parts.append(jnp.where(spot >= 0, value, jnp.zeros_like(value)))
    picked = jnp.concatenate(parts, axis=1)
    return jnp.dot(picked, ztiles[row].reshape(slots * tile, tile), preferred_element_type=jnp.float32)


def density_of(own, total, zinv):
    source = (own.astype(jnp.float32) - total).astype(jnp.bfloat16)
    return jnp.dot(source, zinv, preferred_element_type=jnp.float32).astype(jnp.bfloat16)


def start_all(pairs, sems, base=0):
    copies = [pltpu.make_async_copy(src, dst, sems.at[base + i]) for i, (src, dst) in enumerate(pairs)]
    for copy in copies:
        copy.start()
    return copies


def first_kernel(spots, got, ztiles_hbm, zinv_hbm, incident_hbm, out, spread_out, ztiles, zinv, incident, sems):
    rows, tile = ztiles.shape[0], ztiles.shape[2]
    tiles = start_all([(ztiles_hbm.at[r], ztiles.at[r]) for r in range(rows)], sems)
    rest = start_all([(zinv_hbm, zinv), (incident_hbm.at[0], incident)], sems, rows)
    for row in range(rows):
        tiles[row].wait()
        total = row_sum(spots, got, ztiles, row)
        if row == 0:
            for copy in rest:
                copy.wait()
        density = density_of(incident[:, row * tile : (row + 1) * tile], total, zinv[row])
        out[row] = density
        for to in range(spread_out.shape[0]):
            spread_out[to, row] = density


def first_step(spots, got, ztiles, zinv, incident):
    rows, tile, dirs = ztiles.shape[0], ztiles.shape[2], got.shape[1]
    return kernel_call(
        first_kernel,
        WHOLE,
        out_shape=(
            jax.ShapeDtypeStruct((rows, dirs, tile), jnp.bfloat16),
            jax.ShapeDtypeStruct((Y * Z, rows, dirs, tile), jnp.bfloat16),
        ),
        in_specs=[smem(), vmem(), hbm(), hbm(), hbm()],
        out_specs=(vmem(), vmem()),
        scratch_shapes=[
            pltpu.VMEM(ztiles.shape, ztiles.dtype),
            pltpu.VMEM(zinv.shape, zinv.dtype),
            pltpu.VMEM(incident.shape[1:], incident.dtype),
            pltpu.SemaphoreType.DMA((rows + 2,)),
        ],
    )(spots, got, ztiles, zinv, incident)


def aged_kernel(spots, before, *refs):
    near, cross = refs[:Y], refs[Y : 2 * Y]
    ztiles_hbm, basis_hbm, sums, far, pool, ztiles, basis, sems = refs[2 * Y :]
    rows = ztiles.shape[0]
    cap = near[0].shape[0] // C
    pairs = []
    for shift in range(Y):
        for source, at in ((near[shift], 0), (cross[shift], cap)):
            pairs.append((source.at[pl.ds(at, cap)], pool.at[pl.ds(len(pairs) * cap, cap)]))
    pieces = start_all(pairs, sems)
    tiles = start_all([(ztiles_hbm.at[r], ztiles.at[r]) for r in range(rows)], sems, len(pairs))
    weights = start_all([(basis_hbm, basis)], sems, len(pairs) + rows)
    for copy in pieces:
        copy.wait()
    for row in range(rows):
        tiles[row].wait()
        sums[row] = row_sum(spots, pool, ztiles, row)
    weights[0].wait()
    value = jnp.concatenate([before[row] for row in range(rows)], axis=1)
    far[...] = jnp.dot(value, basis[...], preferred_element_type=jnp.float32)


def aged_step(spots, before, near, cross, ztiles, basis):
    rows, dirs, tile = before.shape
    cap = near[0].shape[0] // C
    return kernel_call(
        aged_kernel,
        WHOLE,
        out_shape=(
            jax.ShapeDtypeStruct((rows, dirs, tile), jnp.float32),
            jax.ShapeDtypeStruct((dirs, basis.shape[1]), jnp.float32),
        ),
        in_specs=[smem(), vmem()] + [anywhere()] * (2 * Y) + [hbm(), hbm()],
        out_specs=(vmem(), vmem()),
        scratch_shapes=[
            pltpu.VMEM((2 * Y * cap, dirs, tile), jnp.bfloat16),
            pltpu.VMEM(ztiles.shape, ztiles.dtype),
            pltpu.VMEM(basis.shape, basis.dtype),
            pltpu.SemaphoreType.DMA((2 * Y + rows + 1,)),
        ],
    )(spots, before, *near, *cross, ztiles, basis)


def second_kernel(table, before, sums, far_first, here, there, ztiles_hbm, zinv_hbm, incident_hbm, basis_hbm, *refs):
    dens, far, pool, ztiles, zinv, incident, basis, flipped, sems, tile_sems = refs
    rows, slots, tile = ztiles.shape[0], ztiles.shape[1], ztiles.shape[2]
    near = here.shape[0]
    chunks = [lax.div(table[2 * rows * slots + row] + (CHUNK - 1), CHUNK) for row in range(rows)]

    def fetch(row, i):
        slot = table[row * slots + i]
        return pltpu.make_async_copy(ztiles_hbm.at[row, slot], ztiles.at[row, i], tile_sems.at[row, i])

    for row in range(rows):

        @pl.loop(0, chunks[row] * CHUNK)
        def _(i):
            fetch(row, i).start()

    blocks = start_all([(here, pool.at[pl.ds(0, near)]), (there, pool.at[pl.ds(near, near)])], sems)
    rest = start_all([(zinv_hbm, zinv), (incident_hbm.at[1], incident), (basis_hbm, basis)], sems, 2)
    for copy in blocks:
        copy.wait()
    for row in range(rows):

        @pl.loop(0, chunks[row] * CHUNK)
        def _(i):
            fetch(row, i).wait()

    for copy in rest:
        copy.wait()
    later = []
    for row in range(rows):

        def add(chunk, total):
            parts = []
            for k in range(CHUNK):
                spot = table[rows * slots + row * slots + chunk * CHUNK + k]
                value = pool[jnp.maximum(spot, 0)]
                parts.append(jnp.where(spot >= 0, value, jnp.zeros_like(value)))
            weights = ztiles[row, pl.ds(chunk * CHUNK, CHUNK)].reshape(CHUNK * tile, tile)
            return total + jnp.dot(jnp.concatenate(parts, axis=1), weights, preferred_element_type=jnp.float32)

        total = lax.fori_loop(0, chunks[row], add, sums[row])
        later.append(density_of(incident[:, row * tile : (row + 1) * tile], total, zinv[row]))
    value = jnp.concatenate(later, axis=1)
    dens[0] = jnp.concatenate([before[row] for row in range(rows)], axis=1)
    dens[1] = value
    far_second = jnp.dot(value, basis[...], preferred_element_type=jnp.float32)
    both = jnp.concatenate([far_first[...], far_second], axis=0)
    lanes = both.shape[0]
    flipped[:, :lanes] = both.T
    owners = far.shape[0]
    each = basis.shape[1] // owners
    cols = [flipped[pl.ds(c, owners, stride=each), :][:, :lanes] for c in range(each)]
    far[...] = jnp.concatenate([*cols, jnp.zeros((owners, far.shape[1] - each * lanes), jnp.float32)], axis=1)


def second_step(table, before, sums, far_first, here, there, ztiles, zinv, incident, basis, owners):
    _, dirs, tile = before.shape
    panels, harmonics = basis.shape
    return kernel_call(
        second_kernel,
        WHOLE,
        out_shape=(
            jax.ShapeDtypeStruct((STEPS, dirs, panels), jnp.bfloat16),
            jax.ShapeDtypeStruct((owners, 128), jnp.float32),
        ),
        in_specs=[smem(), vmem(), vmem(), vmem(), anywhere(), anywhere(), hbm(), hbm(), hbm(), hbm()],
        out_specs=(vmem(), vmem()),
        scratch_shapes=[
            pltpu.VMEM((2 * here.shape[0], dirs, tile), jnp.bfloat16),
            pltpu.VMEM(ztiles.shape, ztiles.dtype),
            pltpu.VMEM(zinv.shape, zinv.dtype),
            pltpu.VMEM(incident.shape[1:], incident.dtype),
            pltpu.VMEM(basis.shape, basis.dtype),
            pltpu.VMEM((harmonics, 128), jnp.float32),
            pltpu.SemaphoreType.DMA((5,)),
            pltpu.SemaphoreType.DMA(ztiles.shape[:2]),
        ],
    )(table, before, sums, far_first, here, there, ztiles, zinv, incident, basis)


def sum_kernel(parts, out):
    total = jnp.sum(parts[...], axis=0, keepdims=True)
    steps, each, dirs = out.shape
    for step in range(steps):
        for c in range(each):
            at = (c * steps + step) * dirs
            out[step, c : c + 1, :] = total[:, at : at + dirs]


def sum_parts(parts, steps, each, dirs):
    return kernel_call(
        sum_kernel,
        SMALL,
        out_shape=jax.ShapeDtypeStruct((steps, each, dirs), jnp.float32),
        in_specs=[vmem()],
        out_specs=vmem(),
    )(parts)


def shifted(value, axis, length, shift):
    return lax.ppermute(value, axis, [(i, (i + shift) % length) for i in range(length)])


def march(history, incident, ztiles, zinv, columns, lags, counts, basis):
    rows, slots, tile = ztiles.shape[0], ztiles.shape[1], ztiles.shape[2]
    levels, dirs, _ = history.shape
    slots_dev = rows * slots
    owners = Y * Z * C
    cap = BLOCK_CAP * Z
    held = lax.all_to_all(fan(history, tile), "z", 0, 0, tiled=True)
    held = held.reshape(Z * levels * rows, dirs, tile)
    flat_cols = columns.reshape(slots_dev)
    flat_lags = lags.reshape(slots_dev) - 1
    owner = flat_cols // rows
    local = flat_cols - owner * rows
    own_c = owner % C
    own_z = (owner // C) % Z
    own_y = owner // (C * Z)
    group = own_y * C + own_c
    spot = (own_z * levels + flat_lags) * rows + local
    ids = jnp.arange(slots_dev, dtype=jnp.int32)
    ahead = (group[:, None] == group[None, :]) & (ids[None, :] < ids[:, None])
    position = jnp.sum(ahead.astype(jnp.int32), axis=1)
    at = group * cap + position
    asks = jnp.arange(GROUPS * cap, dtype=jnp.int32)
    wanted = jnp.sum(jnp.where(at[None, :] == asks[:, None], spot[None, :], 0), axis=1)
    both = jnp.concatenate([wanted, lax.ppermute(wanted, "c", SWAP)])
    lists = [both] + [shifted(both, "y", Y, s) for s in range(1, Y)]
    y, c = lax.axis_index("y"), lax.axis_index("c")
    other = (own_c != c).astype(jnp.int32)
    live = (jnp.arange(slots, dtype=jnp.int32)[None, :] < counts[:, None]).reshape(slots_dev)
    new = live & (flat_lags == 0)
    spots = jnp.where(live, at, -1)
    aged = jnp.where(live & ~new, (((own_y - y) % Y) * C + other) * cap + position, -1)
    fresh = (other * (Y * Z) + own_y * Z + own_z) * rows + local
    new_rows = new.reshape(rows, slots)
    slot_ids = jnp.arange(slots, dtype=jnp.int32)
    rank = jnp.sum((new_rows[:, None, :] & (slot_ids[None, None, :] < slot_ids[None, :, None])).astype(jnp.int32), axis=2)
    put = new_rows[:, None, :] & (rank[:, None, :] == slot_ids[None, :, None])
    order = jnp.sum(jnp.where(put, slot_ids[None, None, :], 0), axis=2)
    where = jnp.sum(jnp.where(put, fresh.reshape(rows, 1, slots) + 1, 0), axis=2) - 1
    table = jnp.concatenate(
        [order.reshape(slots_dev), where.reshape(slots_dev), jnp.sum(new_rows.astype(jnp.int32), axis=1)]
    )
    first, later = picks(jnp.stack([y, c]), lists, held, cap)
    got = lax.all_to_all(first.reshape(GROUPS, cap, dirs, tile), ("y", "c"), 0, 0, tiled=True)
    near = [later[0]] + [shifted(later[s], "y", Y, -s) for s in range(1, Y)]
    cross = [lax.ppermute(piece, "c", SWAP) for piece in near]
    density, fanned = first_step(spots, got.reshape(GROUPS * cap, dirs, tile), ztiles, zinv, incident)
    here = lax.all_to_all(fanned, ("y", "z"), 0, 0, tiled=True).reshape(Y * Z * rows, dirs, tile)
    sums, far_first = aged_step(aged, density, near, cross, ztiles, basis)
    there = lax.ppermute(here, "c", SWAP)
    dens, far = second_step(
        table, density, sums, far_first, here, there, ztiles, zinv, incident, basis, owners
    )
    each = basis.shape[1] // owners
    parts = lax.all_to_all(far.reshape(owners, 1, 128), E, 0, 0, tiled=True).reshape(owners, 128)
    total = sum_parts(parts, STEPS, each, dirs)
    return dens, total.transpose(0, 2, 1)


def solution(mesh):
    fine = Mesh(mesh.devices.reshape(Y, Z, C, mesh.shape["dir"]), ("y", "z", "c", "dir"))
    in_specs = (
        P(None, "dir", E),
        P(None, "dir", E),
        P(E, None, None, None),
        P(E, None, None),
        P(E, None),
        P(E, None),
        P(E),
        P(E, None),
    )
    out_specs = (P(None, "dir", E), P(None, "dir", E))
    return jax.shard_map(march, mesh=fine, in_specs=in_specs, out_specs=out_specs, check_vma=False)
```

time: 90.5 us -> 95.6 us (1.056)
  Pallas kernels: 6.79 us -> 17.3 us
  waiting for transfers between devices: 15.5 us -> 6.64 us
  starting transfers between devices: 25.3 us -> 31.8 us
  local copies, waits for them, and re-layouts: 9.2 us -> 3.3 us
  other arithmetic: 1.12 us -> 3.62 us
    pallas_call x4 -> x7, Pallas kernels: 6.79 us -> 17.3 us  [the longest x1 4.99 us: second_step(): kernel_call(second_kernel, WHOLE, out_shape=(jax.ShapeDtypeStruct((STEPS,...]
    all_to_all x2, waiting for transfers between devices: 9.28 us -> 2.17 us  [the longest x1 2.17 us: march(): held = lax.all_to_all(fan(history, tile), 'z', 0, 0, tiled=True)]
    ppermute x12, starting transfers between devices: 12.4 us -> 17.7 us  [the longest x4 9.07 us: march(): cross = [lax.ppermute(piece, 'c', SWAP) for piece in near]]
    unnamed x28 -> x22, local copies, waits for them, and re-layouts: 6 us -> 2.21 us
    ppermute x12, waiting for transfers between devices: 6.24 us -> 4.47 us  [the longest x6 3.61 us: shifted(): lax.ppermute(value, axis, [(i, (i + shift) % length) for i in range(lengt...]
    broadcast_in_dim x2 -> x0, local copies, waits for them, and re-layouts: 1.54 us -> none  [spread(): whole = jnp.broadcast_to(value[None], (length, *value.shape))]
    all_to_all x2, starting transfers between devices: 12.9 us -> 14.2 us  [the longest x1 9 us: march(): held = lax.all_to_all(fan(history, tile), 'z', 0, 0, tiled=True)]
    reduce_sum x1 -> x4, other arithmetic: 0.17 us -> 1.4 us  [the longest x1 0.9 us: march(): jnp.sum(new_rows.astype(jnp.int32), axis=1)]
  transfers between devices with their start and end apart: 14 -> 14, of which waited for: 7 -> 6; matrix products, arithmetic and copies ran while one was open for 2% -> 5% of each run, Pallas kernels for 0% -> 5%
where the time goes in v3:
time: 95.6 us; the launch traced here: 95 us
  starting transfers between devices  31.8 us (33%)
  blocking collectives  31.5 us (33%)
  Pallas kernels  17.3 us (18%)
  waiting for transfers between devices  6.64 us (7%)
  other arithmetic  3.62 us (4%)
  local copies, waits for them, and re-layouts  3.3 us (3%)
    all_to_all x1, blocking collectives, march(): lax.all_to_all(far.reshape(owners, 1, 128), E, 0, 0, tiled=True)  16.5 us
    all_to_all x1, blocking collectives, march(): lax.all_to_all(first.reshape(GROUPS, cap, dirs, tile), ('y', 'c'), 0, 0,...  15.1 us
    ppermute x4, starting transfers between devices, march(): cross = [lax.ppermute(piece, 'c', SWAP) for piece in near]  9.07 us
    all_to_all x1, starting transfers between devices, march(): held = lax.all_to_all(fan(history, tile), 'z', 0, 0, tiled=True)  9 us
    ppermute x6, starting transfers between devices, shifted(): lax.ppermute(value, axis, [(i, (i + shift) % length) for i in range(lengt...  7.45 us
    all_to_all x1, starting transfers between devices, march(): lax.all_to_all(fanned, ('y', 'z'), 0, 0, tiled=True)  5.16 us
    pallas_call x1, Pallas kernels, second_step(): kernel_call(second_kernel, WHOLE, out_shape=(jax.ShapeDtypeStruct((STEPS,...  4.99 us
    pallas_call x1, Pallas kernels, first_step(): kernel_call(first_kernel, WHOLE, out_shape=(jax.ShapeDtypeStruct((rows, d...  4.57 us
  transfers between devices with their start and end apart: 14, of which 6 were waited for; matrix products, arithmetic and copies ran while one was open for 5% of the time, Pallas kernels for 5%

profile of v3, /device:TPU:1, one launch (start us, length us, event | category | flops | bytes accessed | tf_op | source)
XLA Modules:
  0.0 95.0 jit_solution(5832273760503423513)
XLA Ops:
  0.6 0.8 copy-done.1
  1.4 0.8 shard_map.95
  2.2 9.0 %all-to-all-start = ((bf16[8,24,8,128]{3,2,1,0:T(8,128)(2,1)}), bf16[8,24,8,128]{3,2,1,0:T(8,128)(2,1)S(1)}, u32[]{:S(2)}, u32[]{:S(2)}) async-start(bf16[8,24,8,128]{3,2,1,0:T(8,128)(2,1)} %shard_map.95), calls=%async_computation | async-start | bytes 786432 | tf_op jit(solution)/shard_map/all_to_all | solution.py:322
  11.2 0.8 reshape.221
  12.0 0.9 convert_reduce_fusion.2
  13.0 0.7 iota_compare_fusion.4
  14.0 0.6 broadcast_select_fusion
  14.7 1.0 %collective-permute-start = (s32[256]{0:T(256)S(1)}, s32[256]{0:T(256)S(1)}, u32[]{:S(2)}, u32[]{:S(2)}) collective-permute-start(s32[256]{0:T(256)S(1)} %select_reduce_fusion), channel_id=1, source_target_pairs={{0,4},{4,0},{1,5},{5,1},{2,6},{6,2},{3,7},{7,3},{8,12},{12,8},{9,1... | collective-permute-start | bytes 3080 | tf_op jit(solution)/shard_map/ppermute | solution.py:339
  15.8 0.8 collective-permute-done
  16.6 2.7 %collective-permute-start.3 = (s32[512]{0:T(512)S(1)}, s32[512]{0:T(512)S(1)}, u32[]{:S(2)}, u32[]{:S(2)}) collective-permute-start(s32[512]{0:T(512)S(1)} %pad_add_fusion.refs_0_), channel_id=1, source_target_pairs={{0,192},{64,0},{128,64},{192,128},{1,193},{65,1},{129,65},{193,129... | collective-permute-start | bytes 6152 | tf_op jit(solution)/shard_map/ppermute | solution.py:313
  19.7 0.7 collective-permute-start.1
  20.5 2.8 %collective-permute-done.2.refs_2_ = s32[512]{0:T(512)S(1)} collective-permute-done((s32[512]{0:T(512)S(1)}, s32[512]{0:T(512)S(1)}, u32[]{:S(2)}, u32[]{:S(2)}) %collective-permute-start.2) | collective-permute-done | bytes 2080 | tf_op jit(solution)/shard_map/ppermute | solution.py:313
  23.3 2.2 %all-to-all-done = bf16[8,24,8,128]{3,2,1,0:T(8,128)(2,1)S(1)} async-done(((bf16[8,24,8,128]{3,2,1,0:T(8,128)(2,1)}), bf16[8,24,8,128]{3,2,1,0:T(8,128)(2,1)S(1)}, u32[]{:S(2)}, u32[]{:S(2)}) %all-to-all-start) | async-done | bytes 393248 | tf_op jit(solution)/shard_map/all_to_all | solution.py:322
  25.5 1.1 %shard_map.96 = bf16[256,8,128]{2,1,0:T(8,128)(2,1)S(1)} custom-call(s32[2]{0:T(128)S(1)} %pad_add_fusion.2.place, s32[512]{0:T(512)S(1)} %pad_add_fusion.refs_0_, s32[512]{0:T(512)S(1)} %collective-permute-done.1.refs_1_, s32[512]{0:T(512)S(1)} %collective-permute-done.2.refs_2_, s32[512]{0:T(512)S(1)} %collective-permute-done.3.refs_3_, ...), custom_call_target="tpu_custom_call" | custom-call | tf_op jit(solution)/shard_map/pallas_call | solution.py:102
  26.6 15.1 %all_to_all.20 = bf16[8,32,8,128]{3,2,1,0:T(8,128)(2,1)} all-to-all(bf16[8,32,8,128]{3,2,1,0:T(8,128)(2,1)S(1)} %bitcast.13), channel_id=1, replica_groups=mesh['y'=4,'z'=8,'c'=2,'dir'=4] {'y','c'}, dimensions={0} | all-to-all | bytes 1048576 | tf_op jit(solution)/shard_map/all_to_all | solution.py:358
  41.6 4.6 %shard_map.97 = (bf16[3,8,128]{2,1,0:T(8,128)(2,1)}, bf16[32,3,8,128]{3,2,1,0:T(8,128)(2,1)}) custom-call(s32[96]{0:T(128)} %get-tuple-element.26.spots, bf16[256,8,128]{2,1,0:T(8,128)(2,1)} %bitcast.15, bf16[3,32,128,128]{3,2,1,0:T(8,128)(2,1)} %ztiles_hbm.3, bf16[3,128,128]{2,1,0:T(8,128)(2,1)} %zinv_hbm.3, bf16[2,8,384]{2,1,0:T(8,128)(2,1)} %incident_hbm.3), custom_call_target="tpu_custom_call" | custom-call | tf_op jit(solution)/shard_map/pallas_call | solution.py:152
  46.2 5.2 %all-to-all-start.2 = ((bf16[32,3,8,128]{3,2,1,0:T(8,128)(2,1)}), bf16[32,3,8,128]{3,2,1,0:T(8,128)(2,1)S(1)}, u32[]{:S(2)}, u32[]{:S(2)}) async-start(bf16[32,3,8,128]{3,2,1,0:T(8,128)(2,1)} %get-tuple-element.19), calls=%async_computation.2 | async-start | bytes 393216 | tf_op jit(solution)/shard_map/all_to_all | solution.py:362
  51.4 1.2 %shard_map.98 = (bf16[64,8,128]{2,1,0:T(8,128)(2,1)S(1)}, bf16[64,8,128]{2,1,0:T(8,128)(2,1)S(1)}, bf16[64,8,128]{2,1,0:T(8,128)(2,1)S(1)}, bf16[64,8,128]{2,1,0:T(8,128)(2,1)S(1)}) custom-call(s32[2]{0:T(128)S(1)} %pad_add_fusion.2.place, s32[512]{0:T(512)S(1)} %pad_add_fusion.refs_0_, s32[512]{0:T(512)S(1)} %collective-permute-done.1.refs_1_, ...), custom_call_target="tpu_custom_call" | custom-call | tf_op jit(solution)/shard_map/pallas_call | solution.py:105
  52.6 2.6 %collective-permute-start.4 = (bf16[64,8,128]{2,1,0:T(8,128)(2,1)S(1)}, bf16[64,8,128]{2,1,0:T(8,128)(2,1)S(1)}, u32[]{:S(2)}, u32[]{:S(2)}) collective-permute-start(bf16[64,8,128]{2,1,0:T(8,128)(2,1)S(1)} %get-tuple-element.14), channel_id=1, source_target_pairs={{0,192},{64,0},{128,64},{192,128},{1,193},{65,1},{129,65},{193,129... | collective-permute-start | bytes 393224 | tf_op jit(solution)/shard_map/ppermute | solution.py:313
  55.7 0.6 collective-permute-start.6
  56.6 2.5 %collective-permute-start.7 = (bf16[64,8,128]{2,1,0:T(8,128)(2,1)S(1)}, bf16[64,8,128]{2,1,0:T(8,128)(2,1)S(1)}, u32[]{:S(2)}, u32[]{:S(2)}) collective-permute-start(bf16[64,8,128]{2,1,0:T(8,128)(2,1)S(1)} %get-tuple-element.13.refs_0_), channel_id=1, source_target_pairs={{0,4},{4,0},{1,5},{5,1},{2,6},{6,2},{3,7},{7,3},{8,12},{12,8},{9,1... | collective-permute-start | bytes 393224 | tf_op jit(solution)/shard_map/ppermute | solution.py:360
  59.2 3.9 %collective-permute-start.8 = (bf16[64,8,128]{2,1,0:T(8,128)(2,1)S(1)}, bf16[64,8,128]{2,1,0:T(8,128)(2,1)S(1)}, u32[]{:S(2)}, u32[]{:S(2)}) collective-permute-start(bf16[64,8,128]{2,1,0:T(8,128)(2,1)S(1)} %collective-permute-done.4.refs_1_), channel_id=1, source_target_pairs={{0,4},{4,0},{1,5},{5,1},{2,6},{6,2},{3,7},{7,3},{8,12},{12,8},{9,1... | collective-permute-start | bytes 393224 | tf_op jit(solution)/shard_map/ppermute | solution.py:360
  63.2 1.9 %collective-permute-start.9 = (bf16[64,8,128]{2,1,0:T(8,128)(2,1)S(1)}, bf16[64,8,128]{2,1,0:T(8,128)(2,1)S(1)}, u32[]{:S(2)}, u32[]{:S(2)}) collective-permute-start(bf16[64,8,128]{2,1,0:T(8,128)(2,1)S(1)} %collective-permute-done.5.refs_2_), channel_id=1, source_target_pairs={{0,4},{4,0},{1,5},{5,1},{2,6},{6,2},{3,7},{7,3},{8,12},{12,8},{9,1... | collective-permute-start | bytes 393224 | tf_op jit(solution)/shard_map/ppermute | solution.py:360
  65.0 0.7 collective-permute-done.6.refs_3_
  65.7 0.7 collective-permute-start.10
  66.7 0.6 pad_add_fusion.1.table
  67.5 0.6 copy-done.7
  68.2 4.0 %shard_map.99 = (f32[3,8,128]{2,1,0:T(8,128)}, f32[8,256]{1,0:T(8,128)}) custom-call(s32[96]{0:T(128)} %get-tuple-element.33.spots, bf16[3,8,128]{2,1,0:T(8,128)(2,1)} %get-tuple-element.12.before, bf16[64,8,128]{2,1,0:T(8,128)(2,1)} %copy-done, bf16[64,8,128]{2,1,0:T(8,128)(2,1)} %copy-done.4, bf16[64,8,128]{2,1,0:T(8,128)(2,1)} %copy-done.5, ...), custom_call_target="tpu_custom_call" | custom-call | tf_op jit(solution)/shard_map/pallas_call | solution.py:195
  72.2 0.7 copy-done.3
  72.9 5.0 %shard_map.100 = (bf16[2,8,384]{2,1,0:T(8,128)(2,1)}, f32[64,128]{1,0:T(8,128)}) custom-call(s32[195]{0:T(256)} %pad_add_fusion.1.table, bf16[3,8,128]{2,1,0:T(8,128)(2,1)} %get-tuple-element.12.before, f32[3,8,128]{2,1,0:T(8,128)} %get-tuple-element.17.sums, f32[8,256]{1,0:T(8,128)} %get-tuple-element.18.far_first, bf16[96,8,128]{2,1,0:T(8,128)(2,1)} %bitcast.17, ...), custom_call_target="tpu_custom_call" | custom-call | tf_op jit(solution)/shard_map/pallas_call | solution.py:271
  77.9 16.5 %all_to_all.21 = f32[64,1,128]{2,1,0:T(1,128)S(1)} all-to-all(f32[64,1,128]{2,1,0:T(1,128)} %bitcast.18), channel_id=1, replica_groups=mesh['y'=4,'z'=8,'c'=2,'dir'=4] {'y','z','c'}, dimensions={0} | all-to-all | bytes 65536 | tf_op jit(solution)/shard_map/all_to_all | solution.py:369
  94.3 0.7 shard_map.101
  (46 shorter events, 2.4 us)
Async XLA Ops:
  0.6 0.8 copy-start.1
  2.2 23.3 %all-to-all-start = ((bf16[8,24,8,128]{3,2,1,0:T(8,128)(2,1)}), bf16[8,24,8,128]{3,2,1,0:T(8,128)(2,1)S(1)}, u32[]{:S(2)}, u32[]{:S(2)}) async-start(bf16[8,24,8,128]{3,2,1,0:T(8,128)(2,1)} %shard_map.95), calls=%async_computation | async-start | bytes 786432 | tf_op jit(solution)/shard_map/all_to_all | solution.py:322
  14.7 1.9 %collective-permute-start = (s32[256]{0:T(256)S(1)}, s32[256]{0:T(256)S(1)}, u32[]{:S(2)}, u32[]{:S(2)}) collective-permute-start(s32[256]{0:T(256)S(1)} %select_reduce_fusion), channel_id=1, source_target_pairs={{0,4},{4,0},{1,5},{5,1},{2,6},{6,2},{3,7},{7,3},{8,12},{12,8},{9,1... | collective-permute-start | bytes 3080 | tf_op jit(solution)/shard_map/ppermute | solution.py:339
  16.6 3.9 %collective-permute-start.3 = (s32[512]{0:T(512)S(1)}, s32[512]{0:T(512)S(1)}, u32[]{:S(2)}, u32[]{:S(2)}) collective-permute-start(s32[512]{0:T(512)S(1)} %pad_add_fusion.refs_0_), channel_id=1, source_target_pairs={{0,192},{64,0},{128,64},{192,128},{1,193},{65,1},{129,65},{193,129... | collective-permute-start | bytes 6152 | tf_op jit(solution)/shard_map/ppermute | solution.py:313
  19.3 3.9 %collective-permute-start.2 = (s32[512]{0:T(512)S(1)}, s32[512]{0:T(512)S(1)}, u32[]{:S(2)}, u32[]{:S(2)}) collective-permute-start(s32[512]{0:T(512)S(1)} %pad_add_fusion.refs_0_), channel_id=1, source_target_pairs={{0,128},{64,192},{128,0},{192,64},{1,129},{65,193},{129,1},{193,65... | collective-permute-start | bytes 6152 | tf_op jit(solution)/shard_map/ppermute | solution.py:313
  19.7 3.6 %collective-permute-start.1 = (s32[512]{0:T(512)S(1)}, s32[512]{0:T(512)S(1)}, u32[]{:S(2)}, u32[]{:S(2)}) collective-permute-start(s32[512]{0:T(512)S(1)} %pad_add_fusion.refs_0_), channel_id=1, source_target_pairs={{0,64},{64,128},{128,192},{192,0},{1,65},{65,129},{129,193},{193,1... | collective-permute-start | bytes 6152 | tf_op jit(solution)/shard_map/ppermute | solution.py:313
  46.2 20.2 %all-to-all-start.2 = ((bf16[32,3,8,128]{3,2,1,0:T(8,128)(2,1)}), bf16[32,3,8,128]{3,2,1,0:T(8,128)(2,1)S(1)}, u32[]{:S(2)}, u32[]{:S(2)}) async-start(bf16[32,3,8,128]{3,2,1,0:T(8,128)(2,1)} %get-tuple-element.19), calls=%async_computation.2 | async-start | bytes 393216 | tf_op jit(solution)/shard_map/all_to_all | solution.py:362
  52.6 14.8 %copy-start = (bf16[64,8,128]{2,1,0:T(8,128)(2,1)}, bf16[64,8,128]{2,1,0:T(8,128)(2,1)S(1)}, u32[]{:S(2)}) copy-start(bf16[64,8,128]{2,1,0:T(8,128)(2,1)S(1)} %get-tuple-element.13.refs_0_) | copy-start | bytes 393220
  52.6 6.6 %collective-permute-start.4 = (bf16[64,8,128]{2,1,0:T(8,128)(2,1)S(1)}, bf16[64,8,128]{2,1,0:T(8,128)(2,1)S(1)}, u32[]{:S(2)}, u32[]{:S(2)}) collective-permute-start(bf16[64,8,128]{2,1,0:T(8,128)(2,1)S(1)} %get-tuple-element.14), channel_id=1, source_target_pairs={{0,192},{64,0},{128,64},{192,128},{1,193},{65,1},{129,65},{193,129... | collective-permute-start | bytes 393224 | tf_op jit(solution)/shard_map/ppermute | solution.py:313
  55.2 8.0 %collective-permute-start.5 = (bf16[64,8,128]{2,1,0:T(8,128)(2,1)S(1)}, bf16[64,8,128]{2,1,0:T(8,128)(2,1)S(1)}, u32[]{:S(2)}, u32[]{:S(2)}) collective-permute-start(bf16[64,8,128]{2,1,0:T(8,128)(2,1)S(1)} %get-tuple-element.15), channel_id=1, source_target_pairs={{0,128},{64,192},{128,0},{192,64},{1,129},{65,193},{129,1},{193,65... | collective-permute-start | bytes 393224 | tf_op jit(solution)/shard_map/ppermute | solution.py:313
  55.7 10.0 %collective-permute-start.6 = (bf16[64,8,128]{2,1,0:T(8,128)(2,1)S(1)}, bf16[64,8,128]{2,1,0:T(8,128)(2,1)S(1)}, u32[]{:S(2)}, u32[]{:S(2)}) collective-permute-start(bf16[64,8,128]{2,1,0:T(8,128)(2,1)S(1)} %get-tuple-element.16), channel_id=1, source_target_pairs={{0,64},{64,128},{128,192},{192,0},{1,65},{65,129},{129,193},{193,1... | collective-permute-start | bytes 393224 | tf_op jit(solution)/shard_map/ppermute | solution.py:313
  56.6 10.7 %collective-permute-start.7 = (bf16[64,8,128]{2,1,0:T(8,128)(2,1)S(1)}, bf16[64,8,128]{2,1,0:T(8,128)(2,1)S(1)}, u32[]{:S(2)}, u32[]{:S(2)}) collective-permute-start(bf16[64,8,128]{2,1,0:T(8,128)(2,1)S(1)} %get-tuple-element.13.refs_0_), channel_id=1, source_target_pairs={{0,4},{4,0},{1,5},{5,1},{2,6},{6,2},{3,7},{7,3},{8,12},{12,8},{9,1... | collective-permute-start | bytes 393224 | tf_op jit(solution)/shard_map/ppermute | solution.py:360
  59.2 8.2 %copy-start.4 = (bf16[64,8,128]{2,1,0:T(8,128)(2,1)}, bf16[64,8,128]{2,1,0:T(8,128)(2,1)S(1)}, u32[]{:S(2)}) copy-start(bf16[64,8,128]{2,1,0:T(8,128)(2,1)S(1)} %collective-permute-done.4.refs_1_) | copy-start | bytes 393220
  59.2 8.1 %collective-permute-start.8 = (bf16[64,8,128]{2,1,0:T(8,128)(2,1)S(1)}, bf16[64,8,128]{2,1,0:T(8,128)(2,1)S(1)}, u32[]{:S(2)}, u32[]{:S(2)}) collective-permute-start(bf16[64,8,128]{2,1,0:T(8,128)(2,1)S(1)} %collective-permute-done.4.refs_1_), channel_id=1, source_target_pairs={{0,4},{4,0},{1,5},{5,1},{2,6},{6,2},{3,7},{7,3},{8,12},{12,8},{9,1... | collective-permute-start | bytes 393224 | tf_op jit(solution)/shard_map/ppermute | solution.py:360
  63.2 4.3 %copy-start.5 = (bf16[64,8,128]{2,1,0:T(8,128)(2,1)}, bf16[64,8,128]{2,1,0:T(8,128)(2,1)S(1)}, u32[]{:S(2)}) copy-start(bf16[64,8,128]{2,1,0:T(8,128)(2,1)S(1)} %collective-permute-done.5.refs_2_) | copy-start | bytes 393220
  63.2 4.2 %collective-permute-start.9 = (bf16[64,8,128]{2,1,0:T(8,128)(2,1)S(1)}, bf16[64,8,128]{2,1,0:T(8,128)(2,1)S(1)}, u32[]{:S(2)}, u32[]{:S(2)}) collective-permute-start(bf16[64,8,128]{2,1,0:T(8,128)(2,1)S(1)} %collective-permute-done.5.refs_2_), channel_id=1, source_target_pairs={{0,4},{4,0},{1,5},{5,1},{2,6},{6,2},{3,7},{7,3},{8,12},{12,8},{9,1... | collective-permute-start | bytes 393224 | tf_op jit(solution)/shard_map/ppermute | solution.py:360
  65.7 1.8 %copy-start.6 = (bf16[64,8,128]{2,1,0:T(8,128)(2,1)}, bf16[64,8,128]{2,1,0:T(8,128)(2,1)S(1)}, u32[]{:S(2)}) copy-start(bf16[64,8,128]{2,1,0:T(8,128)(2,1)S(1)} %collective-permute-done.6.refs_3_) | copy-start | bytes 393220
  65.7 1.7 %collective-permute-start.10 = (bf16[64,8,128]{2,1,0:T(8,128)(2,1)S(1)}, bf16[64,8,128]{2,1,0:T(8,128)(2,1)S(1)}, u32[]{:S(2)}, u32[]{:S(2)}) collective-permute-start(bf16[64,8,128]{2,1,0:T(8,128)(2,1)S(1)} %collective-permute-done.6.refs_3_), channel_id=1, source_target_pairs={{0,4},{4,0},{1,5},{5,1},{2,6},{6,2},{3,7},{7,3},{8,12},{12,8},{9,1... | collective-permute-start | bytes 393224 | tf_op jit(solution)/shard_map/ppermute | solution.py:360
  66.5 5.7 %copy-start.2 = (bf16[32,3,8,128]{3,2,1,0:T(8,128)(2,1)}, bf16[32,3,8,128]{3,2,1,0:T(8,128)(2,1)S(1)}, u32[]{:S(2)}) copy-start(bf16[32,3,8,128]{3,2,1,0:T(8,128)(2,1)S(1)} %all-to-all-done.2) | copy-start | bytes 589828
  66.5 5.7 %collective-permute-start.11 = (bf16[96,8,128]{2,1,0:T(8,128)(2,1)S(1)}, bf16[96,8,128]{2,1,0:T(8,128)(2,1)S(1)}, u32[]{:S(2)}, u32[]{:S(2)}) collective-permute-start(bf16[96,8,128]{2,1,0:T(8,128)(2,1)S(1)} %bitcast.16), channel_id=1, source_target_pairs={{0,4},{4,0},{1,5},{5,1},{2,6},{6,2},{3,7},{7,3},{8,12},{12,8},{9,1... | collective-permute-start | bytes 589832 | tf_op jit(solution)/shard_map/ppermute | solution.py:364
  67.4 0.7 copy-start.7
  67.4 0.7 copy-start.8
  67.4 0.8 copy-start.9
  67.4 0.8 copy-start.10
  72.2 0.7 copy-start.3

commit v4 on v3

v4 whole, which is shorter than its diff:
```python
import jax
import jax.numpy as jnp
from jax import lax
from jax.experimental import pallas as pl
from jax.experimental.pallas import tpu as pltpu
from jax.sharding import Mesh, PartitionSpec as P


STEPS = 2
LEVELS = 8
Y, Z, C = 4, 8, 2
GROUPS = Y * C
E = ("y", "z", "c")
BLOCK_CAP = 4
CHUNK = 8
SMALL = 8 << 20
LARGE = 12 << 20
SWAP = [(0, 1), (1, 0)]


def vmem():
    return pl.BlockSpec(memory_space=pltpu.VMEM)


def smem():
    return pl.BlockSpec(memory_space=pltpu.SMEM)


def hbm():
    return pl.BlockSpec(memory_space=pltpu.HBM)


def anywhere():
    return pl.BlockSpec(memory_space=pl.ANY)


def kernel_call(body, grant, **options):
    return pl.pallas_call(body, compiler_params=pltpu.CompilerParams(vmem_limit_bytes=grant), **options)


def near_core(value):
    return pltpu.with_memory_space_constraint(value, pltpu.VMEM)


def off_core(value):
    return pltpu.with_memory_space_constraint(value, pltpu.HBM)


def fan_kernel(history, out):
    levels, _, panels = history.shape
    tile = out.shape[3]
    rows = panels // tile
    for level in range(levels):
        for row in range(rows):
            value = history[level, :, row * tile : (row + 1) * tile]
            for z in range(Z):
                out[z, level * rows + row] = value


def fan(history, tile):
    levels, dirs, panels = history.shape
    return kernel_call(
        fan_kernel,
        SMALL,
        out_shape=pltpu.VMEM((Z, levels * panels // tile, dirs, tile), history.dtype),
        in_specs=[vmem()],
        out_specs=vmem(),
    )(off_core(history))


def whose(place, shift, other):
    y, c = place[0], place[1]
    return lax.rem(y - shift + Y, Y) * C + (c if other == 0 else 1 - c)


def pick_kernel(place, *refs):
    lists, held, first = refs[:Y], refs[Y], refs[Y + 1]
    cap = first.shape[0] // GROUPS
    mine = (place[0] * C + place[1]) * cap
    for shift in range(Y):
        for other in range(C):
            to = whose(place, shift, other) * cap

            @pl.loop(0, cap, step=16)
            def _(base):
                for k in range(16):
                    first[to + base + k] = held[lists[shift][other * GROUPS * cap + mine + base + k]]


def pick_later_kernel(place, *refs):
    lists, held, later = refs[:Y], refs[Y], refs[Y + 1 :]
    cap = later[0].shape[0] // C
    back = held.shape[0] // (Z * LEVELS)
    mine = (place[0] * C + place[1]) * cap
    for shift in range(Y):
        for other in range(C):

            @pl.loop(0, cap, step=16)
            def _(base):
                for k in range(16):
                    spot = lists[shift][other * GROUPS * cap + mine + base + k]
                    later[shift][other * cap + base + k] = held[jnp.maximum(spot - back, 0)]


def picks(place, lists, held, cap):
    def out(entries):
        return pltpu.VMEM((entries, *held.shape[1:]), held.dtype)

    held = near_core(held)
    specs = [smem()] * (1 + Y) + [vmem()]
    first = kernel_call(
        pick_kernel, SMALL, out_shape=out(GROUPS * cap), in_specs=specs, out_specs=vmem()
    )(place, *lists, held)
    later = kernel_call(
        pick_later_kernel, SMALL, out_shape=[out(C * cap)] * Y, in_specs=specs, out_specs=[vmem()] * Y
    )(place, *lists, held)
    return first, later


def pieces_of(spots, base, load):
    parts = []
    for k in range(CHUNK):
        spot = spots[base + k]
        value = load(jnp.maximum(spot, 0))
        parts.append(jnp.where(spot >= 0, value, jnp.zeros_like(value)))
    return jnp.concatenate(parts, axis=1)


def row_sum(spots, base, load, ztiles, row, chunks, total):
    tile = ztiles.shape[-1]

    def add(chunk, total):
        weights = ztiles[row, pl.ds(chunk * CHUNK, CHUNK)].reshape(CHUNK * tile, tile)
        picked = pieces_of(spots, base + row * ztiles.shape[1] + chunk * CHUNK, load)
        return total + jnp.dot(picked, weights, preferred_element_type=jnp.float32)

    return lax.fori_loop(0, chunks, add, total)


def chunks_of(count):
    return lax.div(count + (CHUNK - 1), CHUNK)


def density_of(own, total, zinv):
    source = (own.astype(jnp.float32) - total).astype(jnp.bfloat16)
    return jnp.dot(source, zinv, preferred_element_type=jnp.float32).astype(jnp.bfloat16)


def start_all(pairs, sems, base=0):
    copies = [pltpu.make_async_copy(src, dst, sems.at[base + i]) for i, (src, dst) in enumerate(pairs)]
    for copy in copies:
        copy.start()
    return copies


def chunk_copy(ztiles_hbm, ztiles, sems, row, chunk):
    part = pl.ds(chunk * CHUNK, CHUNK)
    return pltpu.make_async_copy(ztiles_hbm.at[row, part], ztiles.at[row, part], sems.at[row, chunk])


def start_rows(ztiles_hbm, ztiles, sems, chunks):
    for row in range(ztiles.shape[0]):
        for chunk in range(ztiles.shape[1] // CHUNK):

            @pl.when(chunk < chunks[row])
            def _():
                chunk_copy(ztiles_hbm, ztiles, sems, row, chunk).start()


def wait_row(ztiles_hbm, ztiles, sems, chunks, row):
    for chunk in range(ztiles.shape[1] // CHUNK):

        @pl.when(chunk < chunks[row])
        def _():
            chunk_copy(ztiles_hbm, ztiles, sems, row, chunk).wait()


def first_kernel(spots, got, ztiles_hbm, zinv_hbm, incident_hbm, out, spread_out, ztiles, zinv, incident, sems, tile_sems):
    rows, slots, tile = ztiles.shape[0], ztiles.shape[1], ztiles.shape[2]
    chunks = [chunks_of(spots[rows * slots + row]) for row in range(rows)]
    start_rows(ztiles_hbm, ztiles, tile_sems, chunks)
    rest = start_all([(zinv_hbm, zinv), (incident_hbm.at[0], incident)], sems)
    for row in range(rows):
        wait_row(ztiles_hbm, ztiles, tile_sems, chunks, row)
        total = jnp.zeros(incident.shape[:1] + (tile,), jnp.float32)
        total = row_sum(spots, 0, lambda spot: got[spot], ztiles, row, chunks[row], total)
        if row == 0:
            for copy in rest:
                copy.wait()
        density = density_of(incident[:, row * tile : (row + 1) * tile], total, zinv[row])
        out[row] = density
        for to in range(spread_out.shape[0]):
            spread_out[to, row] = density


def first_step(spots, got, ztiles, zinv, incident):
    rows, slots, tile, dirs = ztiles.shape[0], ztiles.shape[1], ztiles.shape[2], got.shape[1]
    return kernel_call(
        first_kernel,
        LARGE,
        out_shape=(
            pltpu.VMEM((rows, dirs, tile), jnp.bfloat16),
            pltpu.VMEM((Y * Z, rows, dirs, tile), jnp.bfloat16),
        ),
        in_specs=[smem(), vmem(), hbm(), hbm(), hbm()],
        out_specs=(vmem(), vmem()),
        scratch_shapes=[
            pltpu.VMEM(ztiles.shape, ztiles.dtype),
            pltpu.VMEM(zinv.shape, zinv.dtype),
            pltpu.VMEM(incident.shape[1:], incident.dtype),
            pltpu.SemaphoreType.DMA((2,)),
            pltpu.SemaphoreType.DMA((rows, slots // CHUNK)),
        ],
    )(spots, near_core(got), off_core(ztiles), off_core(zinv), off_core(incident))


def aged_kernel(spots, table, before, *refs):
    near, cross = refs[:Y], refs[Y : 2 * Y]
    ztiles_hbm, zinv_hbm, incident_hbm, basis_hbm, packed, fresh, zinv, basis, pool, ztiles, incident, sems, tile_sems, fresh_sems = refs[2 * Y :]
    rows, slots, tile = ztiles.shape[0], ztiles.shape[1], ztiles.shape[2]
    cap = near[0].shape[0] // C
    panels = rows * tile
    pairs = []
    for shift in range(Y):
        for source, at in ((near[shift], 0), (cross[shift], cap)):
            pairs.append((source.at[pl.ds(at, cap)], pool.at[pl.ds(len(pairs) * cap, cap)]))
    pieces = start_all(pairs, sems)
    rest = start_all([(basis_hbm, basis), (incident_hbm.at[1], incident), (zinv_hbm, zinv)], sems, len(pairs))
    chunks = [chunks_of(spots[rows * slots + row]) for row in range(rows)]
    start_rows(ztiles_hbm, ztiles, tile_sems, chunks)
    lag_one = []
    for row in range(rows):
        for k in range(CHUNK):
            source = ztiles_hbm.at[row, table[row * slots + k]]
            lag_one.append(pltpu.make_async_copy(source, fresh.at[row, k], fresh_sems.at[row, k]))
    for copy in lag_one:
        copy.start()
    for copy in pieces:
        copy.wait()
    for copy in rest:
        copy.wait()
    for row in range(rows):
        wait_row(ztiles_hbm, ztiles, tile_sems, chunks, row)
        own = incident[:, row * tile : (row + 1) * tile].astype(jnp.float32)
        total = jnp.zeros(own.shape, jnp.float32)
        total = row_sum(spots, 0, lambda spot: pool[spot], ztiles, row, chunks[row], total)
        packed[0, :, row * tile : (row + 1) * tile] = own
        packed[1, :, row * tile : (row + 1) * tile] = total
    value = jnp.concatenate([before[row] for row in range(rows)], axis=1)
    packed[2, :, :] = value.astype(jnp.float32)
    packed[3, :, : basis.shape[1]] = jnp.dot(value, basis[...], preferred_element_type=jnp.float32)
    packed[3, :, basis.shape[1] :] = jnp.zeros((value.shape[0], panels - basis.shape[1]), jnp.float32)
    for copy in lag_one:
        copy.wait()


def aged_step(spots, table, before, near, cross, ztiles, zinv, incident, basis):
    rows, dirs, tile = before.shape
    slots = ztiles.shape[1]
    cap = near[0].shape[0] // C
    return kernel_call(
        aged_kernel,
        LARGE,
        out_shape=(
            pltpu.VMEM((4, dirs, rows * tile), jnp.float32),
            pltpu.VMEM((rows, CHUNK, tile, tile), ztiles.dtype),
            pltpu.VMEM(zinv.shape, zinv.dtype),
            pltpu.VMEM(basis.shape, basis.dtype),
        ),
        in_specs=[smem(), smem(), vmem()] + [anywhere()] * (2 * Y) + [hbm()] * 4,
        out_specs=[vmem()] * 4,
        scratch_shapes=[
            pltpu.VMEM((2 * Y * cap, dirs, tile), jnp.bfloat16),
            pltpu.VMEM(ztiles.shape, ztiles.dtype),
            pltpu.VMEM(incident.shape[1:], incident.dtype),
            pltpu.SemaphoreType.DMA((2 * Y + 3,)),
            pltpu.SemaphoreType.DMA((rows, slots // CHUNK)),
            pltpu.SemaphoreType.DMA((rows, CHUNK)),
        ],
    )(
        spots,
        table,
        near_core(before),
        *near,
        *cross,
        off_core(ztiles),
        off_core(zinv),
        off_core(incident),
        off_core(basis),
    )


def second_kernel(table, packed, fresh, zinv, basis, here, there, ztiles_hbm, dens, far, ztiles, flipped, tile_sems):
    rows, slots, tile = ztiles_hbm.shape[0], ztiles_hbm.shape[1], ztiles_hbm.shape[2]
    near = here.shape[0]

    def load(spot):
        ours = here[jnp.minimum(spot, near - 1)]
        theirs = there[jnp.maximum(spot - near, 0)]
        return jnp.where(spot < near, ours, theirs)

    later = []
    for row in range(rows):
        chunks = chunks_of(table[2 * rows * slots + row])
        at = pl.ds(row * tile, tile)
        first = pieces_of(table, rows * slots + row * slots, load)
        total = packed[1, :, at] + jnp.dot(
            first, fresh[row].reshape(CHUNK * tile, tile), preferred_element_type=jnp.float32
        )

        def more(chunk, total):
            copies = []
            for k in range(CHUNK):
                source = ztiles_hbm.at[row, table[row * slots + chunk * CHUNK + k]]
                copies.append(pltpu.make_async_copy(source, ztiles.at[k], tile_sems.at[k]))
            for copy in copies:
                copy.start()
            for copy in copies:
                copy.wait()
            picked = pieces_of(table, rows * slots + row * slots + chunk * CHUNK, load)
            return total + jnp.dot(
                picked, ztiles[...].reshape(CHUNK * tile, tile), preferred_element_type=jnp.float32
            )

        total = lax.fori_loop(1, chunks, more, total)
        later.append(density_of(packed[0, :, at], total, zinv[row]))
    value = jnp.concatenate(later, axis=1)
    dens[0] = packed[2].astype(dens.dtype)
    dens[1] = value
    far_second = jnp.dot(value, basis[...], preferred_element_type=jnp.float32)
    both = jnp.concatenate([packed[3, :, : basis.shape[1]], far_second], axis=0)
    lanes = both.shape[0]
    flipped[:, :lanes] = both.T
    owners = far.shape[0]
    each = basis.shape[1] // owners
    cols = [flipped[pl.ds(c, owners, stride=each), :][:, :lanes] for c in range(each)]
    far[...] = jnp.concatenate([*cols, jnp.zeros((owners, far.shape[1] - each * lanes), jnp.float32)], axis=1)


def second_step(table, packed, fresh, zinv, basis, here, there, ztiles, owners):
    tile, dirs = here.shape[2], here.shape[1]
    panels, harmonics = basis.shape
    return kernel_call(
        second_kernel,
        LARGE,
        out_shape=(
            jax.ShapeDtypeStruct((STEPS, dirs, panels), jnp.bfloat16),
            pltpu.VMEM((owners, 128), jnp.float32),
        ),
        in_specs=[smem()] + [vmem()] * 6 + [hbm()],
        out_specs=(vmem(), vmem()),
        scratch_shapes=[
            pltpu.VMEM((CHUNK, tile, tile), ztiles.dtype),
            pltpu.VMEM((harmonics, 128), jnp.float32),
            pltpu.SemaphoreType.DMA((CHUNK,)),
        ],
    )(
        table,
        near_core(packed),
        near_core(fresh),
        near_core(zinv),
        near_core(basis),
        near_core(here),
        near_core(there),
        off_core(ztiles),
    )


def sum_kernel(parts, out):
    total = jnp.sum(parts[...], axis=0, keepdims=True)
    steps, each, dirs = out.shape
    for step in range(steps):
        for c in range(each):
            at = (c * steps + step) * dirs
            out[step, c : c + 1, :] = total[:, at : at + dirs]


def sum_parts(parts, steps, each, dirs):
    return kernel_call(
        sum_kernel,
        SMALL,
        out_shape=jax.ShapeDtypeStruct((steps, each, dirs), jnp.float32),
        in_specs=[vmem()],
        out_specs=vmem(),
    )(near_core(parts))


def shifted(value, axis, length, shift):
    return lax.ppermute(value, axis, [(i, (i + shift) % length) for i in range(length)])


def march(history, incident, ztiles, zinv, columns, lags, counts, basis):
    rows, slots, tile = ztiles.shape[0], ztiles.shape[1], ztiles.shape[2]
    levels, dirs, _ = history.shape
    slots_dev = rows * slots
    owners = Y * Z * C
    cap = BLOCK_CAP * Z
    held = lax.all_to_all(fan(history, tile), "z", 0, 0, tiled=True)
    held = held.reshape(Z * levels * rows, dirs, tile)
    flat_cols = columns.reshape(slots_dev)
    flat_lags = lags.reshape(slots_dev) - 1
    owner = flat_cols // rows
    local = flat_cols - owner * rows
    own_c = owner % C
    own_z = (owner // C) % Z
    own_y = owner // (C * Z)
    group = own_y * C + own_c
    spot = (own_z * levels + flat_lags) * rows + local
    ids = jnp.arange(slots_dev, dtype=jnp.int32)
    ahead = (group[:, None] == group[None, :]) & (ids[None, :] < ids[:, None])
    position = jnp.sum(ahead.astype(jnp.int32), axis=1)
    at = group * cap + position
    asks = jnp.arange(GROUPS * cap, dtype=jnp.int32)
    wanted = jnp.sum(jnp.where(at[None, :] == asks[:, None], spot[None, :], 0), axis=1)
    both = jnp.concatenate([wanted, lax.ppermute(wanted, "c", SWAP)])
    lists = [both] + [shifted(both, "y", Y, s) for s in range(1, Y)]
    y, c = lax.axis_index("y"), lax.axis_index("c")
    other = (own_c != c).astype(jnp.int32)
    live = (jnp.arange(slots, dtype=jnp.int32)[None, :] < counts[:, None]).reshape(slots_dev)
    new = live & (flat_lags == 0)
    spots = jnp.concatenate([jnp.where(live, at, -1), counts])
    old = jnp.where(live & ~new, (((own_y - y) % Y) * C + other) * cap + position, -1)
    aged = jnp.concatenate([old, counts])
    fresh = (other * (Y * Z) + own_y * Z + own_z) * rows + local
    new_rows = new.reshape(rows, slots)
    slot_ids = jnp.arange(slots, dtype=jnp.int32)
    rank = jnp.sum((new_rows[:, None, :] & (slot_ids[None, None, :] < slot_ids[None, :, None])).astype(jnp.int32), axis=2)
    put = new_rows[:, None, :] & (rank[:, None, :] == slot_ids[None, :, None])
    order = jnp.sum(jnp.where(put, slot_ids[None, None, :], 0), axis=2)
    where = jnp.sum(jnp.where(put, fresh.reshape(rows, 1, slots) + 1, 0), axis=2) - 1
    table = jnp.concatenate(
        [order.reshape(slots_dev), where.reshape(slots_dev), jnp.sum(new_rows.astype(jnp.int32), axis=1)]
    )
    first, later = picks(jnp.stack([y, c]), lists, held, cap)
    got = lax.all_to_all(first.reshape(GROUPS, cap, dirs, tile), ("y", "c"), 0, 0, tiled=True)
    near = [later[0]] + [shifted(later[s], "y", Y, -s) for s in range(1, Y)]
    cross = [lax.ppermute(piece, "c", SWAP) for piece in near]
    density, fanned = first_step(spots, got.reshape(GROUPS * cap, dirs, tile), ztiles, zinv, incident)
    here = lax.all_to_all(fanned, ("y", "z"), 0, 0, tiled=True).reshape(Y * Z * rows, dirs, tile)
    packed, lag_one, inverse, weights = aged_step(aged, table, density, near, cross, ztiles, zinv, incident, basis)
    there = lax.ppermute(here, "c", SWAP)
    dens, far = second_step(table, packed, lag_one, inverse, weights, here, there, ztiles, owners)
    each = basis.shape[1] // owners
    parts = lax.all_to_all(far.reshape(owners, 1, 128), E, 0, 0, tiled=True).reshape(owners, 128)
    total = sum_parts(parts, STEPS, each, dirs)
    return dens, total.transpose(0, 2, 1)


def solution(mesh):
    fine = Mesh(mesh.devices.reshape(Y, Z, C, mesh.shape["dir"]), ("y", "z", "c", "dir"))
    in_specs = (
        P(None, "dir", E),
        P(None, "dir", E),
        P(E, None, None, None),
        P(E, None, None),
        P(E, None),
        P(E, None),
        P(E),
        P(E, None),
    )
    out_specs = (P(None, "dir", E), P(None, "dir", E))
    return jax.shard_map(march, mesh=fine, in_specs=in_specs, out_specs=out_specs, check_vma=False)
```

time: 95.6 us -> 92.7 us (0.970)
  blocking collectives: 31.5 us -> 16.2 us
  waiting for transfers between devices: 6.64 us -> 18 us
  starting transfers between devices: 31.8 us -> 36.4 us
  local copies, waits for them, and re-layouts: 3.3 us -> 1.1 us
  other arithmetic: 3.62 us -> 2.55 us
    all_to_all x1 -> x0, blocking collectives: 15.1 us -> none  [march(): lax.all_to_all(first.reshape(GROUPS, cap, dirs, tile), ('y', 'c'), 0, 0,...]
    all_to_all x0 -> x1, waiting for transfers between devices: none -> 9.27 us  [march(): lax.all_to_all(first.reshape(GROUPS, cap, dirs, tile), ('y', 'c'), 0, 0,...]
    all_to_all x0 -> x1, starting transfers between devices: none -> 5.84 us  [march(): lax.all_to_all(first.reshape(GROUPS, cap, dirs, tile), ('y', 'c'), 0, 0,...]
    unnamed x22 -> x2, local copies, waits for them, and re-layouts: 2.21 us -> 0.01 us
    ppermute x4, starting transfers between devices: 9.07 us -> 8.09 us  [march(): cross = [lax.ppermute(piece, 'c', SWAP) for piece in near]]
  transfers between devices with their start and end apart: 14 -> 15, of which waited for: 6 -> 8; matrix products, arithmetic and copies ran while one was open for 5% -> 4% of each run, Pallas kernels for 5% -> 7%
where the time goes in v4:
time: 92.7 us; the launch traced here: 92.2 us
  starting transfers between devices  36.4 us (39%)
  waiting for transfers between devices  18 us (19%)
  Pallas kernels  17.2 us (19%)
  blocking collectives  16.2 us (17%)
  other arithmetic  2.55 us (3%)
  local copies, waits for them, and re-layouts  1.1 us (1%)
    all_to_all x1, blocking collectives, march(): lax.all_to_all(far.reshape(owners, 1, 128), E, 0, 0, tiled=True)  16.2 us
    all_to_all x1, waiting for transfers between devices, march(): lax.all_to_all(first.reshape(GROUPS, cap, dirs, tile), ('y', 'c'), 0, 0,...  9.27 us
    all_to_all x1, starting transfers between devices, march(): held = lax.all_to_all(fan(history, tile), 'z', 0, 0, tiled=True)  9 us
    ppermute x4, starting transfers between devices, march(): cross = [lax.ppermute(piece, 'c', SWAP) for piece in near]  8.09 us
    ppermute x6, starting transfers between devices, shifted(): lax.ppermute(value, axis, [(i, (i + shift) % length) for i in range(lengt...  7.45 us
    all_to_all x1, starting transfers between devices, march(): lax.all_to_all(first.reshape(GROUPS, cap, dirs, tile), ('y', 'c'), 0, 0,...  5.84 us
    pallas_call x1, Pallas kernels, aged_step(): kernel_call(aged_kernel, LARGE, out_shape=(pltpu.VMEM((4, dirs, rows * ti...  5.4 us
    all_to_all x1, starting transfers between devices, march(): lax.all_to_all(fanned, ('y', 'z'), 0, 0, tiled=True)  4.9 us
  transfers between devices with their start and end apart: 15, of which 8 were waited for; matrix products, arithmetic and copies ran while one was open for 4% of the time, Pallas kernels for 7%

profile of v4, /device:TPU:1, one launch (start us, length us, event | category | flops | bytes accessed | tf_op | source)
XLA Modules:
  0.0 92.2 jit_solution(17562675750347955972)
XLA Ops:
  0.6 1.6 %shard_map.95 = bf16[8,24,8,128]{3,2,1,0:T(8,128)(2,1)} custom-call(bf16[8,8,384]{2,1,0:T(8,128)(2,1)} %history.1), custom_call_target="tpu_custom_call" | custom-call | tf_op jit(solution)/shard_map/pallas_call | solution.py:62
  2.2 9.0 %all-to-all-start = ((bf16[8,24,8,128]{3,2,1,0:T(8,128)(2,1)}), bf16[8,24,8,128]{3,2,1,0:T(8,128)(2,1)S(1)}, u32[]{:S(2)}, u32[]{:S(2)}) async-start(bf16[8,24,8,128]{3,2,1,0:T(8,128)(2,1)} %shard_map.95), calls=%async_computation | async-start | bytes 786432 | tf_op jit(solution)/shard_map/all_to_all | solution.py:398
  11.2 0.8 reshape.221
  12.0 0.9 convert_reduce_fusion.2
  13.0 0.7 iota_compare_fusion.4
  14.2 1.0 %collective-permute-start = (s32[256]{0:T(256)S(1)}, s32[256]{0:T(256)S(1)}, u32[]{:S(2)}, u32[]{:S(2)}) collective-permute-start(s32[256]{0:T(256)S(1)} %select_reduce_fusion), channel_id=1, source_target_pairs={{0,4},{4,0},{1,5},{5,1},{2,6},{6,2},{3,7},{7,3},{8,12},{12,8},{9,1... | collective-permute-start | bytes 3080 | tf_op jit(solution)/shard_map/ppermute | solution.py:415
  15.2 0.8 collective-permute-done
  16.0 2.7 %collective-permute-start.3 = (s32[512]{0:T(512)S(1)}, s32[512]{0:T(512)S(1)}, u32[]{:S(2)}, u32[]{:S(2)}) collective-permute-start(s32[512]{0:T(512)S(1)} %pad_add_fusion.refs_0_), channel_id=1, source_target_pairs={{0,192},{64,0},{128,64},{192,128},{1,193},{65,1},{129,65},{193,129... | collective-permute-start | bytes 6152 | tf_op jit(solution)/shard_map/ppermute | solution.py:389
  18.8 0.3 collective-permute-start.2
  19.1 0.7 collective-permute-start.1
  19.9 2.8 %collective-permute-done.2.refs_2_ = s32[512]{0:T(512)S(1)} collective-permute-done((s32[512]{0:T(512)S(1)}, s32[512]{0:T(512)S(1)}, u32[]{:S(2)}, u32[]{:S(2)}) %collective-permute-start.2) | collective-permute-done | bytes 2080 | tf_op jit(solution)/shard_map/ppermute | solution.py:389
  22.8 2.7 %all-to-all-done = bf16[8,24,8,128]{3,2,1,0:T(8,128)(2,1)S(1)} async-done(((bf16[8,24,8,128]{3,2,1,0:T(8,128)(2,1)}), bf16[8,24,8,128]{3,2,1,0:T(8,128)(2,1)S(1)}, u32[]{:S(2)}, u32[]{:S(2)}) %all-to-all-start) | async-done | bytes 393248 | tf_op jit(solution)/shard_map/all_to_all | solution.py:398
  25.5 1.8 %shard_map.96 = bf16[256,8,128]{2,1,0:T(8,128)(2,1)} custom-call(s32[2]{0:T(128)S(1)} %pad_add_fusion.4.place, s32[512]{0:T(512)S(1)} %pad_add_fusion.refs_0_, s32[512]{0:T(512)S(1)} %collective-permute-done.1.refs_1_, s32[512]{0:T(512)S(1)} %collective-permute-done.2.refs_2_, s32[512]{0:T(512)S(1)} %collective-permute-done.3.refs_3_, ...), custom_call_target="tpu_custom_call" | custom-call | tf_op jit(solution)/shard_map/pallas_call | solution.py:111
  27.4 5.8 %all-to-all-start.1 = ((bf16[8,32,8,128]{3,2,1,0:T(8,128)(2,1)}), bf16[8,32,8,128]{3,2,1,0:T(8,128)(2,1)S(1)}, u32[]{:S(2)}, u32[]{:S(2)}) async-start(bf16[8,32,8,128]{3,2,1,0:T(8,128)(2,1)} %bitcast.3), calls=%async_computation.1 | async-start | bytes 1048576 | tf_op jit(solution)/shard_map/all_to_all | solution.py:435
  33.3 9.3 %all-to-all-done.1 = bf16[8,32,8,128]{3,2,1,0:T(8,128)(2,1)S(1)} async-done(((bf16[8,32,8,128]{3,2,1,0:T(8,128)(2,1)}), bf16[8,32,8,128]{3,2,1,0:T(8,128)(2,1)S(1)}, u32[]{:S(2)}, u32[]{:S(2)}) %all-to-all-start.1) | async-done | bytes 524320 | tf_op jit(solution)/shard_map/all_to_all | solution.py:435
  42.5 4.5 %shard_map.97 = (bf16[3,8,128]{2,1,0:T(8,128)(2,1)S(1)}, bf16[32,3,8,128]{3,2,1,0:T(8,128)(2,1)}) custom-call(s32[99]{0:T(128)S(1)} %get-tuple-element.38.spots, bf16[256,8,128]{2,1,0:T(8,128)(2,1)S(1)} %bitcast.13, bf16[3,32,128,128]{3,2,1,0:T(8,128)(2,1)} %ztiles_hbm.3, bf16[3,128,128]{2,1,0:T(8,128)(2,1)} %refs_9_.1, bf16[2,8,384]{2,1,0:T(8,128)(2,1)} %refs_10_.1), custom_call_target="tpu_custom_call" | custom-call | tf_op jit(solution)/shard_map/pallas_call | solution.py:198
  47.0 4.9 %all-to-all-start.2 = ((bf16[32,3,8,128]{3,2,1,0:T(8,128)(2,1)}), bf16[32,3,8,128]{3,2,1,0:T(8,128)(2,1)S(1)}, u32[]{:S(2)}, u32[]{:S(2)}) async-start(bf16[32,3,8,128]{3,2,1,0:T(8,128)(2,1)} %get-tuple-element.23), calls=%async_computation.2 | async-start | bytes 393216 | tf_op jit(solution)/shard_map/all_to_all | solution.py:439
  51.9 1.2 %shard_map.98 = (bf16[64,8,128]{2,1,0:T(8,128)(2,1)S(1)}, bf16[64,8,128]{2,1,0:T(8,128)(2,1)S(1)}, bf16[64,8,128]{2,1,0:T(8,128)(2,1)S(1)}, bf16[64,8,128]{2,1,0:T(8,128)(2,1)S(1)}) custom-call(s32[2]{0:T(128)S(1)} %pad_add_fusion.4.place, s32[512]{0:T(512)S(1)} %pad_add_fusion.refs_0_, s32[512]{0:T(512)S(1)} %collective-permute-done.1.refs_1_, ...), custom_call_target="tpu_custom_call" | custom-call | tf_op jit(solution)/shard_map/pallas_call | solution.py:114
  53.2 2.6 %collective-permute-start.4 = (bf16[64,8,128]{2,1,0:T(8,128)(2,1)S(1)}, bf16[64,8,128]{2,1,0:T(8,128)(2,1)S(1)}, u32[]{:S(2)}, u32[]{:S(2)}) collective-permute-start(bf16[64,8,128]{2,1,0:T(8,128)(2,1)S(1)} %get-tuple-element.16), channel_id=1, source_target_pairs={{0,192},{64,0},{128,64},{192,128},{1,193},{65,1},{129,65},{193,129... | collective-permute-start | bytes 393224 | tf_op jit(solution)/shard_map/ppermute | solution.py:389
  55.7 0.5 collective-permute-start.5
  56.3 0.6 collective-permute-start.6
  57.2 2.0 %collective-permute-start.7 = (bf16[64,8,128]{2,1,0:T(8,128)(2,1)S(1)}, bf16[64,8,128]{2,1,0:T(8,128)(2,1)S(1)}, u32[]{:S(2)}, u32[]{:S(2)}) collective-permute-start(bf16[64,8,128]{2,1,0:T(8,128)(2,1)S(1)} %get-tuple-element.15.refs_0_), channel_id=1, source_target_pairs={{0,4},{4,0},{1,5},{5,1},{2,6},{6,2},{3,7},{7,3},{8,12},{12,8},{9,1... | collective-permute-start | bytes 393224 | tf_op jit(solution)/shard_map/ppermute | solution.py:437
  59.2 0.5 collective-permute-done.4.refs_1_
  59.7 4.0 %collective-permute-start.8 = (bf16[64,8,128]{2,1,0:T(8,128)(2,1)S(1)}, bf16[64,8,128]{2,1,0:T(8,128)(2,1)S(1)}, u32[]{:S(2)}, u32[]{:S(2)}) collective-permute-start(bf16[64,8,128]{2,1,0:T(8,128)(2,1)S(1)} %collective-permute-done.4.refs_1_), channel_id=1, source_target_pairs={{0,4},{4,0},{1,5},{5,1},{2,6},{6,2},{3,7},{7,3},{8,12},{12,8},{9,1... | collective-permute-start | bytes 393224 | tf_op jit(solution)/shard_map/ppermute | solution.py:437
  63.7 1.6 %collective-permute-start.9 = (bf16[64,8,128]{2,1,0:T(8,128)(2,1)S(1)}, bf16[64,8,128]{2,1,0:T(8,128)(2,1)S(1)}, u32[]{:S(2)}, u32[]{:S(2)}) collective-permute-start(bf16[64,8,128]{2,1,0:T(8,128)(2,1)S(1)} %collective-permute-done.5.refs_2_), channel_id=1, source_target_pairs={{0,4},{4,0},{1,5},{5,1},{2,6},{6,2},{3,7},{7,3},{8,12},{12,8},{9,1... | collective-permute-start | bytes 393224 | tf_op jit(solution)/shard_map/ppermute | solution.py:437
  65.3 1.2 %collective-permute-done.6.refs_3_ = bf16[64,8,128]{2,1,0:T(8,128)(2,1)S(1)} collective-permute-done((bf16[64,8,128]{2,1,0:T(8,128)(2,1)S(1)}, bf16[64,8,128]{2,1,0:T(8,128)(2,1)S(1)}, u32[]{:S(2)}, u32[]{:S(2)}) %collective-permute-start.6) | collective-permute-done | bytes 131104 | tf_op jit(solution)/shard_map/ppermute | solution.py:389
  66.5 0.4 collective-permute-start.10
  67.2 0.6 collective-permute-done.10.refs_7_
  67.9 5.4 %shard_map.99 = (f32[4,8,384]{2,1,0:T(8,128)S(1)}, bf16[3,8,128,128]{3,2,1,0:T(8,128)(2,1)S(1)}, bf16[3,128,128]{2,1,0:T(8,128)(2,1)S(1)}, bf16[384,256]{1,0:T(8,128)(2,1)S(1)}) custom-call(s32[99]{0:T(128)S(1)} %get-tuple-element.39.spots, s32[195]{0:T(256)S(1)} %pad_add_fusion.1.table, bf16[3,8,128]{2,1,0:T(8,128)(2,1)S(1)} %get-tuple-element.14.before, ...), custom_call_target="tpu_custom_call" | custom-call | tf_op jit(solution)/shard_map/pallas_call | solution.py:261
  73.3 2.0 %shard_map.100 = (bf16[2,8,384]{2,1,0:T(8,128)(2,1)}, f32[64,128]{1,0:T(8,128)S(1)}) custom-call(s32[195]{0:T(256)S(1)} %pad_add_fusion.1.table, f32[4,8,384]{2,1,0:T(8,128)S(1)} %get-tuple-element.19.packed, bf16[3,8,128,128]{3,2,1,0:T(8,128)(2,1)S(1)} %get-tuple-element.20.fresh, bf16[3,128,128]{2,1,0:T(8,128)(2,1)S(1)} %get-tuple-element.21.zinv, ...), custom_call_target="tpu_custom_call" | custom-call | tf_op jit(solution)/shard_map/pallas_call | solution.py:343
  75.3 16.2 %all_to_all.20 = f32[64,1,128]{2,1,0:T(1,128)S(1)} all-to-all(f32[64,1,128]{2,1,0:T(1,128)S(1)} %bitcast.17), channel_id=1, replica_groups=mesh['y'=4,'z'=8,'c'=2,'dir'=4] {'y','z','c'}, dimensions={0} | all-to-all | bytes 65536 | tf_op jit(solution)/shard_map/all_to_all | solution.py:444
  91.5 0.7 shard_map.101
  (28 shorter events, 1.4 us)
Async XLA Ops:
  0.6 32.6 %copy-start = (s32[3]{0:T(128)S(1)}, s32[3]{0:T(128)}, u32[]{:S(2)}) copy-start(s32[3]{0:T(128)} %param.14) | copy-start | bytes 40
  2.2 23.3 %all-to-all-start = ((bf16[8,24,8,128]{3,2,1,0:T(8,128)(2,1)}), bf16[8,24,8,128]{3,2,1,0:T(8,128)(2,1)S(1)}, u32[]{:S(2)}, u32[]{:S(2)}) async-start(bf16[8,24,8,128]{3,2,1,0:T(8,128)(2,1)} %shard_map.95), calls=%async_computation | async-start | bytes 786432 | tf_op jit(solution)/shard_map/all_to_all | solution.py:398
  14.2 1.9 %collective-permute-start = (s32[256]{0:T(256)S(1)}, s32[256]{0:T(256)S(1)}, u32[]{:S(2)}, u32[]{:S(2)}) collective-permute-start(s32[256]{0:T(256)S(1)} %select_reduce_fusion), channel_id=1, source_target_pairs={{0,4},{4,0},{1,5},{5,1},{2,6},{6,2},{3,7},{7,3},{8,12},{12,8},{9,1... | collective-permute-start | bytes 3080 | tf_op jit(solution)/shard_map/ppermute | solution.py:415
  16.0 3.9 %collective-permute-start.3 = (s32[512]{0:T(512)S(1)}, s32[512]{0:T(512)S(1)}, u32[]{:S(2)}, u32[]{:S(2)}) collective-permute-start(s32[512]{0:T(512)S(1)} %pad_add_fusion.refs_0_), channel_id=1, source_target_pairs={{0,192},{64,0},{128,64},{192,128},{1,193},{65,1},{129,65},{193,129... | collective-permute-start | bytes 6152 | tf_op jit(solution)/shard_map/ppermute | solution.py:389
  18.8 3.9 %collective-permute-start.2 = (s32[512]{0:T(512)S(1)}, s32[512]{0:T(512)S(1)}, u32[]{:S(2)}, u32[]{:S(2)}) collective-permute-start(s32[512]{0:T(512)S(1)} %pad_add_fusion.refs_0_), channel_id=1, source_target_pairs={{0,128},{64,192},{128,0},{192,64},{1,129},{65,193},{129,1},{193,65... | collective-permute-start | bytes 6152 | tf_op jit(solution)/shard_map/ppermute | solution.py:389
  19.1 3.6 %collective-permute-start.1 = (s32[512]{0:T(512)S(1)}, s32[512]{0:T(512)S(1)}, u32[]{:S(2)}, u32[]{:S(2)}) collective-permute-start(s32[512]{0:T(512)S(1)} %pad_add_fusion.refs_0_), channel_id=1, source_target_pairs={{0,64},{64,128},{128,192},{192,0},{1,65},{65,129},{129,193},{193,1... | collective-permute-start | bytes 6152 | tf_op jit(solution)/shard_map/ppermute | solution.py:389
  27.4 15.2 %all-to-all-start.1 = ((bf16[8,32,8,128]{3,2,1,0:T(8,128)(2,1)}), bf16[8,32,8,128]{3,2,1,0:T(8,128)(2,1)S(1)}, u32[]{:S(2)}, u32[]{:S(2)}) async-start(bf16[8,32,8,128]{3,2,1,0:T(8,128)(2,1)} %bitcast.3), calls=%async_computation.1 | async-start | bytes 1048576 | tf_op jit(solution)/shard_map/all_to_all | solution.py:435
  47.0 19.9 %all-to-all-start.2 = ((bf16[32,3,8,128]{3,2,1,0:T(8,128)(2,1)}), bf16[32,3,8,128]{3,2,1,0:T(8,128)(2,1)S(1)}, u32[]{:S(2)}, u32[]{:S(2)}) async-start(bf16[32,3,8,128]{3,2,1,0:T(8,128)(2,1)} %get-tuple-element.23), calls=%async_computation.2 | async-start | bytes 393216 | tf_op jit(solution)/shard_map/all_to_all | solution.py:439
  53.2 6.5 %collective-permute-start.4 = (bf16[64,8,128]{2,1,0:T(8,128)(2,1)S(1)}, bf16[64,8,128]{2,1,0:T(8,128)(2,1)S(1)}, u32[]{:S(2)}, u32[]{:S(2)}) collective-permute-start(bf16[64,8,128]{2,1,0:T(8,128)(2,1)S(1)} %get-tuple-element.16), channel_id=1, source_target_pairs={{0,192},{64,0},{128,64},{192,128},{1,193},{65,1},{129,65},{193,129... | collective-permute-start | bytes 393224 | tf_op jit(solution)/shard_map/ppermute | solution.py:389
  55.7 7.9 %collective-permute-start.5 = (bf16[64,8,128]{2,1,0:T(8,128)(2,1)S(1)}, bf16[64,8,128]{2,1,0:T(8,128)(2,1)S(1)}, u32[]{:S(2)}, u32[]{:S(2)}) collective-permute-start(bf16[64,8,128]{2,1,0:T(8,128)(2,1)S(1)} %get-tuple-element.17), channel_id=1, source_target_pairs={{0,128},{64,192},{128,0},{192,64},{1,129},{65,193},{129,1},{193,65... | collective-permute-start | bytes 393224 | tf_op jit(solution)/shard_map/ppermute | solution.py:389
  56.3 10.2 %collective-permute-start.6 = (bf16[64,8,128]{2,1,0:T(8,128)(2,1)S(1)}, bf16[64,8,128]{2,1,0:T(8,128)(2,1)S(1)}, u32[]{:S(2)}, u32[]{:S(2)}) collective-permute-start(bf16[64,8,128]{2,1,0:T(8,128)(2,1)S(1)} %get-tuple-element.18), channel_id=1, source_target_pairs={{0,64},{64,128},{128,192},{192,0},{1,65},{65,129},{129,193},{193,1... | collective-permute-start | bytes 393224 | tf_op jit(solution)/shard_map/ppermute | solution.py:389
  57.2 10.1 %collective-permute-start.7 = (bf16[64,8,128]{2,1,0:T(8,128)(2,1)S(1)}, bf16[64,8,128]{2,1,0:T(8,128)(2,1)S(1)}, u32[]{:S(2)}, u32[]{:S(2)}) collective-permute-start(bf16[64,8,128]{2,1,0:T(8,128)(2,1)S(1)} %get-tuple-element.15.refs_0_), channel_id=1, source_target_pairs={{0,4},{4,0},{1,5},{5,1},{2,6},{6,2},{3,7},{7,3},{8,12},{12,8},{9,1... | collective-permute-start | bytes 393224 | tf_op jit(solution)/shard_map/ppermute | solution.py:437
  59.7 7.6 %collective-permute-start.8 = (bf16[64,8,128]{2,1,0:T(8,128)(2,1)S(1)}, bf16[64,8,128]{2,1,0:T(8,128)(2,1)S(1)}, u32[]{:S(2)}, u32[]{:S(2)}) collective-permute-start(bf16[64,8,128]{2,1,0:T(8,128)(2,1)S(1)} %collective-permute-done.4.refs_1_), channel_id=1, source_target_pairs={{0,4},{4,0},{1,5},{5,1},{2,6},{6,2},{3,7},{7,3},{8,12},{12,8},{9,1... | collective-permute-start | bytes 393224 | tf_op jit(solution)/shard_map/ppermute | solution.py:437
  63.7 3.6 %collective-permute-start.9 = (bf16[64,8,128]{2,1,0:T(8,128)(2,1)S(1)}, bf16[64,8,128]{2,1,0:T(8,128)(2,1)S(1)}, u32[]{:S(2)}, u32[]{:S(2)}) collective-permute-start(bf16[64,8,128]{2,1,0:T(8,128)(2,1)S(1)} %collective-permute-done.5.refs_2_), channel_id=1, source_target_pairs={{0,4},{4,0},{1,5},{5,1},{2,6},{6,2},{3,7},{7,3},{8,12},{12,8},{9,1... | collective-permute-start | bytes 393224 | tf_op jit(solution)/shard_map/ppermute | solution.py:437
  66.5 1.4 %collective-permute-start.10 = (bf16[64,8,128]{2,1,0:T(8,128)(2,1)S(1)}, bf16[64,8,128]{2,1,0:T(8,128)(2,1)S(1)}, u32[]{:S(2)}, u32[]{:S(2)}) collective-permute-start(bf16[64,8,128]{2,1,0:T(8,128)(2,1)S(1)} %collective-permute-done.6.refs_3_), channel_id=1, source_target_pairs={{0,4},{4,0},{1,5},{5,1},{2,6},{6,2},{3,7},{7,3},{8,12},{12,8},{9,1... | collective-permute-start | bytes 393224 | tf_op jit(solution)/shard_map/ppermute | solution.py:437
  66.9 6.4 %collective-permute-start.11 = (bf16[96,8,128]{2,1,0:T(8,128)(2,1)S(1)}, bf16[96,8,128]{2,1,0:T(8,128)(2,1)S(1)}, u32[]{:S(2)}, u32[]{:S(2)}) collective-permute-start(bf16[96,8,128]{2,1,0:T(8,128)(2,1)S(1)} %bitcast.14), channel_id=1, source_target_pairs={{0,4},{4,0},{1,5},{5,1},{2,6},{6,2},{3,7},{7,3},{8,12},{12,8},{9,1... | collective-permute-start | bytes 589832 | tf_op jit(solution)/shard_map/ppermute | solution.py:441

commit v5 on v4

v5 whole, which is shorter than its diff:
```python
import jax
import jax.numpy as jnp
from jax import lax
from jax.experimental import pallas as pl
from jax.experimental.pallas import tpu as pltpu
from jax.sharding import Mesh, PartitionSpec as P


STEPS = 2
LEVELS = 8
Y, Z, C = 4, 8, 2
GROUPS = Y * C
E = ("y", "z", "c")
BLOCK_CAP = 4
CHUNK = 8
SMALL = 8 << 20
SWAP = [(0, 1), (1, 0)]


def vmem():
    return pl.BlockSpec(memory_space=pltpu.VMEM)


def smem():
    return pl.BlockSpec(memory_space=pltpu.SMEM)


def hbm():
    return pl.BlockSpec(memory_space=pltpu.HBM)


def anywhere():
    return pl.BlockSpec(memory_space=pl.ANY)


def kernel_call(body, grant, **options):
    return pl.pallas_call(body, compiler_params=pltpu.CompilerParams(vmem_limit_bytes=grant), **options)


def near_core(value):
    return pltpu.with_memory_space_constraint(value, pltpu.VMEM)


def off_core(value):
    return pltpu.with_memory_space_constraint(value, pltpu.HBM)


def turned(row):
    return jnp.broadcast_to(row, (8, row.shape[1])).T[:, :1]


def open_kernel(place, counts, history, columns, lags, fanned, wanted, spots, aged, table, held, sems):
    levels, rows = held.shape[0], held.shape[1]
    tile = held.shape[3]
    slots = columns.shape[1]
    cap = BLOCK_CAP * Z
    into = [
        pltpu.make_async_copy(history.at[:, :, pl.ds(row * tile, tile)], held.at[:, row], sems.at[row])
        for row in range(rows)
    ]
    for copy in into:
        copy.start()
    y, c = place[0, 0], place[0, 1]
    col, lag = columns[...], lags[...] - 1
    owner = (col * ((1 << 17) // rows + 1)) >> 17
    local = col - owner * rows
    own_c = lax.rem(owner, C)
    own_z = lax.rem(owner // C, Z)
    own_y = owner // (C * Z)
    group = own_y * C + own_c
    spot = (own_z * levels + lag) * rows + local
    other = (own_c != c).astype(jnp.int32)
    across = (lax.rem(own_y - y + Y, Y) * C + other) * cap
    fresh = (other * (Y * Z) + own_y * Z + own_z) * rows + local
    for copy in into:
        copy.wait()
    out = [pltpu.make_async_copy(held, fanned.at[z], sems.at[rows + z]) for z in range(Z)]
    for copy in out:
        copy.start()
    here = lax.broadcasted_iota(jnp.int32, (slots, slots), 1)
    there = lax.broadcasted_iota(jnp.int32, (slots, slots), 0)
    groups = [group[row : row + 1] for row in range(rows)]
    down = [turned(value) for value in groups]
    asks = lax.broadcasted_iota(jnp.int32, (slots, GROUPS * cap), 1)
    total = jnp.zeros((1, GROUPS * cap), jnp.int32)
    lane = lax.broadcasted_iota(jnp.int32, (1, slots), 1)
    spot_parts, aged_parts, order_parts, where_parts, new_counts = [], [], [], [], []
    for row in range(rows):
        same = (down[row] == groups[row]) & (there < here)
        position = jnp.sum(same.astype(jnp.int32), axis=0, keepdims=True)
        for before in range(row):
            position += jnp.sum((down[before] == groups[row]).astype(jnp.int32), axis=0, keepdims=True)
        at = groups[row] * cap + position
        live = lane < counts[row]
        new = live & (lag[row : row + 1] == 0)
        total += jnp.sum(jnp.where(turned(at) == asks, turned(spot[row : row + 1]), 0), axis=0, keepdims=True)
        spot_parts.append(jnp.where(live, at, -1))
        aged_parts.append(jnp.where(live & ~new, across[row : row + 1] + position, -1))
        fresh_row = jnp.where(new, fresh[row : row + 1], -1)
        marked = turned(new.astype(jnp.int32)) == 1
        rank = jnp.sum((marked & (there < here)).astype(jnp.int32), axis=0, keepdims=True)
        put = marked & (turned(rank) == here)
        order_parts.append(jnp.sum(jnp.where(put, there, 0), axis=0, keepdims=True))
        where_parts.append(jnp.sum(jnp.where(put, turned(fresh_row) + 1, 0), axis=0, keepdims=True) - 1)
        new_counts.append(jnp.sum(new.astype(jnp.int32), axis=1, keepdims=True))
    wanted[...] = total
    rest = jnp.zeros((1, spots.shape[1] - rows * slots), jnp.int32)
    spots[...] = jnp.concatenate([*spot_parts, rest], axis=1)
    aged[...] = jnp.concatenate([*aged_parts, rest], axis=1)
    table[0:1, :] = jnp.concatenate([*order_parts, rest], axis=1)
    table[1:2, :] = jnp.concatenate([*where_parts, rest], axis=1)
    table[2:3, :] = jnp.concatenate(
        [jnp.broadcast_to(count, (1, slots)) for count in new_counts] + [rest], axis=1
    )
    for copy in out:
        copy.wait()


def open_up(place, counts, history, columns, lags, tile):
    levels, dirs, panels = history.shape
    rows = panels // tile
    shapes = ((1, GROUPS * BLOCK_CAP * Z), (1, 128), (1, 128), (3, 128))
    return kernel_call(
        open_kernel,
        SMALL,
        out_shape=(
            pltpu.HBM((Z, levels, rows, dirs, tile), history.dtype),
            pltpu.VMEM(shapes[0], jnp.int32),
            *[pltpu.HBM(shape, jnp.int32) for shape in shapes[1:]],
        ),
        in_specs=[smem(), smem(), hbm(), vmem(), vmem()],
        out_specs=(hbm(), *[vmem()] * 4),
        scratch_shapes=[
            pltpu.VMEM((levels, rows, dirs, tile), history.dtype),
            pltpu.SemaphoreType.DMA((rows + Z,)),
        ],
    )(place, off_core(counts), off_core(history), off_core(columns), off_core(lags))


def whose(place, shift, other):
    y, c = place[0, 0], place[0, 1]
    return lax.rem(y - shift + Y, Y) * C + (c if other == 0 else 1 - c)


def pick_kernel(place, *refs):
    lists, held, first = refs[:Y], refs[Y], refs[Y + 1]
    cap = first.shape[0] // GROUPS
    mine = (place[0, 0] * C + place[0, 1]) * cap
    for shift in range(Y):
        for other in range(C):
            to = whose(place, shift, other) * cap

            @pl.loop(0, cap, step=16)
            def _(base):
                for k in range(16):
                    first[to + base + k] = held[lists[shift][0, other * GROUPS * cap + mine + base + k]]


def pick_later_kernel(place, *refs):
    lists, held, later = refs[:Y], refs[Y], refs[Y + 1 :]
    cap = later[0].shape[0] // C
    back = held.shape[0] // (Z * LEVELS)
    mine = (place[0, 0] * C + place[0, 1]) * cap
    for shift in range(Y):
        for other in range(C):

            @pl.loop(0, cap, step=16)
            def _(base):
                for k in range(16):
                    spot = lists[shift][0, other * GROUPS * cap + mine + base + k]
                    later[shift][other * cap + base + k] = held[jnp.maximum(spot - back, 0)]


def picks(place, lists, held, cap):
    def out(entries):
        return pltpu.HBM((entries, *held.shape[1:]), held.dtype)

    held = near_core(held)
    specs = [smem()] * (1 + Y) + [vmem()]
    first = kernel_call(
        pick_kernel, SMALL, out_shape=out(GROUPS * cap), in_specs=specs, out_specs=vmem()
    )(place, *lists, held)
    later = kernel_call(
        pick_later_kernel, SMALL, out_shape=[out(C * cap)] * Y, in_specs=specs, out_specs=[vmem()] * Y
    )(place, *lists, held)
    return first, later


def pieces_of(spot_at, count, load):
    parts = []
    for k in range(count):
        spot = spot_at(k)
        value = load(jnp.maximum(spot, 0))
        parts.append(jnp.where(spot >= 0, value, jnp.zeros_like(value)))
    return jnp.concatenate(parts, axis=1)


def row_sum(spots, load, weights, row):
    slots, tile = weights.shape[0], weights.shape[1]
    picked = pieces_of(lambda k: spots[0, row * slots + k], slots, load)
    return jnp.dot(picked, weights[...].reshape(slots * tile, tile), preferred_element_type=jnp.float32)


def density_of(own, total, zinv):
    source = (own.astype(jnp.float32) - total).astype(jnp.bfloat16)
    return jnp.dot(source, zinv, preferred_element_type=jnp.float32).astype(jnp.bfloat16)


def start_all(pairs, sems, base=0):
    copies = [pltpu.make_async_copy(src, dst, sems.at[base + i]) for i, (src, dst) in enumerate(pairs)]
    for copy in copies:
        copy.start()
    return copies


def stage_kernel(ztiles_hbm, zinv_hbm, incident_hbm, top, zinv, incident, sems):
    kept = top.shape[0]
    pairs = [(ztiles_hbm.at[row], top.at[row]) for row in range(kept)]
    for copy in start_all([*pairs, (zinv_hbm, zinv), (incident_hbm.at[0], incident)], sems):
        copy.wait()


def stage(ztiles, zinv, incident):
    kept = ztiles.shape[0] - 1
    return kernel_call(
        stage_kernel,
        SMALL,
        out_shape=(
            pltpu.VMEM((kept, *ztiles.shape[1:]), ztiles.dtype),
            pltpu.VMEM(zinv.shape, zinv.dtype),
            pltpu.VMEM(incident.shape[1:], incident.dtype),
        ),
        in_specs=[hbm()] * 3,
        out_specs=[vmem()] * 3,
        scratch_shapes=[pltpu.SemaphoreType.DMA((kept + 2,))],
    )(off_core(ztiles), off_core(zinv), off_core(incident))


def first_kernel(spots, got, top, ztiles_hbm, zinv, incident, out, spread_out, last, sems):
    kept, tile = top.shape[0], top.shape[2]
    copy = pltpu.make_async_copy(ztiles_hbm.at[kept], last, sems.at[0])
    copy.start()
    for row in range(kept + 1):
        if row == kept:
            copy.wait()
        total = row_sum(spots, lambda spot: got[spot], top.at[row] if row < kept else last, row)
        density = density_of(incident[:, row * tile : (row + 1) * tile], total, zinv[row])
        out[row] = density
        for to in range(spread_out.shape[0]):
            spread_out[to, row] = density


def first_step(spots, got, top, ztiles, zinv, incident):
    rows, tile, dirs = ztiles.shape[0], ztiles.shape[2], got.shape[1]
    return kernel_call(
        first_kernel,
        SMALL,
        out_shape=(
            pltpu.HBM((rows, dirs, tile), jnp.bfloat16),
            pltpu.HBM((Y * Z, rows, dirs, tile), jnp.bfloat16),
        ),
        in_specs=[smem(), vmem(), vmem(), hbm(), vmem(), vmem()],
        out_specs=(vmem(), vmem()),
        scratch_shapes=[pltpu.VMEM(ztiles.shape[1:], ztiles.dtype), pltpu.SemaphoreType.DMA((1,))],
    )(off_core(spots), near_core(got), near_core(top), off_core(ztiles), near_core(zinv), near_core(incident))


def aged_kernel(spots, table, before, incident, *refs):
    near, cross = refs[:Y], refs[Y : 2 * Y]
    ztiles_hbm, basis_hbm, packed, fresh, basis, pool, ztiles, sems, fresh_sems = refs[2 * Y :]
    rows, slots, tile = ztiles.shape[0], ztiles.shape[1], ztiles.shape[2]
    cap = near[0].shape[0] // C
    panels = rows * tile
    pairs = []
    for shift in range(Y):
        for source, at in ((near[shift], 0), (cross[shift], cap)):
            pairs.append((source.at[pl.ds(at, cap)], pool.at[pl.ds(len(pairs) * cap, cap)]))
    pairs += [(ztiles_hbm.at[row], ztiles.at[row]) for row in range(rows)]
    pairs.append((basis_hbm, basis))
    copies = start_all(pairs, sems)
    lag_one = []
    for row in range(rows):
        for k in range(CHUNK):
            source = ztiles_hbm.at[row, table[0, row * slots + k]]
            lag_one.append(pltpu.make_async_copy(source, fresh.at[row, k], fresh_sems.at[row, k]))
    for copy in lag_one:
        copy.start()
    for copy in copies[: 2 * Y]:
        copy.wait()
    for row in range(rows):
        copies[2 * Y + row].wait()
        at = slice(row * tile, (row + 1) * tile)
        packed[0, :, at] = incident[1, :, at].astype(jnp.float32)
        packed[1, :, at] = row_sum(spots, lambda spot: pool[spot], ztiles.at[row], row)
    value = jnp.concatenate([before[row] for row in range(rows)], axis=1)
    packed[2, :, :] = value.astype(jnp.float32)
    copies[-1].wait()
    packed[3, :, : basis.shape[1]] = jnp.dot(value, basis[...], preferred_element_type=jnp.float32)
    packed[3, :, basis.shape[1] :] = jnp.zeros((value.shape[0], panels - basis.shape[1]), jnp.float32)
    for copy in lag_one:
        copy.wait()


def aged_step(spots, table, before, incident, near, cross, ztiles, basis):
    rows, dirs, tile = before.shape
    cap = near[0].shape[0] // C
    return kernel_call(
        aged_kernel,
        SMALL,
        out_shape=(
            pltpu.VMEM((4, dirs, rows * tile), jnp.float32),
            pltpu.VMEM((rows, CHUNK, tile, tile), ztiles.dtype),
            pltpu.VMEM(basis.shape, basis.dtype),
        ),
        in_specs=[smem(), smem(), vmem(), vmem()] + [anywhere()] * (2 * Y) + [hbm()] * 2,
        out_specs=[vmem()] * 3,
        scratch_shapes=[
            pltpu.VMEM((2 * Y * cap, dirs, tile), jnp.bfloat16),
            pltpu.VMEM(ztiles.shape, ztiles.dtype),
            pltpu.SemaphoreType.DMA((2 * Y + rows + 1,)),
            pltpu.SemaphoreType.DMA((rows, CHUNK)),
        ],
    )(
        off_core(spots),
        off_core(table),
        off_core(before),
        off_core(incident),
        *near,
        *cross,
        off_core(ztiles),
        off_core(basis),
    )


def second_kernel(table, packed, fresh, zinv, basis, here, there, ztiles_hbm, dens, far, ztiles, flipped, tile_sems):
    rows, slots, tile = ztiles_hbm.shape[0], ztiles_hbm.shape[1], ztiles_hbm.shape[2]
    near = here.shape[0]

    def load(spot):
        ours = here[jnp.minimum(spot, near - 1)]
        theirs = there[jnp.maximum(spot - near, 0)]
        return jnp.where(spot < near, ours, theirs)

    later = []
    for row in range(rows):
        chunks = lax.div(table[2, row * slots] + (CHUNK - 1), CHUNK)
        at = pl.ds(row * tile, tile)
        first = pieces_of(lambda k: table[1, row * slots + k], CHUNK, load)
        total = packed[1, :, at] + jnp.dot(
            first, fresh[row].reshape(CHUNK * tile, tile), preferred_element_type=jnp.float32
        )

        def more(chunk, total):
            copies = []
            for k in range(CHUNK):
                source = ztiles_hbm.at[row, table[0, row * slots + chunk * CHUNK + k]]
                copies.append(pltpu.make_async_copy(source, ztiles.at[k], tile_sems.at[k]))
            for copy in copies:
                copy.start()
            for copy in copies:
                copy.wait()
            picked = pieces_of(lambda k: table[1, row * slots + chunk * CHUNK + k], CHUNK, load)
            return total + jnp.dot(
                picked, ztiles[...].reshape(CHUNK * tile, tile), preferred_element_type=jnp.float32
            )

        total = lax.fori_loop(1, chunks, more, total)
        later.append(density_of(packed[0, :, at], total, zinv[row]))
    value = jnp.concatenate(later, axis=1)
    dens[0] = packed[2].astype(dens.dtype)
    dens[1] = value
    far_second = jnp.dot(value, basis[...], preferred_element_type=jnp.float32)
    both = jnp.concatenate([packed[3, :, : basis.shape[1]], far_second], axis=0)
    lanes = both.shape[0]
    flipped[:, :lanes] = both.T
    owners = far.shape[0]
    each = basis.shape[1] // owners
    cols = [flipped[pl.ds(c, owners, stride=each), :][:, :lanes] for c in range(each)]
    far[...] = jnp.concatenate([*cols, jnp.zeros((owners, far.shape[1] - each * lanes), jnp.float32)], axis=1)


def second_step(table, packed, fresh, zinv, basis, here, there, ztiles, owners):
    tile, dirs = here.shape[2], here.shape[1]
    panels, harmonics = basis.shape
    return kernel_call(
        second_kernel,
        SMALL,
        out_shape=(
            jax.ShapeDtypeStruct((STEPS, dirs, panels), jnp.bfloat16),
            pltpu.VMEM((owners, 128), jnp.float32),
        ),
        in_specs=[smem()] + [vmem()] * 6 + [hbm()],
        out_specs=(vmem(), vmem()),
        scratch_shapes=[
            pltpu.VMEM((CHUNK, tile, tile), ztiles.dtype),
            pltpu.VMEM((harmonics, 128), jnp.float32),
            pltpu.SemaphoreType.DMA((CHUNK,)),
        ],
    )(
        off_core(table),
        near_core(packed),
        near_core(fresh),
        near_core(zinv),
        near_core(basis),
        near_core(here),
        near_core(there),
        off_core(ztiles),
    )


def sum_kernel(parts, out):
    total = jnp.sum(parts[...], axis=0, keepdims=True)
    steps, each, dirs = out.shape
    for step in range(steps):
        for c in range(each):
            at = (c * steps + step) * dirs
            out[step, c : c + 1, :] = total[:, at : at + dirs]


def sum_parts(parts, steps, each, dirs):
    return kernel_call(
        sum_kernel,
        SMALL,
        out_shape=jax.ShapeDtypeStruct((steps, each, dirs), jnp.float32),
        in_specs=[vmem()],
        out_specs=vmem(),
    )(near_core(parts))


def shifted(value, axis, length, shift):
    return lax.ppermute(value, axis, [(i, (i + shift) % length) for i in range(length)])


def march(history, incident, ztiles, zinv, columns, lags, counts, basis):
    rows, tile = ztiles.shape[0], ztiles.shape[2]
    dirs = history.shape[1]
    owners = Y * Z * C
    cap = BLOCK_CAP * Z
    place = jnp.stack([lax.axis_index("y"), lax.axis_index("c")]).reshape(1, 2)
    fanned, wanted, spots, aged, table = open_up(place, counts, history, columns, lags, tile)
    held = lax.all_to_all(fanned, "z", 0, 0, tiled=True).reshape(-1, dirs, tile)
    both = jnp.concatenate([wanted, lax.ppermute(wanted, "c", SWAP)], axis=1)
    lists = [both] + [shifted(both, "y", Y, s) for s in range(1, Y)]
    first, later = picks(place, lists, held, cap)
    got = lax.all_to_all(first.reshape(GROUPS, cap, dirs, tile), ("y", "c"), 0, 0, tiled=True)
    near = [later[0]] + [shifted(later[s], "y", Y, -s) for s in range(1, Y)]
    cross = [lax.ppermute(piece, "c", SWAP) for piece in near]
    top, inverse, driven = stage(ztiles, zinv, incident)
    density, fanned = first_step(spots, got.reshape(GROUPS * cap, dirs, tile), top, ztiles, inverse, driven)
    here = lax.all_to_all(fanned, ("y", "z"), 0, 0, tiled=True).reshape(Y * Z * rows, dirs, tile)
    packed, lag_one, weights = aged_step(aged, table, density, incident, near, cross, ztiles, basis)
    there = lax.ppermute(here, "c", SWAP)
    dens, far = second_step(table, packed, lag_one, inverse, weights, here, there, ztiles, owners)
    each = basis.shape[1] // owners
    parts = lax.all_to_all(far.reshape(owners, 1, 128), E, 0, 0, tiled=True).reshape(owners, 128)
    total = sum_parts(parts, STEPS, each, dirs)
    return dens, total.transpose(0, 2, 1)


def solution(mesh):
    fine = Mesh(mesh.devices.reshape(Y, Z, C, mesh.shape["dir"]), ("y", "z", "c", "dir"))
    in_specs = (
        P(None, "dir", E),
        P(None, "dir", E),
        P(E, None, None, None),
        P(E, None, None),
        P(E, None),
        P(E, None),
        P(E),
        P(E, None),
    )
    out_specs = (P(None, "dir", E), P(None, "dir", E))
    return jax.shard_map(march, mesh=fine, in_specs=in_specs, out_specs=out_specs, check_vma=False)
```

time: 92.7 us -> 93.4 us (level)
  waiting for transfers between devices: 18 us -> 21.6 us
  starting transfers between devices: 36.4 us -> 33.7 us
  other arithmetic: 2.55 us -> 0.08 us
  Pallas kernels: 17.2 us -> 19.3 us
    ppermute x4, starting transfers between devices: 8.09 us -> 2.6 us  [march(): cross = [lax.ppermute(piece, 'c', SWAP) for piece in near]]
    all_to_all x1, waiting for transfers between devices: 0.01 us -> 3.87 us  [march(): lax.all_to_all(fanned, ('y', 'z'), 0, 0, tiled=True)]
    all_to_all x1, waiting for transfers between devices: 2.74 us -> 5.83 us  [march(): held = lax.all_to_all(fanned, 'z', 0, 0, tiled=True).reshape(-1, dirs, tile)]
    ppermute x1, starting transfers between devices: 0.08 us -> 2.8 us  [march(): there = lax.ppermute(here, 'c', SWAP)]
    ppermute x6, waiting for transfers between devices: 4.51 us -> 2.38 us  [shifted(): lax.ppermute(value, axis, [(i, (i + shift) % length) for i in range(lengt...]
    reduce_sum x5 -> x0, other arithmetic: 1.51 us -> none  [the longest x1 0.9 us: march(): jnp.sum(new_rows.astype(jnp.int32), axis=1)]
    all_to_all x1, waiting for transfers between devices: 9.27 us -> 7.76 us  [march(): lax.all_to_all(first.reshape(GROUPS, cap, dirs, tile), ('y', 'c'), 0, 0,...]
    pallas_call x4 -> x5, Pallas kernels: 13.4 us -> 14.7 us  [the longest x1 4.58 us: aged_step(): kernel_call(aged_kernel, SMALL, out_shape=(pltpu.VMEM((4, dirs, rows * ti...]
  transfers between devices with their start and end apart: 15 -> 15, of which waited for: 8 -> 8; matrix products, arithmetic and copies ran while one was open for 4% -> 0% of each run, Pallas kernels for 7% -> 9%
where the time goes in v5:
time: 93.4 us; the launch traced here: 92.8 us
  starting transfers between devices  33.7 us (36%)
  waiting for transfers between devices  21.6 us (23%)
  Pallas kernels  19.3 us (21%)
  blocking collectives  16.5 us (18%)
    all_to_all x1, blocking collectives, march(): lax.all_to_all(far.reshape(owners, 1, 128), E, 0, 0, tiled=True)  16.5 us
    all_to_all x1, starting transfers between devices, march(): held = lax.all_to_all(fanned, 'z', 0, 0, tiled=True).reshape(-1, dirs, tile)  9.02 us
    ppermute x6, starting transfers between devices, shifted(): lax.ppermute(value, axis, [(i, (i + shift) % length) for i in range(lengt...  8.57 us
    all_to_all x1, waiting for transfers between devices, march(): lax.all_to_all(first.reshape(GROUPS, cap, dirs, tile), ('y', 'c'), 0, 0,...  7.76 us
    all_to_all x1, starting transfers between devices, march(): lax.all_to_all(first.reshape(GROUPS, cap, dirs, tile), ('y', 'c'), 0, 0,...  5.84 us
    all_to_all x1, waiting for transfers between devices, march(): held = lax.all_to_all(fanned, 'z', 0, 0, tiled=True).reshape(-1, dirs, tile)  5.83 us
    pallas_call x1, Pallas kernels, aged_step(): kernel_call(aged_kernel, SMALL, out_shape=(pltpu.VMEM((4, dirs, rows * ti...  4.58 us
    all_to_all x1, starting transfers between devices, march(): lax.all_to_all(fanned, ('y', 'z'), 0, 0, tiled=True)  3.88 us
  transfers between devices with their start and end apart: 15, of which 8 were waited for; matrix products, arithmetic and copies ran while one was open for 0% of the time, Pallas kernels for 9%

profile of v5, /device:TPU:1, one launch (start us, length us, event | category | flops | bytes accessed | tf_op | source)
XLA Modules:
  0.0 92.8 jit_solution(6286801030524810134)
XLA Ops:
  0.7 3.2 %shard_map.95 = (bf16[8,8,3,8,128]{4,3,2,1,0:T(8,128)(2,1)}, s32[1,256]{1,0:T(1,128)S(1)}, s32[1,128]{1,0:T(1,128)}, s32[1,128]{1,0:T(1,128)}, s32[3,128]{1,0:T(4,128)}) custom-call(s32[1,2]{1,0:T(1,128)S(1)} %add_bitcast_fusion.place, s32[3]{0:T(128)} %counts.1, bf16[8,8,384]{2,1,0:T(8,128)(2,1)} %history.1, s32[3,32]{1,0:T(4,128)} %columns.1, s32[3,32]{1,0:T(4,128)} %lags.1), custom_call_target="tpu_custom_call" | custom-call | tf_op jit(solution)/shard_map/pallas_call | solution.py:123
  3.9 9.0 %all-to-all-start = ((bf16[8,8,3,8,128]{4,3,2,1,0:T(8,128)(2,1)}), bf16[8,8,3,8,128]{4,3,2,1,0:T(8,128)(2,1)S(1)}, u32[]{:S(2)}, u32[]{:S(2)}) async-start(bf16[8,8,3,8,128]{4,3,2,1,0:T(8,128)(2,1)} %get-tuple-element.25), calls=%async_computation | async-start | bytes 786432 | tf_op jit(solution)/shard_map/all_to_all | solution.py:441
  12.9 1.0 %collective-permute-start = (s32[1,256]{1,0:T(1,128)S(1)}, s32[1,256]{1,0:T(1,128)S(1)}, u32[]{:S(2)}, u32[]{:S(2)}) collective-permute-start(s32[1,256]{1,0:T(1,128)S(1)} %get-tuple-element.24), channel_id=1, source_target_pairs={{0,4},{4,0},{1,5},{5,1},{2,6},{6,2},{3,7},{7,3},{8,12},{12,8},{9,1... | collective-permute-start | bytes 3080 | tf_op jit(solution)/shard_map/ppermute | solution.py:442
  13.9 0.8 collective-permute-done
  14.7 1.3 %collective-permute-start.1 = (s32[1,512]{1,0:T(1,128)S(1)}, s32[1,512]{1,0:T(1,128)S(1)}, u32[]{:S(2)}, u32[]{:S(2)}) collective-permute-start(s32[1,512]{1,0:T(1,128)S(1)} %constant_dynamic-update-slice_fusion.refs_0_), channel_id=1, source_target_pairs={{0,64},{64,128},{128,192},{192,0},{1,65},{65,129},{129,193},{193,1... | collective-permute-start | bytes 6152 | tf_op jit(solution)/shard_map/ppermute | solution.py:431
  16.0 2.6 %collective-permute-start.2 = (s32[1,512]{1,0:T(1,128)S(1)}, s32[1,512]{1,0:T(1,128)S(1)}, u32[]{:S(2)}, u32[]{:S(2)}) collective-permute-start(s32[1,512]{1,0:T(1,128)S(1)} %constant_dynamic-update-slice_fusion.refs_0_), channel_id=1, source_target_pairs={{0,128},{64,192},{128,0},{192,64},{1,129},{65,193},{129,1},{193,65... | collective-permute-start | bytes 6152 | tf_op jit(solution)/shard_map/ppermute | solution.py:431
  18.6 1.1 %collective-permute-start.3 = (s32[1,512]{1,0:T(1,128)S(1)}, s32[1,512]{1,0:T(1,128)S(1)}, u32[]{:S(2)}, u32[]{:S(2)}) collective-permute-start(s32[1,512]{1,0:T(1,128)S(1)} %constant_dynamic-update-slice_fusion.refs_0_), channel_id=1, source_target_pairs={{0,192},{64,0},{128,64},{192,128},{1,193},{65,1},{129,65},{193,129... | collective-permute-start | bytes 6152 | tf_op jit(solution)/shard_map/ppermute | solution.py:431
  19.7 0.2 collective-permute-done.2.refs_2_
  19.9 1.4 %collective-permute-done.3.refs_3_ = s32[1,512]{1,0:T(1,128)S(1)} collective-permute-done((s32[1,512]{1,0:T(1,128)S(1)}, s32[1,512]{1,0:T(1,128)S(1)}, u32[]{:S(2)}, u32[]{:S(2)}) %collective-permute-start.3) | collective-permute-done | bytes 2080 | tf_op jit(solution)/shard_map/ppermute | solution.py:431
  21.3 5.8 %all-to-all-done = bf16[8,8,3,8,128]{4,3,2,1,0:T(8,128)(2,1)S(1)} async-done(((bf16[8,8,3,8,128]{4,3,2,1,0:T(8,128)(2,1)}), bf16[8,8,3,8,128]{4,3,2,1,0:T(8,128)(2,1)S(1)}, u32[]{:S(2)}, u32[]{:S(2)}) %all-to-all-start) | async-done | bytes 393248 | tf_op jit(solution)/shard_map/all_to_all | solution.py:441
  27.2 1.9 %shard_map.96 = bf16[256,8,128]{2,1,0:T(8,128)(2,1)} custom-call(s32[1,2]{1,0:T(1,128)S(1)} %add_bitcast_fusion.place, s32[1,512]{1,0:T(1,128)S(1)} %constant_dynamic-update-slice_fusion.refs_0_, s32[1,512]{1,0:T(1,128)S(1)} %collective-permute-done.1.refs_1_, s32[1,512]{1,0:T(1,128)S(1)} %collective-permute-done.2.refs_2_, ...), custom_call_target="tpu_custom_call" | custom-call | tf_op jit(solution)/shard_map/pallas_call | solution.py:180
  29.0 5.8 %all-to-all-start.1 = ((bf16[8,32,8,128]{3,2,1,0:T(8,128)(2,1)}), bf16[8,32,8,128]{3,2,1,0:T(8,128)(2,1)S(1)}, u32[]{:S(2)}, u32[]{:S(2)}) async-start(bf16[8,32,8,128]{3,2,1,0:T(8,128)(2,1)} %bitcast.20), calls=%async_computation.1 | async-start | bytes 1048576 | tf_op jit(solution)/shard_map/all_to_all | solution.py:445
  34.9 1.6 %shard_map.97 = (bf16[2,32,128,128]{3,2,1,0:T(8,128)(2,1)S(1)}, bf16[3,128,128]{2,1,0:T(8,128)(2,1)S(1)}, bf16[8,384]{1,0:T(8,128)(2,1)S(1)}) custom-call(bf16[3,32,128,128]{3,2,1,0:T(8,128)(2,1)} %ztiles_hbm.5, bf16[3,128,128]{2,1,0:T(8,128)(2,1)} %zinv_hbm.1, bf16[2,8,384]{2,1,0:T(8,128)(2,1)} %incident.1), custom_call_target="tpu_custom_call" | custom-call | tf_op jit(solution)/shard_map/pallas_call | solution.py:225
  36.5 7.8 %all-to-all-done.1 = bf16[8,32,8,128]{3,2,1,0:T(8,128)(2,1)S(1)} async-done(((bf16[8,32,8,128]{3,2,1,0:T(8,128)(2,1)}), bf16[8,32,8,128]{3,2,1,0:T(8,128)(2,1)S(1)}, u32[]{:S(2)}, u32[]{:S(2)}) %all-to-all-start.1) | async-done | bytes 524320 | tf_op jit(solution)/shard_map/all_to_all | solution.py:445
  44.2 3.3 %shard_map.98 = (bf16[3,8,128]{2,1,0:T(8,128)(2,1)}, bf16[32,3,8,128]{3,2,1,0:T(8,128)(2,1)}) custom-call(s32[1,128]{1,0:T(1,128)} %get-tuple-element.23.spots, bf16[256,8,128]{2,1,0:T(8,128)(2,1)S(1)} %bitcast.15, bf16[2,32,128,128]{3,2,1,0:T(8,128)(2,1)S(1)} %get-tuple-element.26.top, bf16[3,32,128,128]{3,2,1,0:T(8,128)(2,1)} %ztiles_hbm.5, ...), custom_call_target="tpu_custom_call" | custom-call | tf_op jit(solution)/shard_map/pallas_call | solution.py:255
  47.5 3.9 %all-to-all-start.2 = ((bf16[32,3,8,128]{3,2,1,0:T(8,128)(2,1)}), bf16[32,3,8,128]{3,2,1,0:T(8,128)(2,1)S(1)}, u32[]{:S(2)}, u32[]{:S(2)}) async-start(bf16[32,3,8,128]{3,2,1,0:T(8,128)(2,1)} %get-tuple-element.37), calls=%async_computation.2 | async-start | bytes 393216 | tf_op jit(solution)/shard_map/all_to_all | solution.py:450
  51.4 2.0 %shard_map.99 = (bf16[64,8,128]{2,1,0:T(8,128)(2,1)}, bf16[64,8,128]{2,1,0:T(8,128)(2,1)}, bf16[64,8,128]{2,1,0:T(8,128)(2,1)}, bf16[64,8,128]{2,1,0:T(8,128)(2,1)}) custom-call(s32[1,2]{1,0:T(1,128)S(1)} %add_bitcast_fusion.place, s32[1,512]{1,0:T(1,128)S(1)} %constant_dynamic-update-slice_fusion.refs_0_, s32[1,512]{1,0:T(1,128)S(1)} %collective-permute-done.1.refs_1_, ...), custom_call_target="tpu_custom_call" | custom-call | tf_op jit(solution)/shard_map/pallas_call | solution.py:183
  53.4 2.5 %collective-permute-start.4 = (bf16[64,8,128]{2,1,0:T(8,128)(2,1)}, bf16[64,8,128]{2,1,0:T(8,128)(2,1)S(1)}, u32[]{:S(2)}, u32[]{:S(2)}) collective-permute-start(bf16[64,8,128]{2,1,0:T(8,128)(2,1)} %get-tuple-element.31), channel_id=1, source_target_pairs={{0,192},{64,0},{128,64},{192,128},{1,193},{65,1},{129,65},{193,129... | collective-permute-start | bytes 393224 | tf_op jit(solution)/shard_map/ppermute | solution.py:431
  55.9 0.5 collective-permute-start.5
  56.4 0.6 collective-permute-start.6
  57.0 3.9 %all-to-all-done.2 = bf16[32,3,8,128]{3,2,1,0:T(8,128)(2,1)S(1)} async-done(((bf16[32,3,8,128]{3,2,1,0:T(8,128)(2,1)}), bf16[32,3,8,128]{3,2,1,0:T(8,128)(2,1)S(1)}, u32[]{:S(2)}, u32[]{:S(2)}) %all-to-all-start.2) | async-done | bytes 196640 | tf_op jit(solution)/shard_map/all_to_all | solution.py:450
  60.9 2.8 %collective-permute-start.11 = (bf16[96,8,128]{2,1,0:T(8,128)(2,1)S(1)}, bf16[96,8,128]{2,1,0:T(8,128)(2,1)S(1)}, u32[]{:S(2)}, u32[]{:S(2)}) collective-permute-start(bf16[96,8,128]{2,1,0:T(8,128)(2,1)S(1)} %bitcast.16), channel_id=1, source_target_pairs={{0,4},{4,0},{1,5},{5,1},{2,6},{6,2},{3,7},{7,3},{8,12},{12,8},{9,1... | collective-permute-start | bytes 589832 | tf_op jit(solution)/shard_map/ppermute | solution.py:452
  63.7 0.5 collective-permute-start.8
  64.2 1.4 %collective-permute-start.9 = (bf16[64,8,128]{2,1,0:T(8,128)(2,1)S(1)}, bf16[64,8,128]{2,1,0:T(8,128)(2,1)S(1)}, u32[]{:S(2)}, u32[]{:S(2)}) collective-permute-start(bf16[64,8,128]{2,1,0:T(8,128)(2,1)S(1)} %collective-permute-done.5.refs_2_), channel_id=1, source_target_pairs={{0,4},{4,0},{1,5},{5,1},{2,6},{6,2},{3,7},{7,3},{8,12},{12,8},{9,1... | collective-permute-start | bytes 393224 | tf_op jit(solution)/shard_map/ppermute | solution.py:447
  65.6 0.7 collective-permute-done.6.refs_3_
  66.3 0.7 collective-permute-start.10
  67.0 1.0 %collective-permute-done.10.refs_7_ = bf16[64,8,128]{2,1,0:T(8,128)(2,1)S(1)} collective-permute-done((bf16[64,8,128]{2,1,0:T(8,128)(2,1)S(1)}, bf16[64,8,128]{2,1,0:T(8,128)(2,1)S(1)}, u32[]{:S(2)}, u32[]{:S(2)}) %collective-permute-start.10) | collective-permute-done | bytes 131104 | tf_op jit(solution)/shard_map/ppermute | solution.py:447
  68.0 0.9 copy-done
  68.9 4.6 %shard_map.100 = (f32[4,8,384]{2,1,0:T(8,128)S(1)}, bf16[3,8,128,128]{3,2,1,0:T(8,128)(2,1)S(1)}, bf16[384,256]{1,0:T(8,128)(2,1)S(1)}) custom-call(s32[1,128]{1,0:T(1,128)} %get-tuple-element.22.spots, s32[3,128]{1,0:T(4,128)} %get-tuple-element.21.table, bf16[3,8,128]{2,1,0:T(8,128)(2,1)} %get-tuple-element.29.before, bf16[2,8,384]{2,1,0:T(8,128)(2,1)} %incident.1, ...), custom_call_target="tpu_custom_call" | custom-call | tf_op jit(solution)/shard_map/pallas_call | solution.py:307
  73.5 2.1 %shard_map.101 = (bf16[2,8,384]{2,1,0:T(8,128)(2,1)}, f32[64,128]{1,0:T(8,128)S(1)}) custom-call(s32[3,128]{1,0:T(4,128)} %get-tuple-element.21.table, f32[4,8,384]{2,1,0:T(8,128)S(1)} %get-tuple-element.34.packed, bf16[3,8,128,128]{3,2,1,0:T(8,128)(2,1)S(1)} %get-tuple-element.35.fresh, bf16[3,128,128]{2,1,0:T(8,128)(2,1)S(1)} %get-tuple-element.27.zinv, ...), custom_call_target="tpu_custom_call" | custom-call | tf_op jit(solution)/shard_map/pallas_call | solution.py:385
  75.6 16.5 %all_to_all.20 = f32[64,1,128]{2,1,0:T(1,128)S(1)} all-to-all(f32[64,1,128]{2,1,0:T(1,128)S(1)} %bitcast.19), channel_id=1, replica_groups=mesh['y'=4,'z'=8,'c'=2,'dir'=4] {'y','z','c'}, dimensions={0} | all-to-all | bytes 65536 | tf_op jit(solution)/shard_map/all_to_all | solution.py:455
  92.1 0.7 shard_map.102
  (12 shorter events, 0.1 us)
Async XLA Ops:
  3.9 23.3 %all-to-all-start = ((bf16[8,8,3,8,128]{4,3,2,1,0:T(8,128)(2,1)}), bf16[8,8,3,8,128]{4,3,2,1,0:T(8,128)(2,1)S(1)}, u32[]{:S(2)}, u32[]{:S(2)}) async-start(bf16[8,8,3,8,128]{4,3,2,1,0:T(8,128)(2,1)} %get-tuple-element.25), calls=%async_computation | async-start | bytes 786432 | tf_op jit(solution)/shard_map/all_to_all | solution.py:441
  12.9 1.8 %collective-permute-start = (s32[1,256]{1,0:T(1,128)S(1)}, s32[1,256]{1,0:T(1,128)S(1)}, u32[]{:S(2)}, u32[]{:S(2)}) collective-permute-start(s32[1,256]{1,0:T(1,128)S(1)} %get-tuple-element.24), channel_id=1, source_target_pairs={{0,4},{4,0},{1,5},{5,1},{2,6},{6,2},{3,7},{7,3},{8,12},{12,8},{9,1... | collective-permute-start | bytes 3080 | tf_op jit(solution)/shard_map/ppermute | solution.py:442
  14.7 5.0 %collective-permute-start.1 = (s32[1,512]{1,0:T(1,128)S(1)}, s32[1,512]{1,0:T(1,128)S(1)}, u32[]{:S(2)}, u32[]{:S(2)}) collective-permute-start(s32[1,512]{1,0:T(1,128)S(1)} %constant_dynamic-update-slice_fusion.refs_0_), channel_id=1, source_target_pairs={{0,64},{64,128},{128,192},{192,0},{1,65},{65,129},{129,193},{193,1... | collective-permute-start | bytes 6152 | tf_op jit(solution)/shard_map/ppermute | solution.py:431
  16.0 3.9 %collective-permute-start.2 = (s32[1,512]{1,0:T(1,128)S(1)}, s32[1,512]{1,0:T(1,128)S(1)}, u32[]{:S(2)}, u32[]{:S(2)}) collective-permute-start(s32[1,512]{1,0:T(1,128)S(1)} %constant_dynamic-update-slice_fusion.refs_0_), channel_id=1, source_target_pairs={{0,128},{64,192},{128,0},{192,64},{1,129},{65,193},{129,1},{193,65... | collective-permute-start | bytes 6152 | tf_op jit(solution)/shard_map/ppermute | solution.py:431
  18.6 2.7 %collective-permute-start.3 = (s32[1,512]{1,0:T(1,128)S(1)}, s32[1,512]{1,0:T(1,128)S(1)}, u32[]{:S(2)}, u32[]{:S(2)}) collective-permute-start(s32[1,512]{1,0:T(1,128)S(1)} %constant_dynamic-update-slice_fusion.refs_0_), channel_id=1, source_target_pairs={{0,192},{64,0},{128,64},{192,128},{1,193},{65,1},{129,65},{193,129... | collective-permute-start | bytes 6152 | tf_op jit(solution)/shard_map/ppermute | solution.py:431
  29.0 15.2 %all-to-all-start.1 = ((bf16[8,32,8,128]{3,2,1,0:T(8,128)(2,1)}), bf16[8,32,8,128]{3,2,1,0:T(8,128)(2,1)S(1)}, u32[]{:S(2)}, u32[]{:S(2)}) async-start(bf16[8,32,8,128]{3,2,1,0:T(8,128)(2,1)} %bitcast.20), calls=%async_computation.1 | async-start | bytes 1048576 | tf_op jit(solution)/shard_map/all_to_all | solution.py:445
  47.5 13.4 %all-to-all-start.2 = ((bf16[32,3,8,128]{3,2,1,0:T(8,128)(2,1)}), bf16[32,3,8,128]{3,2,1,0:T(8,128)(2,1)S(1)}, u32[]{:S(2)}, u32[]{:S(2)}) async-start(bf16[32,3,8,128]{3,2,1,0:T(8,128)(2,1)} %get-tuple-element.37), calls=%async_computation.2 | async-start | bytes 393216 | tf_op jit(solution)/shard_map/all_to_all | solution.py:450
  53.4 10.3 %collective-permute-start.4 = (bf16[64,8,128]{2,1,0:T(8,128)(2,1)}, bf16[64,8,128]{2,1,0:T(8,128)(2,1)S(1)}, u32[]{:S(2)}, u32[]{:S(2)}) collective-permute-start(bf16[64,8,128]{2,1,0:T(8,128)(2,1)} %get-tuple-element.31), channel_id=1, source_target_pairs={{0,192},{64,0},{128,64},{192,128},{1,193},{65,1},{129,65},{193,129... | collective-permute-start | bytes 393224 | tf_op jit(solution)/shard_map/ppermute | solution.py:431
  55.9 8.3 %collective-permute-start.5 = (bf16[64,8,128]{2,1,0:T(8,128)(2,1)}, bf16[64,8,128]{2,1,0:T(8,128)(2,1)S(1)}, u32[]{:S(2)}, u32[]{:S(2)}) collective-permute-start(bf16[64,8,128]{2,1,0:T(8,128)(2,1)} %get-tuple-element.32), channel_id=1, source_target_pairs={{0,128},{64,192},{128,0},{192,64},{1,129},{65,193},{129,1},{193,65... | collective-permute-start | bytes 393224 | tf_op jit(solution)/shard_map/ppermute | solution.py:431
  56.4 9.9 %collective-permute-start.6 = (bf16[64,8,128]{2,1,0:T(8,128)(2,1)}, bf16[64,8,128]{2,1,0:T(8,128)(2,1)S(1)}, u32[]{:S(2)}, u32[]{:S(2)}) collective-permute-start(bf16[64,8,128]{2,1,0:T(8,128)(2,1)} %get-tuple-element.33), channel_id=1, source_target_pairs={{0,64},{64,128},{128,192},{192,0},{1,65},{65,129},{129,193},{193,1... | collective-permute-start | bytes 393224 | tf_op jit(solution)/shard_map/ppermute | solution.py:431
  60.9 12.6 %collective-permute-start.11 = (bf16[96,8,128]{2,1,0:T(8,128)(2,1)S(1)}, bf16[96,8,128]{2,1,0:T(8,128)(2,1)S(1)}, u32[]{:S(2)}, u32[]{:S(2)}) collective-permute-start(bf16[96,8,128]{2,1,0:T(8,128)(2,1)S(1)} %bitcast.16), channel_id=1, source_target_pairs={{0,4},{4,0},{1,5},{5,1},{2,6},{6,2},{3,7},{7,3},{8,12},{12,8},{9,1... | collective-permute-start | bytes 589832 | tf_op jit(solution)/shard_map/ppermute | solution.py:452
  63.7 3.3 %collective-permute-start.7 = (bf16[64,8,128]{2,1,0:T(8,128)(2,1)}, bf16[64,8,128]{2,1,0:T(8,128)(2,1)S(1)}, u32[]{:S(2)}, u32[]{:S(2)}) collective-permute-start(bf16[64,8,128]{2,1,0:T(8,128)(2,1)} %get-tuple-element.30.refs_0_), channel_id=1, source_target_pairs={{0,4},{4,0},{1,5},{5,1},{2,6},{6,2},{3,7},{7,3},{8,12},{12,8},{9,1... | collective-permute-start | bytes 393224 | tf_op jit(solution)/shard_map/ppermute | solution.py:447
  63.7 3.3 %collective-permute-start.8 = (bf16[64,8,128]{2,1,0:T(8,128)(2,1)S(1)}, bf16[64,8,128]{2,1,0:T(8,128)(2,1)S(1)}, u32[]{:S(2)}, u32[]{:S(2)}) collective-permute-start(bf16[64,8,128]{2,1,0:T(8,128)(2,1)S(1)} %collective-permute-done.4.refs_1_), channel_id=1, source_target_pairs={{0,4},{4,0},{1,5},{5,1},{2,6},{6,2},{3,7},{7,3},{8,12},{12,8},{9,1... | collective-permute-start | bytes 393224 | tf_op jit(solution)/shard_map/ppermute | solution.py:447
  64.2 2.8 %collective-permute-start.9 = (bf16[64,8,128]{2,1,0:T(8,128)(2,1)S(1)}, bf16[64,8,128]{2,1,0:T(8,128)(2,1)S(1)}, u32[]{:S(2)}, u32[]{:S(2)}) collective-permute-start(bf16[64,8,128]{2,1,0:T(8,128)(2,1)S(1)} %collective-permute-done.5.refs_2_), channel_id=1, source_target_pairs={{0,4},{4,0},{1,5},{5,1},{2,6},{6,2},{3,7},{7,3},{8,12},{12,8},{9,1... | collective-permute-start | bytes 393224 | tf_op jit(solution)/shard_map/ppermute | solution.py:447
  66.3 1.7 %collective-permute-start.10 = (bf16[64,8,128]{2,1,0:T(8,128)(2,1)S(1)}, bf16[64,8,128]{2,1,0:T(8,128)(2,1)S(1)}, u32[]{:S(2)}, u32[]{:S(2)}) collective-permute-start(bf16[64,8,128]{2,1,0:T(8,128)(2,1)S(1)} %collective-permute-done.6.refs_3_), channel_id=1, source_target_pairs={{0,4},{4,0},{1,5},{5,1},{2,6},{6,2},{3,7},{7,3},{8,12},{12,8},{9,1... | collective-permute-start | bytes 393224 | tf_op jit(solution)/shard_map/ppermute | solution.py:447
  68.0 0.9 copy-start

commit v6 on v5

--- a/solution.py
+++ b/solution.py
@@ -49,92 +49,119 @@
     return jnp.broadcast_to(row, (8, row.shape[1])).T[:, :1]
 
 
-def open_kernel(place, counts, history, columns, lags, fanned, wanted, spots, aged, table, held, sems):
-    levels, rows = held.shape[0], held.shape[1]
-    tile = held.shape[3]
-    slots = columns.shape[1]
+def open_kernel(history, fanned, held, sems):
+    rows, tile = held.shape[1], held.shape[3]
+    into = start_all(
+        [(history.at[:, :, pl.ds(row * tile, tile)], held.at[:, row]) for row in range(rows)], sems
+    )
+    for copy in into:
+        copy.wait()
+    for copy in start_all([(held, fanned.at[z]) for z in range(Z)], sems, rows):
+        copy.wait()
+
+
+def open_up(history, tile):
+    levels, dirs, panels = history.shape
+    rows = panels // tile
+    return kernel_call(
+        open_kernel,
+        SMALL,
+        out_shape=pltpu.HBM((Z, levels, rows, dirs, tile), history.dtype),
+        in_specs=[hbm()],
+        out_specs=hbm(),
+        scratch_shapes=[
+            pltpu.VMEM((levels, rows, dirs, tile), history.dtype),
+            pltpu.SemaphoreType.DMA((rows + Z,)),
+        ],
+    )(off_core(history))
+
+
+class Slots:
+    def __init__(self, columns, lags):
+        self.rows, self.count = columns.shape
+        col, self.lag = columns[...], lags[...] - 1
+        owner = (col * ((1 << 17) // self.rows + 1)) >> 17
+        self.local = col - owner * self.rows
+        self.c = lax.rem(owner, C)
+        self.z = lax.rem(owner // C, Z)
+        self.y = owner // (C * Z)
+        group = self.y * C + self.c
+        self.here = lax.broadcasted_iota(jnp.int32, (self.count, self.count), 1)
+        self.there = lax.broadcasted_iota(jnp.int32, (self.count, self.count), 0)
+        groups = [group[row : row + 1] for row in range(self.rows)]
+        down = [turned(value) for value in groups]
+        self.position = []
+        for row in range(self.rows):
+            same = (down[row] == groups[row]) & (self.there < self.here)
+            position = jnp.sum(same.astype(jnp.int32), axis=0, keepdims=True)
+            for before in range(row):
+                position += jnp.sum((down[before] == groups[row]).astype(jnp.int32), axis=0, keepdims=True)
+            self.position.append(position)
+        self.at = [groups[row] * (BLOCK_CAP * Z) + self.position[row] for row in range(self.rows)]
+
+
+def plan_kernel(columns, lags, wanted):
+    slots = Slots(columns, lags)
+    spot = (slots.z * LEVELS + slots.lag) * slots.rows + slots.local
+    asks = lax.broadcasted_iota(jnp.int32, (slots.count, wanted.shape[1]), 1)
+    total = jnp.zeros(wanted.shape, jnp.int32)
+    for row in range(slots.rows):
+        mine = jnp.where(turned(slots.at[row]) == asks, turned(spot[row : row + 1]), 0)
+        total += jnp.sum(mine, axis=0, keepdims=True)
+    wanted[...] = total
+
+
+def plan(columns, lags):
+    return kernel_call(
+        plan_kernel,
+        SMALL,
+        out_shape=pltpu.VMEM((1, GROUPS * BLOCK_CAP * Z), jnp.int32),
+        in_specs=[vmem(), vmem()],
+        out_specs=vmem(),
+    )(off_core(columns), off_core(lags))
+
+
+def chart_kernel(place, counts, columns, lags, spots, aged, table):
+    slots = Slots(columns, lags)
     cap = BLOCK_CAP * Z
-    into = [
-        pltpu.make_async_copy(history.at[:, :, pl.ds(row * tile, tile)], held.at[:, row], sems.at[row])
-        for row in range(rows)
-    ]
-    for copy in into:
-        copy.start()
     y, c = place[0, 0], place[0, 1]
-    col, lag = columns[...], lags[...] - 1
-    owner = (col * ((1 << 17) // rows + 1)) >> 17
-    local = col - owner * rows
-    own_c = lax.rem(owner, C)
-    own_z = lax.rem(owner // C, Z)
-    own_y = owner // (C * Z)
-    group = own_y * C + own_c
-    spot = (own_z * levels + lag) * rows + local
-    other = (own_c != c).astype(jnp.int32)
-    across = (lax.rem(own_y - y + Y, Y) * C + other) * cap
-    fresh = (other * (Y * Z) + own_y * Z + own_z) * rows + local
-    for copy in into:
-        copy.wait()
-    out = [pltpu.make_async_copy(held, fanned.at[z], sems.at[rows + z]) for z in range(Z)]
-    for copy in out:
-        copy.start()
-    here = lax.broadcasted_iota(jnp.int32, (slots, slots), 1)
-    there = lax.broadcasted_iota(jnp.int32, (slots, slots), 0)
-    groups = [group[row : row + 1] for row in range(rows)]
-    down = [turned(value) for value in groups]
-    asks = lax.broadcasted_iota(jnp.int32, (slots, GROUPS * cap), 1)
-    total = jnp.zeros((1, GROUPS * cap), jnp.int32)
-    lane = lax.broadcasted_iota(jnp.int32, (1, slots), 1)
-    spot_parts, aged_parts, order_parts, where_parts, new_counts = [], [], [], [], []
-    for row in range(rows):
-        same = (down[row] == groups[row]) & (there < here)
-        position = jnp.sum(same.astype(jnp.int32), axis=0, keepdims=True)
-        for before in range(row):
-            position += jnp.sum((down[before] == groups[row]).astype(jnp.int32), axis=0, keepdims=True)
-        at = groups[row] * cap + position
+    other = (slots.c != c).astype(jnp.int32)
+    across = (lax.rem(slots.y - y + Y, Y) * C + other) * cap
+    fresh = (other * (Y * Z) + slots.y * Z + slots.z) * slots.rows + slots.local
+    lane = lax.broadcasted_iota(jnp.int32, (1, slots.count), 1)
+    spot_parts, aged_parts, order_parts, where_parts, new_parts = [], [], [], [], []
+    for row in range(slots.rows):
         live = lane < counts[row]
-        new = live & (lag[row : row + 1] == 0)
-        total += jnp.sum(jnp.where(turned(at) == asks, turned(spot[row : row + 1]), 0), axis=0, keepdims=True)
-        spot_parts.append(jnp.where(live, at, -1))
-        aged_parts.append(jnp.where(live & ~new, across[row : row + 1] + position, -1))
+        new = live & (slots.lag[row : row + 1] == 0)
+        spot_parts.append(jnp.where(live, slots.at[row], -1))
+        aged_parts.append(jnp.where(live & ~new, across[row : row + 1] + slots.position[row], -1))
         fresh_row = jnp.where(new, fresh[row : row + 1], -1)
         marked = turned(new.astype(jnp.int32)) == 1
-        rank = jnp.sum((marked & (there < here)).astype(jnp.int32), axis=0, keepdims=True)
-        put = marked & (turned(rank) == here)
-        order_parts.append(jnp.sum(jnp.where(put, there, 0), axis=0, keepdims=True))
+        rank = jnp.sum((marked & (slots.there < slots.here)).astype(jnp.int32), axis=0, keepdims=True)
+        put = marked & (turned(rank) == slots.here)
+        order_parts.append(jnp.sum(jnp.where(put, slots.there, 0), axis=0, keepdims=True))
         where_parts.append(jnp.sum(jnp.where(put, turned(fresh_row) + 1, 0), axis=0, keepdims=True) - 1)
-        new_counts.append(jnp.sum(new.astype(jnp.int32), axis=1, keepdims=True))
-    wanted[...] = total
-    rest = jnp.zeros((1, spots.shape[1] - rows * slots), jnp.int32)
-    spots[...] = jnp.concatenate([*spot_parts, rest], axis=1)
-    aged[...] = jnp.concatenate([*aged_parts, rest], axis=1)
+        new_count = jnp.sum(new.astype(jnp.int32), axis=1, keepdims=True)
+        new_parts.append(jnp.broadcast_to(new_count, (1, slots.count)))
+    rest = jnp.zeros((1, spots.shape[1] - slots.rows * slots.count), jnp.int32)
+    tail = rest
+    for row in range(slots.rows):
+        tail = jnp.where(lax.broadcasted_iota(jnp.int32, rest.shape, 1) == row, counts[row], tail)
+    spots[...] = jnp.concatenate([*spot_parts, tail], axis=1)
+    aged[...] = jnp.concatenate([*aged_parts, tail], axis=1)
     table[0:1, :] = jnp.concatenate([*order_parts, rest], axis=1)
     table[1:2, :] = jnp.concatenate([*where_parts, rest], axis=1)
-    table[2:3, :] = jnp.concatenate(
-        [jnp.broadcast_to(count, (1, slots)) for count in new_counts] + [rest], axis=1
-    )
-    for copy in out:
-        copy.wait()
-
-
-def open_up(place, counts, history, columns, lags, tile):
-    levels, dirs, panels = history.shape
-    rows = panels // tile
-    shapes = ((1, GROUPS * BLOCK_CAP * Z), (1, 128), (1, 128), (3, 128))
-    return kernel_call(
-        open_kernel,
-        SMALL,
-        out_shape=(
-            pltpu.HBM((Z, levels, rows, dirs, tile), history.dtype),
-            pltpu.VMEM(shapes[0], jnp.int32),
-            *[pltpu.HBM(shape, jnp.int32) for shape in shapes[1:]],
-        ),
-        in_specs=[smem(), smem(), hbm(), vmem(), vmem()],
-        out_specs=(hbm(), *[vmem()] * 4),
-        scratch_shapes=[
-            pltpu.VMEM((levels, rows, dirs, tile), history.dtype),
-            pltpu.SemaphoreType.DMA((rows + Z,)),
-        ],
-    )(place, off_core(counts), off_core(history), off_core(columns), off_core(lags))
+    table[2:3, :] = jnp.concatenate([*new_parts, rest], axis=1)
+
+
+def chart(place, counts, columns, lags):
+    return kernel_call(
+        chart_kernel,
+        SMALL,
+        out_shape=tuple(pltpu.VMEM((length, 128), jnp.int32) for length in (1, 1, 3)),
+        in_specs=[smem(), smem(), vmem(), vmem()],
+        out_specs=[vmem()] * 3,
+    )(place, off_core(counts), off_core(columns), off_core(lags))
 
 
 def whose(place, shift, other):
@@ -143,32 +170,45 @@
 
 
 def pick_kernel(place, *refs):
-    lists, held, first = refs[:Y], refs[Y], refs[Y + 1]
+    lists, held, first, kept, sems = refs[:Y], refs[Y], refs[Y + 1], refs[Y + 2], refs[Y + 3]
     cap = first.shape[0] // GROUPS
     mine = (place[0, 0] * C + place[0, 1]) * cap
+    copies = []
     for shift in range(Y):
         for other in range(C):
+            base = len(copies) * cap
+
+            @pl.loop(0, cap, step=16)
+            def _(entry):
+                for k in range(16):
+                    spot = lists[shift][0, other * GROUPS * cap + mine + entry + k]
+                    kept[base + entry + k] = held[spot]
+
             to = whose(place, shift, other) * cap
-
-            @pl.loop(0, cap, step=16)
-            def _(base):
-                for k in range(16):
-                    first[to + base + k] = held[lists[shift][0, other * GROUPS * cap + mine + base + k]]
+            pair = (kept.at[pl.ds(base, cap)], first.at[pl.ds(to, cap)])
+            copies += start_all([pair], sems, len(copies))
+    for copy in copies:
+        copy.wait()
 
 
 def pick_later_kernel(place, *refs):
-    lists, held, later = refs[:Y], refs[Y], refs[Y + 1 :]
+    lists, held, later, kept, sems = refs[:Y], refs[Y], refs[Y + 1 : 2 * Y + 1], refs[2 * Y + 1], refs[2 * Y + 2]
     cap = later[0].shape[0] // C
     back = held.shape[0] // (Z * LEVELS)
     mine = (place[0, 0] * C + place[0, 1]) * cap
+    copies = []
     for shift in range(Y):
         for other in range(C):
 
             @pl.loop(0, cap, step=16)
-            def _(base):
+            def _(entry):
                 for k in range(16):
-                    spot = lists[shift][0, other * GROUPS * cap + mine + base + k]
-                    later[shift][other * cap + base + k] = held[jnp.maximum(spot - back, 0)]
+                    spot = lists[shift][0, other * GROUPS * cap + mine + entry + k]
+                    kept[shift, other * cap + entry + k] = held[jnp.maximum(spot - back, 0)]
+
+        copies += start_all([(kept.at[shift], later[shift])], sems, shift)
+    for copy in copies:
+        copy.wait()
 
 
 def picks(place, lists, held, cap):
@@ -176,12 +216,29 @@
         return pltpu.HBM((entries, *held.shape[1:]), held.dtype)
 
     held = near_core(held)
+    lists = [near_core(value) for value in lists]
     specs = [smem()] * (1 + Y) + [vmem()]
     first = kernel_call(
-        pick_kernel, SMALL, out_shape=out(GROUPS * cap), in_specs=specs, out_specs=vmem()
+        pick_kernel,
+        SMALL,
+        out_shape=out(GROUPS * cap),
+        in_specs=specs,
+        out_specs=hbm(),
+        scratch_shapes=[
+            pltpu.VMEM((GROUPS * cap, *held.shape[1:]), held.dtype),
+            pltpu.SemaphoreType.DMA((GROUPS,)),
+        ],
     )(place, *lists, held)
     later = kernel_call(
-        pick_later_kernel, SMALL, out_shape=[out(C * cap)] * Y, in_specs=specs, out_specs=[vmem()] * Y
+        pick_later_kernel,
+        SMALL,
+        out_shape=[out(C * cap)] * Y,
+        in_specs=specs,
+        out_specs=[hbm()] * Y,
+        scratch_shapes=[
+            pltpu.VMEM((Y, C * cap, *held.shape[1:]), held.dtype),
+            pltpu.SemaphoreType.DMA((Y,)),
+        ],
     )(place, *lists, held)
     return first, later
 
@@ -213,14 +270,37 @@
     return copies
 
 
-def stage_kernel(ztiles_hbm, zinv_hbm, incident_hbm, top, zinv, incident, sems):
+def live_tiles(count, source, target, sems, row, act):
+    slots = target.shape[0]
+    for chunk in range(slots // CHUNK):
+        part = pl.ds(chunk * CHUNK, CHUNK)
+
+        @pl.when(chunk * CHUNK < count)
+        def _():
+            copy = pltpu.make_async_copy(source.at[part], target.at[part], sems.at[row, chunk])
+            if act == "start":
+                copy.start()
+            else:
+                copy.wait()
+
+        if act == "start":
+
+            @pl.when(chunk * CHUNK >= count)
+            def _():
+                target[part] = jnp.zeros((CHUNK, *target.shape[1:]), target.dtype)
+
+
+def stage_kernel(counts, ztiles_hbm, zinv_hbm, incident_hbm, top, zinv, incident, sems, tile_sems):
     kept = top.shape[0]
-    pairs = [(ztiles_hbm.at[row], top.at[row]) for row in range(kept)]
-    for copy in start_all([*pairs, (zinv_hbm, zinv), (incident_hbm.at[0], incident)], sems):
-        copy.wait()
-
-
-def stage(ztiles, zinv, incident):
+    for row in range(kept):
+        live_tiles(counts[row], ztiles_hbm.at[row], top.at[row], tile_sems, row, "start")
+    for copy in start_all([(zinv_hbm, zinv), (incident_hbm.at[0], incident)], sems):
+        copy.wait()
+    for row in range(kept):
+        live_tiles(counts[row], ztiles_hbm.at[row], top.at[row], tile_sems, row, "wait")
+
+
+def stage(counts, ztiles, zinv, incident):
     kept = ztiles.shape[0] - 1
     return kernel_call(
         stage_kernel,
@@ -230,28 +310,35 @@
             pltpu.VMEM(zinv.shape, zinv.dtype),
             pltpu.VMEM(incident.shape[1:], incident.dtype),
         ),
-        in_specs=[hbm()] * 3,
+        in_specs=[smem()] + [hbm()] * 3,
         out_specs=[vmem()] * 3,
-        scratch_shapes=[pltpu.SemaphoreType.DMA((kept + 2,))],
-    )(off_core(ztiles), off_core(zinv), off_core(incident))
-
-
-def first_kernel(spots, got, top, ztiles_hbm, zinv, incident, out, spread_out, last, sems):
-    kept, tile = top.shape[0], top.shape[2]
-    copy = pltpu.make_async_copy(ztiles_hbm.at[kept], last, sems.at[0])
-    copy.start()
+        scratch_shapes=[
+            pltpu.SemaphoreType.DMA((2,)),
+            pltpu.SemaphoreType.DMA((kept, ztiles.shape[1] // CHUNK)),
+        ],
+    )(off_core(counts), off_core(ztiles), off_core(zinv), off_core(incident))
+
+
+def first_kernel(spots, got, top, ztiles_hbm, zinv, incident, out, spread_out, last, kept_out, sems, tile_sems):
+    kept, slots, tile = top.shape[0], top.shape[1], top.shape[2]
+    count = spots[0, (kept + 1) * slots + kept]
+    live_tiles(count, ztiles_hbm.at[kept], last, tile_sems, 0, "start")
+    copies = []
     for row in range(kept + 1):
         if row == kept:
-            copy.wait()
+            live_tiles(count, ztiles_hbm.at[kept], last, tile_sems, 0, "wait")
         total = row_sum(spots, lambda spot: got[spot], top.at[row] if row < kept else last, row)
         density = density_of(incident[:, row * tile : (row + 1) * tile], total, zinv[row])
         out[row] = density
         for to in range(spread_out.shape[0]):
-            spread_out[to, row] = density
+            kept_out[row, to] = density
+        copies += start_all([(kept_out.at[row], spread_out.at[:, row])], sems, row)
+    for copy in copies:
+        copy.wait()
 
 
 def first_step(spots, got, top, ztiles, zinv, incident):
-    rows, tile, dirs = ztiles.shape[0], ztiles.shape[2], got.shape[1]
+    rows, slots, tile, dirs = ztiles.shape[0], ztiles.shape[1], ztiles.shape[2], got.shape[1]
     return kernel_call(
         first_kernel,
         SMALL,
@@ -260,41 +347,46 @@
             pltpu.HBM((Y * Z, rows, dirs, tile), jnp.bfloat16),
         ),
         in_specs=[smem(), vmem(), vmem(), hbm(), vmem(), vmem()],
-        out_specs=(vmem(), vmem()),
-        scratch_shapes=[pltpu.VMEM(ztiles.shape[1:], ztiles.dtype), pltpu.SemaphoreType.DMA((1,))],
-    )(off_core(spots), near_core(got), near_core(top), off_core(ztiles), near_core(zinv), near_core(incident))
+        out_specs=(vmem(), hbm()),
+        scratch_shapes=[
+            pltpu.VMEM(ztiles.shape[1:], ztiles.dtype),
+            pltpu.VMEM((rows, Y * Z, dirs, tile), jnp.bfloat16),
+            pltpu.SemaphoreType.DMA((rows,)),
+            pltpu.SemaphoreType.DMA((1, slots // CHUNK)),
+        ],
+    )(near_core(spots), near_core(got), near_core(top), off_core(ztiles), near_core(zinv), near_core(incident))
 
 
 def aged_kernel(spots, table, before, incident, *refs):
     near, cross = refs[:Y], refs[Y : 2 * Y]
-    ztiles_hbm, basis_hbm, packed, fresh, basis, pool, ztiles, sems, fresh_sems = refs[2 * Y :]
+    ztiles_hbm, basis_hbm, packed, fresh, basis, pool, ztiles, sems, tile_sems, fresh_sems = refs[2 * Y :]
     rows, slots, tile = ztiles.shape[0], ztiles.shape[1], ztiles.shape[2]
     cap = near[0].shape[0] // C
     panels = rows * tile
+    counts = [spots[0, rows * slots + row] for row in range(rows)]
     pairs = []
     for shift in range(Y):
         for source, at in ((near[shift], 0), (cross[shift], cap)):
             pairs.append((source.at[pl.ds(at, cap)], pool.at[pl.ds(len(pairs) * cap, cap)]))
-    pairs += [(ztiles_hbm.at[row], ztiles.at[row]) for row in range(rows)]
-    pairs.append((basis_hbm, basis))
     copies = start_all(pairs, sems)
+    for row in range(rows):
+        live_tiles(counts[row], ztiles_hbm.at[row], ztiles.at[row], tile_sems, row, "start")
+    weights = start_all([(basis_hbm, basis)], sems, len(pairs))[0]
+    for copy in copies:
+        copy.wait()
     lag_one = []
     for row in range(rows):
+        live_tiles(counts[row], ztiles_hbm.at[row], ztiles.at[row], tile_sems, row, "wait")
         for k in range(CHUNK):
-            source = ztiles_hbm.at[row, table[0, row * slots + k]]
+            source = ztiles.at[row, table[0, row * slots + k]]
             lag_one.append(pltpu.make_async_copy(source, fresh.at[row, k], fresh_sems.at[row, k]))
-    for copy in lag_one:
-        copy.start()
-    for copy in copies[: 2 * Y]:
-        copy.wait()
-    for row in range(rows):
-        copies[2 * Y + row].wait()
+            lag_one[-1].start()
         at = slice(row * tile, (row + 1) * tile)
         packed[0, :, at] = incident[1, :, at].astype(jnp.float32)
         packed[1, :, at] = row_sum(spots, lambda spot: pool[spot], ztiles.at[row], row)
     value = jnp.concatenate([before[row] for row in range(rows)], axis=1)
     packed[2, :, :] = value.astype(jnp.float32)
-    copies[-1].wait()
+    weights.wait()
     packed[3, :, : basis.shape[1]] = jnp.dot(value, basis[...], preferred_element_type=jnp.float32)
     packed[3, :, basis.shape[1] :] = jnp.zeros((value.shape[0], panels - basis.shape[1]), jnp.float32)
     for copy in lag_one:
@@ -317,12 +409,13 @@
         scratch_shapes=[
             pltpu.VMEM((2 * Y * cap, dirs, tile), jnp.bfloat16),
             pltpu.VMEM(ztiles.shape, ztiles.dtype),
-            pltpu.SemaphoreType.DMA((2 * Y + rows + 1,)),
+            pltpu.SemaphoreType.DMA((2 * Y + 1,)),
+            pltpu.SemaphoreType.DMA((rows, ztiles.shape[1] // CHUNK)),
             pltpu.SemaphoreType.DMA((rows, CHUNK)),
         ],
     )(
-        off_core(spots),
-        off_core(table),
+        near_core(spots),
+        near_core(table),
         off_core(before),
         off_core(incident),
         *near,
@@ -397,7 +490,7 @@
             pltpu.SemaphoreType.DMA((CHUNK,)),
         ],
     )(
-        off_core(table),
+        near_core(table),
         near_core(packed),
         near_core(fresh),
         near_core(zinv),
@@ -437,15 +530,16 @@
     owners = Y * Z * C
     cap = BLOCK_CAP * Z
     place = jnp.stack([lax.axis_index("y"), lax.axis_index("c")]).reshape(1, 2)
-    fanned, wanted, spots, aged, table = open_up(place, counts, history, columns, lags, tile)
-    held = lax.all_to_all(fanned, "z", 0, 0, tiled=True).reshape(-1, dirs, tile)
+    held = lax.all_to_all(open_up(history, tile), "z", 0, 0, tiled=True).reshape(-1, dirs, tile)
+    wanted = plan(columns, lags)
+    spots, aged, table = chart(place, counts, columns, lags)
     both = jnp.concatenate([wanted, lax.ppermute(wanted, "c", SWAP)], axis=1)
     lists = [both] + [shifted(both, "y", Y, s) for s in range(1, Y)]
     first, later = picks(place, lists, held, cap)
     got = lax.all_to_all(first.reshape(GROUPS, cap, dirs, tile), ("y", "c"), 0, 0, tiled=True)
     near = [later[0]] + [shifted(later[s], "y", Y, -s) for s in range(1, Y)]
     cross = [lax.ppermute(piece, "c", SWAP) for piece in near]
-    top, inverse, driven = stage(ztiles, zinv, incident)
+    top, inverse, driven = stage(counts, ztiles, zinv, incident)
     density, fanned = first_step(spots, got.reshape(GROUPS * cap, dirs, tile), top, ztiles, inverse, driven)
     here = lax.all_to_all(fanned, ("y", "z"), 0, 0, tiled=True).reshape(Y * Z * rows, dirs, tile)
     packed, lag_one, weights = aged_step(aged, table, density, incident, near, cross, ztiles, basis)

time: 93.4 us -> 91.8 us (0.983)
  waiting for transfers between devices: 21.6 us -> 18.5 us
  Pallas kernels: 19.3 us -> 21 us
    all_to_all x1, waiting for transfers between devices: 7.76 us -> 5.75 us  [march(): lax.all_to_all(first.reshape(GROUPS, cap, dirs, tile), ('y', 'c'), 0, 0,...]
    all_to_all x1, waiting for transfers between devices: 5.83 us -> 4.66 us  [march(): lax.all_to_all(open_up(history, tile), 'z', 0, 0, tiled=True)]
    pallas_call x1 -> x3, Pallas kernels: 3.17 us -> 4.11 us  [the longest x1 1.6 us: open_up(): kernel_call(open_kernel, SMALL, out_shape=pltpu.HBM((Z, levels, rows, dir...]
  transfers between devices with their start and end apart: 15 -> 15, of which waited for: 8 -> 8; matrix products, arithmetic and copies ran while one was open for 0% -> 0% of each run, Pallas kernels for 9% -> 13%
where the time goes in v6:
time: 91.8 us; the launch traced here: 91.2 us
  starting transfers between devices  33.7 us (37%)
  Pallas kernels  21 us (23%)
  waiting for transfers between devices  18.5 us (20%)
  blocking collectives  16.4 us (18%)
    all_to_all x1, blocking collectives, march(): lax.all_to_all(far.reshape(owners, 1, 128), E, 0, 0, tiled=True)  16.4 us
    all_to_all x1, starting transfers between devices, march(): lax.all_to_all(open_up(history, tile), 'z', 0, 0, tiled=True)  9.02 us
    ppermute x6, starting transfers between devices, shifted(): lax.ppermute(value, axis, [(i, (i + shift) % length) for i in range(lengt...  8.65 us
    all_to_all x1, starting transfers between devices, march(): lax.all_to_all(first.reshape(GROUPS, cap, dirs, tile), ('y', 'c'), 0, 0,...  5.84 us
    all_to_all x1, waiting for transfers between devices, march(): lax.all_to_all(first.reshape(GROUPS, cap, dirs, tile), ('y', 'c'), 0, 0,...  5.75 us
    pallas_call x1, Pallas kernels, aged_step(): kernel_call(aged_kernel, SMALL, out_shape=(pltpu.VMEM((4, dirs, rows * ti...  4.94 us
    all_to_all x1, waiting for transfers between devices, march(): lax.all_to_all(open_up(history, tile), 'z', 0, 0, tiled=True)  4.66 us
    all_to_all x1, starting transfers between devices, march(): lax.all_to_all(fanned, ('y', 'z'), 0, 0, tiled=True)  3.88 us
  transfers between devices with their start and end apart: 15, of which 8 were waited for; matrix products, arithmetic and copies ran while one was open for 0% of the time, Pallas kernels for 13%

profile of v6, /device:TPU:1, one launch (start us, length us, event | category | flops | bytes accessed | tf_op | source)
XLA Modules:
  0.0 91.2 jit_solution(8527577494246243405)
XLA Ops:
  0.6 1.6 %shard_map.97 = bf16[8,8,3,8,128]{4,3,2,1,0:T(8,128)(2,1)} custom-call(bf16[8,8,384]{2,1,0:T(8,128)(2,1)} %history.1), custom_call_target="tpu_custom_call" | custom-call | tf_op jit(solution)/shard_map/pallas_call | solution.py:66
  2.2 9.0 %all-to-all-start = ((bf16[8,8,3,8,128]{4,3,2,1,0:T(8,128)(2,1)}), bf16[8,8,3,8,128]{4,3,2,1,0:T(8,128)(2,1)S(1)}, u32[]{:S(2)}, u32[]{:S(2)}) async-start(bf16[8,8,3,8,128]{4,3,2,1,0:T(8,128)(2,1)} %shard_map.97), calls=%async_computation | async-start | bytes 786432 | tf_op jit(solution)/shard_map/all_to_all | solution.py:533
  11.3 1.1 %shard_map.96 = s32[1,256]{1,0:T(1,128)S(1)} custom-call(s32[3,32]{1,0:T(4,128)} %columns.3, s32[3,32]{1,0:T(4,128)} %lags.3), custom_call_target="tpu_custom_call" | custom-call | tf_op jit(solution)/shard_map/pallas_call | solution.py:115
  12.3 1.0 %collective-permute-start = (s32[1,256]{1,0:T(1,128)S(1)}, s32[1,256]{1,0:T(1,128)S(1)}, u32[]{:S(2)}, u32[]{:S(2)}) collective-permute-start(s32[1,256]{1,0:T(1,128)S(1)} %shard_map.96), channel_id=1, source_target_pairs={{0,4},{4,0},{1,5},{5,1},{2,6},{6,2},{3,7},{7,3},{8,12},{12,8},{9,1... | collective-permute-start | bytes 3080 | tf_op jit(solution)/shard_map/ppermute | solution.py:536
  13.4 0.8 collective-permute-done
  14.2 1.3 %collective-permute-start.1 = (s32[1,512]{1,0:T(1,128)S(1)}, s32[1,512]{1,0:T(1,128)S(1)}, u32[]{:S(2)}, u32[]{:S(2)}) collective-permute-start(s32[1,512]{1,0:T(1,128)S(1)} %pad_add_fusion.refs_0_), channel_id=1, source_target_pairs={{0,64},{64,128},{128,192},{192,0},{1,65},{65,129},{129,193},{193,1... | collective-permute-start | bytes 6152 | tf_op jit(solution)/shard_map/ppermute | solution.py:524
  15.5 2.6 %collective-permute-start.2 = (s32[1,512]{1,0:T(1,128)S(1)}, s32[1,512]{1,0:T(1,128)S(1)}, u32[]{:S(2)}, u32[]{:S(2)}) collective-permute-start(s32[1,512]{1,0:T(1,128)S(1)} %pad_add_fusion.refs_0_), channel_id=1, source_target_pairs={{0,128},{64,192},{128,0},{192,64},{1,129},{65,193},{129,1},{193,65... | collective-permute-start | bytes 6152 | tf_op jit(solution)/shard_map/ppermute | solution.py:524
  18.1 1.1 %collective-permute-start.3 = (s32[1,512]{1,0:T(1,128)S(1)}, s32[1,512]{1,0:T(1,128)S(1)}, u32[]{:S(2)}, u32[]{:S(2)}) collective-permute-start(s32[1,512]{1,0:T(1,128)S(1)} %pad_add_fusion.refs_0_), channel_id=1, source_target_pairs={{0,192},{64,0},{128,64},{192,128},{1,193},{65,1},{129,65},{193,129... | collective-permute-start | bytes 6152 | tf_op jit(solution)/shard_map/ppermute | solution.py:524
  19.7 1.1 %collective-permute-done.3.refs_3_ = s32[1,512]{1,0:T(1,128)S(1)} collective-permute-done((s32[1,512]{1,0:T(1,128)S(1)}, s32[1,512]{1,0:T(1,128)S(1)}, u32[]{:S(2)}, u32[]{:S(2)}) %collective-permute-start.3) | collective-permute-done | bytes 2080 | tf_op jit(solution)/shard_map/ppermute | solution.py:524
  20.9 4.7 %all-to-all-done = bf16[8,8,3,8,128]{4,3,2,1,0:T(8,128)(2,1)S(1)} async-done(((bf16[8,8,3,8,128]{4,3,2,1,0:T(8,128)(2,1)}), bf16[8,8,3,8,128]{4,3,2,1,0:T(8,128)(2,1)S(1)}, u32[]{:S(2)}, u32[]{:S(2)}) %all-to-all-start) | async-done | bytes 393248 | tf_op jit(solution)/shard_map/all_to_all | solution.py:533
  25.5 1.8 %shard_map.98 = bf16[256,8,128]{2,1,0:T(8,128)(2,1)} custom-call(s32[1,2]{1,0:T(1,128)S(1)} %add_bitcast_fusion.place, s32[1,512]{1,0:T(1,128)S(1)} %pad_add_fusion.refs_0_, s32[1,512]{1,0:T(1,128)S(1)} %collective-permute-done.1.refs_1_, s32[1,512]{1,0:T(1,128)S(1)} %collective-permute-done.2.refs_2_, s32[1,512]{1,0:T(1,128)S(1)} %collective-permute-done.3.refs_3_, ...), custom_call_target="tpu_custom_call" | custom-call | tf_op jit(solution)/shard_map/pallas_call | solution.py:221
  27.3 5.8 %all-to-all-start.1 = ((bf16[8,32,8,128]{3,2,1,0:T(8,128)(2,1)}), bf16[8,32,8,128]{3,2,1,0:T(8,128)(2,1)S(1)}, u32[]{:S(2)}, u32[]{:S(2)}) async-start(bf16[8,32,8,128]{3,2,1,0:T(8,128)(2,1)} %bitcast.20), calls=%async_computation.1 | async-start | bytes 1048576 | tf_op jit(solution)/shard_map/all_to_all | solution.py:539
  33.1 1.4 %shard_map.95 = (s32[1,128]{1,0:T(1,128)S(1)}, s32[1,128]{1,0:T(1,128)S(1)}, s32[3,128]{1,0:T(4,128)S(1)}) custom-call(s32[1,2]{1,0:T(1,128)S(1)} %add_bitcast_fusion.place, s32[3]{0:T(128)} %counts.3, s32[3,32]{1,0:T(4,128)} %columns.3, s32[3,32]{1,0:T(4,128)} %lags.3), custom_call_target="tpu_custom_call" | custom-call | tf_op jit(solution)/shard_map/pallas_call | solution.py:158
  34.6 2.2 %shard_map.99 = (bf16[2,32,128,128]{3,2,1,0:T(8,128)(2,1)S(1)}, bf16[3,128,128]{2,1,0:T(8,128)(2,1)S(1)}, bf16[8,384]{1,0:T(8,128)(2,1)S(1)}) custom-call(s32[3]{0:T(128)} %counts.3, bf16[3,32,128,128]{3,2,1,0:T(8,128)(2,1)} %ztiles_hbm.5, bf16[3,128,128]{2,1,0:T(8,128)(2,1)} %zinv_hbm.1, bf16[2,8,384]{2,1,0:T(8,128)(2,1)} %incident.1), custom_call_target="tpu_custom_call" | custom-call | tf_op jit(solution)/shard_map/pallas_call | solution.py:305
  36.7 5.8 %all-to-all-done.1 = bf16[8,32,8,128]{3,2,1,0:T(8,128)(2,1)S(1)} async-done(((bf16[8,32,8,128]{3,2,1,0:T(8,128)(2,1)}), bf16[8,32,8,128]{3,2,1,0:T(8,128)(2,1)S(1)}, u32[]{:S(2)}, u32[]{:S(2)}) %all-to-all-start.1) | async-done | bytes 524320 | tf_op jit(solution)/shard_map/all_to_all | solution.py:539
  42.5 3.4 %shard_map.100 = (bf16[3,8,128]{2,1,0:T(8,128)(2,1)}, bf16[32,3,8,128]{3,2,1,0:T(8,128)(2,1)}) custom-call(s32[1,128]{1,0:T(1,128)S(1)} %get-tuple-element.21.spots, bf16[256,8,128]{2,1,0:T(8,128)(2,1)S(1)} %bitcast.15, bf16[2,32,128,128]{3,2,1,0:T(8,128)(2,1)S(1)} %get-tuple-element.22.top, bf16[3,32,128,128]{3,2,1,0:T(8,128)(2,1)} %ztiles_hbm.5, ...), custom_call_target="tpu_custom_call" | custom-call | tf_op jit(solution)/shard_map/pallas_call | solution.py:342
  45.9 3.9 %all-to-all-start.2 = ((bf16[32,3,8,128]{3,2,1,0:T(8,128)(2,1)}), bf16[32,3,8,128]{3,2,1,0:T(8,128)(2,1)S(1)}, u32[]{:S(2)}, u32[]{:S(2)}) async-start(bf16[32,3,8,128]{3,2,1,0:T(8,128)(2,1)} %get-tuple-element.33), calls=%async_computation.2 | async-start | bytes 393216 | tf_op jit(solution)/shard_map/all_to_all | solution.py:544
  49.8 1.9 %shard_map.101 = (bf16[64,8,128]{2,1,0:T(8,128)(2,1)}, bf16[64,8,128]{2,1,0:T(8,128)(2,1)}, bf16[64,8,128]{2,1,0:T(8,128)(2,1)}, bf16[64,8,128]{2,1,0:T(8,128)(2,1)}) custom-call(s32[1,2]{1,0:T(1,128)S(1)} %add_bitcast_fusion.place, s32[1,512]{1,0:T(1,128)S(1)} %pad_add_fusion.refs_0_, s32[1,512]{1,0:T(1,128)S(1)} %collective-permute-done.1.refs_1_, ...), custom_call_target="tpu_custom_call" | custom-call | tf_op jit(solution)/shard_map/pallas_call | solution.py:232
  51.7 2.6 %collective-permute-start.4 = (bf16[64,8,128]{2,1,0:T(8,128)(2,1)}, bf16[64,8,128]{2,1,0:T(8,128)(2,1)S(1)}, u32[]{:S(2)}, u32[]{:S(2)}) collective-permute-start(bf16[64,8,128]{2,1,0:T(8,128)(2,1)} %get-tuple-element.27), channel_id=1, source_target_pairs={{0,192},{64,0},{128,64},{192,128},{1,193},{65,1},{129,65},{193,129... | collective-permute-start | bytes 393224 | tf_op jit(solution)/shard_map/ppermute | solution.py:524
  54.7 0.6 collective-permute-start.6
  55.4 3.9 %all-to-all-done.2 = bf16[32,3,8,128]{3,2,1,0:T(8,128)(2,1)S(1)} async-done(((bf16[32,3,8,128]{3,2,1,0:T(8,128)(2,1)}), bf16[32,3,8,128]{3,2,1,0:T(8,128)(2,1)S(1)}, u32[]{:S(2)}, u32[]{:S(2)}) %all-to-all-start.2) | async-done | bytes 196640 | tf_op jit(solution)/shard_map/all_to_all | solution.py:544
  59.2 2.8 %collective-permute-start.11 = (bf16[96,8,128]{2,1,0:T(8,128)(2,1)S(1)}, bf16[96,8,128]{2,1,0:T(8,128)(2,1)S(1)}, u32[]{:S(2)}, u32[]{:S(2)}) collective-permute-start(bf16[96,8,128]{2,1,0:T(8,128)(2,1)S(1)} %bitcast.16), channel_id=1, source_target_pairs={{0,4},{4,0},{1,5},{5,1},{2,6},{6,2},{3,7},{7,3},{8,12},{12,8},{9,1... | collective-permute-start | bytes 589832 | tf_op jit(solution)/shard_map/ppermute | solution.py:546
  62.1 0.5 collective-permute-start.8
  62.6 1.3 %collective-permute-start.9 = (bf16[64,8,128]{2,1,0:T(8,128)(2,1)S(1)}, bf16[64,8,128]{2,1,0:T(8,128)(2,1)S(1)}, u32[]{:S(2)}, u32[]{:S(2)}) collective-permute-start(bf16[64,8,128]{2,1,0:T(8,128)(2,1)S(1)} %collective-permute-done.5.refs_2_), channel_id=1, source_target_pairs={{0,4},{4,0},{1,5},{5,1},{2,6},{6,2},{3,7},{7,3},{8,12},{12,8},{9,1... | collective-permute-start | bytes 393224 | tf_op jit(solution)/shard_map/ppermute | solution.py:541
  63.9 0.8 collective-permute-done.6.refs_3_
  64.7 0.6 collective-permute-start.10
  65.3 1.0 %collective-permute-done.10.refs_7_ = bf16[64,8,128]{2,1,0:T(8,128)(2,1)S(1)} collective-permute-done((bf16[64,8,128]{2,1,0:T(8,128)(2,1)S(1)}, bf16[64,8,128]{2,1,0:T(8,128)(2,1)S(1)}, u32[]{:S(2)}, u32[]{:S(2)}) %collective-permute-start.10) | collective-permute-done | bytes 131104 | tf_op jit(solution)/shard_map/ppermute | solution.py:541
  66.3 0.9 copy-done
  67.2 4.9 %shard_map.102 = (f32[4,8,384]{2,1,0:T(8,128)S(1)}, bf16[3,8,128,128]{3,2,1,0:T(8,128)(2,1)S(1)}, bf16[384,256]{1,0:T(8,128)(2,1)S(1)}) custom-call(s32[1,128]{1,0:T(1,128)S(1)} %get-tuple-element.20.spots, s32[3,128]{1,0:T(4,128)S(1)} %get-tuple-element.19.table, bf16[3,8,128]{2,1,0:T(8,128)(2,1)} %get-tuple-element.25.before, bf16[2,8,384]{2,1,0:T(8,128)(2,1)} %incident.1, ...), custom_call_target="tpu_custom_call" | custom-call | tf_op jit(solution)/shard_map/pallas_call | solution.py:399
  72.1 2.0 %shard_map.103 = (bf16[2,8,384]{2,1,0:T(8,128)(2,1)}, f32[64,128]{1,0:T(8,128)S(1)}) custom-call(s32[3,128]{1,0:T(4,128)S(1)} %get-tuple-element.19.table, f32[4,8,384]{2,1,0:T(8,128)S(1)} %get-tuple-element.30.packed, bf16[3,8,128,128]{3,2,1,0:T(8,128)(2,1)S(1)} %get-tuple-element.31.fresh, bf16[3,128,128]{2,1,0:T(8,128)(2,1)S(1)} %get-tuple-element.23.zinv, ...), custom_call_target="tpu_custom_call" | custom-call | tf_op jit(solution)/shard_map/pallas_call | solution.py:478
  74.2 16.4 %all_to_all.20 = f32[64,1,128]{2,1,0:T(1,128)S(1)} all-to-all(f32[64,1,128]{2,1,0:T(1,128)S(1)} %bitcast.19), channel_id=1, replica_groups=mesh['y'=4,'z'=8,'c'=2,'dir'=4] {'y','z','c'}, dimensions={0} | all-to-all | bytes 65536 | tf_op jit(solution)/shard_map/all_to_all | solution.py:549
  90.5 0.7 shard_map.104
  (13 shorter events, 1.0 us)
Async XLA Ops:
  2.2 23.3 %all-to-all-start = ((bf16[8,8,3,8,128]{4,3,2,1,0:T(8,128)(2,1)}), bf16[8,8,3,8,128]{4,3,2,1,0:T(8,128)(2,1)S(1)}, u32[]{:S(2)}, u32[]{:S(2)}) async-start(bf16[8,8,3,8,128]{4,3,2,1,0:T(8,128)(2,1)} %shard_map.97), calls=%async_computation | async-start | bytes 786432 | tf_op jit(solution)/shard_map/all_to_all | solution.py:533
  12.3 1.9 %collective-permute-start = (s32[1,256]{1,0:T(1,128)S(1)}, s32[1,256]{1,0:T(1,128)S(1)}, u32[]{:S(2)}, u32[]{:S(2)}) collective-permute-start(s32[1,256]{1,0:T(1,128)S(1)} %shard_map.96), channel_id=1, source_target_pairs={{0,4},{4,0},{1,5},{5,1},{2,6},{6,2},{3,7},{7,3},{8,12},{12,8},{9,1... | collective-permute-start | bytes 3080 | tf_op jit(solution)/shard_map/ppermute | solution.py:536
  14.2 5.1 %collective-permute-start.1 = (s32[1,512]{1,0:T(1,128)S(1)}, s32[1,512]{1,0:T(1,128)S(1)}, u32[]{:S(2)}, u32[]{:S(2)}) collective-permute-start(s32[1,512]{1,0:T(1,128)S(1)} %pad_add_fusion.refs_0_), channel_id=1, source_target_pairs={{0,64},{64,128},{128,192},{192,0},{1,65},{65,129},{129,193},{193,1... | collective-permute-start | bytes 6152 | tf_op jit(solution)/shard_map/ppermute | solution.py:524
  15.5 4.2 %collective-permute-start.2 = (s32[1,512]{1,0:T(1,128)S(1)}, s32[1,512]{1,0:T(1,128)S(1)}, u32[]{:S(2)}, u32[]{:S(2)}) collective-permute-start(s32[1,512]{1,0:T(1,128)S(1)} %pad_add_fusion.refs_0_), channel_id=1, source_target_pairs={{0,128},{64,192},{128,0},{192,64},{1,129},{65,193},{129,1},{193,65... | collective-permute-start | bytes 6152 | tf_op jit(solution)/shard_map/ppermute | solution.py:524
  18.1 2.7 %collective-permute-start.3 = (s32[1,512]{1,0:T(1,128)S(1)}, s32[1,512]{1,0:T(1,128)S(1)}, u32[]{:S(2)}, u32[]{:S(2)}) collective-permute-start(s32[1,512]{1,0:T(1,128)S(1)} %pad_add_fusion.refs_0_), channel_id=1, source_target_pairs={{0,192},{64,0},{128,64},{192,128},{1,193},{65,1},{129,65},{193,129... | collective-permute-start | bytes 6152 | tf_op jit(solution)/shard_map/ppermute | solution.py:524
  27.3 15.2 %all-to-all-start.1 = ((bf16[8,32,8,128]{3,2,1,0:T(8,128)(2,1)}), bf16[8,32,8,128]{3,2,1,0:T(8,128)(2,1)S(1)}, u32[]{:S(2)}, u32[]{:S(2)}) async-start(bf16[8,32,8,128]{3,2,1,0:T(8,128)(2,1)} %bitcast.20), calls=%async_computation.1 | async-start | bytes 1048576 | tf_op jit(solution)/shard_map/all_to_all | solution.py:539
  45.9 13.3 %all-to-all-start.2 = ((bf16[32,3,8,128]{3,2,1,0:T(8,128)(2,1)}), bf16[32,3,8,128]{3,2,1,0:T(8,128)(2,1)S(1)}, u32[]{:S(2)}, u32[]{:S(2)}) async-start(bf16[32,3,8,128]{3,2,1,0:T(8,128)(2,1)} %get-tuple-element.33), calls=%async_computation.2 | async-start | bytes 393216 | tf_op jit(solution)/shard_map/all_to_all | solution.py:544
  51.7 10.4 %collective-permute-start.4 = (bf16[64,8,128]{2,1,0:T(8,128)(2,1)}, bf16[64,8,128]{2,1,0:T(8,128)(2,1)S(1)}, u32[]{:S(2)}, u32[]{:S(2)}) collective-permute-start(bf16[64,8,128]{2,1,0:T(8,128)(2,1)} %get-tuple-element.27), channel_id=1, source_target_pairs={{0,192},{64,0},{128,64},{192,128},{1,193},{65,1},{129,65},{193,129... | collective-permute-start | bytes 393224 | tf_op jit(solution)/shard_map/ppermute | solution.py:524
  54.3 8.3 %collective-permute-start.5 = (bf16[64,8,128]{2,1,0:T(8,128)(2,1)}, bf16[64,8,128]{2,1,0:T(8,128)(2,1)S(1)}, u32[]{:S(2)}, u32[]{:S(2)}) collective-permute-start(bf16[64,8,128]{2,1,0:T(8,128)(2,1)} %get-tuple-element.28), channel_id=1, source_target_pairs={{0,128},{64,192},{128,0},{192,64},{1,129},{65,193},{129,1},{193,65... | collective-permute-start | bytes 393224 | tf_op jit(solution)/shard_map/ppermute | solution.py:524
  54.7 10.0 %collective-permute-start.6 = (bf16[64,8,128]{2,1,0:T(8,128)(2,1)}, bf16[64,8,128]{2,1,0:T(8,128)(2,1)S(1)}, u32[]{:S(2)}, u32[]{:S(2)}) collective-permute-start(bf16[64,8,128]{2,1,0:T(8,128)(2,1)} %get-tuple-element.29), channel_id=1, source_target_pairs={{0,64},{64,128},{128,192},{192,0},{1,65},{65,129},{129,193},{193,1... | collective-permute-start | bytes 393224 | tf_op jit(solution)/shard_map/ppermute | solution.py:524
  59.2 12.9 %collective-permute-start.11 = (bf16[96,8,128]{2,1,0:T(8,128)(2,1)S(1)}, bf16[96,8,128]{2,1,0:T(8,128)(2,1)S(1)}, u32[]{:S(2)}, u32[]{:S(2)}) collective-permute-start(bf16[96,8,128]{2,1,0:T(8,128)(2,1)S(1)} %bitcast.16), channel_id=1, source_target_pairs={{0,4},{4,0},{1,5},{5,1},{2,6},{6,2},{3,7},{7,3},{8,12},{12,8},{9,1... | collective-permute-start | bytes 589832 | tf_op jit(solution)/shard_map/ppermute | solution.py:546
  62.1 3.2 %collective-permute-start.7 = (bf16[64,8,128]{2,1,0:T(8,128)(2,1)}, bf16[64,8,128]{2,1,0:T(8,128)(2,1)S(1)}, u32[]{:S(2)}, u32[]{:S(2)}) collective-permute-start(bf16[64,8,128]{2,1,0:T(8,128)(2,1)} %get-tuple-element.26.refs_0_), channel_id=1, source_target_pairs={{0,4},{4,0},{1,5},{5,1},{2,6},{6,2},{3,7},{7,3},{8,12},{12,8},{9,1... | collective-permute-start | bytes 393224 | tf_op jit(solution)/shard_map/ppermute | solution.py:541
  62.1 3.2 %collective-permute-start.8 = (bf16[64,8,128]{2,1,0:T(8,128)(2,1)S(1)}, bf16[64,8,128]{2,1,0:T(8,128)(2,1)S(1)}, u32[]{:S(2)}, u32[]{:S(2)}) collective-permute-start(bf16[64,8,128]{2,1,0:T(8,128)(2,1)S(1)} %collective-permute-done.4.refs_1_), channel_id=1, source_target_pairs={{0,4},{4,0},{1,5},{5,1},{2,6},{6,2},{3,7},{7,3},{8,12},{12,8},{9,1... | collective-permute-start | bytes 393224 | tf_op jit(solution)/shard_map/ppermute | solution.py:541
  62.6 2.7 %collective-permute-start.9 = (bf16[64,8,128]{2,1,0:T(8,128)(2,1)S(1)}, bf16[64,8,128]{2,1,0:T(8,128)(2,1)S(1)}, u32[]{:S(2)}, u32[]{:S(2)}) collective-permute-start(bf16[64,8,128]{2,1,0:T(8,128)(2,1)S(1)} %collective-permute-done.5.refs_2_), channel_id=1, source_target_pairs={{0,4},{4,0},{1,5},{5,1},{2,6},{6,2},{3,7},{7,3},{8,12},{12,8},{9,1... | collective-permute-start | bytes 393224 | tf_op jit(solution)/shard_map/ppermute | solution.py:541
  64.7 1.6 %collective-permute-start.10 = (bf16[64,8,128]{2,1,0:T(8,128)(2,1)S(1)}, bf16[64,8,128]{2,1,0:T(8,128)(2,1)S(1)}, u32[]{:S(2)}, u32[]{:S(2)}) collective-permute-start(bf16[64,8,128]{2,1,0:T(8,128)(2,1)S(1)} %collective-permute-done.6.refs_3_), channel_id=1, source_target_pairs={{0,4},{4,0},{1,5},{5,1},{2,6},{6,2},{3,7},{7,3},{8,12},{12,8},{9,1... | collective-permute-start | bytes 393224 | tf_op jit(solution)/shard_map/ppermute | solution.py:541
  66.3 0.9 copy-start

commit v7 on v6

--- a/solution.py
+++ b/solution.py
@@ -39,6 +39,10 @@
 
 def near_core(value):
     return pltpu.with_memory_space_constraint(value, pltpu.VMEM)
+
+
+def scalar_core(value):
+    return pltpu.with_memory_space_constraint(value, pltpu.SMEM)
 
 
 def off_core(value):
@@ -121,10 +125,10 @@
     )(off_core(columns), off_core(lags))
 
 
-def chart_kernel(place, counts, columns, lags, spots, aged, table):
+def chart_kernel(counts, columns, lags, spots_out, aged_out, table_out, spots, aged, table, sems):
     slots = Slots(columns, lags)
     cap = BLOCK_CAP * Z
-    y, c = place[0, 0], place[0, 1]
+    y, c = lax.axis_index("y"), lax.axis_index("c")
     other = (slots.c != c).astype(jnp.int32)
     across = (lax.rem(slots.y - y + Y, Y) * C + other) * cap
     fresh = (other * (Y * Z) + slots.y * Z + slots.z) * slots.rows + slots.local
@@ -152,27 +156,48 @@
     table[0:1, :] = jnp.concatenate([*order_parts, rest], axis=1)
     table[1:2, :] = jnp.concatenate([*where_parts, rest], axis=1)
     table[2:3, :] = jnp.concatenate([*new_parts, rest], axis=1)
-
-
-def chart(place, counts, columns, lags):
+    for copy in start_all([(spots, spots_out), (aged, aged_out), (table, table_out)], sems):
+        copy.wait()
+
+
+def chart(counts, columns, lags):
+    lengths = (1, 1, 3)
     return kernel_call(
         chart_kernel,
         SMALL,
-        out_shape=tuple(pltpu.VMEM((length, 128), jnp.int32) for length in (1, 1, 3)),
-        in_specs=[smem(), smem(), vmem(), vmem()],
-        out_specs=[vmem()] * 3,
-    )(place, off_core(counts), off_core(columns), off_core(lags))
-
-
-def whose(place, shift, other):
-    y, c = place[0, 0], place[0, 1]
+        out_shape=tuple(pltpu.SMEM((length, 128), jnp.int32) for length in lengths),
+        in_specs=[smem(), vmem(), vmem()],
+        out_specs=[smem()] * 3,
+        scratch_shapes=[pltpu.VMEM((length, 128), jnp.int32) for length in lengths]
+        + [pltpu.SemaphoreType.DMA((3,))],
+    )(off_core(counts), off_core(columns), off_core(lags))
+
+
+def gather_lists_kernel(*refs):
+    for copy in start_all(list(zip(refs[:Y], refs[Y : 2 * Y])), refs[2 * Y]):
+        copy.wait()
+
+
+def gather_lists(lists):
+    return kernel_call(
+        gather_lists_kernel,
+        SMALL,
+        out_shape=tuple(pltpu.SMEM(value.shape, value.dtype) for value in lists),
+        in_specs=[vmem()] * Y,
+        out_specs=[smem()] * Y,
+        scratch_shapes=[pltpu.SemaphoreType.DMA((Y,))],
+    )(*[near_core(value) for value in lists])
+
+
+def whose(shift, other):
+    y, c = lax.axis_index("y"), lax.axis_index("c")
     return lax.rem(y - shift + Y, Y) * C + (c if other == 0 else 1 - c)
 
 
-def pick_kernel(place, *refs):
+def pick_kernel(*refs):
     lists, held, first, kept, sems = refs[:Y], refs[Y], refs[Y + 1], refs[Y + 2], refs[Y + 3]
     cap = first.shape[0] // GROUPS
-    mine = (place[0, 0] * C + place[0, 1]) * cap
+    mine = (lax.axis_index("y") * C + lax.axis_index("c")) * cap
     copies = []
     for shift in range(Y):
         for other in range(C):
@@ -184,18 +209,18 @@
                     spot = lists[shift][0, other * GROUPS * cap + mine + entry + k]
                     kept[base + entry + k] = held[spot]
 
-            to = whose(place, shift, other) * cap
+            to = whose(shift, other) * cap
             pair = (kept.at[pl.ds(base, cap)], first.at[pl.ds(to, cap)])
             copies += start_all([pair], sems, len(copies))
     for copy in copies:
         copy.wait()
 
 
-def pick_later_kernel(place, *refs):
+def pick_later_kernel(*refs):
     lists, held, later, kept, sems = refs[:Y], refs[Y], refs[Y + 1 : 2 * Y + 1], refs[2 * Y + 1], refs[2 * Y + 2]
     cap = later[0].shape[0] // C
     back = held.shape[0] // (Z * LEVELS)
-    mine = (place[0, 0] * C + place[0, 1]) * cap
+    mine = (lax.axis_index("y") * C + lax.axis_index("c")) * cap
     copies = []
     for shift in range(Y):
         for other in range(C):
@@ -211,13 +236,13 @@
         copy.wait()
 
 
-def picks(place, lists, held, cap):
+def picks(lists, held, cap):
     def out(entries):
         return pltpu.HBM((entries, *held.shape[1:]), held.dtype)
 
     held = near_core(held)
-    lists = [near_core(value) for value in lists]
-    specs = [smem()] * (1 + Y) + [vmem()]
+    lists = [scalar_core(value) for value in lists]
+    specs = [smem()] * Y + [vmem()]
     first = kernel_call(
         pick_kernel,
         SMALL,
@@ -228,7 +253,7 @@
             pltpu.VMEM((GROUPS * cap, *held.shape[1:]), held.dtype),
             pltpu.SemaphoreType.DMA((GROUPS,)),
         ],
-    )(place, *lists, held)
+    )(*lists, held)
     later = kernel_call(
         pick_later_kernel,
         SMALL,
@@ -239,7 +264,7 @@
             pltpu.VMEM((Y, C * cap, *held.shape[1:]), held.dtype),
             pltpu.SemaphoreType.DMA((Y,)),
         ],
-    )(place, *lists, held)
+    )(*lists, held)
     return first, later
 
 
@@ -319,7 +344,7 @@
     )(off_core(counts), off_core(ztiles), off_core(zinv), off_core(incident))
 
 
-def first_kernel(spots, got, top, ztiles_hbm, zinv, incident, out, spread_out, last, kept_out, sems, tile_sems):
+def first_kernel(spots, got, top, ztiles_hbm, zinv, incident, spread_out, last, kept_out, sems, tile_sems):
     kept, slots, tile = top.shape[0], top.shape[1], top.shape[2]
     count = spots[0, (kept + 1) * slots + kept]
     live_tiles(count, ztiles_hbm.at[kept], last, tile_sems, 0, "start")
@@ -329,7 +354,6 @@
             live_tiles(count, ztiles_hbm.at[kept], last, tile_sems, 0, "wait")
         total = row_sum(spots, lambda spot: got[spot], top.at[row] if row < kept else last, row)
         density = density_of(incident[:, row * tile : (row + 1) * tile], total, zinv[row])
-        out[row] = density
         for to in range(spread_out.shape[0]):
             kept_out[row, to] = density
         copies += start_all([(kept_out.at[row], spread_out.at[:, row])], sems, row)
@@ -342,24 +366,22 @@
     return kernel_call(
         first_kernel,
         SMALL,
-        out_shape=(
-            pltpu.HBM((rows, dirs, tile), jnp.bfloat16),
-            pltpu.HBM((Y * Z, rows, dirs, tile), jnp.bfloat16),
-        ),
+        out_shape=pltpu.HBM((Y * Z, rows, dirs, tile), jnp.bfloat16),
         in_specs=[smem(), vmem(), vmem(), hbm(), vmem(), vmem()],
-        out_specs=(vmem(), hbm()),
+        out_specs=hbm(),
         scratch_shapes=[
             pltpu.VMEM(ztiles.shape[1:], ztiles.dtype),
             pltpu.VMEM((rows, Y * Z, dirs, tile), jnp.bfloat16),
             pltpu.SemaphoreType.DMA((rows,)),
             pltpu.SemaphoreType.DMA((1, slots // CHUNK)),
         ],
-    )(near_core(spots), near_core(got), near_core(top), off_core(ztiles), near_core(zinv), near_core(incident))
-
-
-def aged_kernel(spots, table, before, incident, *refs):
+    )(scalar_core(spots), near_core(got), near_core(top), off_core(ztiles), near_core(zinv), near_core(incident))
+
+
+def aged_kernel(spots, table, *refs):
     near, cross = refs[:Y], refs[Y : 2 * Y]
-    ztiles_hbm, basis_hbm, packed, fresh, basis, pool, ztiles, sems, tile_sems, fresh_sems = refs[2 * Y :]
+    fanned, incident_hbm, ztiles_hbm, basis_hbm, packed, fresh, basis = refs[2 * Y : 2 * Y + 7]
+    pool, ztiles, before, incident, sems, tile_sems, fresh_sems = refs[2 * Y + 7 :]
     rows, slots, tile = ztiles.shape[0], ztiles.shape[1], ztiles.shape[2]
     cap = near[0].shape[0] // C
     panels = rows * tile
@@ -371,8 +393,9 @@
     copies = start_all(pairs, sems)
     for row in range(rows):
         live_tiles(counts[row], ztiles_hbm.at[row], ztiles.at[row], tile_sems, row, "start")
-    weights = start_all([(basis_hbm, basis)], sems, len(pairs))[0]
-    for copy in copies:
+    pairs += [(incident_hbm.at[1], incident), (fanned.at[0], before), (basis_hbm, basis)]
+    copies += start_all(pairs[2 * Y :], sems, 2 * Y)
+    for copy in copies[:-1]:
         copy.wait()
     lag_one = []
     for row in range(rows):
@@ -382,19 +405,19 @@
             lag_one.append(pltpu.make_async_copy(source, fresh.at[row, k], fresh_sems.at[row, k]))
             lag_one[-1].start()
         at = slice(row * tile, (row + 1) * tile)
-        packed[0, :, at] = incident[1, :, at].astype(jnp.float32)
+        packed[0, :, at] = incident[:, at].astype(jnp.float32)
         packed[1, :, at] = row_sum(spots, lambda spot: pool[spot], ztiles.at[row], row)
     value = jnp.concatenate([before[row] for row in range(rows)], axis=1)
     packed[2, :, :] = value.astype(jnp.float32)
-    weights.wait()
+    copies[-1].wait()
     packed[3, :, : basis.shape[1]] = jnp.dot(value, basis[...], preferred_element_type=jnp.float32)
     packed[3, :, basis.shape[1] :] = jnp.zeros((value.shape[0], panels - basis.shape[1]), jnp.float32)
     for copy in lag_one:
         copy.wait()
 
 
-def aged_step(spots, table, before, incident, near, cross, ztiles, basis):
-    rows, dirs, tile = before.shape
+def aged_step(spots, table, fanned, incident, near, cross, ztiles, basis):
+    rows, dirs, tile = fanned.shape[1:]
     cap = near[0].shape[0] // C
     return kernel_call(
         aged_kernel,
@@ -404,28 +427,30 @@
             pltpu.VMEM((rows, CHUNK, tile, tile), ztiles.dtype),
             pltpu.VMEM(basis.shape, basis.dtype),
         ),
-        in_specs=[smem(), smem(), vmem(), vmem()] + [anywhere()] * (2 * Y) + [hbm()] * 2,
+        in_specs=[smem(), smem()] + [anywhere()] * (2 * Y) + [hbm()] * 4,
         out_specs=[vmem()] * 3,
         scratch_shapes=[
             pltpu.VMEM((2 * Y * cap, dirs, tile), jnp.bfloat16),
             pltpu.VMEM(ztiles.shape, ztiles.dtype),
-            pltpu.SemaphoreType.DMA((2 * Y + 1,)),
+            pltpu.VMEM(fanned.shape[1:], fanned.dtype),
+            pltpu.VMEM(incident.shape[1:], incident.dtype),
+            pltpu.SemaphoreType.DMA((2 * Y + 3,)),
             pltpu.SemaphoreType.DMA((rows, ztiles.shape[1] // CHUNK)),
             pltpu.SemaphoreType.DMA((rows, CHUNK)),
         ],
     )(
-        near_core(spots),
-        near_core(table),
-        off_core(before),
-        off_core(incident),
+        scalar_core(spots),
+        scalar_core(table),
         *near,
         *cross,
+        off_core(fanned),
+        off_core(incident),
         off_core(ztiles),
         off_core(basis),
     )
 
 
-def second_kernel(table, packed, fresh, zinv, basis, here, there, ztiles_hbm, dens, far, ztiles, flipped, tile_sems):
+def second_kernel(table, packed, fresh, zinv, basis, here, there, ztiles_hbm, dens_out, far, ztiles, flipped, dens, sems, tile_sems):
     rows, slots, tile = ztiles_hbm.shape[0], ztiles_hbm.shape[1], ztiles_hbm.shape[2]
     near = here.shape[0]
 
@@ -462,6 +487,7 @@
     value = jnp.concatenate(later, axis=1)
     dens[0] = packed[2].astype(dens.dtype)
     dens[1] = value
+    copy = start_all([(dens, dens_out)], sems)[0]
     far_second = jnp.dot(value, basis[...], preferred_element_type=jnp.float32)
     both = jnp.concatenate([packed[3, :, : basis.shape[1]], far_second], axis=0)
     lanes = both.shape[0]
@@ -470,6 +496,7 @@
     each = basis.shape[1] // owners
     cols = [flipped[pl.ds(c, owners, stride=each), :][:, :lanes] for c in range(each)]
     far[...] = jnp.concatenate([*cols, jnp.zeros((owners, far.shape[1] - each * lanes), jnp.float32)], axis=1)
+    copy.wait()
 
 
 def second_step(table, packed, fresh, zinv, basis, here, there, ztiles, owners):
@@ -479,18 +506,20 @@
         second_kernel,
         SMALL,
         out_shape=(
-            jax.ShapeDtypeStruct((STEPS, dirs, panels), jnp.bfloat16),
+            pltpu.HBM((STEPS, dirs, panels), jnp.bfloat16),
             pltpu.VMEM((owners, 128), jnp.float32),
         ),
         in_specs=[smem()] + [vmem()] * 6 + [hbm()],
-        out_specs=(vmem(), vmem()),
+        out_specs=(hbm(), vmem()),
         scratch_shapes=[
             pltpu.VMEM((CHUNK, tile, tile), ztiles.dtype),
             pltpu.VMEM((harmonics, 128), jnp.float32),
+            pltpu.VMEM((STEPS, dirs, panels), jnp.bfloat16),
+            pltpu.SemaphoreType.DMA((1,)),
             pltpu.SemaphoreType.DMA((CHUNK,)),
         ],
     )(
-        near_core(table),
+        scalar_core(table),
         near_core(packed),
         near_core(fresh),
         near_core(zinv),
@@ -529,20 +558,20 @@
     dirs = history.shape[1]
     owners = Y * Z * C
     cap = BLOCK_CAP * Z
-    place = jnp.stack([lax.axis_index("y"), lax.axis_index("c")]).reshape(1, 2)
     held = lax.all_to_all(open_up(history, tile), "z", 0, 0, tiled=True).reshape(-1, dirs, tile)
     wanted = plan(columns, lags)
-    spots, aged, table = chart(place, counts, columns, lags)
+    spots, aged, table = chart(counts, columns, lags)
     both = jnp.concatenate([wanted, lax.ppermute(wanted, "c", SWAP)], axis=1)
     lists = [both] + [shifted(both, "y", Y, s) for s in range(1, Y)]
-    first, later = picks(place, lists, held, cap)
+    lists = gather_lists(lists)
+    first, later = picks(lists, held, cap)
     got = lax.all_to_all(first.reshape(GROUPS, cap, dirs, tile), ("y", "c"), 0, 0, tiled=True)
     near = [later[0]] + [shifted(later[s], "y", Y, -s) for s in range(1, Y)]
     cross = [lax.ppermute(piece, "c", SWAP) for piece in near]
     top, inverse, driven = stage(counts, ztiles, zinv, incident)
-    density, fanned = first_step(spots, got.reshape(GROUPS * cap, dirs, tile), top, ztiles, inverse, driven)
+    fanned = first_step(spots, got.reshape(GROUPS * cap, dirs, tile), top, ztiles, inverse, driven)
     here = lax.all_to_all(fanned, ("y", "z"), 0, 0, tiled=True).reshape(Y * Z * rows, dirs, tile)
-    packed, lag_one, weights = aged_step(aged, table, density, incident, near, cross, ztiles, basis)
+    packed, lag_one, weights = aged_step(aged, table, fanned, incident, near, cross, ztiles, basis)
     there = lax.ppermute(here, "c", SWAP)
     dens, far = second_step(table, packed, lag_one, inverse, weights, here, there, ztiles, owners)
     each = basis.shape[1] // owners

time: 91.8 us -> 88.4 us (0.963)
  Pallas kernels: 21 us -> 18.9 us
  waiting for transfers between devices: 18.5 us -> 16.5 us
    pallas_call x3 -> x4, Pallas kernels: 6.82 us -> 6.4 us  [the longest x1 2.25 us: first_step(): kernel_call(first_kernel, SMALL, out_shape=pltpu.HBM((Y * Z, rows, dirs,...]
  transfers between devices with their start and end apart: 15 -> 15, of which waited for: 8 -> 8; matrix products, arithmetic and copies ran while one was open for 0% -> 0% of each run, Pallas kernels for 13% -> 14%
where the time goes in v7:
time: 88.4 us; the launch traced here: 87.8 us
  starting transfers between devices  33.6 us (38%)
  Pallas kernels  18.9 us (21%)
  blocking collectives  17.2 us (19%)
  waiting for transfers between devices  16.5 us (19%)
  local copies, waits for them, and re-layouts  0.9 us (1%)
    all_to_all x1, blocking collectives, march(): lax.all_to_all(far.reshape(owners, 1, 128), E, 0, 0, tiled=True)  17.2 us
    ppermute x6, starting transfers between devices, shifted(): lax.ppermute(value, axis, [(i, (i + shift) % length) for i in range(lengt...  9.25 us
    all_to_all x1, starting transfers between devices, march(): lax.all_to_all(open_up(history, tile), 'z', 0, 0, tiled=True)  9.02 us
    all_to_all x1, starting transfers between devices, march(): lax.all_to_all(first.reshape(GROUPS, cap, dirs, tile), ('y', 'c'), 0, 0,...  5.84 us
    all_to_all x1, waiting for transfers between devices, march(): lax.all_to_all(first.reshape(GROUPS, cap, dirs, tile), ('y', 'c'), 0, 0,...  5.16 us
    pallas_call x1, Pallas kernels, aged_step(): kernel_call(aged_kernel, SMALL, out_shape=(pltpu.VMEM((4, dirs, rows * ti...  4.65 us
    all_to_all x1, waiting for transfers between devices, march(): lax.all_to_all(open_up(history, tile), 'z', 0, 0, tiled=True)  3.96 us
    all_to_all x1, waiting for transfers between devices, march(): lax.all_to_all(fanned, ('y', 'z'), 0, 0, tiled=True)  3.88 us
  transfers between devices with their start and end apart: 15, of which 8 were waited for; matrix products, arithmetic and copies ran while one was open for 0% of the time, Pallas kernels for 14%

profile of v7, /device:TPU:1, one launch (start us, length us, event | category | flops | bytes accessed | tf_op | source)
XLA Modules:
  0.0 87.8 jit_solution(12807703686345167440)
XLA Ops:
  0.6 1.6 %shard_map.98 = bf16[8,8,3,8,128]{4,3,2,1,0:T(8,128)(2,1)} custom-call(bf16[8,8,384]{2,1,0:T(8,128)(2,1)} %history.1), custom_call_target="tpu_custom_call" | custom-call | tf_op jit(solution)/shard_map/pallas_call | solution.py:70
  2.2 9.0 %all-to-all-start = ((bf16[8,8,3,8,128]{4,3,2,1,0:T(8,128)(2,1)}), bf16[8,8,3,8,128]{4,3,2,1,0:T(8,128)(2,1)S(1)}, u32[]{:S(2)}, u32[]{:S(2)}) async-start(bf16[8,8,3,8,128]{4,3,2,1,0:T(8,128)(2,1)} %shard_map.98), calls=%async_computation | async-start | bytes 786432 | tf_op jit(solution)/shard_map/all_to_all | solution.py:561
  11.3 1.1 %shard_map.96 = s32[1,256]{1,0:T(1,128)S(1)} custom-call(s32[3,32]{1,0:T(4,128)} %columns.3, s32[3,32]{1,0:T(4,128)} %lags.3), custom_call_target="tpu_custom_call" | custom-call | tf_op jit(solution)/shard_map/pallas_call | solution.py:119
  12.3 1.0 %collective-permute-start = (s32[1,256]{1,0:T(1,128)S(1)}, s32[1,256]{1,0:T(1,128)S(1)}, u32[]{:S(2)}, u32[]{:S(2)}) collective-permute-start(s32[1,256]{1,0:T(1,128)S(1)} %shard_map.96), channel_id=1, source_target_pairs={{0,4},{4,0},{1,5},{5,1},{2,6},{6,2},{3,7},{7,3},{8,12},{12,8},{9,1... | collective-permute-start | bytes 3080 | tf_op jit(solution)/shard_map/ppermute | solution.py:564
  13.4 0.8 collective-permute-done
  14.2 1.3 %collective-permute-start.1 = (s32[1,512]{1,0:T(1,128)S(1)}, s32[1,512]{1,0:T(1,128)S(1)}, u32[]{:S(2)}, u32[]{:S(2)}) collective-permute-start(s32[1,512]{1,0:T(1,128)S(1)} %pad_add_fusion.refs_0_), channel_id=1, source_target_pairs={{0,64},{64,128},{128,192},{192,0},{1,65},{65,129},{129,193},{193,1... | collective-permute-start | bytes 6152 | tf_op jit(solution)/shard_map/ppermute | solution.py:553
  15.5 2.6 %collective-permute-start.2 = (s32[1,512]{1,0:T(1,128)S(1)}, s32[1,512]{1,0:T(1,128)S(1)}, u32[]{:S(2)}, u32[]{:S(2)}) collective-permute-start(s32[1,512]{1,0:T(1,128)S(1)} %pad_add_fusion.refs_0_), channel_id=1, source_target_pairs={{0,128},{64,192},{128,0},{192,64},{1,129},{65,193},{129,1},{193,65... | collective-permute-start | bytes 6152 | tf_op jit(solution)/shard_map/ppermute | solution.py:553
  18.1 1.1 %collective-permute-start.3 = (s32[1,512]{1,0:T(1,128)S(1)}, s32[1,512]{1,0:T(1,128)S(1)}, u32[]{:S(2)}, u32[]{:S(2)}) collective-permute-start(s32[1,512]{1,0:T(1,128)S(1)} %pad_add_fusion.refs_0_), channel_id=1, source_target_pairs={{0,192},{64,0},{128,64},{192,128},{1,193},{65,1},{129,65},{193,129... | collective-permute-start | bytes 6152 | tf_op jit(solution)/shard_map/ppermute | solution.py:553
  19.2 0.5 collective-permute-done.2.refs_2_
  19.7 1.1 %collective-permute-done.3.refs_3_ = s32[1,512]{1,0:T(1,128)S(1)} collective-permute-done((s32[1,512]{1,0:T(1,128)S(1)}, s32[1,512]{1,0:T(1,128)S(1)}, u32[]{:S(2)}, u32[]{:S(2)}) %collective-permute-start.3) | collective-permute-done | bytes 2080 | tf_op jit(solution)/shard_map/ppermute | solution.py:553
  20.9 0.7 shard_map.97
  21.6 4.0 %all-to-all-done = bf16[8,8,3,8,128]{4,3,2,1,0:T(8,128)(2,1)S(1)} async-done(((bf16[8,8,3,8,128]{4,3,2,1,0:T(8,128)(2,1)}), bf16[8,8,3,8,128]{4,3,2,1,0:T(8,128)(2,1)S(1)}, u32[]{:S(2)}, u32[]{:S(2)}) %all-to-all-start) | async-done | bytes 393248 | tf_op jit(solution)/shard_map/all_to_all | solution.py:561
  25.5 1.1 %shard_map.100 = bf16[256,8,128]{2,1,0:T(8,128)(2,1)} custom-call(s32[1,512]{1,0:T(1,128)S(4)} %get-tuple-element.23.refs_0_, s32[1,512]{1,0:T(1,128)S(4)} %get-tuple-element.24.refs_1_, s32[1,512]{1,0:T(1,128)S(4)} %get-tuple-element.25.refs_2_, s32[1,512]{1,0:T(1,128)S(4)} %get-tuple-element.26.refs_3_, bf16[192,8,128]{2,1,0:T(8,128)(2,1)S(1)} %bitcast.9), custom_call_target="tpu_custom_call" | custom-call | tf_op jit(solution)/shard_map/pallas_call | solution.py:246
  26.6 5.8 %all-to-all-start.1 = ((bf16[8,32,8,128]{3,2,1,0:T(8,128)(2,1)}), bf16[8,32,8,128]{3,2,1,0:T(8,128)(2,1)S(1)}, u32[]{:S(2)}, u32[]{:S(2)}) async-start(bf16[8,32,8,128]{3,2,1,0:T(8,128)(2,1)} %bitcast.16), calls=%async_computation.1 | async-start | bytes 1048576 | tf_op jit(solution)/shard_map/all_to_all | solution.py:568
  32.5 2.0 %shard_map.95 = (s32[1,128]{1,0:T(1,128)S(4)}, s32[1,128]{1,0:T(1,128)S(4)}, s32[3,128]{1,0:T(4,128)S(4)}) custom-call(s32[3]{0:T(128)} %counts.3, s32[3,32]{1,0:T(4,128)} %columns.3, s32[3,32]{1,0:T(4,128)} %lags.3), custom_call_target="tpu_custom_call" | custom-call | tf_op jit(solution)/shard_map/pallas_call | solution.py:165
  34.5 2.2 %shard_map.101 = (bf16[2,32,128,128]{3,2,1,0:T(8,128)(2,1)S(1)}, bf16[3,128,128]{2,1,0:T(8,128)(2,1)S(1)}, bf16[8,384]{1,0:T(8,128)(2,1)S(1)}) custom-call(s32[3]{0:T(128)} %counts.3, bf16[3,32,128,128]{3,2,1,0:T(8,128)(2,1)} %ztiles_hbm.5, bf16[3,128,128]{2,1,0:T(8,128)(2,1)} %zinv_hbm.1, bf16[2,8,384]{2,1,0:T(8,128)(2,1)} %refs_9_.1), custom_call_target="tpu_custom_call" | custom-call | tf_op jit(solution)/shard_map/pallas_call | solution.py:330
  36.7 5.2 %all-to-all-done.1 = bf16[8,32,8,128]{3,2,1,0:T(8,128)(2,1)S(1)} async-done(((bf16[8,32,8,128]{3,2,1,0:T(8,128)(2,1)}), bf16[8,32,8,128]{3,2,1,0:T(8,128)(2,1)S(1)}, u32[]{:S(2)}, u32[]{:S(2)}) %all-to-all-start.1) | async-done | bytes 524320 | tf_op jit(solution)/shard_map/all_to_all | solution.py:568
  41.8 2.2 %shard_map.102.refs_8_ = bf16[32,3,8,128]{3,2,1,0:T(8,128)(2,1)} custom-call(s32[1,128]{1,0:T(1,128)S(4)} %get-tuple-element.31.spots, bf16[256,8,128]{2,1,0:T(8,128)(2,1)S(1)} %bitcast.11, bf16[2,32,128,128]{3,2,1,0:T(8,128)(2,1)S(1)} %get-tuple-element.32.top, bf16[3,32,128,128]{3,2,1,0:T(8,128)(2,1)} %ztiles_hbm.5, ...), custom_call_target="tpu_custom_call" | custom-call | tf_op jit(solution)/shard_map/pallas_call | solution.py:366
  44.1 3.9 %all-to-all-start.2 = ((bf16[32,3,8,128]{3,2,1,0:T(8,128)(2,1)}), bf16[32,3,8,128]{3,2,1,0:T(8,128)(2,1)S(1)}, u32[]{:S(2)}, u32[]{:S(2)}) async-start(bf16[32,3,8,128]{3,2,1,0:T(8,128)(2,1)} %shard_map.102.refs_8_), calls=%async_computation.2 | async-start | bytes 393216 | tf_op jit(solution)/shard_map/all_to_all | solution.py:573
  48.0 1.3 %shard_map.99 = (bf16[64,8,128]{2,1,0:T(8,128)(2,1)}, bf16[64,8,128]{2,1,0:T(8,128)(2,1)}, bf16[64,8,128]{2,1,0:T(8,128)(2,1)}, bf16[64,8,128]{2,1,0:T(8,128)(2,1)}) custom-call(s32[1,512]{1,0:T(1,128)S(4)} %get-tuple-element.23.refs_0_, s32[1,512]{1,0:T(1,128)S(4)} %get-tuple-element.24.refs_1_, s32[1,512]{1,0:T(1,128)S(4)} %get-tuple-element.25.refs_2_, ...), custom_call_target="tpu_custom_call" | custom-call | tf_op jit(solution)/shard_map/pallas_call | solution.py:257
  49.2 1.2 %collective-permute-start.6 = (bf16[64,8,128]{2,1,0:T(8,128)(2,1)}, bf16[64,8,128]{2,1,0:T(8,128)(2,1)S(1)}, u32[]{:S(2)}, u32[]{:S(2)}) collective-permute-start(bf16[64,8,128]{2,1,0:T(8,128)(2,1)} %get-tuple-element.30), channel_id=1, source_target_pairs={{0,64},{64,128},{128,192},{192,0},{1,65},{65,129},{129,193},{193,1... | collective-permute-start | bytes 393224 | tf_op jit(solution)/shard_map/ppermute | solution.py:553
  50.5 1.5 %collective-permute-start.4 = (bf16[64,8,128]{2,1,0:T(8,128)(2,1)}, bf16[64,8,128]{2,1,0:T(8,128)(2,1)S(1)}, u32[]{:S(2)}, u32[]{:S(2)}) collective-permute-start(bf16[64,8,128]{2,1,0:T(8,128)(2,1)} %get-tuple-element.28), channel_id=1, source_target_pairs={{0,192},{64,0},{128,64},{192,128},{1,193},{65,1},{129,65},{193,129... | collective-permute-start | bytes 393224 | tf_op jit(solution)/shard_map/ppermute | solution.py:553
  52.0 1.5 %collective-permute-start.5 = (bf16[64,8,128]{2,1,0:T(8,128)(2,1)}, bf16[64,8,128]{2,1,0:T(8,128)(2,1)S(1)}, u32[]{:S(2)}, u32[]{:S(2)}) collective-permute-start(bf16[64,8,128]{2,1,0:T(8,128)(2,1)} %get-tuple-element.29), channel_id=1, source_target_pairs={{0,128},{64,192},{128,0},{192,64},{1,129},{65,193},{129,1},{193,65... | collective-permute-start | bytes 393224 | tf_op jit(solution)/shard_map/ppermute | solution.py:553
  53.5 3.9 %all-to-all-done.2 = bf16[32,3,8,128]{3,2,1,0:T(8,128)(2,1)S(1)} async-done(((bf16[32,3,8,128]{3,2,1,0:T(8,128)(2,1)}), bf16[32,3,8,128]{3,2,1,0:T(8,128)(2,1)S(1)}, u32[]{:S(2)}, u32[]{:S(2)}) %all-to-all-start.2) | async-done | bytes 196640 | tf_op jit(solution)/shard_map/all_to_all | solution.py:573
  57.4 2.9 %collective-permute-start.11 = (bf16[96,8,128]{2,1,0:T(8,128)(2,1)S(1)}, bf16[96,8,128]{2,1,0:T(8,128)(2,1)S(1)}, u32[]{:S(2)}, u32[]{:S(2)}) collective-permute-start(bf16[96,8,128]{2,1,0:T(8,128)(2,1)S(1)} %bitcast.12), channel_id=1, source_target_pairs={{0,4},{4,0},{1,5},{5,1},{2,6},{6,2},{3,7},{7,3},{8,12},{12,8},{9,1... | collective-permute-start | bytes 589832 | tf_op jit(solution)/shard_map/ppermute | solution.py:575
  60.9 1.1 %collective-permute-start.9 = (bf16[64,8,128]{2,1,0:T(8,128)(2,1)S(1)}, bf16[64,8,128]{2,1,0:T(8,128)(2,1)S(1)}, u32[]{:S(2)}, u32[]{:S(2)}) collective-permute-start(bf16[64,8,128]{2,1,0:T(8,128)(2,1)S(1)} %collective-permute-done.5.refs_2_), channel_id=1, source_target_pairs={{0,4},{4,0},{1,5},{5,1},{2,6},{6,2},{3,7},{7,3},{8,12},{12,8},{9,1... | collective-permute-start | bytes 393224 | tf_op jit(solution)/shard_map/ppermute | solution.py:570
  62.2 0.8 collective-permute-done.9.refs_6_
  62.9 0.9 %copy-done = bf16[64,8,128]{2,1,0:T(8,128)(2,1)S(1)} copy-done((bf16[64,8,128]{2,1,0:T(8,128)(2,1)S(1)}, bf16[64,8,128]{2,1,0:T(8,128)(2,1)}, u32[]{:S(2)}) %copy-start) | copy-done | bytes 131096
  63.8 4.7 %shard_map.103 = (f32[4,8,384]{2,1,0:T(8,128)S(1)}, bf16[3,8,128,128]{3,2,1,0:T(8,128)(2,1)S(1)}, bf16[384,256]{1,0:T(8,128)(2,1)S(1)}) custom-call(s32[1,128]{1,0:T(1,128)S(4)} %get-tuple-element.22.spots, s32[3,128]{1,0:T(4,128)S(4)} %get-tuple-element.21.table, bf16[64,8,128]{2,1,0:T(8,128)(2,1)S(1)} %copy-done, ...), custom_call_target="tpu_custom_call" | custom-call | tf_op jit(solution)/shard_map/pallas_call | solution.py:422
  68.5 1.4 %shard_map.104 = (bf16[2,8,384]{2,1,0:T(8,128)(2,1)}, f32[64,128]{1,0:T(8,128)S(1)}) custom-call(s32[3,128]{1,0:T(4,128)S(4)} %get-tuple-element.21.table, f32[4,8,384]{2,1,0:T(8,128)S(1)} %get-tuple-element.35.packed, bf16[3,8,128,128]{3,2,1,0:T(8,128)(2,1)S(1)} %get-tuple-element.36.fresh, bf16[3,128,128]{2,1,0:T(8,128)(2,1)S(1)} %get-tuple-element.33.zinv, ...), custom_call_target="tpu_custom_call" | custom-call | tf_op jit(solution)/shard_map/pallas_call | solution.py:505
  70.0 17.2 %all_to_all.20 = f32[64,1,128]{2,1,0:T(1,128)S(1)} all-to-all(f32[64,1,128]{2,1,0:T(1,128)S(1)} %bitcast.15), channel_id=1, replica_groups=mesh['y'=4,'z'=8,'c'=2,'dir'=4] {'y','z','c'}, dimensions={0} | all-to-all | bytes 65536 | tf_op jit(solution)/shard_map/all_to_all | solution.py:578
  87.2 0.7 shard_map.105
  (13 shorter events, 0.9 us)
Async XLA Ops:
  2.2 23.3 %all-to-all-start = ((bf16[8,8,3,8,128]{4,3,2,1,0:T(8,128)(2,1)}), bf16[8,8,3,8,128]{4,3,2,1,0:T(8,128)(2,1)S(1)}, u32[]{:S(2)}, u32[]{:S(2)}) async-start(bf16[8,8,3,8,128]{4,3,2,1,0:T(8,128)(2,1)} %shard_map.98), calls=%async_computation | async-start | bytes 786432 | tf_op jit(solution)/shard_map/all_to_all | solution.py:561
  12.3 1.9 %collective-permute-start = (s32[1,256]{1,0:T(1,128)S(1)}, s32[1,256]{1,0:T(1,128)S(1)}, u32[]{:S(2)}, u32[]{:S(2)}) collective-permute-start(s32[1,256]{1,0:T(1,128)S(1)} %shard_map.96), channel_id=1, source_target_pairs={{0,4},{4,0},{1,5},{5,1},{2,6},{6,2},{3,7},{7,3},{8,12},{12,8},{9,1... | collective-permute-start | bytes 3080 | tf_op jit(solution)/shard_map/ppermute | solution.py:564
  14.2 5.0 %collective-permute-start.1 = (s32[1,512]{1,0:T(1,128)S(1)}, s32[1,512]{1,0:T(1,128)S(1)}, u32[]{:S(2)}, u32[]{:S(2)}) collective-permute-start(s32[1,512]{1,0:T(1,128)S(1)} %pad_add_fusion.refs_0_), channel_id=1, source_target_pairs={{0,64},{64,128},{128,192},{192,0},{1,65},{65,129},{129,193},{193,1... | collective-permute-start | bytes 6152 | tf_op jit(solution)/shard_map/ppermute | solution.py:553
  15.5 4.2 %collective-permute-start.2 = (s32[1,512]{1,0:T(1,128)S(1)}, s32[1,512]{1,0:T(1,128)S(1)}, u32[]{:S(2)}, u32[]{:S(2)}) collective-permute-start(s32[1,512]{1,0:T(1,128)S(1)} %pad_add_fusion.refs_0_), channel_id=1, source_target_pairs={{0,128},{64,192},{128,0},{192,64},{1,129},{65,193},{129,1},{193,65... | collective-permute-start | bytes 6152 | tf_op jit(solution)/shard_map/ppermute | solution.py:553
  18.1 2.7 %collective-permute-start.3 = (s32[1,512]{1,0:T(1,128)S(1)}, s32[1,512]{1,0:T(1,128)S(1)}, u32[]{:S(2)}, u32[]{:S(2)}) collective-permute-start(s32[1,512]{1,0:T(1,128)S(1)} %pad_add_fusion.refs_0_), channel_id=1, source_target_pairs={{0,192},{64,0},{128,64},{192,128},{1,193},{65,1},{129,65},{193,129... | collective-permute-start | bytes 6152 | tf_op jit(solution)/shard_map/ppermute | solution.py:553
  26.6 15.2 %all-to-all-start.1 = ((bf16[8,32,8,128]{3,2,1,0:T(8,128)(2,1)}), bf16[8,32,8,128]{3,2,1,0:T(8,128)(2,1)S(1)}, u32[]{:S(2)}, u32[]{:S(2)}) async-start(bf16[8,32,8,128]{3,2,1,0:T(8,128)(2,1)} %bitcast.16), calls=%async_computation.1 | async-start | bytes 1048576 | tf_op jit(solution)/shard_map/all_to_all | solution.py:568
  44.1 13.3 %all-to-all-start.2 = ((bf16[32,3,8,128]{3,2,1,0:T(8,128)(2,1)}), bf16[32,3,8,128]{3,2,1,0:T(8,128)(2,1)S(1)}, u32[]{:S(2)}, u32[]{:S(2)}) async-start(bf16[32,3,8,128]{3,2,1,0:T(8,128)(2,1)} %shard_map.102.refs_8_), calls=%async_computation.2 | async-start | bytes 393216 | tf_op jit(solution)/shard_map/all_to_all | solution.py:573
  49.2 11.0 %collective-permute-start.6 = (bf16[64,8,128]{2,1,0:T(8,128)(2,1)}, bf16[64,8,128]{2,1,0:T(8,128)(2,1)S(1)}, u32[]{:S(2)}, u32[]{:S(2)}) collective-permute-start(bf16[64,8,128]{2,1,0:T(8,128)(2,1)} %get-tuple-element.30), channel_id=1, source_target_pairs={{0,64},{64,128},{128,192},{192,0},{1,65},{65,129},{129,193},{193,1... | collective-permute-start | bytes 393224 | tf_op jit(solution)/shard_map/ppermute | solution.py:553
  50.5 10.3 %collective-permute-start.4 = (bf16[64,8,128]{2,1,0:T(8,128)(2,1)}, bf16[64,8,128]{2,1,0:T(8,128)(2,1)S(1)}, u32[]{:S(2)}, u32[]{:S(2)}) collective-permute-start(bf16[64,8,128]{2,1,0:T(8,128)(2,1)} %get-tuple-element.28), channel_id=1, source_target_pairs={{0,192},{64,0},{128,64},{192,128},{1,193},{65,1},{129,65},{193,129... | collective-permute-start | bytes 393224 | tf_op jit(solution)/shard_map/ppermute | solution.py:553
  52.0 8.9 %collective-permute-start.5 = (bf16[64,8,128]{2,1,0:T(8,128)(2,1)}, bf16[64,8,128]{2,1,0:T(8,128)(2,1)S(1)}, u32[]{:S(2)}, u32[]{:S(2)}) collective-permute-start(bf16[64,8,128]{2,1,0:T(8,128)(2,1)} %get-tuple-element.29), channel_id=1, source_target_pairs={{0,128},{64,192},{128,0},{192,64},{1,129},{65,193},{129,1},{193,65... | collective-permute-start | bytes 393224 | tf_op jit(solution)/shard_map/ppermute | solution.py:553
  57.4 11.1 %collective-permute-start.11 = (bf16[96,8,128]{2,1,0:T(8,128)(2,1)S(1)}, bf16[96,8,128]{2,1,0:T(8,128)(2,1)S(1)}, u32[]{:S(2)}, u32[]{:S(2)}) collective-permute-start(bf16[96,8,128]{2,1,0:T(8,128)(2,1)S(1)} %bitcast.12), channel_id=1, source_target_pairs={{0,4},{4,0},{1,5},{5,1},{2,6},{6,2},{3,7},{7,3},{8,12},{12,8},{9,1... | collective-permute-start | bytes 589832 | tf_op jit(solution)/shard_map/ppermute | solution.py:575
  60.2 1.7 %collective-permute-start.7 = (bf16[64,8,128]{2,1,0:T(8,128)(2,1)}, bf16[64,8,128]{2,1,0:T(8,128)(2,1)S(1)}, u32[]{:S(2)}, u32[]{:S(2)}) collective-permute-start(bf16[64,8,128]{2,1,0:T(8,128)(2,1)} %get-tuple-element.27.refs_0_), channel_id=1, source_target_pairs={{0,4},{4,0},{1,5},{5,1},{2,6},{6,2},{3,7},{7,3},{8,12},{12,8},{9,1... | collective-permute-start | bytes 393224 | tf_op jit(solution)/shard_map/ppermute | solution.py:570
  60.2 1.7 %collective-permute-start.10 = (bf16[64,8,128]{2,1,0:T(8,128)(2,1)S(1)}, bf16[64,8,128]{2,1,0:T(8,128)(2,1)S(1)}, u32[]{:S(2)}, u32[]{:S(2)}) collective-permute-start(bf16[64,8,128]{2,1,0:T(8,128)(2,1)S(1)} %collective-permute-done.6.refs_3_), channel_id=1, source_target_pairs={{0,4},{4,0},{1,5},{5,1},{2,6},{6,2},{3,7},{7,3},{8,12},{12,8},{9,1... | collective-permute-start | bytes 393224 | tf_op jit(solution)/shard_map/ppermute | solution.py:570
  60.8 1.4 %collective-permute-start.8 = (bf16[64,8,128]{2,1,0:T(8,128)(2,1)S(1)}, bf16[64,8,128]{2,1,0:T(8,128)(2,1)S(1)}, u32[]{:S(2)}, u32[]{:S(2)}) collective-permute-start(bf16[64,8,128]{2,1,0:T(8,128)(2,1)S(1)} %collective-permute-done.4.refs_1_), channel_id=1, source_target_pairs={{0,4},{4,0},{1,5},{5,1},{2,6},{6,2},{3,7},{7,3},{8,12},{12,8},{9,1... | collective-permute-start | bytes 393224 | tf_op jit(solution)/shard_map/ppermute | solution.py:570
  60.9 2.1 %collective-permute-start.9 = (bf16[64,8,128]{2,1,0:T(8,128)(2,1)S(1)}, bf16[64,8,128]{2,1,0:T(8,128)(2,1)S(1)}, u32[]{:S(2)}, u32[]{:S(2)}) collective-permute-start(bf16[64,8,128]{2,1,0:T(8,128)(2,1)S(1)} %collective-permute-done.5.refs_2_), channel_id=1, source_target_pairs={{0,4},{4,0},{1,5},{5,1},{2,6},{6,2},{3,7},{7,3},{8,12},{12,8},{9,1... | collective-permute-start | bytes 393224 | tf_op jit(solution)/shard_map/ppermute | solution.py:570
  62.9 0.9 %copy-start = (bf16[64,8,128]{2,1,0:T(8,128)(2,1)S(1)}, bf16[64,8,128]{2,1,0:T(8,128)(2,1)}, u32[]{:S(2)}) copy-start(bf16[64,8,128]{2,1,0:T(8,128)(2,1)} %get-tuple-element.27.refs_0_) | copy-start | bytes 393220

commit v8 on v7

--- a/solution.py
+++ b/solution.py
@@ -27,10 +27,6 @@
 
 def hbm():
     return pl.BlockSpec(memory_space=pltpu.HBM)
-
-
-def anywhere():
-    return pl.BlockSpec(memory_space=pl.ANY)
 
 
 def kernel_call(body, grant, **options):
@@ -381,39 +377,30 @@
 def aged_kernel(spots, table, *refs):
     near, cross = refs[:Y], refs[Y : 2 * Y]
     fanned, incident_hbm, ztiles_hbm, basis_hbm, packed, fresh, basis = refs[2 * Y : 2 * Y + 7]
-    pool, ztiles, before, incident, sems, tile_sems, fresh_sems = refs[2 * Y + 7 :]
+    pool, ztiles, before, incident, sems, tile_sems = refs[2 * Y + 7 :]
     rows, slots, tile = ztiles.shape[0], ztiles.shape[1], ztiles.shape[2]
     cap = near[0].shape[0] // C
     panels = rows * tile
     counts = [spots[0, rows * slots + row] for row in range(rows)]
-    pairs = []
-    for shift in range(Y):
-        for source, at in ((near[shift], 0), (cross[shift], cap)):
-            pairs.append((source.at[pl.ds(at, cap)], pool.at[pl.ds(len(pairs) * cap, cap)]))
-    copies = start_all(pairs, sems)
     for row in range(rows):
         live_tiles(counts[row], ztiles_hbm.at[row], ztiles.at[row], tile_sems, row, "start")
-    pairs += [(incident_hbm.at[1], incident), (fanned.at[0], before), (basis_hbm, basis)]
-    copies += start_all(pairs[2 * Y :], sems, 2 * Y)
-    for copy in copies[:-1]:
-        copy.wait()
-    lag_one = []
+    copies = start_all([(incident_hbm.at[1], incident), (fanned.at[0], before), (basis_hbm, basis)], sems)
+    for shift in range(Y):
+        for other, source in enumerate((near[shift], cross[shift])):
+            pool[pl.ds((shift * C + other) * cap, cap)] = source[pl.ds(other * cap, cap)]
     for row in range(rows):
         live_tiles(counts[row], ztiles_hbm.at[row], ztiles.at[row], tile_sems, row, "wait")
         for k in range(CHUNK):
-            source = ztiles.at[row, table[0, row * slots + k]]
-            lag_one.append(pltpu.make_async_copy(source, fresh.at[row, k], fresh_sems.at[row, k]))
-            lag_one[-1].start()
+            fresh[row, k] = ztiles[row, table[0, row * slots + k]]
         at = slice(row * tile, (row + 1) * tile)
-        packed[0, :, at] = incident[:, at].astype(jnp.float32)
         packed[1, :, at] = row_sum(spots, lambda spot: pool[spot], ztiles.at[row], row)
+    for copy in copies:
+        copy.wait()
+    packed[0, :, :] = incident[...].astype(jnp.float32)
     value = jnp.concatenate([before[row] for row in range(rows)], axis=1)
     packed[2, :, :] = value.astype(jnp.float32)
-    copies[-1].wait()
     packed[3, :, : basis.shape[1]] = jnp.dot(value, basis[...], preferred_element_type=jnp.float32)
     packed[3, :, basis.shape[1] :] = jnp.zeros((value.shape[0], panels - basis.shape[1]), jnp.float32)
-    for copy in lag_one:
-        copy.wait()
 
 
 def aged_step(spots, table, fanned, incident, near, cross, ztiles, basis):
@@ -427,22 +414,20 @@
             pltpu.VMEM((rows, CHUNK, tile, tile), ztiles.dtype),
             pltpu.VMEM(basis.shape, basis.dtype),
         ),
-        in_specs=[smem(), smem()] + [anywhere()] * (2 * Y) + [hbm()] * 4,
+        in_specs=[smem(), smem()] + [vmem()] * (2 * Y) + [hbm()] * 4,
         out_specs=[vmem()] * 3,
         scratch_shapes=[
             pltpu.VMEM((2 * Y * cap, dirs, tile), jnp.bfloat16),
             pltpu.VMEM(ztiles.shape, ztiles.dtype),
             pltpu.VMEM(fanned.shape[1:], fanned.dtype),
             pltpu.VMEM(incident.shape[1:], incident.dtype),
-            pltpu.SemaphoreType.DMA((2 * Y + 3,)),
+            pltpu.SemaphoreType.DMA((3,)),
             pltpu.SemaphoreType.DMA((rows, ztiles.shape[1] // CHUNK)),
-            pltpu.SemaphoreType.DMA((rows, CHUNK)),
         ],
     )(
         scalar_core(spots),
         scalar_core(table),
-        *near,
-        *cross,
+        *[near_core(piece) for piece in (*near, *cross)],
         off_core(fanned),
         off_core(incident),
         off_core(ztiles),

time: 88.4 us -> 86 us (0.973)
  Pallas kernels: 18.9 us -> 16.5 us
    pallas_call x1, Pallas kernels: 4.65 us -> 2.24 us  [aged_step(): kernel_call(aged_kernel, SMALL, out_shape=(pltpu.VMEM((4, dirs, rows * ti...]
  transfers between devices with their start and end apart: 15 -> 15, of which waited for: 8 -> 8; matrix products, arithmetic and copies ran while one was open for 0% -> 0% of each run, Pallas kernels for 14% -> 11%
where the time goes in v8:
time: 86 us; the launch traced here: 85.4 us
  starting transfers between devices  33.6 us (39%)
  blocking collectives  17.2 us (20%)
  Pallas kernels  16.5 us (19%)
  waiting for transfers between devices  16.5 us (19%)
  local copies, waits for them, and re-layouts  0.9 us (1%)
    all_to_all x1, blocking collectives, march(): lax.all_to_all(far.reshape(owners, 1, 128), E, 0, 0, tiled=True)  17.2 us
    ppermute x6, starting transfers between devices, shifted(): lax.ppermute(value, axis, [(i, (i + shift) % length) for i in range(lengt...  9.25 us
    all_to_all x1, starting transfers between devices, march(): lax.all_to_all(open_up(history, tile), 'z', 0, 0, tiled=True)  9.02 us
    all_to_all x1, starting transfers between devices, march(): lax.all_to_all(first.reshape(GROUPS, cap, dirs, tile), ('y', 'c'), 0, 0,...  5.84 us
    all_to_all x1, waiting for transfers between devices, march(): lax.all_to_all(first.reshape(GROUPS, cap, dirs, tile), ('y', 'c'), 0, 0,...  5.16 us
    all_to_all x1, waiting for transfers between devices, march(): lax.all_to_all(open_up(history, tile), 'z', 0, 0, tiled=True)  3.96 us
    all_to_all x1, waiting for transfers between devices, march(): lax.all_to_all(fanned, ('y', 'z'), 0, 0, tiled=True)  3.88 us
    all_to_all x1, starting transfers between devices, march(): lax.all_to_all(fanned, ('y', 'z'), 0, 0, tiled=True)  3.87 us
  transfers between devices with their start and end apart: 15, of which 8 were waited for; matrix products, arithmetic and copies ran while one was open for 0% of the time, Pallas kernels for 11%

profile of v8, /device:TPU:1, one launch (start us, length us, event | category | flops | bytes accessed | tf_op | source)
XLA Modules:
  0.0 85.4 jit_solution(5200440024419034328)
XLA Ops:
  0.6 1.6 %shard_map.98 = bf16[8,8,3,8,128]{4,3,2,1,0:T(8,128)(2,1)} custom-call(bf16[8,8,384]{2,1,0:T(8,128)(2,1)} %history.1), custom_call_target="tpu_custom_call" | custom-call | tf_op jit(solution)/shard_map/pallas_call | solution.py:66
  2.2 9.0 %all-to-all-start = ((bf16[8,8,3,8,128]{4,3,2,1,0:T(8,128)(2,1)}), bf16[8,8,3,8,128]{4,3,2,1,0:T(8,128)(2,1)S(1)}, u32[]{:S(2)}, u32[]{:S(2)}) async-start(bf16[8,8,3,8,128]{4,3,2,1,0:T(8,128)(2,1)} %shard_map.98), calls=%async_computation | async-start | bytes 786432 | tf_op jit(solution)/shard_map/all_to_all | solution.py:546
  11.3 1.1 %shard_map.96 = s32[1,256]{1,0:T(1,128)S(1)} custom-call(s32[3,32]{1,0:T(4,128)} %columns.3, s32[3,32]{1,0:T(4,128)} %lags.3), custom_call_target="tpu_custom_call" | custom-call | tf_op jit(solution)/shard_map/pallas_call | solution.py:115
  12.3 1.0 %collective-permute-start = (s32[1,256]{1,0:T(1,128)S(1)}, s32[1,256]{1,0:T(1,128)S(1)}, u32[]{:S(2)}, u32[]{:S(2)}) collective-permute-start(s32[1,256]{1,0:T(1,128)S(1)} %shard_map.96), channel_id=1, source_target_pairs={{0,4},{4,0},{1,5},{5,1},{2,6},{6,2},{3,7},{7,3},{8,12},{12,8},{9,1... | collective-permute-start | bytes 3080 | tf_op jit(solution)/shard_map/ppermute | solution.py:549
  13.4 0.8 collective-permute-done
  14.2 1.3 %collective-permute-start.1 = (s32[1,512]{1,0:T(1,128)S(1)}, s32[1,512]{1,0:T(1,128)S(1)}, u32[]{:S(2)}, u32[]{:S(2)}) collective-permute-start(s32[1,512]{1,0:T(1,128)S(1)} %pad_add_fusion.refs_0_), channel_id=1, source_target_pairs={{0,64},{64,128},{128,192},{192,0},{1,65},{65,129},{129,193},{193,1... | collective-permute-start | bytes 6152 | tf_op jit(solution)/shard_map/ppermute | solution.py:538
  15.5 2.6 %collective-permute-start.2 = (s32[1,512]{1,0:T(1,128)S(1)}, s32[1,512]{1,0:T(1,128)S(1)}, u32[]{:S(2)}, u32[]{:S(2)}) collective-permute-start(s32[1,512]{1,0:T(1,128)S(1)} %pad_add_fusion.refs_0_), channel_id=1, source_target_pairs={{0,128},{64,192},{128,0},{192,64},{1,129},{65,193},{129,1},{193,65... | collective-permute-start | bytes 6152 | tf_op jit(solution)/shard_map/ppermute | solution.py:538
  18.1 1.1 %collective-permute-start.3 = (s32[1,512]{1,0:T(1,128)S(1)}, s32[1,512]{1,0:T(1,128)S(1)}, u32[]{:S(2)}, u32[]{:S(2)}) collective-permute-start(s32[1,512]{1,0:T(1,128)S(1)} %pad_add_fusion.refs_0_), channel_id=1, source_target_pairs={{0,192},{64,0},{128,64},{192,128},{1,193},{65,1},{129,65},{193,129... | collective-permute-start | bytes 6152 | tf_op jit(solution)/shard_map/ppermute | solution.py:538
  19.2 0.5 collective-permute-done.2.refs_2_
  19.7 1.1 %collective-permute-done.3.refs_3_ = s32[1,512]{1,0:T(1,128)S(1)} collective-permute-done((s32[1,512]{1,0:T(1,128)S(1)}, s32[1,512]{1,0:T(1,128)S(1)}, u32[]{:S(2)}, u32[]{:S(2)}) %collective-permute-start.3) | collective-permute-done | bytes 2080 | tf_op jit(solution)/shard_map/ppermute | solution.py:538
  20.9 0.7 shard_map.97
  21.6 4.0 %all-to-all-done = bf16[8,8,3,8,128]{4,3,2,1,0:T(8,128)(2,1)S(1)} async-done(((bf16[8,8,3,8,128]{4,3,2,1,0:T(8,128)(2,1)}), bf16[8,8,3,8,128]{4,3,2,1,0:T(8,128)(2,1)S(1)}, u32[]{:S(2)}, u32[]{:S(2)}) %all-to-all-start) | async-done | bytes 393248 | tf_op jit(solution)/shard_map/all_to_all | solution.py:546
  25.5 1.1 %shard_map.100 = bf16[256,8,128]{2,1,0:T(8,128)(2,1)} custom-call(s32[1,512]{1,0:T(1,128)S(4)} %get-tuple-element.23.refs_0_, s32[1,512]{1,0:T(1,128)S(4)} %get-tuple-element.24.refs_1_, s32[1,512]{1,0:T(1,128)S(4)} %get-tuple-element.25.refs_2_, s32[1,512]{1,0:T(1,128)S(4)} %get-tuple-element.26.refs_3_, bf16[192,8,128]{2,1,0:T(8,128)(2,1)S(1)} %bitcast.9), custom_call_target="tpu_custom_call" | custom-call | tf_op jit(solution)/shard_map/pallas_call | solution.py:242
  26.6 5.8 %all-to-all-start.1 = ((bf16[8,32,8,128]{3,2,1,0:T(8,128)(2,1)}), bf16[8,32,8,128]{3,2,1,0:T(8,128)(2,1)S(1)}, u32[]{:S(2)}, u32[]{:S(2)}) async-start(bf16[8,32,8,128]{3,2,1,0:T(8,128)(2,1)} %bitcast.16), calls=%async_computation.1 | async-start | bytes 1048576 | tf_op jit(solution)/shard_map/all_to_all | solution.py:553
  32.5 2.0 %shard_map.95 = (s32[1,128]{1,0:T(1,128)S(4)}, s32[1,128]{1,0:T(1,128)S(4)}, s32[3,128]{1,0:T(4,128)S(4)}) custom-call(s32[3]{0:T(128)} %counts.3, s32[3,32]{1,0:T(4,128)} %columns.3, s32[3,32]{1,0:T(4,128)} %lags.3), custom_call_target="tpu_custom_call" | custom-call | tf_op jit(solution)/shard_map/pallas_call | solution.py:161
  34.5 2.2 %shard_map.101 = (bf16[2,32,128,128]{3,2,1,0:T(8,128)(2,1)S(1)}, bf16[3,128,128]{2,1,0:T(8,128)(2,1)S(1)}, bf16[8,384]{1,0:T(8,128)(2,1)S(1)}) custom-call(s32[3]{0:T(128)} %counts.3, bf16[3,32,128,128]{3,2,1,0:T(8,128)(2,1)} %ztiles_hbm.5, bf16[3,128,128]{2,1,0:T(8,128)(2,1)} %zinv_hbm.1, bf16[2,8,384]{2,1,0:T(8,128)(2,1)} %refs_9_.1), custom_call_target="tpu_custom_call" | custom-call | tf_op jit(solution)/shard_map/pallas_call | solution.py:326
  36.7 5.2 %all-to-all-done.1 = bf16[8,32,8,128]{3,2,1,0:T(8,128)(2,1)S(1)} async-done(((bf16[8,32,8,128]{3,2,1,0:T(8,128)(2,1)}), bf16[8,32,8,128]{3,2,1,0:T(8,128)(2,1)S(1)}, u32[]{:S(2)}, u32[]{:S(2)}) %all-to-all-start.1) | async-done | bytes 524320 | tf_op jit(solution)/shard_map/all_to_all | solution.py:553
  41.8 2.2 %shard_map.102.refs_8_ = bf16[32,3,8,128]{3,2,1,0:T(8,128)(2,1)} custom-call(s32[1,128]{1,0:T(1,128)S(4)} %get-tuple-element.31.spots, bf16[256,8,128]{2,1,0:T(8,128)(2,1)S(1)} %bitcast.11, bf16[2,32,128,128]{3,2,1,0:T(8,128)(2,1)S(1)} %get-tuple-element.32.top, bf16[3,32,128,128]{3,2,1,0:T(8,128)(2,1)} %ztiles_hbm.5, ...), custom_call_target="tpu_custom_call" | custom-call | tf_op jit(solution)/shard_map/pallas_call | solution.py:362
  44.1 3.9 %all-to-all-start.2 = ((bf16[32,3,8,128]{3,2,1,0:T(8,128)(2,1)}), bf16[32,3,8,128]{3,2,1,0:T(8,128)(2,1)S(1)}, u32[]{:S(2)}, u32[]{:S(2)}) async-start(bf16[32,3,8,128]{3,2,1,0:T(8,128)(2,1)} %shard_map.102.refs_8_), calls=%async_computation.2 | async-start | bytes 393216 | tf_op jit(solution)/shard_map/all_to_all | solution.py:558
  48.0 1.3 %shard_map.99 = (bf16[64,8,128]{2,1,0:T(8,128)(2,1)}, bf16[64,8,128]{2,1,0:T(8,128)(2,1)}, bf16[64,8,128]{2,1,0:T(8,128)(2,1)}, bf16[64,8,128]{2,1,0:T(8,128)(2,1)}) custom-call(s32[1,512]{1,0:T(1,128)S(4)} %get-tuple-element.23.refs_0_, s32[1,512]{1,0:T(1,128)S(4)} %get-tuple-element.24.refs_1_, s32[1,512]{1,0:T(1,128)S(4)} %get-tuple-element.25.refs_2_, ...), custom_call_target="tpu_custom_call" | custom-call | tf_op jit(solution)/shard_map/pallas_call | solution.py:253
  49.2 1.2 %collective-permute-start.6 = (bf16[64,8,128]{2,1,0:T(8,128)(2,1)}, bf16[64,8,128]{2,1,0:T(8,128)(2,1)S(1)}, u32[]{:S(2)}, u32[]{:S(2)}) collective-permute-start(bf16[64,8,128]{2,1,0:T(8,128)(2,1)} %get-tuple-element.30), channel_id=1, source_target_pairs={{0,64},{64,128},{128,192},{192,0},{1,65},{65,129},{129,193},{193,1... | collective-permute-start | bytes 393224 | tf_op jit(solution)/shard_map/ppermute | solution.py:538
  50.5 1.5 %collective-permute-start.4 = (bf16[64,8,128]{2,1,0:T(8,128)(2,1)}, bf16[64,8,128]{2,1,0:T(8,128)(2,1)S(1)}, u32[]{:S(2)}, u32[]{:S(2)}) collective-permute-start(bf16[64,8,128]{2,1,0:T(8,128)(2,1)} %get-tuple-element.28), channel_id=1, source_target_pairs={{0,192},{64,0},{128,64},{192,128},{1,193},{65,1},{129,65},{193,129... | collective-permute-start | bytes 393224 | tf_op jit(solution)/shard_map/ppermute | solution.py:538
  52.0 1.5 %collective-permute-start.5 = (bf16[64,8,128]{2,1,0:T(8,128)(2,1)}, bf16[64,8,128]{2,1,0:T(8,128)(2,1)S(1)}, u32[]{:S(2)}, u32[]{:S(2)}) collective-permute-start(bf16[64,8,128]{2,1,0:T(8,128)(2,1)} %get-tuple-element.29), channel_id=1, source_target_pairs={{0,128},{64,192},{128,0},{192,64},{1,129},{65,193},{129,1},{193,65... | collective-permute-start | bytes 393224 | tf_op jit(solution)/shard_map/ppermute | solution.py:538
  53.5 3.9 %all-to-all-done.2 = bf16[32,3,8,128]{3,2,1,0:T(8,128)(2,1)S(1)} async-done(((bf16[32,3,8,128]{3,2,1,0:T(8,128)(2,1)}), bf16[32,3,8,128]{3,2,1,0:T(8,128)(2,1)S(1)}, u32[]{:S(2)}, u32[]{:S(2)}) %all-to-all-start.2) | async-done | bytes 196640 | tf_op jit(solution)/shard_map/all_to_all | solution.py:558
  57.4 2.9 %collective-permute-start.11 = (bf16[96,8,128]{2,1,0:T(8,128)(2,1)S(1)}, bf16[96,8,128]{2,1,0:T(8,128)(2,1)S(1)}, u32[]{:S(2)}, u32[]{:S(2)}) collective-permute-start(bf16[96,8,128]{2,1,0:T(8,128)(2,1)S(1)} %bitcast.12), channel_id=1, source_target_pairs={{0,4},{4,0},{1,5},{5,1},{2,6},{6,2},{3,7},{7,3},{8,12},{12,8},{9,1... | collective-permute-start | bytes 589832 | tf_op jit(solution)/shard_map/ppermute | solution.py:560
  60.9 1.1 %collective-permute-start.9 = (bf16[64,8,128]{2,1,0:T(8,128)(2,1)S(1)}, bf16[64,8,128]{2,1,0:T(8,128)(2,1)S(1)}, u32[]{:S(2)}, u32[]{:S(2)}) collective-permute-start(bf16[64,8,128]{2,1,0:T(8,128)(2,1)S(1)} %collective-permute-done.5.refs_2_), channel_id=1, source_target_pairs={{0,4},{4,0},{1,5},{5,1},{2,6},{6,2},{3,7},{7,3},{8,12},{12,8},{9,1... | collective-permute-start | bytes 393224 | tf_op jit(solution)/shard_map/ppermute | solution.py:555
  62.2 0.8 collective-permute-done.9.refs_6_
  62.9 0.9 %copy-done = bf16[64,8,128]{2,1,0:T(8,128)(2,1)S(1)} copy-done((bf16[64,8,128]{2,1,0:T(8,128)(2,1)S(1)}, bf16[64,8,128]{2,1,0:T(8,128)(2,1)}, u32[]{:S(2)}) %copy-start) | copy-done | bytes 131096
  63.8 2.2 %shard_map.103 = (f32[4,8,384]{2,1,0:T(8,128)S(1)}, bf16[3,8,128,128]{3,2,1,0:T(8,128)(2,1)S(1)}, bf16[384,256]{1,0:T(8,128)(2,1)S(1)}) custom-call(s32[1,128]{1,0:T(1,128)S(4)} %get-tuple-element.22.spots, s32[3,128]{1,0:T(4,128)S(4)} %get-tuple-element.21.table, bf16[64,8,128]{2,1,0:T(8,128)(2,1)S(1)} %copy-done, ...), custom_call_target="tpu_custom_call" | custom-call | tf_op jit(solution)/shard_map/pallas_call | solution.py:409
  66.1 1.4 %shard_map.104 = (bf16[2,8,384]{2,1,0:T(8,128)(2,1)}, f32[64,128]{1,0:T(8,128)S(1)}) custom-call(s32[3,128]{1,0:T(4,128)S(4)} %get-tuple-element.21.table, f32[4,8,384]{2,1,0:T(8,128)S(1)} %get-tuple-element.35.packed, bf16[3,8,128,128]{3,2,1,0:T(8,128)(2,1)S(1)} %get-tuple-element.36.fresh, bf16[3,128,128]{2,1,0:T(8,128)(2,1)S(1)} %get-tuple-element.33.zinv, ...), custom_call_target="tpu_custom_call" | custom-call | tf_op jit(solution)/shard_map/pallas_call | solution.py:490
  67.5 17.2 %all_to_all.20 = f32[64,1,128]{2,1,0:T(1,128)S(1)} all-to-all(f32[64,1,128]{2,1,0:T(1,128)S(1)} %bitcast.15), channel_id=1, replica_groups=mesh['y'=4,'z'=8,'c'=2,'dir'=4] {'y','z','c'}, dimensions={0} | all-to-all | bytes 65536 | tf_op jit(solution)/shard_map/all_to_all | solution.py:563
  84.8 0.7 shard_map.105
  (13 shorter events, 0.9 us)
Async XLA Ops:
  2.2 23.3 %all-to-all-start = ((bf16[8,8,3,8,128]{4,3,2,1,0:T(8,128)(2,1)}), bf16[8,8,3,8,128]{4,3,2,1,0:T(8,128)(2,1)S(1)}, u32[]{:S(2)}, u32[]{:S(2)}) async-start(bf16[8,8,3,8,128]{4,3,2,1,0:T(8,128)(2,1)} %shard_map.98), calls=%async_computation | async-start | bytes 786432 | tf_op jit(solution)/shard_map/all_to_all | solution.py:546
  12.3 1.9 %collective-permute-start = (s32[1,256]{1,0:T(1,128)S(1)}, s32[1,256]{1,0:T(1,128)S(1)}, u32[]{:S(2)}, u32[]{:S(2)}) collective-permute-start(s32[1,256]{1,0:T(1,128)S(1)} %shard_map.96), channel_id=1, source_target_pairs={{0,4},{4,0},{1,5},{5,1},{2,6},{6,2},{3,7},{7,3},{8,12},{12,8},{9,1... | collective-permute-start | bytes 3080 | tf_op jit(solution)/shard_map/ppermute | solution.py:549
  14.2 5.0 %collective-permute-start.1 = (s32[1,512]{1,0:T(1,128)S(1)}, s32[1,512]{1,0:T(1,128)S(1)}, u32[]{:S(2)}, u32[]{:S(2)}) collective-permute-start(s32[1,512]{1,0:T(1,128)S(1)} %pad_add_fusion.refs_0_), channel_id=1, source_target_pairs={{0,64},{64,128},{128,192},{192,0},{1,65},{65,129},{129,193},{193,1... | collective-permute-start | bytes 6152 | tf_op jit(solution)/shard_map/ppermute | solution.py:538
  15.5 4.2 %collective-permute-start.2 = (s32[1,512]{1,0:T(1,128)S(1)}, s32[1,512]{1,0:T(1,128)S(1)}, u32[]{:S(2)}, u32[]{:S(2)}) collective-permute-start(s32[1,512]{1,0:T(1,128)S(1)} %pad_add_fusion.refs_0_), channel_id=1, source_target_pairs={{0,128},{64,192},{128,0},{192,64},{1,129},{65,193},{129,1},{193,65... | collective-permute-start | bytes 6152 | tf_op jit(solution)/shard_map/ppermute | solution.py:538
  18.1 2.7 %collective-permute-start.3 = (s32[1,512]{1,0:T(1,128)S(1)}, s32[1,512]{1,0:T(1,128)S(1)}, u32[]{:S(2)}, u32[]{:S(2)}) collective-permute-start(s32[1,512]{1,0:T(1,128)S(1)} %pad_add_fusion.refs_0_), channel_id=1, source_target_pairs={{0,192},{64,0},{128,64},{192,128},{1,193},{65,1},{129,65},{193,129... | collective-permute-start | bytes 6152 | tf_op jit(solution)/shard_map/ppermute | solution.py:538
  26.6 15.2 %all-to-all-start.1 = ((bf16[8,32,8,128]{3,2,1,0:T(8,128)(2,1)}), bf16[8,32,8,128]{3,2,1,0:T(8,128)(2,1)S(1)}, u32[]{:S(2)}, u32[]{:S(2)}) async-start(bf16[8,32,8,128]{3,2,1,0:T(8,128)(2,1)} %bitcast.16), calls=%async_computation.1 | async-start | bytes 1048576 | tf_op jit(solution)/shard_map/all_to_all | solution.py:553
  44.1 13.3 %all-to-all-start.2 = ((bf16[32,3,8,128]{3,2,1,0:T(8,128)(2,1)}), bf16[32,3,8,128]{3,2,1,0:T(8,128)(2,1)S(1)}, u32[]{:S(2)}, u32[]{:S(2)}) async-start(bf16[32,3,8,128]{3,2,1,0:T(8,128)(2,1)} %shard_map.102.refs_8_), calls=%async_computation.2 | async-start | bytes 393216 | tf_op jit(solution)/shard_map/all_to_all | solution.py:558
  49.2 11.0 %collective-permute-start.6 = (bf16[64,8,128]{2,1,0:T(8,128)(2,1)}, bf16[64,8,128]{2,1,0:T(8,128)(2,1)S(1)}, u32[]{:S(2)}, u32[]{:S(2)}) collective-permute-start(bf16[64,8,128]{2,1,0:T(8,128)(2,1)} %get-tuple-element.30), channel_id=1, source_target_pairs={{0,64},{64,128},{128,192},{192,0},{1,65},{65,129},{129,193},{193,1... | collective-permute-start | bytes 393224 | tf_op jit(solution)/shard_map/ppermute | solution.py:538
  50.5 10.3 %collective-permute-start.4 = (bf16[64,8,128]{2,1,0:T(8,128)(2,1)}, bf16[64,8,128]{2,1,0:T(8,128)(2,1)S(1)}, u32[]{:S(2)}, u32[]{:S(2)}) collective-permute-start(bf16[64,8,128]{2,1,0:T(8,128)(2,1)} %get-tuple-element.28), channel_id=1, source_target_pairs={{0,192},{64,0},{128,64},{192,128},{1,193},{65,1},{129,65},{193,129... | collective-permute-start | bytes 393224 | tf_op jit(solution)/shard_map/ppermute | solution.py:538
  52.0 8.9 %collective-permute-start.5 = (bf16[64,8,128]{2,1,0:T(8,128)(2,1)}, bf16[64,8,128]{2,1,0:T(8,128)(2,1)S(1)}, u32[]{:S(2)}, u32[]{:S(2)}) collective-permute-start(bf16[64,8,128]{2,1,0:T(8,128)(2,1)} %get-tuple-element.29), channel_id=1, source_target_pairs={{0,128},{64,192},{128,0},{192,64},{1,129},{65,193},{129,1},{193,65... | collective-permute-start | bytes 393224 | tf_op jit(solution)/shard_map/ppermute | solution.py:538
  57.4 8.7 %collective-permute-start.11 = (bf16[96,8,128]{2,1,0:T(8,128)(2,1)S(1)}, bf16[96,8,128]{2,1,0:T(8,128)(2,1)S(1)}, u32[]{:S(2)}, u32[]{:S(2)}) collective-permute-start(bf16[96,8,128]{2,1,0:T(8,128)(2,1)S(1)} %bitcast.12), channel_id=1, source_target_pairs={{0,4},{4,0},{1,5},{5,1},{2,6},{6,2},{3,7},{7,3},{8,12},{12,8},{9,1... | collective-permute-start | bytes 589832 | tf_op jit(solution)/shard_map/ppermute | solution.py:560
  60.2 1.7 %collective-permute-start.7 = (bf16[64,8,128]{2,1,0:T(8,128)(2,1)}, bf16[64,8,128]{2,1,0:T(8,128)(2,1)S(1)}, u32[]{:S(2)}, u32[]{:S(2)}) collective-permute-start(bf16[64,8,128]{2,1,0:T(8,128)(2,1)} %get-tuple-element.27.refs_0_), channel_id=1, source_target_pairs={{0,4},{4,0},{1,5},{5,1},{2,6},{6,2},{3,7},{7,3},{8,12},{12,8},{9,1... | collective-permute-start | bytes 393224 | tf_op jit(solution)/shard_map/ppermute | solution.py:555
  60.2 1.7 %collective-permute-start.10 = (bf16[64,8,128]{2,1,0:T(8,128)(2,1)S(1)}, bf16[64,8,128]{2,1,0:T(8,128)(2,1)S(1)}, u32[]{:S(2)}, u32[]{:S(2)}) collective-permute-start(bf16[64,8,128]{2,1,0:T(8,128)(2,1)S(1)} %collective-permute-done.6.refs_3_), channel_id=1, source_target_pairs={{0,4},{4,0},{1,5},{5,1},{2,6},{6,2},{3,7},{7,3},{8,12},{12,8},{9,1... | collective-permute-start | bytes 393224 | tf_op jit(solution)/shard_map/ppermute | solution.py:555
  60.8 1.4 %collective-permute-start.8 = (bf16[64,8,128]{2,1,0:T(8,128)(2,1)S(1)}, bf16[64,8,128]{2,1,0:T(8,128)(2,1)S(1)}, u32[]{:S(2)}, u32[]{:S(2)}) collective-permute-start(bf16[64,8,128]{2,1,0:T(8,128)(2,1)S(1)} %collective-permute-done.4.refs_1_), channel_id=1, source_target_pairs={{0,4},{4,0},{1,5},{5,1},{2,6},{6,2},{3,7},{7,3},{8,12},{12,8},{9,1... | collective-permute-start | bytes 393224 | tf_op jit(solution)/shard_map/ppermute | solution.py:555
  60.9 2.1 %collective-permute-start.9 = (bf16[64,8,128]{2,1,0:T(8,128)(2,1)S(1)}, bf16[64,8,128]{2,1,0:T(8,128)(2,1)S(1)}, u32[]{:S(2)}, u32[]{:S(2)}) collective-permute-start(bf16[64,8,128]{2,1,0:T(8,128)(2,1)S(1)} %collective-permute-done.5.refs_2_), channel_id=1, source_target_pairs={{0,4},{4,0},{1,5},{5,1},{2,6},{6,2},{3,7},{7,3},{8,12},{12,8},{9,1... | collective-permute-start | bytes 393224 | tf_op jit(solution)/shard_map/ppermute | solution.py:555
  62.9 0.9 %copy-start = (bf16[64,8,128]{2,1,0:T(8,128)(2,1)S(1)}, bf16[64,8,128]{2,1,0:T(8,128)(2,1)}, u32[]{:S(2)}) copy-start(bf16[64,8,128]{2,1,0:T(8,128)(2,1)} %get-tuple-element.27.refs_0_) | copy-start | bytes 393220

commit v9 on v8

--- a/solution.py
+++ b/solution.py
@@ -13,6 +13,7 @@
 E = ("y", "z", "c")
 BLOCK_CAP = 4
 CHUNK = 8
+FETCHED = 8
 SMALL = 8 << 20
 SWAP = [(0, 1), (1, 0)]
 
@@ -49,31 +50,44 @@
     return jnp.broadcast_to(row, (8, row.shape[1])).T[:, :1]
 
 
-def open_kernel(history, fanned, held, sems):
+def open_kernel(history, columns_hbm, lags_hbm, fanned, wanted, held, columns, lags, sems):
     rows, tile = held.shape[1], held.shape[3]
-    into = start_all(
-        [(history.at[:, :, pl.ds(row * tile, tile)], held.at[:, row]) for row in range(rows)], sems
-    )
+    pairs = [(history.at[:, :, pl.ds(row * tile, tile)], held.at[:, row]) for row in range(rows)]
+    into = start_all([*pairs, (columns_hbm, columns), (lags_hbm, lags)], sems)
     for copy in into:
         copy.wait()
-    for copy in start_all([(held, fanned.at[z]) for z in range(Z)], sems, rows):
-        copy.wait()
-
-
-def open_up(history, tile):
+    out = start_all([(held, fanned.at[z]) for z in range(Z)], sems, len(into))
+    slots = Slots(columns, lags)
+    spot = (slots.z * LEVELS + slots.lag) * slots.rows + slots.local
+    asks = lax.broadcasted_iota(jnp.int32, (slots.count, wanted.shape[1]), 1)
+    total = jnp.zeros(wanted.shape, jnp.int32)
+    for row in range(slots.rows):
+        mine = jnp.where(turned(slots.at[row]) == asks, turned(spot[row : row + 1]), 0)
+        total += jnp.sum(mine, axis=0, keepdims=True)
+    wanted[...] = total
+    for copy in out:
+        copy.wait()
+
+
+def open_up(history, columns, lags, tile):
     levels, dirs, panels = history.shape
     rows = panels // tile
     return kernel_call(
         open_kernel,
         SMALL,
-        out_shape=pltpu.HBM((Z, levels, rows, dirs, tile), history.dtype),
-        in_specs=[hbm()],
-        out_specs=hbm(),
+        out_shape=(
+            pltpu.HBM((Z, levels, rows, dirs, tile), history.dtype),
+            pltpu.VMEM((1, GROUPS * BLOCK_CAP * Z), jnp.int32),
+        ),
+        in_specs=[hbm()] * 3,
+        out_specs=(hbm(), vmem()),
         scratch_shapes=[
             pltpu.VMEM((levels, rows, dirs, tile), history.dtype),
-            pltpu.SemaphoreType.DMA((rows + Z,)),
-        ],
-    )(off_core(history))
+            pltpu.VMEM(columns.shape, columns.dtype),
+            pltpu.VMEM(lags.shape, lags.dtype),
+            pltpu.SemaphoreType.DMA((rows + 2 + Z,)),
+        ],
+    )(off_core(history), off_core(columns), off_core(lags))
 
 
 class Slots:
@@ -98,27 +112,6 @@
                 position += jnp.sum((down[before] == groups[row]).astype(jnp.int32), axis=0, keepdims=True)
             self.position.append(position)
         self.at = [groups[row] * (BLOCK_CAP * Z) + self.position[row] for row in range(self.rows)]
-
-
-def plan_kernel(columns, lags, wanted):
-    slots = Slots(columns, lags)
-    spot = (slots.z * LEVELS + slots.lag) * slots.rows + slots.local
-    asks = lax.broadcasted_iota(jnp.int32, (slots.count, wanted.shape[1]), 1)
-    total = jnp.zeros(wanted.shape, jnp.int32)
-    for row in range(slots.rows):
-        mine = jnp.where(turned(slots.at[row]) == asks, turned(spot[row : row + 1]), 0)
-        total += jnp.sum(mine, axis=0, keepdims=True)
-    wanted[...] = total
-
-
-def plan(columns, lags):
-    return kernel_call(
-        plan_kernel,
-        SMALL,
-        out_shape=pltpu.VMEM((1, GROUPS * BLOCK_CAP * Z), jnp.int32),
-        in_specs=[vmem(), vmem()],
-        out_specs=vmem(),
-    )(off_core(columns), off_core(lags))
 
 
 def chart_kernel(counts, columns, lags, spots_out, aged_out, table_out, spots, aged, table, sems):
@@ -273,9 +266,9 @@
     return jnp.concatenate(parts, axis=1)
 
 
-def row_sum(spots, load, weights, row):
+def row_sum(spots, load, weights, base):
     slots, tile = weights.shape[0], weights.shape[1]
-    picked = pieces_of(lambda k: spots[0, row * slots + k], slots, load)
+    picked = pieces_of(lambda k: spots[0, base + k], slots, load)
     return jnp.dot(picked, weights[...].reshape(slots * tile, tile), preferred_element_type=jnp.float32)
 
 
@@ -311,23 +304,29 @@
                 target[part] = jnp.zeros((CHUNK, *target.shape[1:]), target.dtype)
 
 
+def staged_rows(counts, ztiles_hbm, top, sems, act):
+    slots = ztiles_hbm.shape[1]
+    for row in range(ztiles_hbm.shape[0]):
+        length = min(slots, top.shape[0] - row * slots)
+        if length > 0:
+            target = top.at[pl.ds(row * slots, length)]
+            live_tiles(counts[row], ztiles_hbm.at[row, pl.ds(0, length)], target, sems, row, act)
+
+
 def stage_kernel(counts, ztiles_hbm, zinv_hbm, incident_hbm, top, zinv, incident, sems, tile_sems):
-    kept = top.shape[0]
-    for row in range(kept):
-        live_tiles(counts[row], ztiles_hbm.at[row], top.at[row], tile_sems, row, "start")
+    staged_rows(counts, ztiles_hbm, top, tile_sems, "start")
     for copy in start_all([(zinv_hbm, zinv), (incident_hbm.at[0], incident)], sems):
         copy.wait()
-    for row in range(kept):
-        live_tiles(counts[row], ztiles_hbm.at[row], top.at[row], tile_sems, row, "wait")
+    staged_rows(counts, ztiles_hbm, top, tile_sems, "wait")
 
 
 def stage(counts, ztiles, zinv, incident):
-    kept = ztiles.shape[0] - 1
+    rows, slots, tile = ztiles.shape[0], ztiles.shape[1], ztiles.shape[2]
     return kernel_call(
         stage_kernel,
         SMALL,
         out_shape=(
-            pltpu.VMEM((kept, *ztiles.shape[1:]), ztiles.dtype),
+            pltpu.VMEM((rows * slots - FETCHED, tile, tile), ztiles.dtype),
             pltpu.VMEM(zinv.shape, zinv.dtype),
             pltpu.VMEM(incident.shape[1:], incident.dtype),
         ),
@@ -335,20 +334,25 @@
         out_specs=[vmem()] * 3,
         scratch_shapes=[
             pltpu.SemaphoreType.DMA((2,)),
-            pltpu.SemaphoreType.DMA((kept, ztiles.shape[1] // CHUNK)),
+            pltpu.SemaphoreType.DMA((rows, slots // CHUNK)),
         ],
     )(off_core(counts), off_core(ztiles), off_core(zinv), off_core(incident))
 
 
 def first_kernel(spots, got, top, ztiles_hbm, zinv, incident, spread_out, last, kept_out, sems, tile_sems):
-    kept, slots, tile = top.shape[0], top.shape[1], top.shape[2]
-    count = spots[0, (kept + 1) * slots + kept]
-    live_tiles(count, ztiles_hbm.at[kept], last, tile_sems, 0, "start")
+    rows, slots, tile = ztiles_hbm.shape[0], ztiles_hbm.shape[1], ztiles_hbm.shape[2]
+    begin = slots - last.shape[0]
+    rest = ztiles_hbm.at[rows - 1, pl.ds(begin, last.shape[0])]
+    count = spots[0, rows * slots + rows - 1] - begin
+    live_tiles(count, rest, last, tile_sems, 0, "start")
     copies = []
-    for row in range(kept + 1):
-        if row == kept:
-            live_tiles(count, ztiles_hbm.at[kept], last, tile_sems, 0, "wait")
-        total = row_sum(spots, lambda spot: got[spot], top.at[row] if row < kept else last, row)
+    for row in range(rows):
+        length = slots if row < rows - 1 else begin
+        weights = top.at[pl.ds(row * slots, length)]
+        total = row_sum(spots, lambda spot: got[spot], weights, row * slots)
+        if row == rows - 1:
+            live_tiles(count, rest, last, tile_sems, 0, "wait")
+            total += row_sum(spots, lambda spot: got[spot], last, row * slots + begin)
         density = density_of(incident[:, row * tile : (row + 1) * tile], total, zinv[row])
         for to in range(spread_out.shape[0]):
             kept_out[row, to] = density
@@ -358,7 +362,7 @@
 
 
 def first_step(spots, got, top, ztiles, zinv, incident):
-    rows, slots, tile, dirs = ztiles.shape[0], ztiles.shape[1], ztiles.shape[2], got.shape[1]
+    rows, tile, dirs = ztiles.shape[0], ztiles.shape[2], got.shape[1]
     return kernel_call(
         first_kernel,
         SMALL,
@@ -366,10 +370,10 @@
         in_specs=[smem(), vmem(), vmem(), hbm(), vmem(), vmem()],
         out_specs=hbm(),
         scratch_shapes=[
-            pltpu.VMEM(ztiles.shape[1:], ztiles.dtype),
+            pltpu.VMEM((FETCHED, tile, tile), ztiles.dtype),
             pltpu.VMEM((rows, Y * Z, dirs, tile), jnp.bfloat16),
             pltpu.SemaphoreType.DMA((rows,)),
-            pltpu.SemaphoreType.DMA((1, slots // CHUNK)),
+            pltpu.SemaphoreType.DMA((1, FETCHED // CHUNK)),
         ],
     )(scalar_core(spots), near_core(got), near_core(top), off_core(ztiles), near_core(zinv), near_core(incident))
 
@@ -393,7 +397,7 @@
         for k in range(CHUNK):
             fresh[row, k] = ztiles[row, table[0, row * slots + k]]
         at = slice(row * tile, (row + 1) * tile)
-        packed[1, :, at] = row_sum(spots, lambda spot: pool[spot], ztiles.at[row], row)
+        packed[1, :, at] = row_sum(spots, lambda spot: pool[spot], ztiles.at[row], row * slots)
     for copy in copies:
         copy.wait()
     packed[0, :, :] = incident[...].astype(jnp.float32)
@@ -543,8 +547,8 @@
     dirs = history.shape[1]
     owners = Y * Z * C
     cap = BLOCK_CAP * Z
-    held = lax.all_to_all(open_up(history, tile), "z", 0, 0, tiled=True).reshape(-1, dirs, tile)
-    wanted = plan(columns, lags)
+    outgoing, wanted = open_up(history, columns, lags, tile)
+    held = lax.all_to_all(outgoing, "z", 0, 0, tiled=True).reshape(-1, dirs, tile)
     spots, aged, table = chart(counts, columns, lags)
     both = jnp.concatenate([wanted, lax.ppermute(wanted, "c", SWAP)], axis=1)
     lists = [both] + [shifted(both, "y", Y, s) for s in range(1, Y)]

time: 86 us -> 86.6 us (level)
  waiting for transfers between devices: 16.5 us -> 17.5 us
    all_to_all x1, waiting for transfers between devices: 3.96 us -> 5.13 us  [march(): lax.all_to_all(outgoing, 'z', 0, 0, tiled=True).reshape(-1, dirs, tile)]
    pallas_call x3 -> x2, Pallas kernels: 4.84 us -> 4.05 us  [the longest x1 2.44 us: stage(): kernel_call(stage_kernel, SMALL, out_shape=(pltpu.VMEM((rows * slots - FE...]
  transfers between devices with their start and end apart: 15 -> 15, of which waited for: 8 -> 9; matrix products, arithmetic and copies ran while one was open for 0% -> 0% of each run, Pallas kernels for 11% -> 10%
where the time goes in v9:
time: 86.6 us; the launch traced here: 86 us
  starting transfers between devices  33.5 us (39%)
  waiting for transfers between devices  17.5 us (20%)
  blocking collectives  16.9 us (20%)
  Pallas kernels  16.5 us (19%)
  local copies, waits for them, and re-layouts  0.91 us (1%)
    all_to_all x1, blocking collectives, march(): lax.all_to_all(far.reshape(owners, 1, 128), E, 0, 0, tiled=True)  16.9 us
    ppermute x6, starting transfers between devices, shifted(): lax.ppermute(value, axis, [(i, (i + shift) % length) for i in range(lengt...  9.25 us
    all_to_all x1, starting transfers between devices, march(): lax.all_to_all(outgoing, 'z', 0, 0, tiled=True).reshape(-1, dirs, tile)  9.02 us
    all_to_all x1, starting transfers between devices, march(): lax.all_to_all(first.reshape(GROUPS, cap, dirs, tile), ('y', 'c'), 0, 0,...  5.84 us
    all_to_all x1, waiting for transfers between devices, march(): lax.all_to_all(outgoing, 'z', 0, 0, tiled=True).reshape(-1, dirs, tile)  5.13 us
    all_to_all x1, waiting for transfers between devices, march(): lax.all_to_all(first.reshape(GROUPS, cap, dirs, tile), ('y', 'c'), 0, 0,...  4.99 us
    all_to_all x1, starting transfers between devices, march(): lax.all_to_all(fanned, ('y', 'z'), 0, 0, tiled=True)  3.87 us
    all_to_all x1, waiting for transfers between devices, march(): lax.all_to_all(fanned, ('y', 'z'), 0, 0, tiled=True)  3.87 us
  transfers between devices with their start and end apart: 15, of which 9 were waited for; matrix products, arithmetic and copies ran while one was open for 0% of the time, Pallas kernels for 10%

profile of v9, /device:TPU:1, one launch (start us, length us, event | category | flops | bytes accessed | tf_op | source)
XLA Modules:
  0.0 86.0 jit_solution(17169068868176582774)
XLA Ops:
  0.6 1.6 %shard_map.96 = (bf16[8,8,3,8,128]{4,3,2,1,0:T(8,128)(2,1)}, s32[1,256]{1,0:T(1,128)S(1)}) custom-call(bf16[8,8,384]{2,1,0:T(8,128)(2,1)} %history.1, s32[3,32]{1,0:T(4,128)} %columns_hbm.1, s32[3,32]{1,0:T(4,128)} %lags_hbm.1), custom_call_target="tpu_custom_call" | custom-call | tf_op jit(solution)/shard_map/pallas_call | solution.py:75
  2.2 9.0 %all-to-all-start = ((bf16[8,8,3,8,128]{4,3,2,1,0:T(8,128)(2,1)}), bf16[8,8,3,8,128]{4,3,2,1,0:T(8,128)(2,1)S(1)}, u32[]{:S(2)}, u32[]{:S(2)}) async-start(bf16[8,8,3,8,128]{4,3,2,1,0:T(8,128)(2,1)} %get-tuple-element.30), calls=%async_computation | async-start | bytes 786432 | tf_op jit(solution)/shard_map/all_to_all | solution.py:551
  11.3 1.0 %collective-permute-start = (s32[1,256]{1,0:T(1,128)S(1)}, s32[1,256]{1,0:T(1,128)S(1)}, u32[]{:S(2)}, u32[]{:S(2)}) collective-permute-start(s32[1,256]{1,0:T(1,128)S(1)} %get-tuple-element.25), channel_id=1, source_target_pairs={{0,4},{4,0},{1,5},{5,1},{2,6},{6,2},{3,7},{7,3},{8,12},{12,8},{9,1... | collective-permute-start | bytes 3080 | tf_op jit(solution)/shard_map/ppermute | solution.py:553
  12.2 0.8 collective-permute-done
  13.0 1.3 %collective-permute-start.1 = (s32[1,512]{1,0:T(1,128)S(1)}, s32[1,512]{1,0:T(1,128)S(1)}, u32[]{:S(2)}, u32[]{:S(2)}) collective-permute-start(s32[1,512]{1,0:T(1,128)S(1)} %constant_dynamic-update-slice_fusion.refs_0_), channel_id=1, source_target_pairs={{0,64},{64,128},{128,192},{192,0},{1,65},{65,129},{129,193},{193,1... | collective-permute-start | bytes 6152 | tf_op jit(solution)/shard_map/ppermute | solution.py:542
  14.3 2.6 %collective-permute-start.2 = (s32[1,512]{1,0:T(1,128)S(1)}, s32[1,512]{1,0:T(1,128)S(1)}, u32[]{:S(2)}, u32[]{:S(2)}) collective-permute-start(s32[1,512]{1,0:T(1,128)S(1)} %constant_dynamic-update-slice_fusion.refs_0_), channel_id=1, source_target_pairs={{0,128},{64,192},{128,0},{192,64},{1,129},{65,193},{129,1},{193,65... | collective-permute-start | bytes 6152 | tf_op jit(solution)/shard_map/ppermute | solution.py:542
  17.0 1.1 %collective-permute-start.3 = (s32[1,512]{1,0:T(1,128)S(1)}, s32[1,512]{1,0:T(1,128)S(1)}, u32[]{:S(2)}, u32[]{:S(2)}) collective-permute-start(s32[1,512]{1,0:T(1,128)S(1)} %constant_dynamic-update-slice_fusion.refs_0_), channel_id=1, source_target_pairs={{0,192},{64,0},{128,64},{192,128},{1,193},{65,1},{129,65},{193,129... | collective-permute-start | bytes 6152 | tf_op jit(solution)/shard_map/ppermute | solution.py:542
  18.0 0.2 collective-permute-done.2.refs_2_
  18.3 1.4 %collective-permute-done.3.refs_3_ = s32[1,512]{1,0:T(1,128)S(1)} collective-permute-done((s32[1,512]{1,0:T(1,128)S(1)}, s32[1,512]{1,0:T(1,128)S(1)}, u32[]{:S(2)}, u32[]{:S(2)}) %collective-permute-start.3) | collective-permute-done | bytes 2080 | tf_op jit(solution)/shard_map/ppermute | solution.py:542
  19.7 0.7 shard_map.97
  20.4 5.1 %all-to-all-done = bf16[8,8,3,8,128]{4,3,2,1,0:T(8,128)(2,1)S(1)} async-done(((bf16[8,8,3,8,128]{4,3,2,1,0:T(8,128)(2,1)}), bf16[8,8,3,8,128]{4,3,2,1,0:T(8,128)(2,1)S(1)}, u32[]{:S(2)}, u32[]{:S(2)}) %all-to-all-start) | async-done | bytes 393248 | tf_op jit(solution)/shard_map/all_to_all | solution.py:551
  25.5 1.1 %shard_map.99 = bf16[256,8,128]{2,1,0:T(8,128)(2,1)} custom-call(s32[1,512]{1,0:T(1,128)S(4)} %get-tuple-element.26.refs_0_, s32[1,512]{1,0:T(1,128)S(4)} %get-tuple-element.27.refs_1_, s32[1,512]{1,0:T(1,128)S(4)} %get-tuple-element.28.refs_2_, s32[1,512]{1,0:T(1,128)S(4)} %get-tuple-element.29.refs_3_, bf16[192,8,128]{2,1,0:T(8,128)(2,1)S(1)} %bitcast.9), custom_call_target="tpu_custom_call" | custom-call | tf_op jit(solution)/shard_map/pallas_call | solution.py:235
  26.6 5.8 %all-to-all-start.1 = ((bf16[8,32,8,128]{3,2,1,0:T(8,128)(2,1)}), bf16[8,32,8,128]{3,2,1,0:T(8,128)(2,1)}, u32[]{:S(2)}, u32[]{:S(2)}) async-start(bf16[8,32,8,128]{3,2,1,0:T(8,128)(2,1)} %bitcast.15), calls=%async_computation.1 | async-start | bytes 1048576 | tf_op jit(solution)/shard_map/all_to_all | solution.py:557
  32.5 2.0 %shard_map.95 = (s32[1,128]{1,0:T(1,128)S(4)}, s32[1,128]{1,0:T(1,128)S(4)}, s32[3,128]{1,0:T(4,128)S(4)}) custom-call(s32[3]{0:T(128)} %counts.3, s32[3,32]{1,0:T(4,128)} %columns_hbm.1, s32[3,32]{1,0:T(4,128)} %lags_hbm.1), custom_call_target="tpu_custom_call" | custom-call | tf_op jit(solution)/shard_map/pallas_call | solution.py:154
  34.5 2.4 %shard_map.100 = (bf16[88,128,128]{2,1,0:T(8,128)(2,1)S(1)}, bf16[3,128,128]{2,1,0:T(8,128)(2,1)S(1)}, bf16[8,384]{1,0:T(8,128)(2,1)S(1)}) custom-call(s32[3]{0:T(128)} %counts.3, bf16[3,32,128,128]{3,2,1,0:T(8,128)(2,1)} %ztiles_hbm.5, bf16[3,128,128]{2,1,0:T(8,128)(2,1)} %zinv_hbm.1, bf16[2,8,384]{2,1,0:T(8,128)(2,1)} %refs_9_.1), custom_call_target="tpu_custom_call" | custom-call | tf_op jit(solution)/shard_map/pallas_call | solution.py:325
  36.9 5.0 %all-to-all-done.1 = bf16[8,32,8,128]{3,2,1,0:T(8,128)(2,1)} async-done(((bf16[8,32,8,128]{3,2,1,0:T(8,128)(2,1)}), bf16[8,32,8,128]{3,2,1,0:T(8,128)(2,1)}, u32[]{:S(2)}, u32[]{:S(2)}) %all-to-all-start.1) | async-done | bytes 524320 | tf_op jit(solution)/shard_map/all_to_all | solution.py:557
  41.9 3.0 %shard_map.101.refs_8_ = bf16[32,3,8,128]{3,2,1,0:T(8,128)(2,1)} custom-call(s32[1,128]{1,0:T(1,128)S(4)} %get-tuple-element.35.spots, bf16[256,8,128]{2,1,0:T(8,128)(2,1)} %bitcast.2.got, bf16[88,128,128]{2,1,0:T(8,128)(2,1)S(1)} %get-tuple-element.36.top, bf16[3,32,128,128]{3,2,1,0:T(8,128)(2,1)} %ztiles_hbm.5, ...), custom_call_target="tpu_custom_call" | custom-call | tf_op jit(solution)/shard_map/pallas_call | solution.py:366
  45.0 3.9 %all-to-all-start.2 = ((bf16[32,3,8,128]{3,2,1,0:T(8,128)(2,1)}), bf16[32,3,8,128]{3,2,1,0:T(8,128)(2,1)S(1)}, u32[]{:S(2)}, u32[]{:S(2)}) async-start(bf16[32,3,8,128]{3,2,1,0:T(8,128)(2,1)} %shard_map.101.refs_8_), calls=%async_computation.2 | async-start | bytes 393216 | tf_op jit(solution)/shard_map/all_to_all | solution.py:562
  48.8 1.2 %shard_map.98 = (bf16[64,8,128]{2,1,0:T(8,128)(2,1)}, bf16[64,8,128]{2,1,0:T(8,128)(2,1)}, bf16[64,8,128]{2,1,0:T(8,128)(2,1)}, bf16[64,8,128]{2,1,0:T(8,128)(2,1)}) custom-call(s32[1,512]{1,0:T(1,128)S(4)} %get-tuple-element.26.refs_0_, s32[1,512]{1,0:T(1,128)S(4)} %get-tuple-element.27.refs_1_, s32[1,512]{1,0:T(1,128)S(4)} %get-tuple-element.28.refs_2_, ...), custom_call_target="tpu_custom_call" | custom-call | tf_op jit(solution)/shard_map/pallas_call | solution.py:246
  50.1 1.2 %collective-permute-start.6 = (bf16[64,8,128]{2,1,0:T(8,128)(2,1)}, bf16[64,8,128]{2,1,0:T(8,128)(2,1)S(1)}, u32[]{:S(2)}, u32[]{:S(2)}) collective-permute-start(bf16[64,8,128]{2,1,0:T(8,128)(2,1)} %get-tuple-element.34), channel_id=1, source_target_pairs={{0,64},{64,128},{128,192},{192,0},{1,65},{65,129},{129,193},{193,1... | collective-permute-start | bytes 393224 | tf_op jit(solution)/shard_map/ppermute | solution.py:542
  51.3 1.5 %collective-permute-start.4 = (bf16[64,8,128]{2,1,0:T(8,128)(2,1)}, bf16[64,8,128]{2,1,0:T(8,128)(2,1)S(1)}, u32[]{:S(2)}, u32[]{:S(2)}) collective-permute-start(bf16[64,8,128]{2,1,0:T(8,128)(2,1)} %get-tuple-element.32), channel_id=1, source_target_pairs={{0,192},{64,0},{128,64},{192,128},{1,193},{65,1},{129,65},{193,129... | collective-permute-start | bytes 393224 | tf_op jit(solution)/shard_map/ppermute | solution.py:542
  52.9 1.5 %collective-permute-start.5 = (bf16[64,8,128]{2,1,0:T(8,128)(2,1)}, bf16[64,8,128]{2,1,0:T(8,128)(2,1)S(1)}, u32[]{:S(2)}, u32[]{:S(2)}) collective-permute-start(bf16[64,8,128]{2,1,0:T(8,128)(2,1)} %get-tuple-element.33), channel_id=1, source_target_pairs={{0,128},{64,192},{128,0},{192,64},{1,129},{65,193},{129,1},{193,65... | collective-permute-start | bytes 393224 | tf_op jit(solution)/shard_map/ppermute | solution.py:542
  54.4 3.9 %all-to-all-done.2 = bf16[32,3,8,128]{3,2,1,0:T(8,128)(2,1)S(1)} async-done(((bf16[32,3,8,128]{3,2,1,0:T(8,128)(2,1)}), bf16[32,3,8,128]{3,2,1,0:T(8,128)(2,1)S(1)}, u32[]{:S(2)}, u32[]{:S(2)}) %all-to-all-start.2) | async-done | bytes 196640 | tf_op jit(solution)/shard_map/all_to_all | solution.py:562
  58.2 2.9 %collective-permute-start.11 = (bf16[96,8,128]{2,1,0:T(8,128)(2,1)S(1)}, bf16[96,8,128]{2,1,0:T(8,128)(2,1)S(1)}, u32[]{:S(2)}, u32[]{:S(2)}) collective-permute-start(bf16[96,8,128]{2,1,0:T(8,128)(2,1)S(1)} %bitcast.11), channel_id=1, source_target_pairs={{0,4},{4,0},{1,5},{5,1},{2,6},{6,2},{3,7},{7,3},{8,12},{12,8},{9,1... | collective-permute-start | bytes 589832 | tf_op jit(solution)/shard_map/ppermute | solution.py:564
  61.2 0.5 collective-permute-start.10
  61.8 1.0 %collective-permute-start.9 = (bf16[64,8,128]{2,1,0:T(8,128)(2,1)S(1)}, bf16[64,8,128]{2,1,0:T(8,128)(2,1)S(1)}, u32[]{:S(2)}, u32[]{:S(2)}) collective-permute-start(bf16[64,8,128]{2,1,0:T(8,128)(2,1)S(1)} %collective-permute-done.5.refs_2_), channel_id=1, source_target_pairs={{0,4},{4,0},{1,5},{5,1},{2,6},{6,2},{3,7},{7,3},{8,12},{12,8},{9,1... | collective-permute-start | bytes 393224 | tf_op jit(solution)/shard_map/ppermute | solution.py:559
  63.1 0.7 collective-permute-done.9.refs_6_
  63.8 0.9 %copy-done = bf16[64,8,128]{2,1,0:T(8,128)(2,1)S(1)} copy-done((bf16[64,8,128]{2,1,0:T(8,128)(2,1)S(1)}, bf16[64,8,128]{2,1,0:T(8,128)(2,1)}, u32[]{:S(2)}) %copy-start) | copy-done | bytes 131096
  64.7 2.2 %shard_map.102 = (f32[4,8,384]{2,1,0:T(8,128)S(1)}, bf16[3,8,128,128]{3,2,1,0:T(8,128)(2,1)S(1)}, bf16[384,256]{1,0:T(8,128)(2,1)S(1)}) custom-call(s32[1,128]{1,0:T(1,128)S(4)} %get-tuple-element.24.spots, s32[3,128]{1,0:T(4,128)S(4)} %get-tuple-element.23.table, bf16[64,8,128]{2,1,0:T(8,128)(2,1)S(1)} %copy-done, ...), custom_call_target="tpu_custom_call" | custom-call | tf_op jit(solution)/shard_map/pallas_call | solution.py:413
  67.0 1.4 %shard_map.103 = (bf16[2,8,384]{2,1,0:T(8,128)(2,1)}, f32[64,128]{1,0:T(8,128)S(1)}) custom-call(s32[3,128]{1,0:T(4,128)S(4)} %get-tuple-element.23.table, f32[4,8,384]{2,1,0:T(8,128)S(1)} %get-tuple-element.39.packed, bf16[3,8,128,128]{3,2,1,0:T(8,128)(2,1)S(1)} %get-tuple-element.40.fresh, bf16[3,128,128]{2,1,0:T(8,128)(2,1)S(1)} %get-tuple-element.37.zinv, ...), custom_call_target="tpu_custom_call" | custom-call | tf_op jit(solution)/shard_map/pallas_call | solution.py:494
  68.4 16.9 %all_to_all.20 = f32[64,1,128]{2,1,0:T(1,128)S(1)} all-to-all(f32[64,1,128]{2,1,0:T(1,128)S(1)} %bitcast.14), channel_id=1, replica_groups=mesh['y'=4,'z'=8,'c'=2,'dir'=4] {'y','z','c'}, dimensions={0} | all-to-all | bytes 65536 | tf_op jit(solution)/shard_map/all_to_all | solution.py:567
  85.3 0.7 shard_map.104
  (13 shorter events, 0.4 us)
Async XLA Ops:
  2.2 23.3 %all-to-all-start = ((bf16[8,8,3,8,128]{4,3,2,1,0:T(8,128)(2,1)}), bf16[8,8,3,8,128]{4,3,2,1,0:T(8,128)(2,1)S(1)}, u32[]{:S(2)}, u32[]{:S(2)}) async-start(bf16[8,8,3,8,128]{4,3,2,1,0:T(8,128)(2,1)} %get-tuple-element.30), calls=%async_computation | async-start | bytes 786432 | tf_op jit(solution)/shard_map/all_to_all | solution.py:551
  11.3 1.8 %collective-permute-start = (s32[1,256]{1,0:T(1,128)S(1)}, s32[1,256]{1,0:T(1,128)S(1)}, u32[]{:S(2)}, u32[]{:S(2)}) collective-permute-start(s32[1,256]{1,0:T(1,128)S(1)} %get-tuple-element.25), channel_id=1, source_target_pairs={{0,4},{4,0},{1,5},{5,1},{2,6},{6,2},{3,7},{7,3},{8,12},{12,8},{9,1... | collective-permute-start | bytes 3080 | tf_op jit(solution)/shard_map/ppermute | solution.py:553
  13.0 5.0 %collective-permute-start.1 = (s32[1,512]{1,0:T(1,128)S(1)}, s32[1,512]{1,0:T(1,128)S(1)}, u32[]{:S(2)}, u32[]{:S(2)}) collective-permute-start(s32[1,512]{1,0:T(1,128)S(1)} %constant_dynamic-update-slice_fusion.refs_0_), channel_id=1, source_target_pairs={{0,64},{64,128},{128,192},{192,0},{1,65},{65,129},{129,193},{193,1... | collective-permute-start | bytes 6152 | tf_op jit(solution)/shard_map/ppermute | solution.py:542
  14.3 3.9 %collective-permute-start.2 = (s32[1,512]{1,0:T(1,128)S(1)}, s32[1,512]{1,0:T(1,128)S(1)}, u32[]{:S(2)}, u32[]{:S(2)}) collective-permute-start(s32[1,512]{1,0:T(1,128)S(1)} %constant_dynamic-update-slice_fusion.refs_0_), channel_id=1, source_target_pairs={{0,128},{64,192},{128,0},{192,64},{1,129},{65,193},{129,1},{193,65... | collective-permute-start | bytes 6152 | tf_op jit(solution)/shard_map/ppermute | solution.py:542
  17.0 2.7 %collective-permute-start.3 = (s32[1,512]{1,0:T(1,128)S(1)}, s32[1,512]{1,0:T(1,128)S(1)}, u32[]{:S(2)}, u32[]{:S(2)}) collective-permute-start(s32[1,512]{1,0:T(1,128)S(1)} %constant_dynamic-update-slice_fusion.refs_0_), channel_id=1, source_target_pairs={{0,192},{64,0},{128,64},{192,128},{1,193},{65,1},{129,65},{193,129... | collective-permute-start | bytes 6152 | tf_op jit(solution)/shard_map/ppermute | solution.py:542
  26.6 15.3 %all-to-all-start.1 = ((bf16[8,32,8,128]{3,2,1,0:T(8,128)(2,1)}), bf16[8,32,8,128]{3,2,1,0:T(8,128)(2,1)}, u32[]{:S(2)}, u32[]{:S(2)}) async-start(bf16[8,32,8,128]{3,2,1,0:T(8,128)(2,1)} %bitcast.15), calls=%async_computation.1 | async-start | bytes 1048576 | tf_op jit(solution)/shard_map/all_to_all | solution.py:557
  45.0 13.3 %all-to-all-start.2 = ((bf16[32,3,8,128]{3,2,1,0:T(8,128)(2,1)}), bf16[32,3,8,128]{3,2,1,0:T(8,128)(2,1)S(1)}, u32[]{:S(2)}, u32[]{:S(2)}) async-start(bf16[32,3,8,128]{3,2,1,0:T(8,128)(2,1)} %shard_map.101.refs_8_), calls=%async_computation.2 | async-start | bytes 393216 | tf_op jit(solution)/shard_map/all_to_all | solution.py:562
  50.1 11.1 %collective-permute-start.6 = (bf16[64,8,128]{2,1,0:T(8,128)(2,1)}, bf16[64,8,128]{2,1,0:T(8,128)(2,1)S(1)}, u32[]{:S(2)}, u32[]{:S(2)}) collective-permute-start(bf16[64,8,128]{2,1,0:T(8,128)(2,1)} %get-tuple-element.34), channel_id=1, source_target_pairs={{0,64},{64,128},{128,192},{192,0},{1,65},{65,129},{129,193},{193,1... | collective-permute-start | bytes 393224 | tf_op jit(solution)/shard_map/ppermute | solution.py:542
  51.3 10.3 %collective-permute-start.4 = (bf16[64,8,128]{2,1,0:T(8,128)(2,1)}, bf16[64,8,128]{2,1,0:T(8,128)(2,1)S(1)}, u32[]{:S(2)}, u32[]{:S(2)}) collective-permute-start(bf16[64,8,128]{2,1,0:T(8,128)(2,1)} %get-tuple-element.32), channel_id=1, source_target_pairs={{0,192},{64,0},{128,64},{192,128},{1,193},{65,1},{129,65},{193,129... | collective-permute-start | bytes 393224 | tf_op jit(solution)/shard_map/ppermute | solution.py:542
  52.9 8.9 %collective-permute-start.5 = (bf16[64,8,128]{2,1,0:T(8,128)(2,1)}, bf16[64,8,128]{2,1,0:T(8,128)(2,1)S(1)}, u32[]{:S(2)}, u32[]{:S(2)}) collective-permute-start(bf16[64,8,128]{2,1,0:T(8,128)(2,1)} %get-tuple-element.33), channel_id=1, source_target_pairs={{0,128},{64,192},{128,0},{192,64},{1,129},{65,193},{129,1},{193,65... | collective-permute-start | bytes 393224 | tf_op jit(solution)/shard_map/ppermute | solution.py:542
  58.2 8.7 %collective-permute-start.11 = (bf16[96,8,128]{2,1,0:T(8,128)(2,1)S(1)}, bf16[96,8,128]{2,1,0:T(8,128)(2,1)S(1)}, u32[]{:S(2)}, u32[]{:S(2)}) collective-permute-start(bf16[96,8,128]{2,1,0:T(8,128)(2,1)S(1)} %bitcast.11), channel_id=1, source_target_pairs={{0,4},{4,0},{1,5},{5,1},{2,6},{6,2},{3,7},{7,3},{8,12},{12,8},{9,1... | collective-permute-start | bytes 589832 | tf_op jit(solution)/shard_map/ppermute | solution.py:564
  61.2 1.7 %collective-permute-start.7 = (bf16[64,8,128]{2,1,0:T(8,128)(2,1)}, bf16[64,8,128]{2,1,0:T(8,128)(2,1)S(1)}, u32[]{:S(2)}, u32[]{:S(2)}) collective-permute-start(bf16[64,8,128]{2,1,0:T(8,128)(2,1)} %get-tuple-element.31.refs_0_), channel_id=1, source_target_pairs={{0,4},{4,0},{1,5},{5,1},{2,6},{6,2},{3,7},{7,3},{8,12},{12,8},{9,1... | collective-permute-start | bytes 393224 | tf_op jit(solution)/shard_map/ppermute | solution.py:559
  61.2 1.7 %collective-permute-start.10 = (bf16[64,8,128]{2,1,0:T(8,128)(2,1)S(1)}, bf16[64,8,128]{2,1,0:T(8,128)(2,1)S(1)}, u32[]{:S(2)}, u32[]{:S(2)}) collective-permute-start(bf16[64,8,128]{2,1,0:T(8,128)(2,1)S(1)} %collective-permute-done.6.refs_3_), channel_id=1, source_target_pairs={{0,4},{4,0},{1,5},{5,1},{2,6},{6,2},{3,7},{7,3},{8,12},{12,8},{9,1... | collective-permute-start | bytes 393224 | tf_op jit(solution)/shard_map/ppermute | solution.py:559
  61.7 1.4 %collective-permute-start.8 = (bf16[64,8,128]{2,1,0:T(8,128)(2,1)S(1)}, bf16[64,8,128]{2,1,0:T(8,128)(2,1)S(1)}, u32[]{:S(2)}, u32[]{:S(2)}) collective-permute-start(bf16[64,8,128]{2,1,0:T(8,128)(2,1)S(1)} %collective-permute-done.4.refs_1_), channel_id=1, source_target_pairs={{0,4},{4,0},{1,5},{5,1},{2,6},{6,2},{3,7},{7,3},{8,12},{12,8},{9,1... | collective-permute-start | bytes 393224 | tf_op jit(solution)/shard_map/ppermute | solution.py:559
  61.8 2.0 %collective-permute-start.9 = (bf16[64,8,128]{2,1,0:T(8,128)(2,1)S(1)}, bf16[64,8,128]{2,1,0:T(8,128)(2,1)S(1)}, u32[]{:S(2)}, u32[]{:S(2)}) collective-permute-start(bf16[64,8,128]{2,1,0:T(8,128)(2,1)S(1)} %collective-permute-done.5.refs_2_), channel_id=1, source_target_pairs={{0,4},{4,0},{1,5},{5,1},{2,6},{6,2},{3,7},{7,3},{8,12},{12,8},{9,1... | collective-permute-start | bytes 393224 | tf_op jit(solution)/shard_map/ppermute | solution.py:559
  63.8 0.9 %copy-start = (bf16[64,8,128]{2,1,0:T(8,128)(2,1)S(1)}, bf16[64,8,128]{2,1,0:T(8,128)(2,1)}, u32[]{:S(2)}) copy-start(bf16[64,8,128]{2,1,0:T(8,128)(2,1)} %get-tuple-element.31.refs_0_) | copy-start | bytes 393220

commit v10 on v9

--- a/solution.py
+++ b/solution.py
@@ -13,7 +13,7 @@
 E = ("y", "z", "c")
 BLOCK_CAP = 4
 CHUNK = 8
-FETCHED = 8
+FETCHED = 24
 SMALL = 8 << 20
 SWAP = [(0, 1), (1, 0)]
 
@@ -556,7 +556,8 @@
     first, later = picks(lists, held, cap)
     got = lax.all_to_all(first.reshape(GROUPS, cap, dirs, tile), ("y", "c"), 0, 0, tiled=True)
     near = [later[0]] + [shifted(later[s], "y", Y, -s) for s in range(1, Y)]
-    cross = [lax.ppermute(piece, "c", SWAP) for piece in near]
+    cross = [lax.ppermute(near[0], "c", SWAP)]
+    cross += [lax.ppermute(piece, "c", SWAP) for piece in near[1:]]
     top, inverse, driven = stage(counts, ztiles, zinv, incident)
     fanned = first_step(spots, got.reshape(GROUPS * cap, dirs, tile), top, ztiles, inverse, driven)
     here = lax.all_to_all(fanned, ("y", "z"), 0, 0, tiled=True).reshape(Y * Z * rows, dirs, tile)

time: 86.6 us -> 85.6 us (0.988)
  Pallas kernels: 16.5 us -> 15.5 us
    pallas_call x1, Pallas kernels: 3.04 us -> 2.17 us  [first_step(): kernel_call(first_kernel, SMALL, out_shape=pltpu.HBM((Y * Z, rows, dirs,...]
  transfers between devices with their start and end apart: 15 -> 15, of which waited for: 9 -> 8; matrix products, arithmetic and copies ran while one was open for 0% -> 0% of each run, Pallas kernels for 10% -> 10%
where the time goes in v10:
time: 85.6 us; the launch traced here: 85.1 us
  starting transfers between devices  33.5 us (39%)
  waiting for transfers between devices  17.5 us (20%)
  blocking collectives  16.9 us (20%)
  Pallas kernels  15.5 us (18%)
  local copies, waits for them, and re-layouts  0.91 us (1%)
    all_to_all x1, blocking collectives, march(): lax.all_to_all(far.reshape(owners, 1, 128), E, 0, 0, tiled=True)  16.9 us
    ppermute x6, starting transfers between devices, shifted(): lax.ppermute(value, axis, [(i, (i + shift) % length) for i in range(lengt...  9.25 us
    all_to_all x1, starting transfers between devices, march(): lax.all_to_all(outgoing, 'z', 0, 0, tiled=True).reshape(-1, dirs, tile)  9.02 us
    all_to_all x1, starting transfers between devices, march(): lax.all_to_all(first.reshape(GROUPS, cap, dirs, tile), ('y', 'c'), 0, 0,...  5.86 us
    all_to_all x1, waiting for transfers between devices, march(): lax.all_to_all(outgoing, 'z', 0, 0, tiled=True).reshape(-1, dirs, tile)  5.13 us
    all_to_all x1, waiting for transfers between devices, march(): lax.all_to_all(first.reshape(GROUPS, cap, dirs, tile), ('y', 'c'), 0, 0,...  5.04 us
    all_to_all x1, starting transfers between devices, march(): lax.all_to_all(fanned, ('y', 'z'), 0, 0, tiled=True)  3.88 us
    all_to_all x1, waiting for transfers between devices, march(): lax.all_to_all(fanned, ('y', 'z'), 0, 0, tiled=True)  3.87 us
  transfers between devices with their start and end apart: 15, of which 8 were waited for; matrix products, arithmetic and copies ran while one was open for 0% of the time, Pallas kernels for 10%

profile of v10, /device:TPU:1, one launch (start us, length us, event | category | flops | bytes accessed | tf_op | source)
XLA Modules:
  0.0 85.1 jit_solution(1724020242736051401)
XLA Ops:
  0.6 1.6 %shard_map.96 = (bf16[8,8,3,8,128]{4,3,2,1,0:T(8,128)(2,1)}, s32[1,256]{1,0:T(1,128)S(1)}) custom-call(bf16[8,8,384]{2,1,0:T(8,128)(2,1)} %history.1, s32[3,32]{1,0:T(4,128)} %columns_hbm.1, s32[3,32]{1,0:T(4,128)} %lags_hbm.1), custom_call_target="tpu_custom_call" | custom-call | tf_op jit(solution)/shard_map/pallas_call | solution.py:75
  2.2 9.0 %all-to-all-start = ((bf16[8,8,3,8,128]{4,3,2,1,0:T(8,128)(2,1)}), bf16[8,8,3,8,128]{4,3,2,1,0:T(8,128)(2,1)S(1)}, u32[]{:S(2)}, u32[]{:S(2)}) async-start(bf16[8,8,3,8,128]{4,3,2,1,0:T(8,128)(2,1)} %get-tuple-element.30), calls=%async_computation | async-start | bytes 786432 | tf_op jit(solution)/shard_map/all_to_all | solution.py:551
  11.3 1.0 %collective-permute-start = (s32[1,256]{1,0:T(1,128)S(1)}, s32[1,256]{1,0:T(1,128)S(1)}, u32[]{:S(2)}, u32[]{:S(2)}) collective-permute-start(s32[1,256]{1,0:T(1,128)S(1)} %get-tuple-element.25), channel_id=1, source_target_pairs={{0,4},{4,0},{1,5},{5,1},{2,6},{6,2},{3,7},{7,3},{8,12},{12,8},{9,1... | collective-permute-start | bytes 3080 | tf_op jit(solution)/shard_map/ppermute | solution.py:553
  12.2 0.8 collective-permute-done
  13.0 1.3 %collective-permute-start.1 = (s32[1,512]{1,0:T(1,128)S(1)}, s32[1,512]{1,0:T(1,128)S(1)}, u32[]{:S(2)}, u32[]{:S(2)}) collective-permute-start(s32[1,512]{1,0:T(1,128)S(1)} %constant_dynamic-update-slice_fusion.refs_0_), channel_id=1, source_target_pairs={{0,64},{64,128},{128,192},{192,0},{1,65},{65,129},{129,193},{193,1... | collective-permute-start | bytes 6152 | tf_op jit(solution)/shard_map/ppermute | solution.py:542
  14.3 2.6 %collective-permute-start.2 = (s32[1,512]{1,0:T(1,128)S(1)}, s32[1,512]{1,0:T(1,128)S(1)}, u32[]{:S(2)}, u32[]{:S(2)}) collective-permute-start(s32[1,512]{1,0:T(1,128)S(1)} %constant_dynamic-update-slice_fusion.refs_0_), channel_id=1, source_target_pairs={{0,128},{64,192},{128,0},{192,64},{1,129},{65,193},{129,1},{193,65... | collective-permute-start | bytes 6152 | tf_op jit(solution)/shard_map/ppermute | solution.py:542
  17.0 1.1 %collective-permute-start.3 = (s32[1,512]{1,0:T(1,128)S(1)}, s32[1,512]{1,0:T(1,128)S(1)}, u32[]{:S(2)}, u32[]{:S(2)}) collective-permute-start(s32[1,512]{1,0:T(1,128)S(1)} %constant_dynamic-update-slice_fusion.refs_0_), channel_id=1, source_target_pairs={{0,192},{64,0},{128,64},{192,128},{1,193},{65,1},{129,65},{193,129... | collective-permute-start | bytes 6152 | tf_op jit(solution)/shard_map/ppermute | solution.py:542
  18.0 0.2 collective-permute-done.2.refs_2_
  18.3 1.4 %collective-permute-done.3.refs_3_ = s32[1,512]{1,0:T(1,128)S(1)} collective-permute-done((s32[1,512]{1,0:T(1,128)S(1)}, s32[1,512]{1,0:T(1,128)S(1)}, u32[]{:S(2)}, u32[]{:S(2)}) %collective-permute-start.3) | collective-permute-done | bytes 2080 | tf_op jit(solution)/shard_map/ppermute | solution.py:542
  19.7 0.7 shard_map.97
  20.4 5.1 %all-to-all-done = bf16[8,8,3,8,128]{4,3,2,1,0:T(8,128)(2,1)S(1)} async-done(((bf16[8,8,3,8,128]{4,3,2,1,0:T(8,128)(2,1)}), bf16[8,8,3,8,128]{4,3,2,1,0:T(8,128)(2,1)S(1)}, u32[]{:S(2)}, u32[]{:S(2)}) %all-to-all-start) | async-done | bytes 393248 | tf_op jit(solution)/shard_map/all_to_all | solution.py:551
  25.5 1.1 %shard_map.99 = bf16[256,8,128]{2,1,0:T(8,128)(2,1)} custom-call(s32[1,512]{1,0:T(1,128)S(4)} %get-tuple-element.26.refs_0_, s32[1,512]{1,0:T(1,128)S(4)} %get-tuple-element.27.refs_1_, s32[1,512]{1,0:T(1,128)S(4)} %get-tuple-element.28.refs_2_, s32[1,512]{1,0:T(1,128)S(4)} %get-tuple-element.29.refs_3_, bf16[192,8,128]{2,1,0:T(8,128)(2,1)S(1)} %bitcast.9), custom_call_target="tpu_custom_call" | custom-call | tf_op jit(solution)/shard_map/pallas_call | solution.py:235
  26.6 5.9 %all-to-all-start.1 = ((bf16[8,32,8,128]{3,2,1,0:T(8,128)(2,1)}), bf16[8,32,8,128]{3,2,1,0:T(8,128)(2,1)S(1)}, u32[]{:S(2)}, u32[]{:S(2)}) async-start(bf16[8,32,8,128]{3,2,1,0:T(8,128)(2,1)} %bitcast.16), calls=%async_computation.1 | async-start | bytes 1048576 | tf_op jit(solution)/shard_map/all_to_all | solution.py:557
  32.5 2.0 %shard_map.95 = (s32[1,128]{1,0:T(1,128)S(4)}, s32[1,128]{1,0:T(1,128)S(4)}, s32[3,128]{1,0:T(4,128)S(4)}) custom-call(s32[3]{0:T(128)} %counts.3, s32[3,32]{1,0:T(4,128)} %columns_hbm.1, s32[3,32]{1,0:T(4,128)} %lags_hbm.1), custom_call_target="tpu_custom_call" | custom-call | tf_op jit(solution)/shard_map/pallas_call | solution.py:154
  34.5 2.3 %shard_map.100 = (bf16[72,128,128]{2,1,0:T(8,128)(2,1)S(1)}, bf16[3,128,128]{2,1,0:T(8,128)(2,1)S(1)}, bf16[8,384]{1,0:T(8,128)(2,1)S(1)}) custom-call(s32[3]{0:T(128)} %counts.3, bf16[3,32,128,128]{3,2,1,0:T(8,128)(2,1)} %ztiles_hbm.5, bf16[3,128,128]{2,1,0:T(8,128)(2,1)} %zinv_hbm.1, bf16[2,8,384]{2,1,0:T(8,128)(2,1)} %refs_9_.1), custom_call_target="tpu_custom_call" | custom-call | tf_op jit(solution)/shard_map/pallas_call | solution.py:325
  36.8 5.0 %all-to-all-done.1 = bf16[8,32,8,128]{3,2,1,0:T(8,128)(2,1)S(1)} async-done(((bf16[8,32,8,128]{3,2,1,0:T(8,128)(2,1)}), bf16[8,32,8,128]{3,2,1,0:T(8,128)(2,1)S(1)}, u32[]{:S(2)}, u32[]{:S(2)}) %all-to-all-start.1) | async-done | bytes 524320 | tf_op jit(solution)/shard_map/all_to_all | solution.py:557
  41.8 2.2 %shard_map.101.refs_8_ = bf16[32,3,8,128]{3,2,1,0:T(8,128)(2,1)} custom-call(s32[1,128]{1,0:T(1,128)S(4)} %get-tuple-element.35.spots, bf16[256,8,128]{2,1,0:T(8,128)(2,1)S(1)} %bitcast.11, bf16[72,128,128]{2,1,0:T(8,128)(2,1)S(1)} %get-tuple-element.36.top, bf16[3,32,128,128]{3,2,1,0:T(8,128)(2,1)} %ztiles_hbm.5, ...), custom_call_target="tpu_custom_call" | custom-call | tf_op jit(solution)/shard_map/pallas_call | solution.py:366
  44.0 3.9 %all-to-all-start.2 = ((bf16[32,3,8,128]{3,2,1,0:T(8,128)(2,1)}), bf16[32,3,8,128]{3,2,1,0:T(8,128)(2,1)S(1)}, u32[]{:S(2)}, u32[]{:S(2)}) async-start(bf16[32,3,8,128]{3,2,1,0:T(8,128)(2,1)} %shard_map.101.refs_8_), calls=%async_computation.2 | async-start | bytes 393216 | tf_op jit(solution)/shard_map/all_to_all | solution.py:563
  47.9 1.3 %shard_map.98 = (bf16[64,8,128]{2,1,0:T(8,128)(2,1)}, bf16[64,8,128]{2,1,0:T(8,128)(2,1)}, bf16[64,8,128]{2,1,0:T(8,128)(2,1)}, bf16[64,8,128]{2,1,0:T(8,128)(2,1)}) custom-call(s32[1,512]{1,0:T(1,128)S(4)} %get-tuple-element.26.refs_0_, s32[1,512]{1,0:T(1,128)S(4)} %get-tuple-element.27.refs_1_, s32[1,512]{1,0:T(1,128)S(4)} %get-tuple-element.28.refs_2_, ...), custom_call_target="tpu_custom_call" | custom-call | tf_op jit(solution)/shard_map/pallas_call | solution.py:246
  49.1 1.2 %collective-permute-start.6 = (bf16[64,8,128]{2,1,0:T(8,128)(2,1)}, bf16[64,8,128]{2,1,0:T(8,128)(2,1)S(1)}, u32[]{:S(2)}, u32[]{:S(2)}) collective-permute-start(bf16[64,8,128]{2,1,0:T(8,128)(2,1)} %get-tuple-element.34), channel_id=1, source_target_pairs={{0,64},{64,128},{128,192},{192,0},{1,65},{65,129},{129,193},{193,1... | collective-permute-start | bytes 393224 | tf_op jit(solution)/shard_map/ppermute | solution.py:542
  50.4 1.5 %collective-permute-start.4 = (bf16[64,8,128]{2,1,0:T(8,128)(2,1)}, bf16[64,8,128]{2,1,0:T(8,128)(2,1)S(1)}, u32[]{:S(2)}, u32[]{:S(2)}) collective-permute-start(bf16[64,8,128]{2,1,0:T(8,128)(2,1)} %get-tuple-element.32), channel_id=1, source_target_pairs={{0,192},{64,0},{128,64},{192,128},{1,193},{65,1},{129,65},{193,129... | collective-permute-start | bytes 393224 | tf_op jit(solution)/shard_map/ppermute | solution.py:542
  51.9 1.5 %collective-permute-start.5 = (bf16[64,8,128]{2,1,0:T(8,128)(2,1)}, bf16[64,8,128]{2,1,0:T(8,128)(2,1)S(1)}, u32[]{:S(2)}, u32[]{:S(2)}) collective-permute-start(bf16[64,8,128]{2,1,0:T(8,128)(2,1)} %get-tuple-element.33), channel_id=1, source_target_pairs={{0,128},{64,192},{128,0},{192,64},{1,129},{65,193},{129,1},{193,65... | collective-permute-start | bytes 393224 | tf_op jit(solution)/shard_map/ppermute | solution.py:542
  53.4 3.9 %all-to-all-done.2 = bf16[32,3,8,128]{3,2,1,0:T(8,128)(2,1)S(1)} async-done(((bf16[32,3,8,128]{3,2,1,0:T(8,128)(2,1)}), bf16[32,3,8,128]{3,2,1,0:T(8,128)(2,1)S(1)}, u32[]{:S(2)}, u32[]{:S(2)}) %all-to-all-start.2) | async-done | bytes 196640 | tf_op jit(solution)/shard_map/all_to_all | solution.py:563
  57.3 2.9 %collective-permute-start.11 = (bf16[96,8,128]{2,1,0:T(8,128)(2,1)S(1)}, bf16[96,8,128]{2,1,0:T(8,128)(2,1)S(1)}, u32[]{:S(2)}, u32[]{:S(2)}) collective-permute-start(bf16[96,8,128]{2,1,0:T(8,128)(2,1)S(1)} %bitcast.12), channel_id=1, source_target_pairs={{0,4},{4,0},{1,5},{5,1},{2,6},{6,2},{3,7},{7,3},{8,12},{12,8},{9,1... | collective-permute-start | bytes 589832 | tf_op jit(solution)/shard_map/ppermute | solution.py:565
  60.2 0.5 collective-permute-start.10
  60.8 1.1 %collective-permute-start.9 = (bf16[64,8,128]{2,1,0:T(8,128)(2,1)S(1)}, bf16[64,8,128]{2,1,0:T(8,128)(2,1)S(1)}, u32[]{:S(2)}, u32[]{:S(2)}) collective-permute-start(bf16[64,8,128]{2,1,0:T(8,128)(2,1)S(1)} %collective-permute-done.5.refs_2_), channel_id=1, source_target_pairs={{0,4},{4,0},{1,5},{5,1},{2,6},{6,2},{3,7},{7,3},{8,12},{12,8},{9,1... | collective-permute-start | bytes 393224 | tf_op jit(solution)/shard_map/ppermute | solution.py:560
  62.1 0.8 collective-permute-done.9.refs_6_
  62.9 0.9 %copy-done = bf16[64,8,128]{2,1,0:T(8,128)(2,1)S(1)} copy-done((bf16[64,8,128]{2,1,0:T(8,128)(2,1)S(1)}, bf16[64,8,128]{2,1,0:T(8,128)(2,1)}, u32[]{:S(2)}) %copy-start) | copy-done | bytes 131096
  63.8 2.2 %shard_map.102 = (f32[4,8,384]{2,1,0:T(8,128)S(1)}, bf16[3,8,128,128]{3,2,1,0:T(8,128)(2,1)S(1)}, bf16[384,256]{1,0:T(8,128)(2,1)S(1)}) custom-call(s32[1,128]{1,0:T(1,128)S(4)} %get-tuple-element.24.spots, s32[3,128]{1,0:T(4,128)S(4)} %get-tuple-element.23.table, bf16[64,8,128]{2,1,0:T(8,128)(2,1)S(1)} %copy-done, ...), custom_call_target="tpu_custom_call" | custom-call | tf_op jit(solution)/shard_map/pallas_call | solution.py:413
  66.0 1.4 %shard_map.103 = (bf16[2,8,384]{2,1,0:T(8,128)(2,1)}, f32[64,128]{1,0:T(8,128)S(1)}) custom-call(s32[3,128]{1,0:T(4,128)S(4)} %get-tuple-element.23.table, f32[4,8,384]{2,1,0:T(8,128)S(1)} %get-tuple-element.39.packed, bf16[3,8,128,128]{3,2,1,0:T(8,128)(2,1)S(1)} %get-tuple-element.40.fresh, bf16[3,128,128]{2,1,0:T(8,128)(2,1)S(1)} %get-tuple-element.37.zinv, ...), custom_call_target="tpu_custom_call" | custom-call | tf_op jit(solution)/shard_map/pallas_call | solution.py:494
  67.5 16.9 %all_to_all.20 = f32[64,1,128]{2,1,0:T(1,128)S(1)} all-to-all(f32[64,1,128]{2,1,0:T(1,128)S(1)} %bitcast.15), channel_id=1, replica_groups=mesh['y'=4,'z'=8,'c'=2,'dir'=4] {'y','z','c'}, dimensions={0} | all-to-all | bytes 65536 | tf_op jit(solution)/shard_map/all_to_all | solution.py:568
  84.4 0.7 shard_map.104
  (13 shorter events, 0.4 us)
Async XLA Ops:
  2.2 23.3 %all-to-all-start = ((bf16[8,8,3,8,128]{4,3,2,1,0:T(8,128)(2,1)}), bf16[8,8,3,8,128]{4,3,2,1,0:T(8,128)(2,1)S(1)}, u32[]{:S(2)}, u32[]{:S(2)}) async-start(bf16[8,8,3,8,128]{4,3,2,1,0:T(8,128)(2,1)} %get-tuple-element.30), calls=%async_computation | async-start | bytes 786432 | tf_op jit(solution)/shard_map/all_to_all | solution.py:551
  11.3 1.8 %collective-permute-start = (s32[1,256]{1,0:T(1,128)S(1)}, s32[1,256]{1,0:T(1,128)S(1)}, u32[]{:S(2)}, u32[]{:S(2)}) collective-permute-start(s32[1,256]{1,0:T(1,128)S(1)} %get-tuple-element.25), channel_id=1, source_target_pairs={{0,4},{4,0},{1,5},{5,1},{2,6},{6,2},{3,7},{7,3},{8,12},{12,8},{9,1... | collective-permute-start | bytes 3080 | tf_op jit(solution)/shard_map/ppermute | solution.py:553
  13.0 5.0 %collective-permute-start.1 = (s32[1,512]{1,0:T(1,128)S(1)}, s32[1,512]{1,0:T(1,128)S(1)}, u32[]{:S(2)}, u32[]{:S(2)}) collective-permute-start(s32[1,512]{1,0:T(1,128)S(1)} %constant_dynamic-update-slice_fusion.refs_0_), channel_id=1, source_target_pairs={{0,64},{64,128},{128,192},{192,0},{1,65},{65,129},{129,193},{193,1... | collective-permute-start | bytes 6152 | tf_op jit(solution)/shard_map/ppermute | solution.py:542
  14.3 3.9 %collective-permute-start.2 = (s32[1,512]{1,0:T(1,128)S(1)}, s32[1,512]{1,0:T(1,128)S(1)}, u32[]{:S(2)}, u32[]{:S(2)}) collective-permute-start(s32[1,512]{1,0:T(1,128)S(1)} %constant_dynamic-update-slice_fusion.refs_0_), channel_id=1, source_target_pairs={{0,128},{64,192},{128,0},{192,64},{1,129},{65,193},{129,1},{193,65... | collective-permute-start | bytes 6152 | tf_op jit(solution)/shard_map/ppermute | solution.py:542
  17.0 2.7 %collective-permute-start.3 = (s32[1,512]{1,0:T(1,128)S(1)}, s32[1,512]{1,0:T(1,128)S(1)}, u32[]{:S(2)}, u32[]{:S(2)}) collective-permute-start(s32[1,512]{1,0:T(1,128)S(1)} %constant_dynamic-update-slice_fusion.refs_0_), channel_id=1, source_target_pairs={{0,192},{64,0},{128,64},{192,128},{1,193},{65,1},{129,65},{193,129... | collective-permute-start | bytes 6152 | tf_op jit(solution)/shard_map/ppermute | solution.py:542
  26.6 15.2 %all-to-all-start.1 = ((bf16[8,32,8,128]{3,2,1,0:T(8,128)(2,1)}), bf16[8,32,8,128]{3,2,1,0:T(8,128)(2,1)S(1)}, u32[]{:S(2)}, u32[]{:S(2)}) async-start(bf16[8,32,8,128]{3,2,1,0:T(8,128)(2,1)} %bitcast.16), calls=%async_computation.1 | async-start | bytes 1048576 | tf_op jit(solution)/shard_map/all_to_all | solution.py:557
  44.0 13.3 %all-to-all-start.2 = ((bf16[32,3,8,128]{3,2,1,0:T(8,128)(2,1)}), bf16[32,3,8,128]{3,2,1,0:T(8,128)(2,1)S(1)}, u32[]{:S(2)}, u32[]{:S(2)}) async-start(bf16[32,3,8,128]{3,2,1,0:T(8,128)(2,1)} %shard_map.101.refs_8_), calls=%async_computation.2 | async-start | bytes 393216 | tf_op jit(solution)/shard_map/all_to_all | solution.py:563
  49.1 11.0 %collective-permute-start.6 = (bf16[64,8,128]{2,1,0:T(8,128)(2,1)}, bf16[64,8,128]{2,1,0:T(8,128)(2,1)S(1)}, u32[]{:S(2)}, u32[]{:S(2)}) collective-permute-start(bf16[64,8,128]{2,1,0:T(8,128)(2,1)} %get-tuple-element.34), channel_id=1, source_target_pairs={{0,64},{64,128},{128,192},{192,0},{1,65},{65,129},{129,193},{193,1... | collective-permute-start | bytes 393224 | tf_op jit(solution)/shard_map/ppermute | solution.py:542
  50.4 10.3 %collective-permute-start.4 = (bf16[64,8,128]{2,1,0:T(8,128)(2,1)}, bf16[64,8,128]{2,1,0:T(8,128)(2,1)S(1)}, u32[]{:S(2)}, u32[]{:S(2)}) collective-permute-start(bf16[64,8,128]{2,1,0:T(8,128)(2,1)} %get-tuple-element.32), channel_id=1, source_target_pairs={{0,192},{64,0},{128,64},{192,128},{1,193},{65,1},{129,65},{193,129... | collective-permute-start | bytes 393224 | tf_op jit(solution)/shard_map/ppermute | solution.py:542
  51.9 8.9 %collective-permute-start.5 = (bf16[64,8,128]{2,1,0:T(8,128)(2,1)}, bf16[64,8,128]{2,1,0:T(8,128)(2,1)S(1)}, u32[]{:S(2)}, u32[]{:S(2)}) collective-permute-start(bf16[64,8,128]{2,1,0:T(8,128)(2,1)} %get-tuple-element.33), channel_id=1, source_target_pairs={{0,128},{64,192},{128,0},{192,64},{1,129},{65,193},{129,1},{193,65... | collective-permute-start | bytes 393224 | tf_op jit(solution)/shard_map/ppermute | solution.py:542
  57.3 8.7 %collective-permute-start.11 = (bf16[96,8,128]{2,1,0:T(8,128)(2,1)S(1)}, bf16[96,8,128]{2,1,0:T(8,128)(2,1)S(1)}, u32[]{:S(2)}, u32[]{:S(2)}) collective-permute-start(bf16[96,8,128]{2,1,0:T(8,128)(2,1)S(1)} %bitcast.12), channel_id=1, source_target_pairs={{0,4},{4,0},{1,5},{5,1},{2,6},{6,2},{3,7},{7,3},{8,12},{12,8},{9,1... | collective-permute-start | bytes 589832 | tf_op jit(solution)/shard_map/ppermute | solution.py:565
  60.2 1.7 %collective-permute-start.7 = (bf16[64,8,128]{2,1,0:T(8,128)(2,1)}, bf16[64,8,128]{2,1,0:T(8,128)(2,1)S(1)}, u32[]{:S(2)}, u32[]{:S(2)}) collective-permute-start(bf16[64,8,128]{2,1,0:T(8,128)(2,1)} %get-tuple-element.31.refs_0_), channel_id=1, source_target_pairs={{0,4},{4,0},{1,5},{5,1},{2,6},{6,2},{3,7},{7,3},{8,12},{12,8},{9,1... | collective-permute-start | bytes 393224 | tf_op jit(solution)/shard_map/ppermute | solution.py:559
  60.2 1.7 %collective-permute-start.10 = (bf16[64,8,128]{2,1,0:T(8,128)(2,1)S(1)}, bf16[64,8,128]{2,1,0:T(8,128)(2,1)S(1)}, u32[]{:S(2)}, u32[]{:S(2)}) collective-permute-start(bf16[64,8,128]{2,1,0:T(8,128)(2,1)S(1)} %collective-permute-done.6.refs_3_), channel_id=1, source_target_pairs={{0,4},{4,0},{1,5},{5,1},{2,6},{6,2},{3,7},{7,3},{8,12},{12,8},{9,1... | collective-permute-start | bytes 393224 | tf_op jit(solution)/shard_map/ppermute | solution.py:560
  60.7 1.4 %collective-permute-start.8 = (bf16[64,8,128]{2,1,0:T(8,128)(2,1)S(1)}, bf16[64,8,128]{2,1,0:T(8,128)(2,1)S(1)}, u32[]{:S(2)}, u32[]{:S(2)}) collective-permute-start(bf16[64,8,128]{2,1,0:T(8,128)(2,1)S(1)} %collective-permute-done.4.refs_1_), channel_id=1, source_target_pairs={{0,4},{4,0},{1,5},{5,1},{2,6},{6,2},{3,7},{7,3},{8,12},{12,8},{9,1... | collective-permute-start | bytes 393224 | tf_op jit(solution)/shard_map/ppermute | solution.py:560
  60.8 2.1 %collective-permute-start.9 = (bf16[64,8,128]{2,1,0:T(8,128)(2,1)S(1)}, bf16[64,8,128]{2,1,0:T(8,128)(2,1)S(1)}, u32[]{:S(2)}, u32[]{:S(2)}) collective-permute-start(bf16[64,8,128]{2,1,0:T(8,128)(2,1)S(1)} %collective-permute-done.5.refs_2_), channel_id=1, source_target_pairs={{0,4},{4,0},{1,5},{5,1},{2,6},{6,2},{3,7},{7,3},{8,12},{12,8},{9,1... | collective-permute-start | bytes 393224 | tf_op jit(solution)/shard_map/ppermute | solution.py:560
  62.9 0.9 %copy-start = (bf16[64,8,128]{2,1,0:T(8,128)(2,1)S(1)}, bf16[64,8,128]{2,1,0:T(8,128)(2,1)}, u32[]{:S(2)}) copy-start(bf16[64,8,128]{2,1,0:T(8,128)(2,1)} %get-tuple-element.31.refs_0_) | copy-start | bytes 393220

commit v11 on v10

--- a/solution.py
+++ b/solution.py
@@ -388,10 +388,17 @@
     counts = [spots[0, rows * slots + row] for row in range(rows)]
     for row in range(rows):
         live_tiles(counts[row], ztiles_hbm.at[row], ztiles.at[row], tile_sems, row, "start")
-    copies = start_all([(incident_hbm.at[1], incident), (fanned.at[0], before), (basis_hbm, basis)], sems)
-    for shift in range(Y):
+    own = [
+        (source.at[pl.ds(other * cap, cap)], pool.at[pl.ds(other * cap, cap)])
+        for other, source in enumerate((near[0], cross[0]))
+    ]
+    own = start_all(own, sems)
+    copies = start_all([(incident_hbm.at[1], incident), (fanned.at[0], before), (basis_hbm, basis)], sems, C)
+    for shift in range(1, Y):
         for other, source in enumerate((near[shift], cross[shift])):
             pool[pl.ds((shift * C + other) * cap, cap)] = source[pl.ds(other * cap, cap)]
+    for copy in own:
+        copy.wait()
     for row in range(rows):
         live_tiles(counts[row], ztiles_hbm.at[row], ztiles.at[row], tile_sems, row, "wait")
         for k in range(CHUNK):
@@ -418,20 +425,23 @@
             pltpu.VMEM((rows, CHUNK, tile, tile), ztiles.dtype),
             pltpu.VMEM(basis.shape, basis.dtype),
         ),
-        in_specs=[smem(), smem()] + [vmem()] * (2 * Y) + [hbm()] * 4,
+        in_specs=[smem(), smem()] + ([hbm()] + [vmem()] * (Y - 1)) * 2 + [hbm()] * 4,
         out_specs=[vmem()] * 3,
         scratch_shapes=[
             pltpu.VMEM((2 * Y * cap, dirs, tile), jnp.bfloat16),
             pltpu.VMEM(ztiles.shape, ztiles.dtype),
             pltpu.VMEM(fanned.shape[1:], fanned.dtype),
             pltpu.VMEM(incident.shape[1:], incident.dtype),
-            pltpu.SemaphoreType.DMA((3,)),
+            pltpu.SemaphoreType.DMA((C + 3,)),
             pltpu.SemaphoreType.DMA((rows, ztiles.shape[1] // CHUNK)),
         ],
     )(
         scalar_core(spots),
         scalar_core(table),
-        *[near_core(piece) for piece in (*near, *cross)],
+        off_core(near[0]),
+        *[near_core(piece) for piece in near[1:]],
+        off_core(cross[0]),
+        *[near_core(piece) for piece in cross[1:]],
         off_core(fanned),
         off_core(incident),
         off_core(ztiles),

time: 85.6 us -> 85.1 us (level)
  local copies, waits for them, and re-layouts: 0.91 us -> 0.01 us
    unnamed x3, local copies, waits for them, and re-layouts: 0.91 us -> 0.01 us
  transfers between devices with their start and end apart: 15 -> 15, of which waited for: 8 -> 8; matrix products, arithmetic and copies ran while one was open for 0% -> 0% of each run, Pallas kernels for 10% -> 11%
where the time goes in v11:
time: 85.1 us; the launch traced here: 84.6 us
  starting transfers between devices  33.5 us (39%)
  waiting for transfers between devices  17.5 us (21%)
  blocking collectives  16.8 us (20%)
  Pallas kernels  16 us (19%)
    all_to_all x1, blocking collectives, march(): lax.all_to_all(far.reshape(owners, 1, 128), E, 0, 0, tiled=True)  16.8 us
    ppermute x6, starting transfers between devices, shifted(): lax.ppermute(value, axis, [(i, (i + shift) % length) for i in range(lengt...  9.25 us
    all_to_all x1, starting transfers between devices, march(): lax.all_to_all(outgoing, 'z', 0, 0, tiled=True).reshape(-1, dirs, tile)  9.02 us
    all_to_all x1, starting transfers between devices, march(): lax.all_to_all(first.reshape(GROUPS, cap, dirs, tile), ('y', 'c'), 0, 0,...  5.86 us
    all_to_all x1, waiting for transfers between devices, march(): lax.all_to_all(outgoing, 'z', 0, 0, tiled=True).reshape(-1, dirs, tile)  5.13 us
    all_to_all x1, waiting for transfers between devices, march(): lax.all_to_all(first.reshape(GROUPS, cap, dirs, tile), ('y', 'c'), 0, 0,...  5.04 us
    all_to_all x1, starting transfers between devices, march(): lax.all_to_all(fanned, ('y', 'z'), 0, 0, tiled=True)  3.88 us
    all_to_all x1, waiting for transfers between devices, march(): lax.all_to_all(fanned, ('y', 'z'), 0, 0, tiled=True)  3.87 us
  transfers between devices with their start and end apart: 15, of which 8 were waited for; matrix products, arithmetic and copies ran while one was open for 0% of the time, Pallas kernels for 11%

profile of v11, /device:TPU:1, one launch (start us, length us, event | category | flops | bytes accessed | tf_op | source)
XLA Modules:
  0.0 84.6 jit_solution(18128944844574032094)
XLA Ops:
  0.6 1.6 %shard_map.96 = (bf16[8,8,3,8,128]{4,3,2,1,0:T(8,128)(2,1)}, s32[1,256]{1,0:T(1,128)S(1)}) custom-call(bf16[8,8,384]{2,1,0:T(8,128)(2,1)} %history.1, s32[3,32]{1,0:T(4,128)} %columns_hbm.1, s32[3,32]{1,0:T(4,128)} %lags_hbm.1), custom_call_target="tpu_custom_call" | custom-call | tf_op jit(solution)/shard_map/pallas_call | solution.py:75
  2.2 9.0 %all-to-all-start = ((bf16[8,8,3,8,128]{4,3,2,1,0:T(8,128)(2,1)}), bf16[8,8,3,8,128]{4,3,2,1,0:T(8,128)(2,1)S(1)}, u32[]{:S(2)}, u32[]{:S(2)}) async-start(bf16[8,8,3,8,128]{4,3,2,1,0:T(8,128)(2,1)} %get-tuple-element.30), calls=%async_computation | async-start | bytes 786432 | tf_op jit(solution)/shard_map/all_to_all | solution.py:561
  11.3 1.0 %collective-permute-start = (s32[1,256]{1,0:T(1,128)S(1)}, s32[1,256]{1,0:T(1,128)S(1)}, u32[]{:S(2)}, u32[]{:S(2)}) collective-permute-start(s32[1,256]{1,0:T(1,128)S(1)} %get-tuple-element.25), channel_id=1, source_target_pairs={{0,4},{4,0},{1,5},{5,1},{2,6},{6,2},{3,7},{7,3},{8,12},{12,8},{9,1... | collective-permute-start | bytes 3080 | tf_op jit(solution)/shard_map/ppermute | solution.py:563
  12.2 0.8 collective-permute-done
  13.0 1.3 %collective-permute-start.1 = (s32[1,512]{1,0:T(1,128)S(1)}, s32[1,512]{1,0:T(1,128)S(1)}, u32[]{:S(2)}, u32[]{:S(2)}) collective-permute-start(s32[1,512]{1,0:T(1,128)S(1)} %constant_dynamic-update-slice_fusion.refs_0_), channel_id=1, source_target_pairs={{0,64},{64,128},{128,192},{192,0},{1,65},{65,129},{129,193},{193,1... | collective-permute-start | bytes 6152 | tf_op jit(solution)/shard_map/ppermute | solution.py:552
  14.3 2.6 %collective-permute-start.2 = (s32[1,512]{1,0:T(1,128)S(1)}, s32[1,512]{1,0:T(1,128)S(1)}, u32[]{:S(2)}, u32[]{:S(2)}) collective-permute-start(s32[1,512]{1,0:T(1,128)S(1)} %constant_dynamic-update-slice_fusion.refs_0_), channel_id=1, source_target_pairs={{0,128},{64,192},{128,0},{192,64},{1,129},{65,193},{129,1},{193,65... | collective-permute-start | bytes 6152 | tf_op jit(solution)/shard_map/ppermute | solution.py:552
  17.0 1.1 %collective-permute-start.3 = (s32[1,512]{1,0:T(1,128)S(1)}, s32[1,512]{1,0:T(1,128)S(1)}, u32[]{:S(2)}, u32[]{:S(2)}) collective-permute-start(s32[1,512]{1,0:T(1,128)S(1)} %constant_dynamic-update-slice_fusion.refs_0_), channel_id=1, source_target_pairs={{0,192},{64,0},{128,64},{192,128},{1,193},{65,1},{129,65},{193,129... | collective-permute-start | bytes 6152 | tf_op jit(solution)/shard_map/ppermute | solution.py:552
  18.0 0.2 collective-permute-done.2.refs_2_
  18.3 1.4 %collective-permute-done.3.refs_3_ = s32[1,512]{1,0:T(1,128)S(1)} collective-permute-done((s32[1,512]{1,0:T(1,128)S(1)}, s32[1,512]{1,0:T(1,128)S(1)}, u32[]{:S(2)}, u32[]{:S(2)}) %collective-permute-start.3) | collective-permute-done | bytes 2080 | tf_op jit(solution)/shard_map/ppermute | solution.py:552
  19.7 0.7 shard_map.97
  20.4 5.1 %all-to-all-done = bf16[8,8,3,8,128]{4,3,2,1,0:T(8,128)(2,1)S(1)} async-done(((bf16[8,8,3,8,128]{4,3,2,1,0:T(8,128)(2,1)}), bf16[8,8,3,8,128]{4,3,2,1,0:T(8,128)(2,1)S(1)}, u32[]{:S(2)}, u32[]{:S(2)}) %all-to-all-start) | async-done | bytes 393248 | tf_op jit(solution)/shard_map/all_to_all | solution.py:561
  25.5 1.1 %shard_map.99 = bf16[256,8,128]{2,1,0:T(8,128)(2,1)} custom-call(s32[1,512]{1,0:T(1,128)S(4)} %get-tuple-element.26.refs_0_, s32[1,512]{1,0:T(1,128)S(4)} %get-tuple-element.27.refs_1_, s32[1,512]{1,0:T(1,128)S(4)} %get-tuple-element.28.refs_2_, s32[1,512]{1,0:T(1,128)S(4)} %get-tuple-element.29.refs_3_, bf16[192,8,128]{2,1,0:T(8,128)(2,1)S(1)} %bitcast.9), custom_call_target="tpu_custom_call" | custom-call | tf_op jit(solution)/shard_map/pallas_call | solution.py:235
  26.6 5.9 %all-to-all-start.1 = ((bf16[8,32,8,128]{3,2,1,0:T(8,128)(2,1)}), bf16[8,32,8,128]{3,2,1,0:T(8,128)(2,1)S(1)}, u32[]{:S(2)}, u32[]{:S(2)}) async-start(bf16[8,32,8,128]{3,2,1,0:T(8,128)(2,1)} %bitcast.16), calls=%async_computation.1 | async-start | bytes 1048576 | tf_op jit(solution)/shard_map/all_to_all | solution.py:567
  32.5 2.0 %shard_map.95 = (s32[1,128]{1,0:T(1,128)S(4)}, s32[1,128]{1,0:T(1,128)S(4)}, s32[3,128]{1,0:T(4,128)S(4)}) custom-call(s32[3]{0:T(128)} %counts.3, s32[3,32]{1,0:T(4,128)} %columns_hbm.1, s32[3,32]{1,0:T(4,128)} %lags_hbm.1), custom_call_target="tpu_custom_call" | custom-call | tf_op jit(solution)/shard_map/pallas_call | solution.py:154
  34.5 2.3 %shard_map.100 = (bf16[72,128,128]{2,1,0:T(8,128)(2,1)S(1)}, bf16[3,128,128]{2,1,0:T(8,128)(2,1)S(1)}, bf16[8,384]{1,0:T(8,128)(2,1)S(1)}) custom-call(s32[3]{0:T(128)} %counts.3, bf16[3,32,128,128]{3,2,1,0:T(8,128)(2,1)} %ztiles_hbm.5, bf16[3,128,128]{2,1,0:T(8,128)(2,1)} %zinv_hbm.1, bf16[2,8,384]{2,1,0:T(8,128)(2,1)} %refs_9_.1), custom_call_target="tpu_custom_call" | custom-call | tf_op jit(solution)/shard_map/pallas_call | solution.py:325
  36.8 5.0 %all-to-all-done.1 = bf16[8,32,8,128]{3,2,1,0:T(8,128)(2,1)S(1)} async-done(((bf16[8,32,8,128]{3,2,1,0:T(8,128)(2,1)}), bf16[8,32,8,128]{3,2,1,0:T(8,128)(2,1)S(1)}, u32[]{:S(2)}, u32[]{:S(2)}) %all-to-all-start.1) | async-done | bytes 524320 | tf_op jit(solution)/shard_map/all_to_all | solution.py:567
  41.8 2.2 %shard_map.101.refs_8_ = bf16[32,3,8,128]{3,2,1,0:T(8,128)(2,1)} custom-call(s32[1,128]{1,0:T(1,128)S(4)} %get-tuple-element.35.spots, bf16[256,8,128]{2,1,0:T(8,128)(2,1)S(1)} %bitcast.11, bf16[72,128,128]{2,1,0:T(8,128)(2,1)S(1)} %get-tuple-element.36.top, bf16[3,32,128,128]{3,2,1,0:T(8,128)(2,1)} %ztiles_hbm.5, ...), custom_call_target="tpu_custom_call" | custom-call | tf_op jit(solution)/shard_map/pallas_call | solution.py:366
  44.0 3.9 %all-to-all-start.2 = ((bf16[32,3,8,128]{3,2,1,0:T(8,128)(2,1)}), bf16[32,3,8,128]{3,2,1,0:T(8,128)(2,1)S(1)}, u32[]{:S(2)}, u32[]{:S(2)}) async-start(bf16[32,3,8,128]{3,2,1,0:T(8,128)(2,1)} %shard_map.101.refs_8_), calls=%async_computation.2 | async-start | bytes 393216 | tf_op jit(solution)/shard_map/all_to_all | solution.py:573
  47.9 1.3 %shard_map.98 = (bf16[64,8,128]{2,1,0:T(8,128)(2,1)}, bf16[64,8,128]{2,1,0:T(8,128)(2,1)}, bf16[64,8,128]{2,1,0:T(8,128)(2,1)}, bf16[64,8,128]{2,1,0:T(8,128)(2,1)}) custom-call(s32[1,512]{1,0:T(1,128)S(4)} %get-tuple-element.26.refs_0_, s32[1,512]{1,0:T(1,128)S(4)} %get-tuple-element.27.refs_1_, s32[1,512]{1,0:T(1,128)S(4)} %get-tuple-element.28.refs_2_, ...), custom_call_target="tpu_custom_call" | custom-call | tf_op jit(solution)/shard_map/pallas_call | solution.py:246
  49.1 1.2 %collective-permute-start.6 = (bf16[64,8,128]{2,1,0:T(8,128)(2,1)}, bf16[64,8,128]{2,1,0:T(8,128)(2,1)S(1)}, u32[]{:S(2)}, u32[]{:S(2)}) collective-permute-start(bf16[64,8,128]{2,1,0:T(8,128)(2,1)} %get-tuple-element.34), channel_id=1, source_target_pairs={{0,64},{64,128},{128,192},{192,0},{1,65},{65,129},{129,193},{193,1... | collective-permute-start | bytes 393224 | tf_op jit(solution)/shard_map/ppermute | solution.py:552
  50.4 1.5 %collective-permute-start.4 = (bf16[64,8,128]{2,1,0:T(8,128)(2,1)}, bf16[64,8,128]{2,1,0:T(8,128)(2,1)S(1)}, u32[]{:S(2)}, u32[]{:S(2)}) collective-permute-start(bf16[64,8,128]{2,1,0:T(8,128)(2,1)} %get-tuple-element.32), channel_id=1, source_target_pairs={{0,192},{64,0},{128,64},{192,128},{1,193},{65,1},{129,65},{193,129... | collective-permute-start | bytes 393224 | tf_op jit(solution)/shard_map/ppermute | solution.py:552
  51.9 1.5 %collective-permute-start.5 = (bf16[64,8,128]{2,1,0:T(8,128)(2,1)}, bf16[64,8,128]{2,1,0:T(8,128)(2,1)S(1)}, u32[]{:S(2)}, u32[]{:S(2)}) collective-permute-start(bf16[64,8,128]{2,1,0:T(8,128)(2,1)} %get-tuple-element.33), channel_id=1, source_target_pairs={{0,128},{64,192},{128,0},{192,64},{1,129},{65,193},{129,1},{193,65... | collective-permute-start | bytes 393224 | tf_op jit(solution)/shard_map/ppermute | solution.py:552
  53.4 3.9 %all-to-all-done.2 = bf16[32,3,8,128]{3,2,1,0:T(8,128)(2,1)S(1)} async-done(((bf16[32,3,8,128]{3,2,1,0:T(8,128)(2,1)}), bf16[32,3,8,128]{3,2,1,0:T(8,128)(2,1)S(1)}, u32[]{:S(2)}, u32[]{:S(2)}) %all-to-all-start.2) | async-done | bytes 196640 | tf_op jit(solution)/shard_map/all_to_all | solution.py:573
  57.3 2.9 %collective-permute-start.11 = (bf16[96,8,128]{2,1,0:T(8,128)(2,1)S(1)}, bf16[96,8,128]{2,1,0:T(8,128)(2,1)S(1)}, u32[]{:S(2)}, u32[]{:S(2)}) collective-permute-start(bf16[96,8,128]{2,1,0:T(8,128)(2,1)S(1)} %bitcast.12), channel_id=1, source_target_pairs={{0,4},{4,0},{1,5},{5,1},{2,6},{6,2},{3,7},{7,3},{8,12},{12,8},{9,1... | collective-permute-start | bytes 589832 | tf_op jit(solution)/shard_map/ppermute | solution.py:575
  60.2 0.5 collective-permute-start.10
  60.8 1.1 %collective-permute-start.9 = (bf16[64,8,128]{2,1,0:T(8,128)(2,1)S(1)}, bf16[64,8,128]{2,1,0:T(8,128)(2,1)S(1)}, u32[]{:S(2)}, u32[]{:S(2)}) collective-permute-start(bf16[64,8,128]{2,1,0:T(8,128)(2,1)S(1)} %collective-permute-done.5.refs_2_), channel_id=1, source_target_pairs={{0,4},{4,0},{1,5},{5,1},{2,6},{6,2},{3,7},{7,3},{8,12},{12,8},{9,1... | collective-permute-start | bytes 393224 | tf_op jit(solution)/shard_map/ppermute | solution.py:570
  61.9 0.2 collective-permute-done.8.refs_5_
  62.1 0.8 collective-permute-done.9.refs_6_
  62.9 2.8 %shard_map.102 = (f32[4,8,384]{2,1,0:T(8,128)S(1)}, bf16[3,8,128,128]{3,2,1,0:T(8,128)(2,1)S(1)}, bf16[384,256]{1,0:T(8,128)(2,1)S(1)}) custom-call(s32[1,128]{1,0:T(1,128)S(4)} %get-tuple-element.24.spots, s32[3,128]{1,0:T(4,128)S(4)} %get-tuple-element.23.table, bf16[64,8,128]{2,1,0:T(8,128)(2,1)} %get-tuple-element.31.refs_0_, ...), custom_call_target="tpu_custom_call" | custom-call | tf_op jit(solution)/shard_map/pallas_call | solution.py:420
  65.6 1.4 %shard_map.103 = (bf16[2,8,384]{2,1,0:T(8,128)(2,1)}, f32[64,128]{1,0:T(8,128)S(1)}) custom-call(s32[3,128]{1,0:T(4,128)S(4)} %get-tuple-element.23.table, f32[4,8,384]{2,1,0:T(8,128)S(1)} %get-tuple-element.39.packed, bf16[3,8,128,128]{3,2,1,0:T(8,128)(2,1)S(1)} %get-tuple-element.40.fresh, bf16[3,128,128]{2,1,0:T(8,128)(2,1)S(1)} %get-tuple-element.37.zinv, ...), custom_call_target="tpu_custom_call" | custom-call | tf_op jit(solution)/shard_map/pallas_call | solution.py:504
  67.1 16.8 %all_to_all.20 = f32[64,1,128]{2,1,0:T(1,128)S(1)} all-to-all(f32[64,1,128]{2,1,0:T(1,128)S(1)} %bitcast.15), channel_id=1, replica_groups=mesh['y'=4,'z'=8,'c'=2,'dir'=4] {'y','z','c'}, dimensions={0} | all-to-all | bytes 65536 | tf_op jit(solution)/shard_map/all_to_all | solution.py:578
  83.9 0.7 shard_map.104
  (13 shorter events, 0.2 us)
Async XLA Ops:
  2.2 23.3 %all-to-all-start = ((bf16[8,8,3,8,128]{4,3,2,1,0:T(8,128)(2,1)}), bf16[8,8,3,8,128]{4,3,2,1,0:T(8,128)(2,1)S(1)}, u32[]{:S(2)}, u32[]{:S(2)}) async-start(bf16[8,8,3,8,128]{4,3,2,1,0:T(8,128)(2,1)} %get-tuple-element.30), calls=%async_computation | async-start | bytes 786432 | tf_op jit(solution)/shard_map/all_to_all | solution.py:561
  11.3 1.8 %collective-permute-start = (s32[1,256]{1,0:T(1,128)S(1)}, s32[1,256]{1,0:T(1,128)S(1)}, u32[]{:S(2)}, u32[]{:S(2)}) collective-permute-start(s32[1,256]{1,0:T(1,128)S(1)} %get-tuple-element.25), channel_id=1, source_target_pairs={{0,4},{4,0},{1,5},{5,1},{2,6},{6,2},{3,7},{7,3},{8,12},{12,8},{9,1... | collective-permute-start | bytes 3080 | tf_op jit(solution)/shard_map/ppermute | solution.py:563
  13.0 5.0 %collective-permute-start.1 = (s32[1,512]{1,0:T(1,128)S(1)}, s32[1,512]{1,0:T(1,128)S(1)}, u32[]{:S(2)}, u32[]{:S(2)}) collective-permute-start(s32[1,512]{1,0:T(1,128)S(1)} %constant_dynamic-update-slice_fusion.refs_0_), channel_id=1, source_target_pairs={{0,64},{64,128},{128,192},{192,0},{1,65},{65,129},{129,193},{193,1... | collective-permute-start | bytes 6152 | tf_op jit(solution)/shard_map/ppermute | solution.py:552
  14.3 3.9 %collective-permute-start.2 = (s32[1,512]{1,0:T(1,128)S(1)}, s32[1,512]{1,0:T(1,128)S(1)}, u32[]{:S(2)}, u32[]{:S(2)}) collective-permute-start(s32[1,512]{1,0:T(1,128)S(1)} %constant_dynamic-update-slice_fusion.refs_0_), channel_id=1, source_target_pairs={{0,128},{64,192},{128,0},{192,64},{1,129},{65,193},{129,1},{193,65... | collective-permute-start | bytes 6152 | tf_op jit(solution)/shard_map/ppermute | solution.py:552
  17.0 2.7 %collective-permute-start.3 = (s32[1,512]{1,0:T(1,128)S(1)}, s32[1,512]{1,0:T(1,128)S(1)}, u32[]{:S(2)}, u32[]{:S(2)}) collective-permute-start(s32[1,512]{1,0:T(1,128)S(1)} %constant_dynamic-update-slice_fusion.refs_0_), channel_id=1, source_target_pairs={{0,192},{64,0},{128,64},{192,128},{1,193},{65,1},{129,65},{193,129... | collective-permute-start | bytes 6152 | tf_op jit(solution)/shard_map/ppermute | solution.py:552
  26.6 15.2 %all-to-all-start.1 = ((bf16[8,32,8,128]{3,2,1,0:T(8,128)(2,1)}), bf16[8,32,8,128]{3,2,1,0:T(8,128)(2,1)S(1)}, u32[]{:S(2)}, u32[]{:S(2)}) async-start(bf16[8,32,8,128]{3,2,1,0:T(8,128)(2,1)} %bitcast.16), calls=%async_computation.1 | async-start | bytes 1048576 | tf_op jit(solution)/shard_map/all_to_all | solution.py:567
  44.0 13.3 %all-to-all-start.2 = ((bf16[32,3,8,128]{3,2,1,0:T(8,128)(2,1)}), bf16[32,3,8,128]{3,2,1,0:T(8,128)(2,1)S(1)}, u32[]{:S(2)}, u32[]{:S(2)}) async-start(bf16[32,3,8,128]{3,2,1,0:T(8,128)(2,1)} %shard_map.101.refs_8_), calls=%async_computation.2 | async-start | bytes 393216 | tf_op jit(solution)/shard_map/all_to_all | solution.py:573
  49.1 11.0 %collective-permute-start.6 = (bf16[64,8,128]{2,1,0:T(8,128)(2,1)}, bf16[64,8,128]{2,1,0:T(8,128)(2,1)S(1)}, u32[]{:S(2)}, u32[]{:S(2)}) collective-permute-start(bf16[64,8,128]{2,1,0:T(8,128)(2,1)} %get-tuple-element.34), channel_id=1, source_target_pairs={{0,64},{64,128},{128,192},{192,0},{1,65},{65,129},{129,193},{193,1... | collective-permute-start | bytes 393224 | tf_op jit(solution)/shard_map/ppermute | solution.py:552
  50.4 10.3 %collective-permute-start.4 = (bf16[64,8,128]{2,1,0:T(8,128)(2,1)}, bf16[64,8,128]{2,1,0:T(8,128)(2,1)S(1)}, u32[]{:S(2)}, u32[]{:S(2)}) collective-permute-start(bf16[64,8,128]{2,1,0:T(8,128)(2,1)} %get-tuple-element.32), channel_id=1, source_target_pairs={{0,192},{64,0},{128,64},{192,128},{1,193},{65,1},{129,65},{193,129... | collective-permute-start | bytes 393224 | tf_op jit(solution)/shard_map/ppermute | solution.py:552
  51.9 8.9 %collective-permute-start.5 = (bf16[64,8,128]{2,1,0:T(8,128)(2,1)}, bf16[64,8,128]{2,1,0:T(8,128)(2,1)S(1)}, u32[]{:S(2)}, u32[]{:S(2)}) collective-permute-start(bf16[64,8,128]{2,1,0:T(8,128)(2,1)} %get-tuple-element.33), channel_id=1, source_target_pairs={{0,128},{64,192},{128,0},{192,64},{1,129},{65,193},{129,1},{193,65... | collective-permute-start | bytes 393224 | tf_op jit(solution)/shard_map/ppermute | solution.py:552
  57.3 8.4 %collective-permute-start.11 = (bf16[96,8,128]{2,1,0:T(8,128)(2,1)S(1)}, bf16[96,8,128]{2,1,0:T(8,128)(2,1)S(1)}, u32[]{:S(2)}, u32[]{:S(2)}) collective-permute-start(bf16[96,8,128]{2,1,0:T(8,128)(2,1)S(1)} %bitcast.12), channel_id=1, source_target_pairs={{0,4},{4,0},{1,5},{5,1},{2,6},{6,2},{3,7},{7,3},{8,12},{12,8},{9,1... | collective-permute-start | bytes 589832 | tf_op jit(solution)/shard_map/ppermute | solution.py:575
  60.2 1.7 %collective-permute-start.7 = (bf16[64,8,128]{2,1,0:T(8,128)(2,1)}, bf16[64,8,128]{2,1,0:T(8,128)(2,1)S(1)}, u32[]{:S(2)}, u32[]{:S(2)}) collective-permute-start(bf16[64,8,128]{2,1,0:T(8,128)(2,1)} %get-tuple-element.31.refs_0_), channel_id=1, source_target_pairs={{0,4},{4,0},{1,5},{5,1},{2,6},{6,2},{3,7},{7,3},{8,12},{12,8},{9,1... | collective-permute-start | bytes 393224 | tf_op jit(solution)/shard_map/ppermute | solution.py:569
  60.2 1.7 %collective-permute-start.10 = (bf16[64,8,128]{2,1,0:T(8,128)(2,1)S(1)}, bf16[64,8,128]{2,1,0:T(8,128)(2,1)S(1)}, u32[]{:S(2)}, u32[]{:S(2)}) collective-permute-start(bf16[64,8,128]{2,1,0:T(8,128)(2,1)S(1)} %collective-permute-done.6.refs_3_), channel_id=1, source_target_pairs={{0,4},{4,0},{1,5},{5,1},{2,6},{6,2},{3,7},{7,3},{8,12},{12,8},{9,1... | collective-permute-start | bytes 393224 | tf_op jit(solution)/shard_map/ppermute | solution.py:570
  60.7 1.4 %collective-permute-start.8 = (bf16[64,8,128]{2,1,0:T(8,128)(2,1)S(1)}, bf16[64,8,128]{2,1,0:T(8,128)(2,1)S(1)}, u32[]{:S(2)}, u32[]{:S(2)}) collective-permute-start(bf16[64,8,128]{2,1,0:T(8,128)(2,1)S(1)} %collective-permute-done.4.refs_1_), channel_id=1, source_target_pairs={{0,4},{4,0},{1,5},{5,1},{2,6},{6,2},{3,7},{7,3},{8,12},{12,8},{9,1... | collective-permute-start | bytes 393224 | tf_op jit(solution)/shard_map/ppermute | solution.py:570
  60.8 2.1 %collective-permute-start.9 = (bf16[64,8,128]{2,1,0:T(8,128)(2,1)S(1)}, bf16[64,8,128]{2,1,0:T(8,128)(2,1)S(1)}, u32[]{:S(2)}, u32[]{:S(2)}) collective-permute-start(bf16[64,8,128]{2,1,0:T(8,128)(2,1)S(1)} %collective-permute-done.5.refs_2_), channel_id=1, source_target_pairs={{0,4},{4,0},{1,5},{5,1},{2,6},{6,2},{3,7},{7,3},{8,12},{12,8},{9,1... | collective-permute-start | bytes 393224 | tf_op jit(solution)/shard_map/ppermute | solution.py:570
  61.9 1.0 %copy-start = (bf16[64,8,128]{2,1,0:T(8,128)(2,1)}, bf16[64,8,128]{2,1,0:T(8,128)(2,1)S(1)}, u32[]{:S(2)}) copy-start(bf16[64,8,128]{2,1,0:T(8,128)(2,1)S(1)} %collective-permute-done.7.refs_4_) | copy-start | bytes 393220

commit v12 on v11

--- a/solution.py
+++ b/solution.py
@@ -304,23 +304,18 @@
                 target[part] = jnp.zeros((CHUNK, *target.shape[1:]), target.dtype)
 
 
-def staged_rows(counts, ztiles_hbm, top, sems, act):
+def stage_kernel(ztiles_hbm, zinv_hbm, incident_hbm, top, zinv, incident, sems):
     slots = ztiles_hbm.shape[1]
+    pairs = []
     for row in range(ztiles_hbm.shape[0]):
         length = min(slots, top.shape[0] - row * slots)
         if length > 0:
-            target = top.at[pl.ds(row * slots, length)]
-            live_tiles(counts[row], ztiles_hbm.at[row, pl.ds(0, length)], target, sems, row, act)
-
-
-def stage_kernel(counts, ztiles_hbm, zinv_hbm, incident_hbm, top, zinv, incident, sems, tile_sems):
-    staged_rows(counts, ztiles_hbm, top, tile_sems, "start")
-    for copy in start_all([(zinv_hbm, zinv), (incident_hbm.at[0], incident)], sems):
-        copy.wait()
-    staged_rows(counts, ztiles_hbm, top, tile_sems, "wait")
-
-
-def stage(counts, ztiles, zinv, incident):
+            pairs.append((ztiles_hbm.at[row, pl.ds(0, length)], top.at[pl.ds(row * slots, length)]))
+    for copy in start_all([*pairs, (zinv_hbm, zinv), (incident_hbm.at[0], incident)], sems):
+        copy.wait()
+
+
+def stage(ztiles, zinv, incident):
     rows, slots, tile = ztiles.shape[0], ztiles.shape[1], ztiles.shape[2]
     return kernel_call(
         stage_kernel,
@@ -330,13 +325,10 @@
             pltpu.VMEM(zinv.shape, zinv.dtype),
             pltpu.VMEM(incident.shape[1:], incident.dtype),
         ),
-        in_specs=[smem()] + [hbm()] * 3,
+        in_specs=[hbm()] * 3,
         out_specs=[vmem()] * 3,
-        scratch_shapes=[
-            pltpu.SemaphoreType.DMA((2,)),
-            pltpu.SemaphoreType.DMA((rows, slots // CHUNK)),
-        ],
-    )(off_core(counts), off_core(ztiles), off_core(zinv), off_core(incident))
+        scratch_shapes=[pltpu.SemaphoreType.DMA((rows + 2,))],
+    )(off_core(ztiles), off_core(zinv), off_core(incident))
 
 
 def first_kernel(spots, got, top, ztiles_hbm, zinv, incident, spread_out, last, kept_out, sems, tile_sems):
@@ -568,7 +560,7 @@
     near = [later[0]] + [shifted(later[s], "y", Y, -s) for s in range(1, Y)]
     cross = [lax.ppermute(near[0], "c", SWAP)]
     cross += [lax.ppermute(piece, "c", SWAP) for piece in near[1:]]
-    top, inverse, driven = stage(counts, ztiles, zinv, incident)
+    top, inverse, driven = stage(ztiles, zinv, incident)
     fanned = first_step(spots, got.reshape(GROUPS * cap, dirs, tile), top, ztiles, inverse, driven)
     here = lax.all_to_all(fanned, ("y", "z"), 0, 0, tiled=True).reshape(Y * Z * rows, dirs, tile)
     packed, lag_one, weights = aged_step(aged, table, fanned, incident, near, cross, ztiles, basis)

time: 85.1 us -> 85.1 us (level)
  transfers between devices with their start and end apart: 15 -> 15, of which waited for: 8 -> 8; matrix products, arithmetic and copies ran while one was open for 0% -> 0% of each run, Pallas kernels for 11% -> 10%
where the time goes in v12:
time: 85.1 us; the launch traced here: 84.6 us
  starting transfers between devices  33.5 us (39%)
  waiting for transfers between devices  18.1 us (21%)
  blocking collectives  16.8 us (20%)
  Pallas kernels  15.4 us (18%)
    all_to_all x1, blocking collectives, march(): lax.all_to_all(far.reshape(owners, 1, 128), E, 0, 0, tiled=True)  16.8 us
    ppermute x6, starting transfers between devices, shifted(): lax.ppermute(value, axis, [(i, (i + shift) % length) for i in range(lengt...  9.25 us
    all_to_all x1, starting transfers between devices, march(): lax.all_to_all(outgoing, 'z', 0, 0, tiled=True).reshape(-1, dirs, tile)  9.02 us
    all_to_all x1, starting transfers between devices, march(): lax.all_to_all(first.reshape(GROUPS, cap, dirs, tile), ('y', 'c'), 0, 0,...  5.86 us
    all_to_all x1, waiting for transfers between devices, march(): lax.all_to_all(first.reshape(GROUPS, cap, dirs, tile), ('y', 'c'), 0, 0,...  5.67 us
    all_to_all x1, waiting for transfers between devices, march(): lax.all_to_all(outgoing, 'z', 0, 0, tiled=True).reshape(-1, dirs, tile)  5.13 us
    all_to_all x1, starting transfers between devices, march(): lax.all_to_all(fanned, ('y', 'z'), 0, 0, tiled=True)  3.88 us
    all_to_all x1, waiting for transfers between devices, march(): lax.all_to_all(fanned, ('y', 'z'), 0, 0, tiled=True)  3.87 us
  transfers between devices with their start and end apart: 15, of which 8 were waited for; matrix products, arithmetic and copies ran while one was open for 0% of the time, Pallas kernels for 10%

profile of v12, /device:TPU:1, one launch (start us, length us, event | category | flops | bytes accessed | tf_op | source)
XLA Modules:
  0.0 84.6 jit_solution(2764780991216920790)
XLA Ops:
  0.6 1.6 %shard_map.96 = (bf16[8,8,3,8,128]{4,3,2,1,0:T(8,128)(2,1)}, s32[1,256]{1,0:T(1,128)S(1)}) custom-call(bf16[8,8,384]{2,1,0:T(8,128)(2,1)} %history.1, s32[3,32]{1,0:T(4,128)} %columns_hbm.1, s32[3,32]{1,0:T(4,128)} %lags_hbm.1), custom_call_target="tpu_custom_call" | custom-call | tf_op jit(solution)/shard_map/pallas_call | solution.py:75
  2.2 9.0 %all-to-all-start = ((bf16[8,8,3,8,128]{4,3,2,1,0:T(8,128)(2,1)}), bf16[8,8,3,8,128]{4,3,2,1,0:T(8,128)(2,1)S(1)}, u32[]{:S(2)}, u32[]{:S(2)}) async-start(bf16[8,8,3,8,128]{4,3,2,1,0:T(8,128)(2,1)} %get-tuple-element.30), calls=%async_computation | async-start | bytes 786432 | tf_op jit(solution)/shard_map/all_to_all | solution.py:553
  11.3 1.0 %collective-permute-start = (s32[1,256]{1,0:T(1,128)S(1)}, s32[1,256]{1,0:T(1,128)S(1)}, u32[]{:S(2)}, u32[]{:S(2)}) collective-permute-start(s32[1,256]{1,0:T(1,128)S(1)} %get-tuple-element.25), channel_id=1, source_target_pairs={{0,4},{4,0},{1,5},{5,1},{2,6},{6,2},{3,7},{7,3},{8,12},{12,8},{9,1... | collective-permute-start | bytes 3080 | tf_op jit(solution)/shard_map/ppermute | solution.py:555
  12.2 0.8 collective-permute-done
  13.0 1.3 %collective-permute-start.1 = (s32[1,512]{1,0:T(1,128)S(1)}, s32[1,512]{1,0:T(1,128)S(1)}, u32[]{:S(2)}, u32[]{:S(2)}) collective-permute-start(s32[1,512]{1,0:T(1,128)S(1)} %constant_dynamic-update-slice_fusion.refs_0_), channel_id=1, source_target_pairs={{0,64},{64,128},{128,192},{192,0},{1,65},{65,129},{129,193},{193,1... | collective-permute-start | bytes 6152 | tf_op jit(solution)/shard_map/ppermute | solution.py:544
  14.3 2.6 %collective-permute-start.2 = (s32[1,512]{1,0:T(1,128)S(1)}, s32[1,512]{1,0:T(1,128)S(1)}, u32[]{:S(2)}, u32[]{:S(2)}) collective-permute-start(s32[1,512]{1,0:T(1,128)S(1)} %constant_dynamic-update-slice_fusion.refs_0_), channel_id=1, source_target_pairs={{0,128},{64,192},{128,0},{192,64},{1,129},{65,193},{129,1},{193,65... | collective-permute-start | bytes 6152 | tf_op jit(solution)/shard_map/ppermute | solution.py:544
  17.0 1.1 %collective-permute-start.3 = (s32[1,512]{1,0:T(1,128)S(1)}, s32[1,512]{1,0:T(1,128)S(1)}, u32[]{:S(2)}, u32[]{:S(2)}) collective-permute-start(s32[1,512]{1,0:T(1,128)S(1)} %constant_dynamic-update-slice_fusion.refs_0_), channel_id=1, source_target_pairs={{0,192},{64,0},{128,64},{192,128},{1,193},{65,1},{129,65},{193,129... | collective-permute-start | bytes 6152 | tf_op jit(solution)/shard_map/ppermute | solution.py:544
  18.0 0.2 collective-permute-done.2.refs_2_
  18.3 1.4 %collective-permute-done.3.refs_3_ = s32[1,512]{1,0:T(1,128)S(1)} collective-permute-done((s32[1,512]{1,0:T(1,128)S(1)}, s32[1,512]{1,0:T(1,128)S(1)}, u32[]{:S(2)}, u32[]{:S(2)}) %collective-permute-start.3) | collective-permute-done | bytes 2080 | tf_op jit(solution)/shard_map/ppermute | solution.py:544
  19.7 0.7 shard_map.97
  20.4 5.1 %all-to-all-done = bf16[8,8,3,8,128]{4,3,2,1,0:T(8,128)(2,1)S(1)} async-done(((bf16[8,8,3,8,128]{4,3,2,1,0:T(8,128)(2,1)}), bf16[8,8,3,8,128]{4,3,2,1,0:T(8,128)(2,1)S(1)}, u32[]{:S(2)}, u32[]{:S(2)}) %all-to-all-start) | async-done | bytes 393248 | tf_op jit(solution)/shard_map/all_to_all | solution.py:553
  25.5 1.1 %shard_map.99 = bf16[256,8,128]{2,1,0:T(8,128)(2,1)} custom-call(s32[1,512]{1,0:T(1,128)S(4)} %get-tuple-element.26.refs_0_, s32[1,512]{1,0:T(1,128)S(4)} %get-tuple-element.27.refs_1_, s32[1,512]{1,0:T(1,128)S(4)} %get-tuple-element.28.refs_2_, s32[1,512]{1,0:T(1,128)S(4)} %get-tuple-element.29.refs_3_, bf16[192,8,128]{2,1,0:T(8,128)(2,1)S(1)} %bitcast.9), custom_call_target="tpu_custom_call" | custom-call | tf_op jit(solution)/shard_map/pallas_call | solution.py:235
  26.6 5.9 %all-to-all-start.1 = ((bf16[8,32,8,128]{3,2,1,0:T(8,128)(2,1)}), bf16[8,32,8,128]{3,2,1,0:T(8,128)(2,1)S(1)}, u32[]{:S(2)}, u32[]{:S(2)}) async-start(bf16[8,32,8,128]{3,2,1,0:T(8,128)(2,1)} %bitcast.16), calls=%async_computation.1 | async-start | bytes 1048576 | tf_op jit(solution)/shard_map/all_to_all | solution.py:559
  32.5 2.0 %shard_map.95 = (s32[1,128]{1,0:T(1,128)S(4)}, s32[1,128]{1,0:T(1,128)S(4)}, s32[3,128]{1,0:T(4,128)S(4)}) custom-call(s32[3]{0:T(128)} %counts.1, s32[3,32]{1,0:T(4,128)} %columns_hbm.1, s32[3,32]{1,0:T(4,128)} %lags_hbm.1), custom_call_target="tpu_custom_call" | custom-call | tf_op jit(solution)/shard_map/pallas_call | solution.py:154
  34.5 1.7 %shard_map.100 = (bf16[72,128,128]{2,1,0:T(8,128)(2,1)S(1)}, bf16[3,128,128]{2,1,0:T(8,128)(2,1)S(1)}, bf16[8,384]{1,0:T(8,128)(2,1)S(1)}) custom-call(bf16[3,32,128,128]{3,2,1,0:T(8,128)(2,1)} %ztiles_hbm.5, bf16[3,128,128]{2,1,0:T(8,128)(2,1)} %zinv_hbm.1, bf16[2,8,384]{2,1,0:T(8,128)(2,1)} %refs_9_.1), custom_call_target="tpu_custom_call" | custom-call | tf_op jit(solution)/shard_map/pallas_call | solution.py:320
  36.2 5.7 %all-to-all-done.1 = bf16[8,32,8,128]{3,2,1,0:T(8,128)(2,1)S(1)} async-done(((bf16[8,32,8,128]{3,2,1,0:T(8,128)(2,1)}), bf16[8,32,8,128]{3,2,1,0:T(8,128)(2,1)S(1)}, u32[]{:S(2)}, u32[]{:S(2)}) %all-to-all-start.1) | async-done | bytes 524320 | tf_op jit(solution)/shard_map/all_to_all | solution.py:559
  41.8 2.2 %shard_map.101.refs_8_ = bf16[32,3,8,128]{3,2,1,0:T(8,128)(2,1)} custom-call(s32[1,128]{1,0:T(1,128)S(4)} %get-tuple-element.35.spots, bf16[256,8,128]{2,1,0:T(8,128)(2,1)S(1)} %bitcast.11, bf16[72,128,128]{2,1,0:T(8,128)(2,1)S(1)} %get-tuple-element.36.top, bf16[3,32,128,128]{3,2,1,0:T(8,128)(2,1)} %ztiles_hbm.5, ...), custom_call_target="tpu_custom_call" | custom-call | tf_op jit(solution)/shard_map/pallas_call | solution.py:358
  44.0 3.9 %all-to-all-start.2 = ((bf16[32,3,8,128]{3,2,1,0:T(8,128)(2,1)}), bf16[32,3,8,128]{3,2,1,0:T(8,128)(2,1)S(1)}, u32[]{:S(2)}, u32[]{:S(2)}) async-start(bf16[32,3,8,128]{3,2,1,0:T(8,128)(2,1)} %shard_map.101.refs_8_), calls=%async_computation.2 | async-start | bytes 393216 | tf_op jit(solution)/shard_map/all_to_all | solution.py:565
  47.9 1.3 %shard_map.98 = (bf16[64,8,128]{2,1,0:T(8,128)(2,1)}, bf16[64,8,128]{2,1,0:T(8,128)(2,1)}, bf16[64,8,128]{2,1,0:T(8,128)(2,1)}, bf16[64,8,128]{2,1,0:T(8,128)(2,1)}) custom-call(s32[1,512]{1,0:T(1,128)S(4)} %get-tuple-element.26.refs_0_, s32[1,512]{1,0:T(1,128)S(4)} %get-tuple-element.27.refs_1_, s32[1,512]{1,0:T(1,128)S(4)} %get-tuple-element.28.refs_2_, ...), custom_call_target="tpu_custom_call" | custom-call | tf_op jit(solution)/shard_map/pallas_call | solution.py:246
  49.1 1.2 %collective-permute-start.6 = (bf16[64,8,128]{2,1,0:T(8,128)(2,1)}, bf16[64,8,128]{2,1,0:T(8,128)(2,1)S(1)}, u32[]{:S(2)}, u32[]{:S(2)}) collective-permute-start(bf16[64,8,128]{2,1,0:T(8,128)(2,1)} %get-tuple-element.34), channel_id=1, source_target_pairs={{0,64},{64,128},{128,192},{192,0},{1,65},{65,129},{129,193},{193,1... | collective-permute-start | bytes 393224 | tf_op jit(solution)/shard_map/ppermute | solution.py:544
  50.4 1.5 %collective-permute-start.4 = (bf16[64,8,128]{2,1,0:T(8,128)(2,1)}, bf16[64,8,128]{2,1,0:T(8,128)(2,1)S(1)}, u32[]{:S(2)}, u32[]{:S(2)}) collective-permute-start(bf16[64,8,128]{2,1,0:T(8,128)(2,1)} %get-tuple-element.32), channel_id=1, source_target_pairs={{0,192},{64,0},{128,64},{192,128},{1,193},{65,1},{129,65},{193,129... | collective-permute-start | bytes 393224 | tf_op jit(solution)/shard_map/ppermute | solution.py:544
  51.9 1.5 %collective-permute-start.5 = (bf16[64,8,128]{2,1,0:T(8,128)(2,1)}, bf16[64,8,128]{2,1,0:T(8,128)(2,1)S(1)}, u32[]{:S(2)}, u32[]{:S(2)}) collective-permute-start(bf16[64,8,128]{2,1,0:T(8,128)(2,1)} %get-tuple-element.33), channel_id=1, source_target_pairs={{0,128},{64,192},{128,0},{192,64},{1,129},{65,193},{129,1},{193,65... | collective-permute-start | bytes 393224 | tf_op jit(solution)/shard_map/ppermute | solution.py:544
  53.4 3.9 %all-to-all-done.2 = bf16[32,3,8,128]{3,2,1,0:T(8,128)(2,1)S(1)} async-done(((bf16[32,3,8,128]{3,2,1,0:T(8,128)(2,1)}), bf16[32,3,8,128]{3,2,1,0:T(8,128)(2,1)S(1)}, u32[]{:S(2)}, u32[]{:S(2)}) %all-to-all-start.2) | async-done | bytes 196640 | tf_op jit(solution)/shard_map/all_to_all | solution.py:565
  57.3 2.9 %collective-permute-start.11 = (bf16[96,8,128]{2,1,0:T(8,128)(2,1)S(1)}, bf16[96,8,128]{2,1,0:T(8,128)(2,1)S(1)}, u32[]{:S(2)}, u32[]{:S(2)}) collective-permute-start(bf16[96,8,128]{2,1,0:T(8,128)(2,1)S(1)} %bitcast.12), channel_id=1, source_target_pairs={{0,4},{4,0},{1,5},{5,1},{2,6},{6,2},{3,7},{7,3},{8,12},{12,8},{9,1... | collective-permute-start | bytes 589832 | tf_op jit(solution)/shard_map/ppermute | solution.py:567
  60.2 0.5 collective-permute-start.10
  60.8 1.1 %collective-permute-start.9 = (bf16[64,8,128]{2,1,0:T(8,128)(2,1)S(1)}, bf16[64,8,128]{2,1,0:T(8,128)(2,1)S(1)}, u32[]{:S(2)}, u32[]{:S(2)}) collective-permute-start(bf16[64,8,128]{2,1,0:T(8,128)(2,1)S(1)} %collective-permute-done.5.refs_2_), channel_id=1, source_target_pairs={{0,4},{4,0},{1,5},{5,1},{2,6},{6,2},{3,7},{7,3},{8,12},{12,8},{9,1... | collective-permute-start | bytes 393224 | tf_op jit(solution)/shard_map/ppermute | solution.py:562
  61.9 0.2 collective-permute-done.8.refs_5_
  62.1 0.8 collective-permute-done.9.refs_6_
  62.9 2.8 %shard_map.102 = (f32[4,8,384]{2,1,0:T(8,128)S(1)}, bf16[3,8,128,128]{3,2,1,0:T(8,128)(2,1)S(1)}, bf16[384,256]{1,0:T(8,128)(2,1)S(1)}) custom-call(s32[1,128]{1,0:T(1,128)S(4)} %get-tuple-element.24.spots, s32[3,128]{1,0:T(4,128)S(4)} %get-tuple-element.23.table, bf16[64,8,128]{2,1,0:T(8,128)(2,1)} %get-tuple-element.31.refs_0_, ...), custom_call_target="tpu_custom_call" | custom-call | tf_op jit(solution)/shard_map/pallas_call | solution.py:412
  65.6 1.4 %shard_map.103 = (bf16[2,8,384]{2,1,0:T(8,128)(2,1)}, f32[64,128]{1,0:T(8,128)S(1)}) custom-call(s32[3,128]{1,0:T(4,128)S(4)} %get-tuple-element.23.table, f32[4,8,384]{2,1,0:T(8,128)S(1)} %get-tuple-element.39.packed, bf16[3,8,128,128]{3,2,1,0:T(8,128)(2,1)S(1)} %get-tuple-element.40.fresh, bf16[3,128,128]{2,1,0:T(8,128)(2,1)S(1)} %get-tuple-element.37.zinv, ...), custom_call_target="tpu_custom_call" | custom-call | tf_op jit(solution)/shard_map/pallas_call | solution.py:496
  67.1 16.8 %all_to_all.20 = f32[64,1,128]{2,1,0:T(1,128)S(1)} all-to-all(f32[64,1,128]{2,1,0:T(1,128)S(1)} %bitcast.15), channel_id=1, replica_groups=mesh['y'=4,'z'=8,'c'=2,'dir'=4] {'y','z','c'}, dimensions={0} | all-to-all | bytes 65536 | tf_op jit(solution)/shard_map/all_to_all | solution.py:570
  83.9 0.7 shard_map.104
  (13 shorter events, 0.2 us)
Async XLA Ops:
  2.2 23.3 %all-to-all-start = ((bf16[8,8,3,8,128]{4,3,2,1,0:T(8,128)(2,1)}), bf16[8,8,3,8,128]{4,3,2,1,0:T(8,128)(2,1)S(1)}, u32[]{:S(2)}, u32[]{:S(2)}) async-start(bf16[8,8,3,8,128]{4,3,2,1,0:T(8,128)(2,1)} %get-tuple-element.30), calls=%async_computation | async-start | bytes 786432 | tf_op jit(solution)/shard_map/all_to_all | solution.py:553
  11.3 1.8 %collective-permute-start = (s32[1,256]{1,0:T(1,128)S(1)}, s32[1,256]{1,0:T(1,128)S(1)}, u32[]{:S(2)}, u32[]{:S(2)}) collective-permute-start(s32[1,256]{1,0:T(1,128)S(1)} %get-tuple-element.25), channel_id=1, source_target_pairs={{0,4},{4,0},{1,5},{5,1},{2,6},{6,2},{3,7},{7,3},{8,12},{12,8},{9,1... | collective-permute-start | bytes 3080 | tf_op jit(solution)/shard_map/ppermute | solution.py:555
  13.0 5.0 %collective-permute-start.1 = (s32[1,512]{1,0:T(1,128)S(1)}, s32[1,512]{1,0:T(1,128)S(1)}, u32[]{:S(2)}, u32[]{:S(2)}) collective-permute-start(s32[1,512]{1,0:T(1,128)S(1)} %constant_dynamic-update-slice_fusion.refs_0_), channel_id=1, source_target_pairs={{0,64},{64,128},{128,192},{192,0},{1,65},{65,129},{129,193},{193,1... | collective-permute-start | bytes 6152 | tf_op jit(solution)/shard_map/ppermute | solution.py:544
  14.3 3.9 %collective-permute-start.2 = (s32[1,512]{1,0:T(1,128)S(1)}, s32[1,512]{1,0:T(1,128)S(1)}, u32[]{:S(2)}, u32[]{:S(2)}) collective-permute-start(s32[1,512]{1,0:T(1,128)S(1)} %constant_dynamic-update-slice_fusion.refs_0_), channel_id=1, source_target_pairs={{0,128},{64,192},{128,0},{192,64},{1,129},{65,193},{129,1},{193,65... | collective-permute-start | bytes 6152 | tf_op jit(solution)/shard_map/ppermute | solution.py:544
  17.0 2.7 %collective-permute-start.3 = (s32[1,512]{1,0:T(1,128)S(1)}, s32[1,512]{1,0:T(1,128)S(1)}, u32[]{:S(2)}, u32[]{:S(2)}) collective-permute-start(s32[1,512]{1,0:T(1,128)S(1)} %constant_dynamic-update-slice_fusion.refs_0_), channel_id=1, source_target_pairs={{0,192},{64,0},{128,64},{192,128},{1,193},{65,1},{129,65},{193,129... | collective-permute-start | bytes 6152 | tf_op jit(solution)/shard_map/ppermute | solution.py:544
  26.6 15.2 %all-to-all-start.1 = ((bf16[8,32,8,128]{3,2,1,0:T(8,128)(2,1)}), bf16[8,32,8,128]{3,2,1,0:T(8,128)(2,1)S(1)}, u32[]{:S(2)}, u32[]{:S(2)}) async-start(bf16[8,32,8,128]{3,2,1,0:T(8,128)(2,1)} %bitcast.16), calls=%async_computation.1 | async-start | bytes 1048576 | tf_op jit(solution)/shard_map/all_to_all | solution.py:559
  44.0 13.3 %all-to-all-start.2 = ((bf16[32,3,8,128]{3,2,1,0:T(8,128)(2,1)}), bf16[32,3,8,128]{3,2,1,0:T(8,128)(2,1)S(1)}, u32[]{:S(2)}, u32[]{:S(2)}) async-start(bf16[32,3,8,128]{3,2,1,0:T(8,128)(2,1)} %shard_map.101.refs_8_), calls=%async_computation.2 | async-start | bytes 393216 | tf_op jit(solution)/shard_map/all_to_all | solution.py:565
  49.1 11.0 %collective-permute-start.6 = (bf16[64,8,128]{2,1,0:T(8,128)(2,1)}, bf16[64,8,128]{2,1,0:T(8,128)(2,1)S(1)}, u32[]{:S(2)}, u32[]{:S(2)}) collective-permute-start(bf16[64,8,128]{2,1,0:T(8,128)(2,1)} %get-tuple-element.34), channel_id=1, source_target_pairs={{0,64},{64,128},{128,192},{192,0},{1,65},{65,129},{129,193},{193,1... | collective-permute-start | bytes 393224 | tf_op jit(solution)/shard_map/ppermute | solution.py:544
  50.4 10.3 %collective-permute-start.4 = (bf16[64,8,128]{2,1,0:T(8,128)(2,1)}, bf16[64,8,128]{2,1,0:T(8,128)(2,1)S(1)}, u32[]{:S(2)}, u32[]{:S(2)}) collective-permute-start(bf16[64,8,128]{2,1,0:T(8,128)(2,1)} %get-tuple-element.32), channel_id=1, source_target_pairs={{0,192},{64,0},{128,64},{192,128},{1,193},{65,1},{129,65},{193,129... | collective-permute-start | bytes 393224 | tf_op jit(solution)/shard_map/ppermute | solution.py:544
  51.9 8.9 %collective-permute-start.5 = (bf16[64,8,128]{2,1,0:T(8,128)(2,1)}, bf16[64,8,128]{2,1,0:T(8,128)(2,1)S(1)}, u32[]{:S(2)}, u32[]{:S(2)}) collective-permute-start(bf16[64,8,128]{2,1,0:T(8,128)(2,1)} %get-tuple-element.33), channel_id=1, source_target_pairs={{0,128},{64,192},{128,0},{192,64},{1,129},{65,193},{129,1},{193,65... | collective-permute-start | bytes 393224 | tf_op jit(solution)/shard_map/ppermute | solution.py:544
  57.3 8.4 %collective-permute-start.11 = (bf16[96,8,128]{2,1,0:T(8,128)(2,1)S(1)}, bf16[96,8,128]{2,1,0:T(8,128)(2,1)S(1)}, u32[]{:S(2)}, u32[]{:S(2)}) collective-permute-start(bf16[96,8,128]{2,1,0:T(8,128)(2,1)S(1)} %bitcast.12), channel_id=1, source_target_pairs={{0,4},{4,0},{1,5},{5,1},{2,6},{6,2},{3,7},{7,3},{8,12},{12,8},{9,1... | collective-permute-start | bytes 589832 | tf_op jit(solution)/shard_map/ppermute | solution.py:567
  60.2 1.7 %collective-permute-start.7 = (bf16[64,8,128]{2,1,0:T(8,128)(2,1)}, bf16[64,8,128]{2,1,0:T(8,128)(2,1)S(1)}, u32[]{:S(2)}, u32[]{:S(2)}) collective-permute-start(bf16[64,8,128]{2,1,0:T(8,128)(2,1)} %get-tuple-element.31.refs_0_), channel_id=1, source_target_pairs={{0,4},{4,0},{1,5},{5,1},{2,6},{6,2},{3,7},{7,3},{8,12},{12,8},{9,1... | collective-permute-start | bytes 393224 | tf_op jit(solution)/shard_map/ppermute | solution.py:561
  60.2 1.7 %collective-permute-start.10 = (bf16[64,8,128]{2,1,0:T(8,128)(2,1)S(1)}, bf16[64,8,128]{2,1,0:T(8,128)(2,1)S(1)}, u32[]{:S(2)}, u32[]{:S(2)}) collective-permute-start(bf16[64,8,128]{2,1,0:T(8,128)(2,1)S(1)} %collective-permute-done.6.refs_3_), channel_id=1, source_target_pairs={{0,4},{4,0},{1,5},{5,1},{2,6},{6,2},{3,7},{7,3},{8,12},{12,8},{9,1... | collective-permute-start | bytes 393224 | tf_op jit(solution)/shard_map/ppermute | solution.py:562
  60.7 1.4 %collective-permute-start.8 = (bf16[64,8,128]{2,1,0:T(8,128)(2,1)S(1)}, bf16[64,8,128]{2,1,0:T(8,128)(2,1)S(1)}, u32[]{:S(2)}, u32[]{:S(2)}) collective-permute-start(bf16[64,8,128]{2,1,0:T(8,128)(2,1)S(1)} %collective-permute-done.4.refs_1_), channel_id=1, source_target_pairs={{0,4},{4,0},{1,5},{5,1},{2,6},{6,2},{3,7},{7,3},{8,12},{12,8},{9,1... | collective-permute-start | bytes 393224 | tf_op jit(solution)/shard_map/ppermute | solution.py:562
  60.8 2.1 %collective-permute-start.9 = (bf16[64,8,128]{2,1,0:T(8,128)(2,1)S(1)}, bf16[64,8,128]{2,1,0:T(8,128)(2,1)S(1)}, u32[]{:S(2)}, u32[]{:S(2)}) collective-permute-start(bf16[64,8,128]{2,1,0:T(8,128)(2,1)S(1)} %collective-permute-done.5.refs_2_), channel_id=1, source_target_pairs={{0,4},{4,0},{1,5},{5,1},{2,6},{6,2},{3,7},{7,3},{8,12},{12,8},{9,1... | collective-permute-start | bytes 393224 | tf_op jit(solution)/shard_map/ppermute | solution.py:562
  61.9 1.0 %copy-start = (bf16[64,8,128]{2,1,0:T(8,128)(2,1)}, bf16[64,8,128]{2,1,0:T(8,128)(2,1)S(1)}, u32[]{:S(2)}) copy-start(bf16[64,8,128]{2,1,0:T(8,128)(2,1)S(1)} %collective-permute-done.7.refs_4_) | copy-start | bytes 393220
